TPU v7x, 32 devices: a whole 2x2x4 slice. The times are simulated.
32 devices in a mesh: space: 4 (over y, core), shard: 8 (over z, x).
Axes of the slice: x: 2, y: 2, z: 4, core: 2. Of those that a mesh axis runs over, the one named last changes fastest.
Arguments:
- volume_field: float32 [2, 16, 16, 128, 128], P(None, None, 'space', 'shard'), may hold values from -6 to 6
- source: float32 [2, 16, 16, 128, 128], P(None, None, 'space', 'shard'), may hold values from -6 to 6
- material: int32 [16, 128, 128], P('space', 'shard'), may hold values from 0 to 7
- mat_real: float32 [8], replicated, may hold values from 0.5 to 4
- mat_loss: float32 [8], replicated, may hold values from 0.1 to 1.5
- surface_map: int32 [512, 128], P(('space', 'shard')), may hold values from 0 to 8191
- near_boxes: int32 [512, 4], P(('space', 'shard')), may hold values from 0 to 511, as said below
- near_blocks: bfloat16 [4, 256, 256], replicated, may hold values from -0.1875 to 0.1875
- radiate: bfloat16 [2, 128, 512], replicated, may hold values from -0.375 to 0.375
- interp: bfloat16 [512, 2048], replicated, may hold values from -0.25 to 0.25
- phase_angle: float32 [8, 2048], replicated, may hold values from -3.140625 to 3.140625
- far_parents: int32 [64, 8], replicated, may hold values from 0 to 63
- far_kind: int32 [64, 8], replicated, may hold values from 0 to 315
- translate: float32 [316, 2, 2048], P(None, None, 'shard'), may hold values from -0.18 to 0.18
Outputs:
- volume_out: float32 [2, 16, 16, 128, 128], P(None, None, 'space', 'shard')
- forcing: float32 [512, 16, 256], P(('space', 'shard'))
Inputs may be any that keep to these rules, and one draw needn't show every extreme that they name: near_boxes[b, 0] = b; every other entry is a box of the same group of 128 boxes (boxes g * 128 to (g + 1) * 128 - 1) whose index lies from 16 below to 31 above the first box of b's run of 16 boxes.
All inputs are finite; a program needn't handle non-finite values.
Results may differ from a plain program's by a relative error of at most 0.015.
Values may be sent and summed in bfloat16 or wider, within the bound.
No kernel may reach another device: no remote copies, remote signals or barrier semaphores. Data moves between devices by JAX's collectives and lax.ppermute only.
A program may use at most 128 MiB of HBM per device.

v0:
```python
import math

import jax
import jax.numpy as jnp
from jax import lax
from jax.sharding import PartitionSpec as P

relaxation = 0.8


def padded_2(array, sides, width):
    for axis, dim in sides:
        peers, length = (lax.axis_size(axis), array.shape[dim])
        up = [(i, (i + 1) % peers) for i in range(peers - 1)]
        down = [(j, i) for i, j in up]
        last = lax.slice_in_dim(array, length - width, length, axis=dim)
        leading = lax.slice_in_dim(array, 0, width, axis=dim)
        before = lax.ppermute(last, axis, up)
        after = lax.ppermute(leading, axis, down)
        array = jnp.concatenate([before, array, after], axis=dim)
    return array


def neighbour_sum(padded):
    core = padded[:, :, 1:-1, 1:-1]
    result = padded[:, :, 2:, 1:-1] + padded[:, :, :-2, 1:-1]
    result = result + padded[:, :, 1:-1, 2:] + padded[:, :, 1:-1, :-2]
    zero_layer = jnp.zeros(core.shape[:-1] + (1,), core.dtype)
    upper = jnp.concatenate([core[..., 1:], zero_layer], axis=-1)
    lower = jnp.concatenate([zero_layer, core[..., :-1]], axis=-1)
    return result + upper + lower


def relax_sweep(current, neighbours, source, diagonal_coef, loss_coef):
    real_part = diagonal_coef * current[0] - neighbours[0] - loss_coef * current[1]
    imag_part = diagonal_coef * current[1] - neighbours[1] + loss_coef * current[0]
    applied = jnp.stack([real_part, imag_part])
    return current + relaxation * (source - applied) / diagonal_coef


def block_matrix(radiate):
    upper = jnp.concatenate([radiate[0], radiate[1]], axis=1)
    lower = jnp.concatenate([-radiate[1], radiate[0]], axis=1)
    return jnp.concatenate([upper, lower], axis=0)


def aggregate(leaf_rows, interp, cosine, sine_part):
    parent_count = leaf_rows.shape[0] // 8
    excite = leaf_rows.shape[1]
    spread = jnp.dot(
        leaf_rows.reshape(-1, interp.shape[0]), interp, preferred_element_type=jnp.float32
    )
    spread = spread.reshape(parent_count, 8, excite, 2, interp.shape[1])
    cosine_wide = cosine[None, :, None, :]
    sine_wide = sine_part[None, :, None, :]
    real_part = jnp.sum(cosine_wide * spread[:, :, :, 0] - sine_wide * spread[:, :, :, 1], axis=1)
    imag_part = jnp.sum(sine_wide * spread[:, :, :, 0] + cosine_wide * spread[:, :, :, 1], axis=1)
    return jnp.stack([real_part, imag_part], axis=2).astype(jnp.bfloat16)


def combine_far(sources, table):
    real_table = table[:, :, None, 0]
    imag_table = table[:, :, None, 1]
    real_part = jnp.sum(real_table * sources[:, :, :, 0] - imag_table * sources[:, :, :, 1], axis=1)
    imag_part = jnp.sum(imag_table * sources[:, :, :, 0] + real_table * sources[:, :, :, 1], axis=1)
    return jnp.stack([real_part, imag_part], axis=2)


def disaggregate(incoming_rows, interp, cosine, sine_part, weights):
    parent_count = incoming_rows.shape[0]
    excite = incoming_rows.shape[1]
    widened = incoming_rows.astype(jnp.float32)[:, None]
    cosine_wide = cosine[None, :, None, :]
    sine_wide = sine_part[None, :, None, :]
    real_part = cosine_wide * widened[:, :, :, 0] + sine_wide * widened[:, :, :, 1]
    imag_part = cosine_wide * widened[:, :, :, 1] - sine_wide * widened[:, :, :, 0]
    shifted = jnp.stack([real_part, imag_part], axis=3).astype(jnp.bfloat16)
    leaf_in = jnp.dot(
        shifted.reshape(-1, interp.shape[1]), interp.T, preferred_element_type=jnp.float32
    ).astype(jnp.bfloat16)
    leaf_in = leaf_in.reshape(parent_count * 8 * excite, 2 * interp.shape[0])
    far_part = jnp.dot(leaf_in, weights.T, preferred_element_type=jnp.float32)
    return far_part.reshape(parent_count * 8, excite, weights.shape[0])


def select_cells(flat_field, cell_keys):
    cell_total = flat_field.shape[1]
    block_cells = math.gcd(cell_total, 1024)
    block_total = cell_total // block_cells
    positions = jnp.arange(block_cells, dtype=jnp.int32)

    def add_block(block_index, total):
        first = block_index * block_cells
        piece = lax.dynamic_slice_in_dim(flat_field, first, block_cells, 1)
        selector = (cell_keys[None, :] == (first + positions)[:, None]).astype(jnp.bfloat16)
        return total + jnp.dot(piece, selector, preferred_element_type=jnp.float32)

    empty = jnp.zeros((flat_field.shape[0], cell_keys.shape[0]), jnp.float32)
    return lax.fori_loop(0, block_total, add_block, empty)


def shards(
    volume_field,
    source,
    material,
    mat_real,
    mat_loss,
    surface_map,
    near_boxes,
    near_blocks,
    radiate,
    interp,
    phase_angle,
    far_parents,
    far_kind,
    translate,
):
    excite = volume_field.shape[1]
    cells_x = volume_field.shape[2]
    cells_y = volume_field.shape[3]
    cells_z = volume_field.shape[4]
    diagonal_coef = jnp.full(material.shape, 6.0, jnp.float32)
    loss_coef = jnp.zeros(material.shape, jnp.float32)
    for material_kind in range(mat_real.shape[0]):
        present = material == material_kind
        diagonal_coef = diagonal_coef + jnp.where(present, mat_real[material_kind], 0.0)
        loss_coef = loss_coef + jnp.where(present, mat_loss[material_kind], 0.0)
    channels = 2 * excite
    stacked = jnp.concatenate(
        [
            volume_field.reshape(channels, cells_x, cells_y, cells_z),
            source.reshape(channels, cells_x, cells_y, cells_z),
            diagonal_coef[None],
            loss_coef[None],
        ],
        axis=0,
    )
    widened = padded_2(stacked.astype(jnp.bfloat16), (("space", 1), ("shard", 2)), 2).astype(
        stacked.dtype
    )
    outer_field = widened[:channels].reshape(2, excite, cells_x + 4, cells_y + 4, cells_z)
    outer_source = widened[channels : 2 * channels, 1:-1, 1:-1].reshape(
        2, excite, cells_x + 2, cells_y + 2, cells_z
    )
    row_global = lax.axis_index("space") * cells_x - 1 + jnp.arange(cells_x + 2, dtype=jnp.int32)
    column_global = lax.axis_index("shard") * cells_y - 1 + jnp.arange(cells_y + 2, dtype=jnp.int32)
    row_inside = (row_global >= 0) & (row_global < cells_x * lax.axis_size("space"))
    column_inside = (column_global >= 0) & (column_global < cells_y * lax.axis_size("shard"))
    inside = row_inside[:, None, None] & column_inside[None, :, None]
    outer_diagonal = jnp.where(inside, widened[2 * channels, 1:-1, 1:-1], 1.0)
    outer_loss = widened[2 * channels + 1, 1:-1, 1:-1]
    first_sweep = relax_sweep(
        outer_field[:, :, 1:-1, 1:-1],
        neighbour_sum(outer_field),
        outer_source,
        outer_diagonal,
        outer_loss,
    )
    first_sweep = jnp.where(inside, first_sweep, 0.0)
    current = relax_sweep(
        first_sweep[:, :, 1:-1, 1:-1], neighbour_sum(first_sweep), source, diagonal_coef, loss_coef
    )
    box_count = surface_map.shape[0]
    unknowns = surface_map.shape[1]
    flat_field = current.reshape(2 * excite, cells_x * cells_y * cells_z).astype(jnp.bfloat16)
    sampled = select_cells(flat_field, surface_map.reshape(-1)).astype(jnp.bfloat16)
    sampled = sampled.reshape(2, excite, box_count, unknowns)
    currents = jnp.transpose(sampled, (2, 1, 0, 3)).reshape(box_count, excite, 2 * unknowns)
    device_rank = lax.axis_index("space") * lax.axis_size("shard") + lax.axis_index("shard")
    beside_all = padded_2(currents, (("shard", 0),), box_count)
    local_near = near_boxes - (device_rank * box_count - box_count)
    near_force = jnp.zeros((box_count, excite, 2 * unknowns), jnp.float32)
    for slot_index in range(near_boxes.shape[1]):
        picked = jnp.take(beside_all, local_near[:, slot_index], axis=0).reshape(
            box_count * excite, 2 * unknowns
        )
        near_force = near_force + jnp.dot(
            picked, near_blocks[slot_index], preferred_element_type=jnp.float32
        ).reshape(box_count, excite, 2 * unknowns)
    weights = block_matrix(radiate)
    leaf_dirs = interp.shape[0]
    leaf = jnp.dot(
        currents.reshape(box_count * excite, 2 * unknowns),
        weights,
        preferred_element_type=jnp.float32,
    ).astype(jnp.bfloat16)
    leaf = leaf.reshape(box_count, excite, 2, leaf_dirs)
    cosine = jnp.cos(phase_angle)
    sine_part = jnp.sin(phase_angle)
    parent_patterns = aggregate(leaf, interp, cosine, sine_part)
    directed = lax.all_to_all(parent_patterns, "shard", split_axis=3, concat_axis=0, tiled=True)
    group_parents = directed.shape[0]
    group_index = lax.axis_index("space")
    target_ids = lax.dynamic_slice_in_dim(
        far_parents, group_index * group_parents, group_parents, 0
    )
    target_kinds = lax.dynamic_slice_in_dim(far_kind, group_index * group_parents, group_parents, 0)
    table = jnp.take(translate, target_kinds, axis=0)
    gathered = lax.all_gather(directed, "space", axis=0, tiled=True)
    sources = jnp.take(gathered, target_ids, axis=0).astype(jnp.float32)
    incoming = combine_far(sources, table).astype(jnp.bfloat16)
    far_force = disaggregate(
        lax.all_to_all(incoming, "shard", split_axis=0, concat_axis=3, tiled=True),
        interp,
        cosine,
        sine_part,
        weights,
    )
    forcing = near_force + far_force
    return (current, forcing)


def solution(mesh):
    return jax.shard_map(
        shards,
        mesh=mesh,
        in_specs=(
            P(None, None, "space", "shard", None),
            P(None, None, "space", "shard", None),
            P("space", "shard", None),
            P(),
            P(),
            P(("space", "shard"), None),
            P(("space", "shard"), None),
            P(),
            P(),
            P(),
            P(),
            P(),
            P(),
            P(None, None, "shard"),
        ),
        out_specs=(P(None, None, "space", "shard", None), P(("space", "shard"), None, None)),
        check_vma=False,
    )
```

profile of v0, /device:TPU:0, one launch (start us, length us, event | category | flops | bytes accessed | tf_op | source)
XLA Modules:
  0.0 182.6 jit_solution(5220939384639286865)
XLA Ops:
  7.2 1.6 fusion.71
  8.8 1.6 fusion.70
  10.4 1.3 convert.41
  11.9 5.7 %convert_bitcast_fusion.7 = (bf16[1,4,16,128]{3,2,1,0:T(8,128)(2,1)S(1)}, f32[4,16,128]{2,1,0:T(8,128)}, pred[4,16,128]{2,1,0:T(8,128)(4,1)S(1)}, pred[4,16,128]...) fusion(f32[]{:T(128)} %bitcast.9, f32[]{:T(128)} %bitcast.8, ...), kind=kLoop, calls=%fused_computation.120 | loop fusion | flops 204800 | bytes 147488 | tf_op jit(solution)/shard_map/broadcast_in_dim | solution.py:133
  17.6 5.6 %convert_bitcast_fusion.6 = (bf16[1,4,16,128]{3,2,1,0:T(8,128)(2,1)S(1)}, f32[4,16,128]{2,1,0:T(8,128)}) fusion(pred[4,16,128]{2,1,0:T(8,128)(4,1)S(1)} %get-tuple-element.150, f32[]{:T(128)} %bitcast.18, pred[4,16,128]{2,1,0:T(8,128)(4,1)S(1)} %get-tuple-element.149, f32[]{:T(128)} %bitcast.17, pred[4,16,128]{2,1,0:T(8,128)(4,1)S(1)} %get-tuple-element.148, ...), kind=kLoop, calls=%fused_computation.119 | loop fusion | flops 131072 | bytes 114720 | tf_op jit(solution)/shard_map/broadcast_in_dim | solution.py:134
  24.6 3.2 %collective-permute-start = (bf16[66,2,16,128]{3,2,1,0:T(8,128)(2,1)}, bf16[66,2,16,128]{3,2,1,0:T(8,128)(2,1)}, u32[]{:S(2)}, u32[]{:S(2)}) collective-permute-start(bf16[66,2,16,128]{3,2,1,0:T(8,128)(2,1)} %get-tuple-element.165), channel_id=1, source_target_pairs={{0,8},{8,16},{16,24},{1,9},{9,17},{17,25},{2,10},{10,18},{18,26},{... | collective-permute-start | bytes 1622024 | tf_op jit(solution)/shard_map/ppermute | solution.py:18
  27.8 1.3 collective-permute-start.1
  30.9 2.4 %collective-permute-done.1 = bf16[66,2,16,128]{3,2,1,0:T(8,128)(2,1)} collective-permute-done((bf16[66,2,16,128]{3,2,1,0:T(8,128)(2,1)}, bf16[66,2,16,128]{3,2,1,0:T(8,128)(2,1)}, u32[]{:S(2)}, u32[]{:S(2)}) %collective-permute-start.1) | collective-permute-done | bytes 540704 | tf_op jit(solution)/shard_map/ppermute | solution.py:19
  33.3 4.5 %pad_maximum_fusion.7 = (bf16[66,8,2,128]{3,2,1,0:T(2,128)(2,1)}, bf16[66,8,2,128]{3,2,1,0:T(2,128)(2,1)}) fusion(bf16[66,2,16,128]{3,2,1,0:T(8,128)(2,1)} %collective-permute-done.1, bf16[66,2,16,128]{3,2,1,0:T(8,128)(2,1)} %collective-permute-done, bf16[1,4,16,128]{3,2,1,0:T(8,128)(2,1)} %copy-done.11, bf16[1,4,16,128]{3,2,1,0:T(8,128)(2,1)S(1)} %get-tuple-element.141, ...), kind=kLoop, calls=%fused_computation.74 | loop fusion | flops 3244032 | bytes 2703360 | tf_op jit(solution)/shard_map/slice | solution.py:16
  37.8 4.1 %collective-permute-start.2 = (bf16[66,8,2,128]{3,2,1,0:T(2,128)(2,1)}, bf16[66,8,2,128]{3,2,1,0:T(2,128)(2,1)}, u32[]{:S(2)}, u32[]{:S(2)}) collective-permute-start(bf16[66,8,2,128]{3,2,1,0:T(2,128)(2,1)} %get-tuple-element.163), channel_id=1, source_target_pairs={{0,1},{1,2},{2,3},{3,4},{4,5},{5,6},{6,7},{8,9},{9,10},{10,11},{11... | collective-permute-start | bytes 811016 | tf_op jit(solution)/shard_map/ppermute | solution.py:18
  41.9 1.5 collective-permute-start.3
  45.5 5.1 %collective-permute-done.3 = bf16[66,8,2,128]{3,2,1,0:T(2,128)(2,1)} collective-permute-done((bf16[66,8,2,128]{3,2,1,0:T(2,128)(2,1)}, bf16[66,8,2,128]{3,2,1,0:T(2,128)(2,1)}, u32[]{:S(2)}, u32[]{:S(2)}) %collective-permute-start.3) | collective-permute-done | bytes 270368 | tf_op jit(solution)/shard_map/ppermute | solution.py:19
  50.6 7.1 %maximum_convert_fusion = f32[66,8,20,128]{3,2,1,0:T(8,128)S(1)} fusion(bf16[66,8,2,128]{3,2,1,0:T(2,128)(2,1)} %collective-permute-done.3, bf16[66,2,16,128]{3,2,1,0:T(8,128)(2,1)} %collective-permute-done.1, bf16[1,4,16,128]{3,2,1,0:T(8,128)(2,1)} %copy-done.11, bf16[1,4,16,128]{3,2,1,0:T(8,128)(2,1)S(1)} %get-tuple-element.141, ...), kind=kLoop, calls=%fused_computation.15 | loop fusion | flops 21626880 | bytes 8110080 | tf_op jit(solution)/shard_map/convert_element_type | solution.py:138
  63.7 1.3 fusion.64
  65.3 12.8 %while.14 = (s32[]{:T(128)}, f32[32,2048]{1,0:T(8,128)S(1)}, bf16[32,8192]{1,0:T(8,128)(2,1)S(1)}, s32[16,128]{1,0:T(8,128)S(1)}, s32[]{:T(128)}, /*index=5*/s32[]{:T(128)}, s32[]{:T(128)}, s32[]{:T(128)}) while((s32[]{:T(128)}, f32[32,2048]{1,0:T(8,128)S(1)}, bf16[32,8192]{1,0:T(8,128)(2,1)S(1)}, s32[16,128]{1,0:T(8,128)S(1)}, ...), condition=%wide.region_1.2_spmd.clone, body=%wide.region_0.1_spmd.clone.sunk | while | flops 136446976 | bytes 606365 | solution.py:99
  65.4 1.6 fusion.80
  67.0 1.6 fusion.80
  68.6 1.6 fusion.80
  70.2 1.6 fusion.80
  71.8 1.6 fusion.80
  73.4 1.6 fusion.80
  75.0 1.6 fusion.80
  76.6 1.6 fusion.80
  81.0 3.7 %copy.57 = bf16[2,16,2,2048]{1,2,0,3:T(2,128)(2,1)} copy(bf16[2,16,2,2048]{3,1,0,2:T(8,128)(2,1)S(1)} %pad_maximum_fusion.8) | data formatting | bytes 524288 | tf_op jit(solution)/shard_map/stack | solution.py:58
  84.7 4.0 %reshape.250 = bf16[8,2,8192]{2,1,0:T(2,128)(2,1)} reshape(bf16[2048,2,2,16]{3,2,1,0:T(2,128)(2,1)} %bitcast.164) | data formatting | bytes 524288
  88.8 5.2 %all-to-all-start = ((bf16[8,2,8192]{2,1,0:T(2,128)(2,1)}), bf16[8,2,8192]{2,1,0:T(2,128)(2,1)S(1)}, u32[]{:S(2)}, u32[]{:S(2)}) async-start(bf16[8,2,8192]{2,1,0:T(2,128)(2,1)} %reshape.250), calls=%async_computation | async-start | bytes 524288 | tf_op jit(solution)/shard_map/all_to_all | solution.py:191
  95.1 2.0 %gather_fusion = f32[128,2,256]{2,1,0:T(2,128)S(1)} fusion(f32[316,2,256]{2,1,0:T(2,128)} %param.31, s32[1024]{0:T(1024)S(1)} %pad_clamp_fusion.1), kind=kCustom, calls=%fused_computation.4 | custom fusion | bytes 524800 | tf_op jit(solution)/shard_map/jit(_take)/gather | solution.py:198
  97.1 5.1 %all-to-all-done = bf16[8,2,8192]{2,1,0:T(2,128)(2,1)S(1)} async-done(((bf16[8,2,8192]{2,1,0:T(2,128)(2,1)}), bf16[8,2,8192]{2,1,0:T(2,128)(2,1)S(1)}, u32[]{:S(2)}, u32[]{:S(2)}) %all-to-all-start) | async-done | bytes 262176 | tf_op jit(solution)/shard_map/all_to_all | solution.py:191
  102.2 2.4 %reshape.251 = bf16[2048,2,2,16]{3,2,1,0:T(2,128)(2,1)} reshape(bf16[8,2,8192]{2,1,0:T(2,128)(2,1)S(1)} %all-to-all-done) | data formatting | bytes 524288
  104.5 5.6 %copy.65 = bf16[2,16,2,8,256]{4,1,2,0,3:T(8,128)(2,1)} copy(bf16[2,16,2,8,256]{1,2,0,4,3:T(2,128)(2,1)} %bitcast.165) | data formatting | bytes 524288 | tf_op jit(solution)/shard_map/all_to_all | solution.py:191
  111.3 1.9 %collective-permute-start.4 = (bf16[16,16,256]{2,1,0:T(8,128)(2,1)S(1)}, bf16[16,16,256]{2,1,0:T(8,128)(2,1)S(1)}, u32[]{:S(2)}, u32[]{:S(2)}) collective-permute-start(bf16[16,16,256]{2,1,0:T(8,128)(2,1)S(1)} %reshape.177), channel_id=1, source_target_pairs={{0,1},{1,2},{2,3},{3,4},{4,5},{5,6},{6,7},{8,9},{9,10},{10,11},{11... | collective-permute-start | bytes 393224 | tf_op jit(solution)/shard_map/ppermute | solution.py:18
  115.9 1.3 collective-permute-start.5
  117.3 5.5 %collective-permute-done.5 = bf16[16,16,256]{2,1,0:T(8,128)(2,1)S(1)} collective-permute-done((bf16[16,16,256]{2,1,0:T(8,128)(2,1)S(1)}, bf16[16,16,256]{2,1,0:T(8,128)(2,1)S(1)}, u32[]{:S(2)}, u32[]{:S(2)}) %collective-permute-start.5) | collective-permute-done | bytes 131104 | tf_op jit(solution)/shard_map/ppermute | solution.py:19
  122.8 1.3 gather_fusion.5
  124.1 1.3 gather_fusion.4
  129.0 1.8 all-gather.2.cloned.1.call-done
  130.8 3.2 %gather_fusion.1 = bf16[128,16,2,256]{3,1,2,0:T(8,128)(2,1)} fusion(bf16[64,16,2,256]{3,1,2,0:T(8,128)(2,1)} %all-gather.2.cloned.1.call-done, s32[1024]{0:T(1024)S(1)} %pad_clamp_fusion), kind=kCustom, calls=%fused_computation.5 | custom fusion | bytes 4194816 | tf_op jit(solution)/shard_map/jit(_take)/gather | solution.py:200
  134.1 2.0 %select_convert_fusion = f32[16,8,16,2,256]{4,2,3,1,0:T(8,128)S(1)} fusion(bf16[16,8,16,2,256]{4,2,3,1,0:T(8,128)(2,1)} %bitcast.166, pred[16,8]{1,0:T(8,128)(4,1)S(1)} %copy.54), kind=kLoop, calls=%fused_computation.37 | loop fusion | flops 2097152 | bytes 6291584 | tf_op jit(solution)/shard_map/convert_element_type | solution.py:200
  137.6 5.5 %all-to-all-start.1 = ((bf16[16,16,2,256]{3,1,2,0:T(8,128)(2,1)}), bf16[16,16,2,256]{3,1,2,0:T(8,128)(2,1)S(1)}, u32[]{:S(2)}, u32[]{:S(2)}) async-start(bf16[16,16,2,256]{3,1,2,0:T(8,128)(2,1)} %pad_maximum_fusion.9), calls=%async_computation.1 | async-start | bytes 524288 | tf_op jit(solution)/shard_map/all_to_all | solution.py:203
  143.1 1.8 %fusion.36 = f32[16,16,256]{2,1,0:T(8,128)} fusion(bf16[16,16,256]{2,1,0:T(8,128)(2,1)} %gather_fusion.4, bf16[4,256,256]{2,1,0:T(8,128)(2,1)S(1)} %copy-done.6, pred[16]{0:T(512)(128)(4,1)S(1)} %copy-done.25), kind=kOutput, calls=%fused_computation.86 | convolution fusion | flops 33619968 | bytes 524800 | tf_op jit(solution)/shard_map/dot_general | solution.py:177
  145.9 6.5 %all-to-all-done.1 = bf16[16,16,2,256]{3,1,2,0:T(8,128)(2,1)S(1)} async-done(((bf16[16,16,2,256]{3,1,2,0:T(8,128)(2,1)}), bf16[16,16,2,256]{3,1,2,0:T(8,128)(2,1)S(1)}, u32[]{:S(2)}, u32[]{:S(2)}) %all-to-all-start.1) | async-done | bytes 262176 | tf_op jit(solution)/shard_map/all_to_all | solution.py:203
  152.9 4.4 %add_convert_fusion = (bf16[2,8,16,1,2048]{4,3,2,1,0:T(2,128)(2,1)S(1)}, bf16[2,8,16,1,2048]{4,3,2,1,0:T(2,128)(2,1)S(1)}) fusion(f32[2,16,2048]{2,1,0:T(8,128)S(1)} %get-tuple-element.170, f32[8,2048]{1,0:T(8,128)S(1)} %get-tuple-element.178, f32[2,16,2048]{2,1,0:T(8,128)S(1)} %get-tuple-element.169, f32[8,2048]{1,0:T(8,128)S(1)} %get-tuple-element.177), kind=kLoop, calls=%fused_computation.34 | loop fusion | flops 4194304 | bytes 2752512 | tf_op jit(solution)/shard_map/convert.3
  157.3 5.2 %pad_maximum_fusion = bf16[2,8,16,2,2048]{4,3,2,1,0:T(2,128)(2,1)} fusion(bf16[2,8,16,1,2048]{4,3,2,1,0:T(2,128)(2,1)S(1)} %get-tuple-element.168, bf16[2,8,16,1,2048]{4,3,2,1,0:T(2,128)(2,1)S(1)} %get-tuple-element.167), kind=kLoop, calls=%fused_computation.30 | loop fusion | flops 4194304 | bytes 4194304 | tf_op jit(solution)/shard_map/stack | solution.py:77
  162.5 4.1 %convert_element_type.61 = bf16[512,2048]{1,0:T(8,128)(2,1)} reshape(bf16[2,8,16,2,2048]{4,3,2,1,0:T(2,128)(2,1)} %pad_maximum_fusion) | data formatting | bytes 4194304 | tf_op jit(solution)/shard_map/convert_element_type | solution.py:77
  166.6 3.7 %convolution_convert_fusion = bf16[512,512]{1,0:T(8,128)(2,1)} fusion(bf16[512,2048]{1,0:T(8,128)(2,1)} %convert_element_type.61, bf16[512,2048]{1,0:T(8,128)(2,1)S(1)} %copy-done), kind=kOutput, calls=%fused_computation.40 | convolution fusion | flops 1074003968 | bytes 4718592 | tf_op jit(solution)/shard_map/dot_general | solution.py:78
  170.3 2.1 %dot_general.43 = bf16[16,16,1024]{2,1,0:T(8,128)(2,1)} reshape(bf16[512,512]{1,0:T(8,128)(2,1)} %convolution_convert_fusion) | data formatting | bytes 1048576 | tf_op jit(solution)/shard_map/dot_general | solution.py:82
  172.4 1.4 fusion.29
  173.9 1.9 %fusion.22 = f32[16,16,256]{2,1,0:T(8,128)} fusion(f32[16,16,256]{2,1,0:T(8,128)S(1)} %fusion.29, f32[16,16,256]{2,1,0:T(8,128)S(1)} %copy-done.4, f32[16,16,256]{2,1,0:T(8,128)S(1)} %copy-done.3, f32[16,16,256]{2,1,0:T(8,128)S(1)} %fusion.38, bf16[16,16,256]{2,1,0:T(8,128)(2,1)S(1)} %copy-done.7, bf16[4,256,256]{2,1,0:T(8,128)(2,1)} %param.25, ...), kind=kOutput, calls=%fused_computation.49 | convolution fusion | flops 33882112 | bytes 1572880 | tf_op jit(solution)/shard_map/dot_general | solution.py:177
  (130 shorter events, 25.8 us)
Async XLA Ops:
  7.2 71.9 %copy-start = (bf16[512,2048]{1,0:T(8,128)(2,1)S(1)}, bf16[512,2048]{1,0:T(8,128)(2,1)}, u32[]{:S(2)}) copy-start(bf16[512,2048]{1,0:T(8,128)(2,1)} %param.27) | copy-start | bytes 6291460
  7.2 4.6 %copy-start.1 = (f32[2,16,4,16,128]{4,3,2,1,0:T(8,128)S(1)}, f32[2,16,4,16,128]{4,3,2,1,0:T(8,128)}, u32[]{:S(2)}) copy-start(f32[2,16,4,16,128]{4,3,2,1,0:T(8,128)} %param.19) | copy-start | bytes 3145732
  7.2 4.7 %copy-start.19 = (s32[4,16,128]{2,1,0:T(8,128)S(1)}, s32[4,16,128]{2,1,0:T(8,128)}, u32[]{:S(2)}) copy-start(s32[4,16,128]{2,1,0:T(8,128)} %param.20) | copy-start | bytes 98308
  23.2 1.4 copy-start.11
  23.2 5.9 %copy-start.5 = (bf16[2,128,512]{2,1,0:T(8,128)(2,1)S(1)}, bf16[2,128,512]{2,1,0:T(8,128)(2,1)}, u32[]{:S(2)}) copy-start(bf16[2,128,512]{2,1,0:T(8,128)(2,1)} %param.26) | copy-start | bytes 786436
  24.6 6.3 %collective-permute-start = (bf16[66,2,16,128]{3,2,1,0:T(8,128)(2,1)}, bf16[66,2,16,128]{3,2,1,0:T(8,128)(2,1)}, u32[]{:S(2)}, u32[]{:S(2)}) collective-permute-start(bf16[66,2,16,128]{3,2,1,0:T(8,128)(2,1)} %get-tuple-element.165), channel_id=1, source_target_pairs={{0,8},{8,16},{16,24},{1,9},{9,17},{17,25},{2,10},{10,18},{18,26},{... | collective-permute-start | bytes 1622024 | tf_op jit(solution)/shard_map/ppermute | solution.py:18
  27.8 5.5 %collective-permute-start.1 = (bf16[66,2,16,128]{3,2,1,0:T(8,128)(2,1)}, bf16[66,2,16,128]{3,2,1,0:T(8,128)(2,1)}, u32[]{:S(2)}, u32[]{:S(2)}) collective-permute-start(bf16[66,2,16,128]{3,2,1,0:T(8,128)(2,1)} %get-tuple-element.166), channel_id=1, source_target_pairs={{8,0},{16,8},{24,16},{9,1},{17,9},{25,17},{10,2},{18,10},{26,18},{... | collective-permute-start | bytes 1622024 | tf_op jit(solution)/shard_map/ppermute | solution.py:19
  37.8 7.7 %collective-permute-start.2 = (bf16[66,8,2,128]{3,2,1,0:T(2,128)(2,1)}, bf16[66,8,2,128]{3,2,1,0:T(2,128)(2,1)}, u32[]{:S(2)}, u32[]{:S(2)}) collective-permute-start(bf16[66,8,2,128]{3,2,1,0:T(2,128)(2,1)} %get-tuple-element.163), channel_id=1, source_target_pairs={{0,1},{1,2},{2,3},{3,4},{4,5},{5,6},{6,7},{8,9},{9,10},{10,11},{11... | collective-permute-start | bytes 811016 | tf_op jit(solution)/shard_map/ppermute | solution.py:18
  41.9 8.7 %collective-permute-start.3 = (bf16[66,8,2,128]{3,2,1,0:T(2,128)(2,1)}, bf16[66,8,2,128]{3,2,1,0:T(2,128)(2,1)}, u32[]{:S(2)}, u32[]{:S(2)}) collective-permute-start(bf16[66,8,2,128]{3,2,1,0:T(2,128)(2,1)} %get-tuple-element.164), channel_id=1, source_target_pairs={{1,0},{2,1},{3,2},{4,3},{5,4},{6,5},{7,6},{9,8},{10,9},{11,10},{12... | collective-permute-start | bytes 811016 | tf_op jit(solution)/shard_map/ppermute | solution.py:19
  44.7 12.9 %copy-start.20 = (pred[6,18]{1,0:T(8,128)(4,1)S(1)}, pred[6,18]{1,0:T(8,128)(4,1)}, u32[]{:S(2)}) copy-start(pred[6,18]{1,0:T(8,128)(4,1)} %broadcast_and_fusion) | copy-start | bytes 328
  61.9 0.8 copy-start.10
  61.9 0.8 copy-start.13
  62.5 1.2 copy-start.2
  63.7 1.6 copy-start.12
  63.7 1.6 copy-start.27
  65.3 13.1 %copy-start.14 = (bf16[128,512]{1,0:T(8,128)(2,1)S(1)}, bf16[128,512]{1,0:T(8,128)(2,1)}, u32[]{:S(2)}) copy-start(bf16[128,512]{1,0:T(8,128)(2,1)} %fusion.63) | copy-start | bytes 393220
  65.3 13.1 %copy-start.16 = (bf16[128,512]{1,0:T(8,128)(2,1)S(1)}, bf16[128,512]{1,0:T(8,128)(2,1)}, u32[]{:S(2)}) copy-start(bf16[128,512]{1,0:T(8,128)(2,1)} %get-tuple-element.173) | copy-start | bytes 393220
  65.3 13.1 %copy-start.18 = (bf16[128,512]{1,0:T(8,128)(2,1)S(1)}, bf16[128,512]{1,0:T(8,128)(2,1)}, u32[]{:S(2)}) copy-start(bf16[128,512]{1,0:T(8,128)(2,1)} %get-tuple-element.174) | copy-start | bytes 393220
  81.0 13.0 %copy-start.21 = (s32[64,8]{0,1:T(8,128)S(1)}, s32[64,8]{0,1:T(8,128)}, u32[]{:S(2)}) copy-start(s32[64,8]{0,1:T(8,128)} %param.29) | copy-start | bytes 6148
  81.0 13.0 %copy-start.22 = (s32[64,8]{0,1:T(8,128)S(1)}, s32[64,8]{0,1:T(8,128)}, u32[]{:S(2)}) copy-start(s32[64,8]{0,1:T(8,128)} %param.30) | copy-start | bytes 6148
  84.7 12.4 %copy-start.26 = (s32[16,4]{0,1:T(4,128)S(1)}, s32[16,4]{0,1:T(4,128)}, u32[]{:S(2)}) copy-start(s32[16,4]{0,1:T(4,128)} %param.24) | copy-start | bytes 772
  88.8 13.4 %all-to-all-start = ((bf16[8,2,8192]{2,1,0:T(2,128)(2,1)}), bf16[8,2,8192]{2,1,0:T(2,128)(2,1)S(1)}, u32[]{:S(2)}, u32[]{:S(2)}) async-start(bf16[8,2,8192]{2,1,0:T(2,128)(2,1)} %reshape.250), calls=%async_computation | async-start | bytes 524288 | tf_op jit(solution)/shard_map/all_to_all | solution.py:191
  93.9 36.9 %all-gather.2.cloned.1.call-start = ((), (), s32[]{:S(2)}) async-start(), calls=%async_computation.2 | async-start | bytes 1310720 | tf_op jit(solution)/shard_map/all_gather | solution.py:199
  110.2 17.7 %copy-start.6 = (bf16[4,256,256]{2,1,0:T(8,128)(2,1)S(1)}, bf16[4,256,256]{2,1,0:T(8,128)(2,1)}, u32[]{:S(2)}) copy-start(bf16[4,256,256]{2,1,0:T(8,128)(2,1)} %param.25) | copy-start | bytes 1572868
  111.3 5.9 %collective-permute-start.4 = (bf16[16,16,256]{2,1,0:T(8,128)(2,1)S(1)}, bf16[16,16,256]{2,1,0:T(8,128)(2,1)S(1)}, u32[]{:S(2)}, u32[]{:S(2)}) collective-permute-start(bf16[16,16,256]{2,1,0:T(8,128)(2,1)S(1)} %reshape.177), channel_id=1, source_target_pairs={{0,1},{1,2},{2,3},{3,4},{4,5},{5,6},{6,7},{8,9},{9,10},{10,11},{11... | collective-permute-start | bytes 393224 | tf_op jit(solution)/shard_map/ppermute | solution.py:18
  115.9 6.8 %collective-permute-start.5 = (bf16[16,16,256]{2,1,0:T(8,128)(2,1)S(1)}, bf16[16,16,256]{2,1,0:T(8,128)(2,1)S(1)}, u32[]{:S(2)}, u32[]{:S(2)}) collective-permute-start(bf16[16,16,256]{2,1,0:T(8,128)(2,1)S(1)} %reshape.177), channel_id=1, source_target_pairs={{1,0},{2,1},{3,2},{4,3},{5,4},{6,5},{7,6},{9,8},{10,9},{11,10},{12... | collective-permute-start | bytes 393224 | tf_op jit(solution)/shard_map/ppermute | solution.py:19
  134.1 2.0 %copy-start.8 = (f32[16,8,1,256]{3,1,2,0:T(8,128)S(1)}, f32[16,8,1,256]{3,1,2,0:T(8,128)}, u32[]{:S(2)}) copy-start(f32[16,8,1,256]{3,1,2,0:T(8,128)} %copy.82) | copy-start | bytes 393220
  136.0 7.1 %copy-start.25 = (pred[16]{0:T(512)(128)(4,1)S(1)}, pred[16]{0:T(512)(128)(4,1)}, u32[]{:S(2)}) copy-start(pred[16]{0:T(512)(128)(4,1)} %get-tuple-element.181) | copy-start | bytes 52
  136.0 8.9 %copy-start.9 = (bf16[16,16,256]{2,1,0:T(8,128)(2,1)S(1)}, bf16[16,16,256]{2,1,0:T(8,128)(2,1)}, u32[]{:S(2)}) copy-start(bf16[16,16,256]{2,1,0:T(8,128)(2,1)} %gather_fusion.5) | copy-start | bytes 393220
  136.1 8.9 %copy-start.24 = (pred[16]{0:T(512)(128)(4,1)S(1)}, pred[16]{0:T(512)(128)(4,1)}, u32[]{:S(2)}) copy-start(pred[16]{0:T(512)(128)(4,1)} %get-tuple-element.179) | copy-start | bytes 52
  137.6 14.8 %all-to-all-start.1 = ((bf16[16,16,2,256]{3,1,2,0:T(8,128)(2,1)}), bf16[16,16,2,256]{3,1,2,0:T(8,128)(2,1)S(1)}, u32[]{:S(2)}, u32[]{:S(2)}) async-start(bf16[16,16,2,256]{3,1,2,0:T(8,128)(2,1)} %pad_maximum_fusion.9), calls=%async_computation.1 | async-start | bytes 524288 | tf_op jit(solution)/shard_map/all_to_all | solution.py:203
  166.6 5.8 %copy-start.15 = (bf16[128,512]{1,0:T(8,128)(2,1)S(1)}, bf16[128,512]{1,0:T(8,128)(2,1)}, u32[]{:S(2)}) copy-start(bf16[128,512]{1,0:T(8,128)(2,1)} %fusion.63) | copy-start | bytes 393220
  166.6 5.8 %copy-start.17 = (bf16[128,512]{1,0:T(8,128)(2,1)S(1)}, bf16[128,512]{1,0:T(8,128)(2,1)}, u32[]{:S(2)}) copy-start(bf16[128,512]{1,0:T(8,128)(2,1)} %get-tuple-element.173) | copy-start | bytes 393220
  170.3 3.5 %copy-start.3 = (f32[16,16,256]{2,1,0:T(8,128)S(1)}, f32[16,16,256]{2,1,0:T(8,128)}, u32[]{:S(2)}) copy-start(f32[16,16,256]{2,1,0:T(8,128)} %fusion.36) | copy-start | bytes 786436
  170.3 3.5 %copy-start.4 = (f32[16,16,256]{2,1,0:T(8,128)S(1)}, f32[16,16,256]{2,1,0:T(8,128)}, u32[]{:S(2)}) copy-start(f32[16,16,256]{2,1,0:T(8,128)} %fusion.34) | copy-start | bytes 786436
  170.3 3.5 %copy-start.7 = (bf16[16,16,256]{2,1,0:T(8,128)(2,1)S(1)}, bf16[16,16,256]{2,1,0:T(8,128)(2,1)}, u32[]{:S(2)}) copy-start(bf16[16,16,256]{2,1,0:T(8,128)(2,1)} %gather_fusion.2) | copy-start | bytes 393220
  170.3 3.6 %copy-start.23 = (pred[16]{0:T(512)(128)(4,1)S(1)}, pred[16]{0:T(512)(128)(4,1)}, u32[]{:S(2)}) copy-start(pred[16]{0:T(512)(128)(4,1)} %get-tuple-element.127) | copy-start | bytes 52
Sparse Core Ops, SparseCore 0:
  110.3 20.4 all-gather.1
where the time goes:
time: 184 us; the launch traced here: 183 us
  other arithmetic  46.8 us (25%)
  local copies, waits for them, and re-layouts  44.7 us (24%)
  waiting for transfers between devices  27.1 us (15%)
  matrix products  25 us (14%)
  starting transfers between devices  23.9 us (13%)
  between operations  14.7 us (8%)
    ppermute x3, waiting for transfers between devices, padded_2(): after = lax.ppermute(leading, axis, down)  13 us
    dot_general x8, matrix products, add_block(): return total + jnp.dot(piece, selector, preferred_element_type=jnp.float32)  12.5 us
    ppermute x3, starting transfers between devices, padded_2(): before = lax.ppermute(last, axis, up)  9.22 us
    unnamed x63, local copies, waits for them, and re-layouts  8.24 us
    convert_element_type x1, other arithmetic, shards(): padded_2(stacked.astype(jnp.bfloat16), (('space', 1), ('shard', 2)), 2)  7.05 us
    all_to_all x1, waiting for transfers between devices, shards(): lax.all_to_all(incoming, 'shard', split_axis=0, concat_axis=3, tiled=True)  6.52 us
    another operation x3, other arithmetic  5.8 us
    dot_general x4, matrix products, shards(): jnp.dot(picked, near_blocks[slot_index], preferred_element_type=jnp.float32)  5.76 us
  transfers between devices with their start and end apart: 9, of which 7 were waited for; matrix products, arithmetic and copies ran while one was open for 10% of the time, Pallas kernels for 0%

commit v1 on v0

v1 whole, which is shorter than its diff:
```python
import jax
import jax.numpy as jnp
from jax import lax
from jax.experimental import pallas as pl
from jax.experimental.pallas import tpu as pltpu
from jax.sharding import PartitionSpec as P

relaxation = 0.8
f32 = jnp.float32
bf16 = jnp.bfloat16
CHILDREN = 8


def dot(a, b):
    return jnp.dot(a, b, preferred_element_type=f32)


def dot_t(a, b):
    return lax.dot_general(a, b, (((1,), (1,)), ((), ())), preferred_element_type=f32)


def half_turn(v):
    half = v.shape[-2] // 2
    rows = lax.broadcasted_iota(jnp.int32, v.shape, v.ndim - 2)
    swapped = pltpu.roll(v, half, v.ndim - 2)
    return jnp.where(rows < half, -swapped, swapped)


def log2(n):
    assert n & (n - 1) == 0
    return n.bit_length() - 1


def swap_pairs(n, first):
    pairs = []
    for i in range(first, n - 1, 2):
        pairs += [(i, i + 1), (i + 1, i)]
    return pairs


def swap(for_even, for_odd, axis):
    n = lax.axis_size(axis)
    return [lax.ppermute(v, axis, swap_pairs(n, k)) for k, v in enumerate((for_even, for_odd))]


def up_body(field, smap, radiate, interp, cosine, sine, cur, out, cells, rows, *, groups, slices):
    channels, cx, cy, nz = field.shape
    excite = channels // 2
    group = excite // groups
    boxes, unknowns = smap.shape
    for c in range(channels):
        t, e = divmod(c, excite)
        place = (e // group) * 2 * group + t * group + e % group
        for x in range(cx):
            for y in range(0, cy, 8):
                cells[x, pl.ds(y * channels + place, 8, stride=channels), :] = field[c, x, y : y + 8, :]
    lhs = jnp.concatenate([cells[x].astype(bf16) for x in range(cx)], axis=1)
    pair = 2
    for b in range(0, boxes, pair):
        keys = jnp.concatenate([smap[b + j : b + j + 1, :] for j in range(pair)], axis=1)
        key_z = keys & (nz - 1)
        key_y = (keys >> log2(nz)) & (cy - 1)
        key_x = keys >> (log2(nz) + log2(cy))
        level = lax.broadcasted_iota(jnp.int32, (nz, pair * unknowns), 0)
        hot = [
            jnp.where(level == jnp.where(key_x == x, key_z, -1), 1.0, 0.0).astype(bf16) for x in range(cx)
        ]
        picked = dot(lhs, jnp.concatenate(hot, axis=0))
        found = jnp.zeros((channels, pair * unknowns), f32)
        for y in range(cy):
            found = jnp.where(key_y == y, picked[y * channels : (y + 1) * channels], found)
        for j in range(pair):
            own = found[:, j * unknowns : (j + 1) * unknowns].reshape(groups, 2 * group, unknowns)
            turned = half_turn(own)
            both = jnp.concatenate([own, turned], axis=2).reshape(channels, 2 * unknowns)
            rows[(b + j) * channels : (b + j + 1) * channels, :] = both.astype(bf16)
            parts = [
                jnp.concatenate([own[s, t * group : (t + 1) * group] for s in range(groups)], axis=0)
                for t in range(2)
            ]
            cur[b + j] = jnp.concatenate(parts, axis=1).astype(bf16)
    leaf = dot(rows[...], radiate[...]).astype(bf16)
    directions = interp.shape[1]
    width = directions // slices
    tile = max(width, 256)
    parents = boxes // CHILDREN
    for n in range(0, directions, tile):
        spread = dot(leaf, interp[:, n : n + tile]).reshape(parents, CHILDREN, groups, 2 * group, tile)
        along = jnp.zeros((parents, groups, 2 * group, tile), f32)
        across = jnp.zeros((parents, groups, 2 * group, tile), f32)
        for child in range(CHILDREN):
            along = along + cosine[child : child + 1, n : n + tile] * spread[:, child]
            across = across + sine[child : child + 1, n : n + tile] * spread[:, child]
        whole = (along + half_turn(across)).astype(bf16)
        for s in range(groups):
            piece = jnp.concatenate([whole[p, s] for p in range(parents)], axis=0)
            for k in range(tile // width):
                out[s * slices + n // width + k] = piece[:, k * width : (k + 1) * width]


def up(field, smap, radiate, interp, cosine, sine, groups, slices):
    channels, cx, cy, nz = field.shape
    boxes, unknowns = smap.shape
    width = interp.shape[1] // slices
    piece_rows = boxes // CHILDREN * (channels // groups)
    return pl.pallas_call(
        lambda *refs: up_body(*refs, groups=groups, slices=slices),
        out_shape=(
            jax.ShapeDtypeStruct((boxes, channels // 2, 2 * unknowns), bf16),
            jax.ShapeDtypeStruct((groups * slices, piece_rows, width), bf16),
        ),
        scratch_shapes=[
            pltpu.VMEM((cx, cy * channels, nz), f32),
            pltpu.VMEM((boxes * channels, 2 * unknowns), bf16),
        ],
        name="up",
    )(field, smap, radiate, interp, cosine, sine)


def far_body(lists, kinds, sources, translate, out, plain, turned):
    targets, far = lists.shape
    devices, piece_rows, width = sources.shape
    per = targets // devices
    tile = piece_rows // per
    wide = sources[...].astype(f32).reshape(targets, tile, width)
    plain[...] = wide
    turned[...] = half_turn(wide)

    def one(d, _):
        results = []
        for j in range(per):
            t = d * per + j
            total = jnp.zeros((tile, width), f32)
            for f in range(far):
                p = lists[t, f]
                k = kinds[t, f]
                factor = translate[k]
                total = total + factor[0:1] * plain[p] + factor[1:2] * turned[p]
            results.append(total)
        out[d] = jnp.concatenate(results, axis=0).astype(bf16)
        return 0

    lax.fori_loop(0, devices, one, 0)


def far_combine(lists, kinds, sources, translate):
    targets = lists.shape[0]
    devices, piece_rows, width = sources.shape
    tile = piece_rows // (targets // devices)
    smem = pl.BlockSpec(memory_space=pltpu.SMEM)
    vmem = pl.BlockSpec(memory_space=pltpu.VMEM)
    return pl.pallas_call(
        far_body,
        out_shape=jax.ShapeDtypeStruct(sources.shape, bf16),
        in_specs=[smem, smem, vmem, vmem],
        out_specs=vmem,
        scratch_shapes=[pltpu.VMEM((targets, tile, width), f32)] * 2,
        name="far",
    )(lists, kinds, sources, translate)


def near_body(spots, own, first, second, blocks, out, boxes_all, rows):
    boxes, excite, k = own.shape
    slots = spots.shape[1]
    boxes_all[0:boxes] = own[...]
    boxes_all[boxes : 2 * boxes] = first[...]
    boxes_all[2 * boxes : 3 * boxes] = second[...]
    for b in range(boxes):
        for s in range(slots):
            rows[b * excite : (b + 1) * excite, s * k : (s + 1) * k] = boxes_all[spots[b, s]]
    out[...] = dot(rows[...], blocks[...]).reshape(out.shape)


def near_force(spots, own, first, second, blocks):
    boxes, excite, k = own.shape
    slots = spots.shape[1]
    smem = pl.BlockSpec(memory_space=pltpu.SMEM)
    vmem = pl.BlockSpec(memory_space=pltpu.VMEM)
    return pl.pallas_call(
        near_body,
        out_shape=jax.ShapeDtypeStruct((boxes, excite, k), f32),
        in_specs=[smem, vmem, vmem, vmem, vmem],
        out_specs=vmem,
        scratch_shapes=[
            pltpu.VMEM((3 * boxes, excite, k), bf16),
            pltpu.VMEM((boxes * excite, slots * k), bf16),
        ],
        name="near",
    )(spots, own, first, second, blocks.reshape(slots * k, k))


def down_body(pieces, near, radiate, interp, cosine, sine, out, shifted, *, groups, slices):
    _, piece_rows, width = pieces.shape
    boxes, excite, both = out.shape
    unknowns = both // 2
    group = excite // groups
    tile = 2 * group
    parents = boxes // CHILDREN
    for h in range(slices):
        lanes = slice(h * width, (h + 1) * width)
        for s in range(groups):
            incoming = pieces[s * slices + h].astype(f32).reshape(parents, tile, width)
            turned = half_turn(incoming)
            for p in range(parents):
                for child in range(0, CHILDREN):
                    row = ((p * CHILDREN + child) * groups + s) * tile
                    value = cosine[child : child + 1, lanes] * incoming[p] - sine[child : child + 1, lanes] * turned[p]
                    shifted[row : row + tile, lanes] = value
    leaf_in = dot_t(shifted[...].astype(bf16), interp[...]).astype(bf16)
    back = dot_t(leaf_in, radiate[...]).reshape(boxes, groups, tile, both)
    own = back[..., :unknowns] - half_turn(back[..., unknowns:])
    for b in range(boxes):
        parts = [
            jnp.concatenate([own[b, s, t * group : (t + 1) * group] for s in range(groups)], axis=0)
            for t in range(2)
        ]
        out[b] = jnp.concatenate(parts, axis=1) + near[b]


def down(pieces, near, radiate, interp, cosine, sine, groups, slices):
    boxes, excite, both = near.shape
    return pl.pallas_call(
        lambda *refs: down_body(*refs, groups=groups, slices=slices),
        out_shape=jax.ShapeDtypeStruct(near.shape, f32),
        scratch_shapes=[pltpu.VMEM((boxes * excite * 2, interp.shape[1]), f32)],
        name="down",
    )(pieces, near, radiate, interp, cosine, sine)


def padded_2(array, sides, width):
    for axis, dim in sides:
        peers, length = (lax.axis_size(axis), array.shape[dim])
        up_pairs = [(i, (i + 1) % peers) for i in range(peers - 1)]
        down_pairs = [(j, i) for i, j in up_pairs]
        last = lax.slice_in_dim(array, length - width, length, axis=dim)
        leading = lax.slice_in_dim(array, 0, width, axis=dim)
        before = lax.ppermute(last, axis, up_pairs)
        after = lax.ppermute(leading, axis, down_pairs)
        array = jnp.concatenate([before, array, after], axis=dim)
    return array


def neighbour_sum(padded):
    core = padded[:, :, 1:-1, 1:-1]
    result = padded[:, :, 2:, 1:-1] + padded[:, :, :-2, 1:-1]
    result = result + padded[:, :, 1:-1, 2:] + padded[:, :, 1:-1, :-2]
    zero_layer = jnp.zeros(core.shape[:-1] + (1,), core.dtype)
    upper = jnp.concatenate([core[..., 1:], zero_layer], axis=-1)
    lower = jnp.concatenate([zero_layer, core[..., :-1]], axis=-1)
    return result + upper + lower


def relax_sweep(current, neighbours, source, diagonal_coef, loss_coef):
    real_part = diagonal_coef * current[0] - neighbours[0] - loss_coef * current[1]
    imag_part = diagonal_coef * current[1] - neighbours[1] + loss_coef * current[0]
    applied = jnp.stack([real_part, imag_part])
    return current + relaxation * (source - applied) / diagonal_coef


def relax(volume_field, source, material, mat_real, mat_loss):
    excite, cells_x, cells_y, cells_z = volume_field.shape[1:]
    diagonal_coef = jnp.full(material.shape, 6.0, f32)
    loss_coef = jnp.zeros(material.shape, f32)
    for kind in range(mat_real.shape[0]):
        present = material == kind
        diagonal_coef = diagonal_coef + jnp.where(present, mat_real[kind], 0.0)
        loss_coef = loss_coef + jnp.where(present, mat_loss[kind], 0.0)
    channels = 2 * excite
    stacked = jnp.concatenate(
        [
            volume_field.reshape(channels, cells_x, cells_y, cells_z),
            source.reshape(channels, cells_x, cells_y, cells_z),
            diagonal_coef[None],
            loss_coef[None],
        ],
        axis=0,
    )
    widened = padded_2(stacked.astype(bf16), (("space", 1), ("shard", 2)), 2).astype(f32)
    outer_field = widened[:channels].reshape(2, excite, cells_x + 4, cells_y + 4, cells_z)
    outer_source = widened[channels : 2 * channels, 1:-1, 1:-1].reshape(
        2, excite, cells_x + 2, cells_y + 2, cells_z
    )
    row_global = lax.axis_index("space") * cells_x - 1 + jnp.arange(cells_x + 2, dtype=jnp.int32)
    column_global = lax.axis_index("shard") * cells_y - 1 + jnp.arange(cells_y + 2, dtype=jnp.int32)
    row_inside = (row_global >= 0) & (row_global < cells_x * lax.axis_size("space"))
    column_inside = (column_global >= 0) & (column_global < cells_y * lax.axis_size("shard"))
    inside = row_inside[:, None, None] & column_inside[None, :, None]
    outer_diagonal = jnp.where(inside, widened[2 * channels, 1:-1, 1:-1], 1.0)
    outer_loss = widened[2 * channels + 1, 1:-1, 1:-1]
    first_sweep = relax_sweep(
        outer_field[:, :, 1:-1, 1:-1], neighbour_sum(outer_field), outer_source, outer_diagonal, outer_loss
    )
    first_sweep = jnp.where(inside, first_sweep, 0.0)
    return relax_sweep(
        first_sweep[:, :, 1:-1, 1:-1], neighbour_sum(first_sweep), source, diagonal_coef, loss_coef
    )


def shards(
    volume_field,
    source,
    material,
    mat_real,
    mat_loss,
    surface_map,
    near_boxes,
    near_blocks,
    radiate,
    interp,
    phase_angle,
    far_parents,
    far_kind,
    translate,
):
    every = ("space", "shard")
    groups = lax.axis_size("space")
    slices = lax.axis_size("shard")
    excite, cells_x, cells_y, cells_z = volume_field.shape[1:]
    cosine = jnp.cos(phase_angle)
    sine = jnp.sin(phase_angle)
    weights = radiate.reshape(2 * radiate.shape[1], radiate.shape[2])
    current = relax(volume_field, source, material, mat_real, mat_loss)
    currents, pieces = up(
        current.reshape(2 * excite, cells_x, cells_y, cells_z),
        surface_map,
        weights,
        interp,
        cosine,
        sine,
        groups,
        slices,
    )
    directed = lax.all_to_all(pieces, every, split_axis=0, concat_axis=0, tiled=True)
    combined = far_combine(far_parents, far_kind, directed, translate)
    incoming = lax.all_to_all(combined, every, split_axis=0, concat_axis=0, tiled=True)

    shard = lax.axis_index("shard")
    rank = lax.axis_index("space") * slices + shard
    boxes = near_boxes.shape[0]
    first, second = swap(currents, currents, "shard")
    offset = near_boxes - rank * boxes
    even = shard % 2 == 0
    above = jnp.where(even, 0, boxes)
    below = jnp.where(even, 2 * boxes, boxes) + boxes
    spots = offset + jnp.where(offset < 0, below, jnp.where(offset < boxes, 0, above))
    near = near_force(spots, currents, first, second, near_blocks)
    forcing = down(incoming, near, weights, interp, cosine, sine, groups, slices)
    return (current, forcing)


def solution(mesh):
    return jax.shard_map(
        shards,
        mesh=mesh,
        in_specs=(
            P(None, None, "space", "shard", None),
            P(None, None, "space", "shard", None),
            P("space", "shard", None),
            P(),
            P(),
            P(("space", "shard"), None),
            P(("space", "shard"), None),
            P(),
            P(),
            P(),
            P(),
            P(),
            P(),
            P(None, None, "shard"),
        ),
        out_specs=(P(None, None, "space", "shard", None), P(("space", "shard"), None, None)),
        check_vma=False,
    )
```

time: 184 us -> 108 us (0.59)
  local copies, waits for them, and re-layouts: 44.7 us -> 10.6 us
  matrix products: 25 us -> 0 us
  other arithmetic: 46.8 us -> 26.8 us
  Pallas kernels: 0 us -> 16.3 us
  between operations: 14.7 us -> 0.93 us
  starting transfers between devices: 23.9 us -> 27.7 us
  waiting for transfers between devices: 27.1 us -> 25 us
    dot_general x16 -> x0, matrix products: 25 us -> none  [the longest x8 12.5 us: add_block(): return total + jnp.dot(piece, selector, preferred_element_type=jnp.float32)]
    pallas_call x0 -> x4, Pallas kernels: none -> 16.3 us  [the longest x1 5.95 us: up(): pl.pallas_call(lambda *refs: up_body(*refs, groups=groups, slices=slices)...]
    gather x6 -> x0, local copies, waits for them, and re-layouts: 10.3 us -> none  [the longest x4 5.07 us: shards(): jnp.take(beside_all, local_near[:, slot_index], axis=0)]
    another operation x6 -> x2, other arithmetic: 11.8 us -> 2.62 us
    all_to_all x1 -> x0, local copies, waits for them, and re-layouts: 5.63 us -> none  [shards(): lax.all_to_all(parent_patterns, 'shard', split_axis=3, concat_axis=0, til...]
    convert_element_type x4 -> x0, local copies, waits for them, and re-layouts: 4.71 us -> none  [the longest x1 4.09 us: disaggregate(): shifted = jnp.stack([real_part, imag_part], axis=3).astype(jnp.bfloat16)]
    convert_element_type x4 -> x1, other arithmetic: 10.4 us -> 6.03 us  [relax(): padded_2(stacked.astype(bf16), (('space', 1), ('shard', 2)), 2).astype(f32)]
    unnamed x63 -> x25, local copies, waits for them, and re-layouts: 8.24 us -> 4.49 us
  transfers between devices with their start and end apart: 9 -> 8, of which waited for: 7 -> 5; matrix products, arithmetic and copies ran while one was open for 10% -> 3% of each run, Pallas kernels for 0% -> 2%
where the time goes in v1:
time: 108 us; the launch traced here: 107 us
  starting transfers between devices  27.7 us (26%)
  other arithmetic  26.8 us (25%)
  waiting for transfers between devices  25 us (23%)
  Pallas kernels  16.3 us (15%)
  local copies, waits for them, and re-layouts  10.6 us (10%)
    all_to_all x1, starting transfers between devices, shards(): lax.all_to_all(pieces, every, split_axis=0, concat_axis=0, tiled=True)  11.3 us
    all_to_all x1, waiting for transfers between devices, shards(): lax.all_to_all(pieces, every, split_axis=0, concat_axis=0, tiled=True)  9.05 us
    ppermute x2, waiting for transfers between devices, padded_2(): after = lax.ppermute(leading, axis, down_pairs)  8.09 us
    convert_element_type x1, other arithmetic, relax(): padded_2(stacked.astype(bf16), (('space', 1), ('shard', 2)), 2).astype(f32)  6.03 us
    pallas_call x1, Pallas kernels, up(): pl.pallas_call(lambda *refs: up_body(*refs, groups=groups, slices=slices)...  5.95 us
    ppermute x2, starting transfers between devices, padded_2(): before = lax.ppermute(last, axis, up_pairs)  5.84 us
    ppermute x2, waiting for transfers between devices, swap(): lax.ppermute(v, axis, swap_pairs(n, k))  5.45 us
    ppermute x2, starting transfers between devices, swap(): lax.ppermute(v, axis, swap_pairs(n, k))  5.14 us
  transfers between devices with their start and end apart: 8, of which 5 were waited for; matrix products, arithmetic and copies ran while one was open for 3% of the time, Pallas kernels for 2%

profile of v1, /device:TPU:0, one launch (start us, length us, event | category | flops | bytes accessed | tf_op | source)
XLA Modules:
  0.0 107.3 jit_solution(9246767209801101901)
XLA Ops:
  0.6 1.6 %fusion.18 = (f32[1]{0:T(128)}, f32[1]{0:T(128)}, f32[1]{0:T(128)}, f32[1]{0:T(128)}, f32[1]{0:T(128)}, /*index=5*/f32[1]{0:T(128)}, f32[1]{0:T(128)}, f32[1]{0:T(128)}) fusion(f32[8]{0:T(128)} %param.17), kind=kLoop, calls=%fused_computation.59 | loop fusion | bytes 64 | tf_op jit(solution)/shard_map/slice | solution.py:266
  2.3 1.6 %fusion.17 = (f32[1]{0:T(128)}, f32[1]{0:T(128)}, f32[1]{0:T(128)}, f32[1]{0:T(128)}, f32[1]{0:T(128)}, /*index=5*/f32[1]{0:T(128)}, f32[1]{0:T(128)}, f32[1]{0:T(128)}) fusion(f32[8]{0:T(128)} %param.18), kind=kLoop, calls=%fused_computation.58 | loop fusion | bytes 64 | tf_op jit(solution)/shard_map/slice | solution.py:267
  3.9 1.3 %convert.16 = bf16[2,16,4,16,128]{4,3,2,1,0:T(8,128)(2,1)S(1)} convert(f32[2,16,4,16,128]{4,3,2,1,0:T(8,128)} %param.14) | non-fusion elementwise | flops 262144 | bytes 1572864 | tf_op jit(solution)/shard_map/convert.7
  5.2 1.3 %convert.17 = bf16[2,16,4,16,128]{4,3,2,1,0:T(8,128)(2,1)S(1)} convert(f32[2,16,4,16,128]{4,3,2,1,0:T(8,128)} %param.15) | non-fusion elementwise | flops 262144 | bytes 1572864 | tf_op jit(solution)/shard_map/convert.6
  6.5 5.1 %convert_bitcast_fusion.1 = (bf16[1,4,16,128]{3,2,1,0:T(8,128)(2,1)S(1)}, f32[4,16,128]{2,1,0:T(8,128)S(1)}, pred[4,16,128]{2,1,0:T(8,128)(4,1)S(1)}, pred[4,16,...) fusion(f32[]{:T(128)} %bitcast.9, f32[]{:T(128)} %bitcast.8, ...), kind=kLoop, calls=%fused_computation.41 | loop fusion | flops 204800 | bytes 147488 | tf_op jit(solution)/shard_map/broadcast_in_dim | solution.py:273
  11.6 5.0 %convert_bitcast_fusion = (bf16[1,4,16,128]{3,2,1,0:T(8,128)(2,1)S(1)}, f32[4,16,128]{2,1,0:T(8,128)S(1)}) fusion(pred[4,16,128]{2,1,0:T(8,128)(4,1)S(1)} %get-tuple-element.15, f32[]{:T(128)} %bitcast.18, pred[4,16,128]{2,1,0:T(8,128)(4,1)S(1)} %get-tuple-element.14, f32[]{:T(128)} %bitcast.17, pred[4,16,128]{2,1,0:T(8,128)(4,1)S(1)} %get-tuple-element.13, ...), kind=kLoop, calls=%fused_computation.40 | loop fusion | flops 131072 | bytes 114720 | tf_op jit(solution)/shard_map/broadcast_in_dim | solution.py:274
  16.6 0.2 pad_maximum_fusion
  16.8 0.2 fusion.15
  17.0 2.4 %collective-permute-start = (bf16[66,2,16,128]{3,2,1,0:T(8,128)(2,1)S(1)}, bf16[66,2,16,128]{3,2,1,0:T(8,128)(2,1)S(1)}, u32[]{:S(2)}, u32[]{:S(2)}) collective-permute-start(bf16[66,2,16,128]{3,2,1,0:T(8,128)(2,1)S(1)} %get-tuple-element.30), channel_id=1, source_target_pairs={{0,8},{8,16},{16,24},{1,9},{9,17},{17,25},{2,10},{10,18},{18,26},{... | collective-permute-start | bytes 1622024 | tf_op jit(solution)/shard_map/ppermute | solution.py:237
  19.4 1.3 %collective-permute-start.1 = (bf16[66,2,16,128]{3,2,1,0:T(8,128)(2,1)S(1)}, bf16[66,2,16,128]{3,2,1,0:T(8,128)(2,1)S(1)}, u32[]{:S(2)}, u32[]{:S(2)}) collective-permute-start(bf16[66,2,16,128]{3,2,1,0:T(8,128)(2,1)S(1)} %get-tuple-element.31), channel_id=1, source_target_pairs={{8,0},{16,8},{24,16},{9,1},{17,9},{25,17},{10,2},{18,10},{26,18},{... | collective-permute-start | bytes 1622024 | tf_op jit(solution)/shard_map/ppermute | solution.py:238
  20.8 0.9 fusion.16
  21.7 3.7 %collective-permute-done.1 = bf16[66,2,16,128]{3,2,1,0:T(8,128)(2,1)S(1)} collective-permute-done((bf16[66,2,16,128]{3,2,1,0:T(8,128)(2,1)S(1)}, bf16[66,2,16,128]{3,2,1,0:T(8,128)(2,1)S(1)}, u32[]{:S(2)}, u32[]{:S(2)}) %collective-permute-start.1) | collective-permute-done | bytes 540704 | tf_op jit(solution)/shard_map/ppermute | solution.py:238
  25.4 2.7 %pad_maximum_fusion.6 = (bf16[66,8,2,128]{3,2,1,0:T(2,128)(2,1)S(1)}, bf16[66,8,2,128]{3,2,1,0:T(2,128)(2,1)S(1)}) fusion(bf16[66,2,16,128]{3,2,1,0:T(8,128)(2,1)S(1)} %collective-permute-done.1, bf16[66,2,16,128]{3,2,1,0:T(8,128)(2,1)S(1)} %collective-permute-done, bf16[1,4,16,128]{3,2,1,0:T(8,128)(2,1)S(1)} %get-tuple-element.16, ...), kind=kLoop, calls=%fused_computation.34 | loop fusion | flops 3244032 | bytes 2703360 | tf_op jit(solution)/shard_map/slice | solution.py:235
  28.1 3.4 %collective-permute-start.2 = (bf16[66,8,2,128]{3,2,1,0:T(2,128)(2,1)S(1)}, bf16[66,8,2,128]{3,2,1,0:T(2,128)(2,1)S(1)}, u32[]{:S(2)}, u32[]{:S(2)}) collective-permute-start(bf16[66,8,2,128]{3,2,1,0:T(2,128)(2,1)S(1)} %get-tuple-element.28), channel_id=1, source_target_pairs={{0,1},{1,2},{2,3},{3,4},{4,5},{5,6},{6,7},{8,9},{9,10},{10,11},{11... | collective-permute-start | bytes 811016 | tf_op jit(solution)/shard_map/ppermute | solution.py:237
  31.5 1.5 %collective-permute-start.3 = (bf16[66,8,2,128]{3,2,1,0:T(2,128)(2,1)S(1)}, bf16[66,8,2,128]{3,2,1,0:T(2,128)(2,1)S(1)}, u32[]{:S(2)}, u32[]{:S(2)}) collective-permute-start(bf16[66,8,2,128]{3,2,1,0:T(2,128)(2,1)S(1)} %get-tuple-element.29), channel_id=1, source_target_pairs={{1,0},{2,1},{3,2},{4,3},{5,4},{6,5},{7,6},{9,8},{10,9},{11,10},{12... | collective-permute-start | bytes 811016 | tf_op jit(solution)/shard_map/ppermute | solution.py:238
  33.0 2.4 %collective-permute-done.2 = bf16[66,8,2,128]{3,2,1,0:T(2,128)(2,1)S(1)} collective-permute-done((bf16[66,8,2,128]{3,2,1,0:T(2,128)(2,1)S(1)}, bf16[66,8,2,128]{3,2,1,0:T(2,128)(2,1)S(1)}, u32[]{:S(2)}, u32[]{:S(2)}) %collective-permute-start.2) | collective-permute-done | bytes 270368 | tf_op jit(solution)/shard_map/ppermute | solution.py:237
  35.4 4.4 %collective-permute-done.3 = bf16[66,8,2,128]{3,2,1,0:T(2,128)(2,1)S(1)} collective-permute-done((bf16[66,8,2,128]{3,2,1,0:T(2,128)(2,1)S(1)}, bf16[66,8,2,128]{3,2,1,0:T(2,128)(2,1)S(1)}, u32[]{:S(2)}, u32[]{:S(2)}) %collective-permute-start.3) | collective-permute-done | bytes 270368 | tf_op jit(solution)/shard_map/ppermute | solution.py:238
  39.8 6.0 %maximum_convert_fusion = f32[66,8,20,128]{3,2,1,0:T(8,128)S(1)} fusion(bf16[66,8,2,128]{3,2,1,0:T(2,128)(2,1)S(1)} %collective-permute-done.3, bf16[66,2,16,128]{3,2,1,0:T(8,128)(2,1)S(1)} %collective-permute-done.1, bf16[1,4,16,128]{3,2,1,0:T(8,128)(2,1)S(1)} %get-tuple-element.16, bf16[1,4,16,128]{3,2,1,0:T(8,128)(2,1)S(1)} %get-tuple-element.6, ...), kind=kLoop, calls=%fused_computation | loop fusion | flops 21626880 | bytes 8110080 | tf_op jit(solution)/shard_map/convert_element_type | solution.py:278
  45.9 0.1 bitcast_select_fusion
  46.0 0.1 select_bitcast_fusion
  46.0 0.3 slice.202
  46.3 0.2 slice.200
  46.5 0.9 fusion.13
  47.4 1.1 %fusion.1 = f32[2,16,6,18,128]{4,3,2,1,0:T(8,128)S(1)} fusion(f32[2,16,8,20,128]{4,3,2,1,0:T(8,128)S(1)} %bitcast.34, f32[2,16,6,18,127]{4,3,2,1,0:T(8,128)S(1)} %get-tuple-element.25, f32[2,16,6,18,127]{4,3,2,1,0:T(8,128)S(1)} %get-tuple-element.24), kind=kLoop, calls=%fused_computation.3 | loop fusion | flops 2211840 | bytes 12358656 | tf_op jit(solution)/shard_map/add | solution.py:250
  48.6 0.5 fusion.6
  49.0 0.7 fusion.2
  49.8 0.4 fusion.14
  50.2 0.5 fusion.8
  50.7 0.3 fusion.12
  50.9 1.0 copy-done
  51.9 1.3 %slice_add_fusion.7 = f32[2,16,4,16,128]{4,3,2,1,0:T(8,128)} fusion(f32[2,16,6,18,128]{4,3,2,1,0:T(8,128)S(1)} %fusion.2, f32[2,16,4,16,128]{4,3,2,1,0:T(8,128)S(1)} %copy-done, f32[1,16,4,16,128]{4,3,2,1,0:T(8,128)S(1)} %get-tuple-element.23, f32[1,16,4,16,128]{4,3,2,1,0:T(8,128)S(1)} %get-tuple-element.22, f32[4,16,128]{2,1,0:T(8,128)S(1)} %get-tuple-element.7), kind=kLoop, calls=%fused_computation.21 | loop fusion | flops 1310720 | bytes 4227072 | tf_op jit(solution)/shard_map/add | solution.py:257
  53.2 6.0 %up.1 = (bf16[16,16,256]{2,1,0:T(8,128)(2,1)}, bf16[32,16,256]{2,1,0:T(8,128)(2,1)}) custom-call(f32[32,4,16,128]{3,2,1,0:T(8,128)} %bitcast.44, s32[16,128]{1,0:T(8,128)} %refs_1_.1, bf16[256,512]{1,0:T(8,128)(2,1)} %bitcast.45, bf16[512,2048]{1,0:T(8,128)(2,1)} %refs_3_.3, f32[8,2048]{1,0:T(8,128)} %get-tuple-element.33.refs_4_, ...), custom_call_target="tpu_custom_call" | custom-call | tf_op jit(solution)/shard_map/up/pallas_call | solution.py:106
  59.2 11.3 %all-to-all-start = ((bf16[32,16,256]{2,1,0:T(8,128)(2,1)}), bf16[32,16,256]{2,1,0:T(8,128)(2,1)S(1)}, u32[]{:S(2)}, u32[]{:S(2)}) async-start(bf16[32,16,256]{2,1,0:T(8,128)(2,1)} %get-tuple-element.4), calls=%async_computation | async-start | bytes 524288 | tf_op jit(solution)/shard_map/all_to_all | solution.py:333
  70.5 0.7 copy.16.lists
  71.2 0.7 copy.17.kinds
  71.9 9.1 %all-to-all-done.sources = bf16[32,16,256]{2,1,0:T(8,128)(2,1)S(1)} async-done(((bf16[32,16,256]{2,1,0:T(8,128)(2,1)}), bf16[32,16,256]{2,1,0:T(8,128)(2,1)S(1)}, u32[]{:S(2)}, u32[]{:S(2)}) %all-to-all-start) | async-done | bytes 262176 | tf_op jit(solution)/shard_map/all_to_all | solution.py:333
  81.0 0.7 copy-done.2
  81.7 4.1 %far.1 = bf16[32,16,256]{2,1,0:T(8,128)(2,1)} custom-call(s32[64,8]{1,0:T(8,128)} %copy.16.lists, s32[64,8]{1,0:T(8,128)} %copy.17.kinds, bf16[32,16,256]{2,1,0:T(8,128)(2,1)} %copy-done.2, f32[316,2,256]{2,1,0:T(2,128)} %translate.1), custom_call_target="tpu_custom_call" | custom-call | tf_op jit(solution)/shard_map/far/pallas_call | solution.py:152
  85.7 2.6 %all-to-all-start.1 = ((bf16[32,16,256]{2,1,0:T(8,128)(2,1)}), bf16[32,16,256]{2,1,0:T(8,128)(2,1)S(1)}, u32[]{:S(2)}, u32[]{:S(2)}) async-start(bf16[32,16,256]{2,1,0:T(8,128)(2,1)} %far.1), calls=%async_computation.1 | async-start | bytes 524288 | tf_op jit(solution)/shard_map/all_to_all | solution.py:335
  88.4 0.1 copy.18
  88.4 0.7 collective-permute-start.5
  89.1 4.5 %collective-permute-start.4 = (bf16[16,16,256]{2,1,0:T(8,128)(2,1)S(1)}, bf16[16,16,256]{2,1,0:T(8,128)(2,1)S(1)}, u32[]{:S(2)}, u32[]{:S(2)}) collective-permute-start(bf16[16,16,256]{2,1,0:T(8,128)(2,1)S(1)} %copy-done.3), channel_id=1, source_target_pairs={{0,1},{1,0},{2,3},{3,2},{4,5},{5,4},{6,7},{7,6},{8,9},{9,8},{10,11... | collective-permute-start | bytes 393224 | tf_op jit(solution)/shard_map/ppermute | solution.py:43
  93.6 0.6 select_add_fusion.2.spots
  94.2 5.4 %collective-permute-done.4.first = bf16[16,16,256]{2,1,0:T(8,128)(2,1)S(1)} collective-permute-done((bf16[16,16,256]{2,1,0:T(8,128)(2,1)S(1)}, bf16[16,16,256]{2,1,0:T(8,128)(2,1)S(1)}, u32[]{:S(2)}, u32[]{:S(2)}) %collective-permute-start.4) | collective-permute-done | bytes 131104 | tf_op jit(solution)/shard_map/ppermute | solution.py:43
  99.7 0.7 copy-done.5
  100.3 2.3 %near.1.refs_1_ = f32[16,16,256]{2,1,0:T(8,128)} custom-call(s32[16,4]{1,0:T(8,128)} %select_add_fusion.2.spots, bf16[16,16,256]{2,1,0:T(8,128)(2,1)} %get-tuple-element.5.own, bf16[16,16,256]{2,1,0:T(8,128)(2,1)} %copy-done.5, bf16[16,16,256]{2,1,0:T(8,128)(2,1)} %copy-done.4, bf16[1024,256]{1,0:T(8,128)(2,1)} %bitcast.47), custom_call_target="tpu_custom_call" | custom-call | tf_op jit(solution)/shard_map/near/pallas_call | solution.py:179
  102.6 0.7 copy-done.1
  103.3 4.0 %down.1 = f32[16,16,256]{2,1,0:T(8,128)} custom-call(bf16[32,16,256]{2,1,0:T(8,128)(2,1)} %copy-done.1, f32[16,16,256]{2,1,0:T(8,128)} %near.1.refs_1_, bf16[256,512]{1,0:T(8,128)(2,1)} %bitcast.46, bf16[512,2048]{1,0:T(8,128)(2,1)} %refs_3_.3, f32[8,2048]{1,0:T(8,128)} %get-tuple-element.33.refs_4_, f32[8,2048]{1,0:T(8,128)} %get-tuple-element.32.refs_5_), custom_call_target="tpu_custom_call" | custom-call | tf_op jit(solution)/shard_map/down/pallas_call | solution.py:222
  (24 shorter events, 0.1 us)
Async XLA Ops:
  0.6 5.9 %copy-start.7 = (s32[4,16,128]{2,1,0:T(8,128)S(1)}, s32[4,16,128]{2,1,0:T(8,128)}, u32[]{:S(2)}) copy-start(s32[4,16,128]{2,1,0:T(8,128)} %param.16) | copy-start | bytes 98308
  6.5 14.2 %copy-start.6 = (f32[8,2048]{1,0:T(8,128)S(1)}, f32[8,2048]{1,0:T(8,128)}, u32[]{:S(2)}) copy-start(f32[8,2048]{1,0:T(8,128)} %param.24) | copy-start | bytes 196612
  17.0 4.7 %collective-permute-start = (bf16[66,2,16,128]{3,2,1,0:T(8,128)(2,1)S(1)}, bf16[66,2,16,128]{3,2,1,0:T(8,128)(2,1)S(1)}, u32[]{:S(2)}, u32[]{:S(2)}) collective-permute-start(bf16[66,2,16,128]{3,2,1,0:T(8,128)(2,1)S(1)} %get-tuple-element.30), channel_id=1, source_target_pairs={{0,8},{8,16},{16,24},{1,9},{9,17},{17,25},{2,10},{10,18},{18,26},{... | collective-permute-start | bytes 1622024 | tf_op jit(solution)/shard_map/ppermute | solution.py:237
  19.4 5.9 %collective-permute-start.1 = (bf16[66,2,16,128]{3,2,1,0:T(8,128)(2,1)S(1)}, bf16[66,2,16,128]{3,2,1,0:T(8,128)(2,1)S(1)}, u32[]{:S(2)}, u32[]{:S(2)}) collective-permute-start(bf16[66,2,16,128]{3,2,1,0:T(8,128)(2,1)S(1)} %get-tuple-element.31), channel_id=1, source_target_pairs={{8,0},{16,8},{24,16},{9,1},{17,9},{25,17},{10,2},{18,10},{26,18},{... | collective-permute-start | bytes 1622024 | tf_op jit(solution)/shard_map/ppermute | solution.py:238
  28.1 7.4 %collective-permute-start.2 = (bf16[66,8,2,128]{3,2,1,0:T(2,128)(2,1)S(1)}, bf16[66,8,2,128]{3,2,1,0:T(2,128)(2,1)S(1)}, u32[]{:S(2)}, u32[]{:S(2)}) collective-permute-start(bf16[66,8,2,128]{3,2,1,0:T(2,128)(2,1)S(1)} %get-tuple-element.28), channel_id=1, source_target_pairs={{0,1},{1,2},{2,3},{3,4},{4,5},{5,6},{6,7},{8,9},{9,10},{10,11},{11... | collective-permute-start | bytes 811016 | tf_op jit(solution)/shard_map/ppermute | solution.py:237
  31.5 8.4 %collective-permute-start.3 = (bf16[66,8,2,128]{3,2,1,0:T(2,128)(2,1)S(1)}, bf16[66,8,2,128]{3,2,1,0:T(2,128)(2,1)S(1)}, u32[]{:S(2)}, u32[]{:S(2)}) collective-permute-start(bf16[66,8,2,128]{3,2,1,0:T(2,128)(2,1)S(1)} %get-tuple-element.29), channel_id=1, source_target_pairs={{1,0},{2,1},{3,2},{4,3},{5,4},{6,5},{7,6},{9,8},{10,9},{11,10},{12... | collective-permute-start | bytes 811016 | tf_op jit(solution)/shard_map/ppermute | solution.py:238
  50.7 1.2 %copy-start = (f32[2,16,4,16,128]{4,3,2,1,0:T(8,128)S(1)}, f32[2,16,4,16,128]{4,3,2,1,0:T(8,128)}, u32[]{:S(2)}) copy-start(f32[2,16,4,16,128]{4,3,2,1,0:T(8,128)} %param.15) | copy-start | bytes 3145732
  53.2 17.3 %copy-start.8 = (s32[64,8]{0,1:T(8,128)S(1)}, s32[64,8]{0,1:T(8,128)}, u32[]{:S(2)}) copy-start(s32[64,8]{0,1:T(8,128)} %param.25) | copy-start | bytes 6148
  53.2 18.0 %copy-start.9 = (s32[64,8]{0,1:T(8,128)S(1)}, s32[64,8]{0,1:T(8,128)}, u32[]{:S(2)}) copy-start(s32[64,8]{0,1:T(8,128)} %param.26) | copy-start | bytes 6148
  53.2 35.1 %copy-start.10 = (s32[16,4]{0,1:T(4,128)S(1)}, s32[16,4]{0,1:T(4,128)}, u32[]{:S(2)}) copy-start(s32[16,4]{0,1:T(4,128)} %param.20) | copy-start | bytes 772
  59.2 29.3 %copy-start.3 = (bf16[16,16,256]{2,1,0:T(8,128)(2,1)S(1)}, bf16[16,16,256]{2,1,0:T(8,128)(2,1)}, u32[]{:S(2)}) copy-start(bf16[16,16,256]{2,1,0:T(8,128)(2,1)} %get-tuple-element.5.own) | copy-start | bytes 393220
  59.2 21.8 %all-to-all-start = ((bf16[32,16,256]{2,1,0:T(8,128)(2,1)}), bf16[32,16,256]{2,1,0:T(8,128)(2,1)S(1)}, u32[]{:S(2)}, u32[]{:S(2)}) async-start(bf16[32,16,256]{2,1,0:T(8,128)(2,1)} %get-tuple-element.4), calls=%async_computation | async-start | bytes 524288 | tf_op jit(solution)/shard_map/all_to_all | solution.py:333
  81.0 0.7 copy-start.2
  85.7 16.8 %all-to-all-start.1 = ((bf16[32,16,256]{2,1,0:T(8,128)(2,1)}), bf16[32,16,256]{2,1,0:T(8,128)(2,1)S(1)}, u32[]{:S(2)}, u32[]{:S(2)}) async-start(bf16[32,16,256]{2,1,0:T(8,128)(2,1)} %far.1), calls=%async_computation.1 | async-start | bytes 524288 | tf_op jit(solution)/shard_map/all_to_all | solution.py:335
  88.4 5.8 %collective-permute-start.5 = (bf16[16,16,256]{2,1,0:T(8,128)(2,1)S(1)}, bf16[16,16,256]{2,1,0:T(8,128)(2,1)S(1)}, u32[]{:S(2)}, u32[]{:S(2)}) collective-permute-start(bf16[16,16,256]{2,1,0:T(8,128)(2,1)S(1)} %copy-done.3), channel_id=1, source_target_pairs={{1,2},{2,1},{3,4},{4,3},{5,6},{6,5},{9,10},{10,9},{11,12},{12,11},... | collective-permute-start | bytes 393224 | tf_op jit(solution)/shard_map/ppermute | solution.py:43
  89.1 10.5 %collective-permute-start.4 = (bf16[16,16,256]{2,1,0:T(8,128)(2,1)S(1)}, bf16[16,16,256]{2,1,0:T(8,128)(2,1)S(1)}, u32[]{:S(2)}, u32[]{:S(2)}) collective-permute-start(bf16[16,16,256]{2,1,0:T(8,128)(2,1)S(1)} %copy-done.3), channel_id=1, source_target_pairs={{0,1},{1,0},{2,3},{3,2},{4,5},{5,4},{6,7},{7,6},{8,9},{9,8},{10,11... | collective-permute-start | bytes 393224 | tf_op jit(solution)/shard_map/ppermute | solution.py:43
  94.2 5.5 %copy-start.4 = (bf16[16,16,256]{2,1,0:T(8,128)(2,1)}, bf16[16,16,256]{2,1,0:T(8,128)(2,1)S(1)}, u32[]{:S(2)}) copy-start(bf16[16,16,256]{2,1,0:T(8,128)(2,1)S(1)} %collective-permute-done.5.second) | copy-start | bytes 393220
  99.6 0.7 copy-start.5
  102.6 0.7 copy-start.1

commit v2 on v1

--- a/solution.py
+++ b/solution.py
@@ -43,17 +43,77 @@
     return [lax.ppermute(v, axis, swap_pairs(n, k)) for k, v in enumerate((for_even, for_odd))]
 
 
-def up_body(field, smap, radiate, interp, cosine, sine, cur, out, cells, rows, *, groups, slices):
-    channels, cx, cy, nz = field.shape
+def second_sweep(mat_real, mat_loss, field, sweep, columns, column_a, source, kinds, got_first, got_second, out, beside, store, cx, cy):
+    total = field.shape[0] // cy
+    channels = total // cx
+    excite = channels // 2
+    plane = channels * cy
+    even = is_even("space")
+    a, b = coefficients(kinds[...], mat_real, mat_loss, 0)
+
+    def halo(side, start, size):
+        one = got_first[start : start + size, :].astype(f32)
+        two = got_second[start : start + size, :].astype(f32)
+        return jnp.where(even, two, one) if side == 0 else jnp.where(even, one, two)
+
+    faces = (0, cx - 1)
+    for y_side in range(2):
+        beside[y_side] = columns[y_side]
+        for x_side, x in enumerate(faces):
+            corner = halo(x_side, 2 * plane + y_side * channels, channels)
+            factor = column_a[y_side, x : x + 1, :]
+            for c in range(0, channels, 8):
+                rows = pl.ds(c * cx + x, 8, stride=cx)
+                beside.at[y_side][rows, :] = beside.at[y_side][rows, :] + factor * corner[c : c + 8]
+    face_a = []
+    for x_side in range(2):
+        kind = halo(x_side, 2 * plane + 2 * channels, cy).astype(jnp.int32)
+        face_a.append(coefficients(kind, mat_real, mat_loss, 1)[0])
+    for e in range(excite):
+        v = []
+        for p in range(2):
+            c = p * excite + e
+            own = [sweep[(c * cx + x) * cy : (c * cx + x + 1) * cy, :] for x in range(cx)]
+            outer = []
+            for x_side, x in enumerate(faces):
+                own[x] = own[x] + a[x * cy : (x + 1) * cy] * halo(x_side, c * cy, cy)
+                before = field[(c * cx + x) * cy : (c * cx + x + 1) * cy, :]
+                outer.append(halo(x_side, plane + c * cy, cy) + face_a[x_side] * before)
+            v.append([outer[0]] + own + [outer[1]])
+        for x in range(cx):
+            sums = []
+            for p in range(2):
+                at = (p * excite + e) * cx + x
+                w = v[p][x + 1]
+                n = source[at * cy : (at + 1) * cy, :] + along_z(w)
+                n = n + along_y(w, beside[0, at : at + 1, :], beside[1, at : at + 1, :])
+                sums.append(n + v[p][x] + v[p][x + 2])
+            new = relaxed((v[0][x + 1], v[1][x + 1]), sums, a[x * cy : (x + 1) * cy], b[x * cy : (x + 1) * cy])
+            for p in range(2):
+                at = (p * excite + e) * cx + x
+                out[at * cy : (at + 1) * cy, :] = new[p]
+                store(p, e, x, new[p])
+
+
+def up_body(
+    mat_real, mat_loss, field, sweep, columns, column_a, source, kinds, got_first, got_second,
+    smap, radiate, interp, cosine, sine, volume, cur, out, beside, cells, rows, *, cx, cy, groups, slices
+):
+    nz = field.shape[1]
+    channels = field.shape[0] // (cx * cy)
     excite = channels // 2
     group = excite // groups
     boxes, unknowns = smap.shape
-    for c in range(channels):
-        t, e = divmod(c, excite)
+
+    def store(t, e, x, value):
         place = (e // group) * 2 * group + t * group + e % group
-        for x in range(cx):
-            for y in range(0, cy, 8):
-                cells[x, pl.ds(y * channels + place, 8, stride=channels), :] = field[c, x, y : y + 8, :]
+        for y in range(0, cy, 8):
+            cells.at[x][pl.ds(y * channels + place, 8, stride=channels), :] = value[y : y + 8]
+
+    second_sweep(
+        mat_real, mat_loss, field, sweep, columns, column_a, source, kinds, got_first, got_second,
+        volume, beside, store, cx, cy
+    )
     lhs = jnp.concatenate([cells[x].astype(bf16) for x in range(cx)], axis=1)
     pair = 2
     for b in range(0, boxes, pair):
@@ -98,23 +158,32 @@
                 out[s * slices + n // width + k] = piece[:, k * width : (k + 1) * width]
 
 
-def up(field, smap, radiate, interp, cosine, sine, groups, slices):
-    channels, cx, cy, nz = field.shape
+def up(volume_args, smap, radiate, interp, cosine, sine, cx, cy, groups, slices):
+    field = volume_args[2]
+    nz = field.shape[1]
+    total = field.shape[0] // cy
+    channels = total // cx
     boxes, unknowns = smap.shape
     width = interp.shape[1] // slices
     piece_rows = boxes // CHILDREN * (channels // groups)
+    smem = pl.BlockSpec(memory_space=pltpu.SMEM)
+    vmem = pl.BlockSpec(memory_space=pltpu.VMEM)
     return pl.pallas_call(
-        lambda *refs: up_body(*refs, groups=groups, slices=slices),
+        lambda *refs: up_body(*refs, cx=cx, cy=cy, groups=groups, slices=slices),
         out_shape=(
+            jax.ShapeDtypeStruct(field.shape, f32),
             jax.ShapeDtypeStruct((boxes, channels // 2, 2 * unknowns), bf16),
             jax.ShapeDtypeStruct((groups * slices, piece_rows, width), bf16),
         ),
+        in_specs=[smem, smem] + [vmem] * 13,
+        out_specs=(vmem,) * 3,
         scratch_shapes=[
+            pltpu.VMEM((2, total, nz), f32),
             pltpu.VMEM((cx, cy * channels, nz), f32),
             pltpu.VMEM((boxes * channels, 2 * unknowns), bf16),
         ],
         name="up",
-    )(field, smap, radiate, interp, cosine, sine)
+    )(*volume_args, smap, radiate, interp, cosine, sine)
 
 
 def far_body(lists, kinds, sources, translate, out, plain, turned):
@@ -227,73 +296,166 @@
     )(pieces, near, radiate, interp, cosine, sine)
 
 
-def padded_2(array, sides, width):
-    for axis, dim in sides:
-        peers, length = (lax.axis_size(axis), array.shape[dim])
-        up_pairs = [(i, (i + 1) % peers) for i in range(peers - 1)]
-        down_pairs = [(j, i) for i, j in up_pairs]
-        last = lax.slice_in_dim(array, length - width, length, axis=dim)
-        leading = lax.slice_in_dim(array, 0, width, axis=dim)
-        before = lax.ppermute(last, axis, up_pairs)
-        after = lax.ppermute(leading, axis, down_pairs)
-        array = jnp.concatenate([before, array, after], axis=dim)
-    return array
-
-
-def neighbour_sum(padded):
-    core = padded[:, :, 1:-1, 1:-1]
-    result = padded[:, :, 2:, 1:-1] + padded[:, :, :-2, 1:-1]
-    result = result + padded[:, :, 1:-1, 2:] + padded[:, :, 1:-1, :-2]
-    zero_layer = jnp.zeros(core.shape[:-1] + (1,), core.dtype)
-    upper = jnp.concatenate([core[..., 1:], zero_layer], axis=-1)
-    lower = jnp.concatenate([zero_layer, core[..., :-1]], axis=-1)
-    return result + upper + lower
-
-
-def relax_sweep(current, neighbours, source, diagonal_coef, loss_coef):
-    real_part = diagonal_coef * current[0] - neighbours[0] - loss_coef * current[1]
-    imag_part = diagonal_coef * current[1] - neighbours[1] + loss_coef * current[0]
-    applied = jnp.stack([real_part, imag_part])
-    return current + relaxation * (source - applied) / diagonal_coef
-
-
-def relax(volume_field, source, material, mat_real, mat_loss):
-    excite, cells_x, cells_y, cells_z = volume_field.shape[1:]
-    diagonal_coef = jnp.full(material.shape, 6.0, f32)
-    loss_coef = jnp.zeros(material.shape, f32)
-    for kind in range(mat_real.shape[0]):
-        present = material == kind
-        diagonal_coef = diagonal_coef + jnp.where(present, mat_real[kind], 0.0)
-        loss_coef = loss_coef + jnp.where(present, mat_loss[kind], 0.0)
-    channels = 2 * excite
-    stacked = jnp.concatenate(
-        [
-            volume_field.reshape(channels, cells_x, cells_y, cells_z),
-            source.reshape(channels, cells_x, cells_y, cells_z),
-            diagonal_coef[None],
-            loss_coef[None],
-        ],
-        axis=0,
+def is_even(axis):
+    return lax.rem(lax.axis_index(axis), 2) == 0
+
+
+def coefficients(kinds, mat_real, mat_loss, base):
+    diagonal = jnp.full(kinds.shape, 6.0, f32)
+    loss = jnp.zeros(kinds.shape, f32)
+    for k in range(mat_real.shape[0]):
+        present = kinds == k + base
+        diagonal = jnp.where(present, 6.0 + mat_real[k], diagonal)
+        loss = jnp.where(present, mat_loss[k], loss)
+    a = relaxation / diagonal
+    if base > 0:
+        a = jnp.where(kinds < base, 0.0, a)
+    return a, a * loss
+
+
+def along_z(v):
+    lanes = v.shape[-1]
+    lane = lax.broadcasted_iota(jnp.int32, v.shape, v.ndim - 1)
+    lower = jnp.where(lane == 0, 0.0, pltpu.roll(v, 1, v.ndim - 1))
+    upper = jnp.where(lane == lanes - 1, 0.0, pltpu.roll(v, lanes - 1, v.ndim - 1))
+    return lower + upper
+
+
+def along_y(v, low, high):
+    rows = v.shape[0]
+    row = lax.broadcasted_iota(jnp.int32, v.shape, 0)
+    lower = jnp.where(row == 0, low, pltpu.roll(v, 1, 0))
+    upper = jnp.where(row == rows - 1, high, pltpu.roll(v, rows - 1, 0))
+    return lower + upper
+
+
+def relaxed(v, total, a, b):
+    keep = 1.0 - relaxation
+    return (
+        keep * v[0] + a * total[0] + b * v[1],
+        keep * v[1] + a * total[1] - b * v[0],
     )
-    widened = padded_2(stacked.astype(bf16), (("space", 1), ("shard", 2)), 2).astype(f32)
-    outer_field = widened[:channels].reshape(2, excite, cells_x + 4, cells_y + 4, cells_z)
-    outer_source = widened[channels : 2 * channels, 1:-1, 1:-1].reshape(
-        2, excite, cells_x + 2, cells_y + 2, cells_z
-    )
-    row_global = lax.axis_index("space") * cells_x - 1 + jnp.arange(cells_x + 2, dtype=jnp.int32)
-    column_global = lax.axis_index("shard") * cells_y - 1 + jnp.arange(cells_y + 2, dtype=jnp.int32)
-    row_inside = (row_global >= 0) & (row_global < cells_x * lax.axis_size("space"))
-    column_inside = (column_global >= 0) & (column_global < cells_y * lax.axis_size("shard"))
-    inside = row_inside[:, None, None] & column_inside[None, :, None]
-    outer_diagonal = jnp.where(inside, widened[2 * channels, 1:-1, 1:-1], 1.0)
-    outer_loss = widened[2 * channels + 1, 1:-1, 1:-1]
-    first_sweep = relax_sweep(
-        outer_field[:, :, 1:-1, 1:-1], neighbour_sum(outer_field), outer_source, outer_diagonal, outer_loss
-    )
-    first_sweep = jnp.where(inside, first_sweep, 0.0)
-    return relax_sweep(
-        first_sweep[:, :, 1:-1, 1:-1], neighbour_sum(first_sweep), source, diagonal_coef, loss_coef
-    )
+
+
+def edge_body(field, source, kinds, first, second, *, cx, cy):
+    total = field.shape[0] // cy
+    even = is_even("shard")
+
+    def face(inner, outer):
+        def layer(ref, y):
+            return jnp.concatenate(
+                [ref[pl.ds(r * cy + y, 8, stride=cy), :] for r in range(0, total, 8)], axis=0
+            )
+
+        kind = kinds[pl.ds(outer, cx, stride=cy), :].astype(f32) + 1.0
+        kind = jnp.concatenate([kind] * (16 // cx), axis=0)
+        return jnp.concatenate([layer(field, inner), layer(field, outer), layer(source, outer), kind], axis=0)
+
+    high = face(cy - 2, cy - 1)
+    low = face(1, 0)
+    first[...] = jnp.where(even, high, low).astype(bf16)
+    second[...] = jnp.where(even, low, high).astype(bf16)
+
+
+def edges(field, source, kinds, cx, cy):
+    rows = 3 * (field.shape[0] // cy) + 16
+    message = jax.ShapeDtypeStruct((rows, field.shape[1]), bf16)
+    return pl.pallas_call(
+        lambda *refs: edge_body(*refs, cx=cx, cy=cy), out_shape=(message, message), name="edges"
+    )(field, source, kinds)
+
+
+def first_body(
+    mat_real, mat_loss, field, source, kinds, got_first, got_second,
+    sweep, columns, column_a, to_first, to_second, near, *, cx, cy
+):
+    total = field.shape[0] // cy
+    channels = total // cx
+    excite = channels // 2
+    even_y = is_even("shard")
+    a, b = coefficients(kinds[...], mat_real, mat_loss, 0)
+    row = lax.broadcasted_iota(jnp.int32, (8, field.shape[1]), 0) & (cx - 1)
+    one = got_first[...].astype(f32)
+    two = got_second[...].astype(f32)
+    for side, own_y in ((0, 0), (1, cy - 1)):
+        halo = jnp.where(even_y, two, one) if side == 0 else jnp.where(even_y, one, two)
+        kind = halo[3 * total : 3 * total + 8].astype(jnp.int32)
+        col_a, col_b = coefficients(kind, mat_real, mat_loss, 1)
+        column_a[side] = col_a
+        near[side] = halo[total : 2 * total]
+        for j in range(0, total // 2, 8):
+            v, sums = [], []
+            for part in range(2):
+                at = part * (total // 2) + j
+                beside = halo[total + at : total + at + 8]
+                nbr = halo[at : at + 8] + halo[2 * total + at : 2 * total + at + 8] + along_z(beside)
+                nbr = nbr + field[pl.ds(at * cy + own_y, 8, stride=cy), :]
+                nbr = nbr + jnp.where(row == 0, 0.0, pltpu.roll(beside, 1, 0))
+                nbr = nbr + jnp.where(row == cx - 1, 0.0, pltpu.roll(beside, 7, 0))
+                v.append(beside)
+                sums.append(nbr)
+            new = relaxed(v, sums, col_a, col_b)
+            for part in range(2):
+                at = part * (total // 2) + j
+                columns[side, at : at + 8] = new[part]
+    for e in range(excite):
+        v = [
+            [field[at * cy : (at + 1) * cy, :] for at in range((p * excite + e) * cx, (p * excite + e + 1) * cx)]
+            for p in range(2)
+        ]
+        for x in range(cx):
+            sums = []
+            for p in range(2):
+                at = (p * excite + e) * cx + x
+                n = source[at * cy : (at + 1) * cy, :] + along_z(v[p][x])
+                n = n + along_y(v[p][x], near[0, at : at + 1, :], near[1, at : at + 1, :])
+                if x > 0:
+                    n = n + v[p][x - 1]
+                if x < cx - 1:
+                    n = n + v[p][x + 1]
+                sums.append(n)
+            new = relaxed((v[0][x], v[1][x]), sums, a[x * cy : (x + 1) * cy], b[x * cy : (x + 1) * cy])
+            for p in range(2):
+                at = (p * excite + e) * cx + x
+                sweep[at * cy : (at + 1) * cy, :] = new[p]
+    even_x = is_even("space")
+    plane = channels * cy
+    for message, x in ((to_first, jnp.where(even_x, cx - 1, 0)), (to_second, jnp.where(even_x, 0, cx - 1))):
+        for c in range(channels):
+            rows = pl.ds(pl.multiple_of((c * cx + x) * cy, cy), cy)
+            message[c * cy : (c + 1) * cy, :] = field[rows, :].astype(bf16)
+            message[plane + c * cy : plane + (c + 1) * cy, :] = sweep[rows, :].astype(bf16)
+        for side in range(2):
+            corner = jnp.concatenate(
+                [near.at[side][pl.ds(c * cx + x, 8, stride=cx), :] for c in range(0, channels, 8)], axis=0
+            )
+            at = 2 * plane + side * channels
+            message[at : at + channels, :] = corner.astype(bf16)
+        at = 2 * plane + 2 * channels
+        kind = kinds[pl.ds(pl.multiple_of(x * cy, cy), cy), :].astype(f32) + 1.0
+        message[at : at + cy, :] = kind.astype(bf16)
+
+
+def first_sweep(mat_real, mat_loss, field, source, kinds, got_first, got_second, cx, cy):
+    total, nz = field.shape[0] // cy, field.shape[1]
+    channels = total // cx
+    smem = pl.BlockSpec(memory_space=pltpu.SMEM)
+    vmem = pl.BlockSpec(memory_space=pltpu.VMEM)
+    message = jax.ShapeDtypeStruct((2 * channels * cy + 2 * channels + cy, nz), bf16)
+    return pl.pallas_call(
+        lambda *refs: first_body(*refs, cx=cx, cy=cy),
+        out_shape=(
+            jax.ShapeDtypeStruct(field.shape, f32),
+            jax.ShapeDtypeStruct((2, total, nz), f32),
+            jax.ShapeDtypeStruct((2, 8, nz), f32),
+            message,
+            message,
+        ),
+        in_specs=[smem, smem] + [vmem] * 5,
+        out_specs=(vmem,) * 5,
+        scratch_shapes=[pltpu.VMEM((2, total, nz), f32)],
+        name="first_sweep",
+    )(mat_real, mat_loss, field, source, kinds, got_first, got_second)
 
 
 def shards(
@@ -319,14 +481,23 @@
     cosine = jnp.cos(phase_angle)
     sine = jnp.sin(phase_angle)
     weights = radiate.reshape(2 * radiate.shape[1], radiate.shape[2])
-    current = relax(volume_field, source, material, mat_real, mat_loss)
-    currents, pieces = up(
-        current.reshape(2 * excite, cells_x, cells_y, cells_z),
+    field = volume_field.reshape(-1, cells_z)
+    flat_source = source.reshape(-1, cells_z)
+    kinds = material.reshape(-1, cells_z)
+    got_y = swap(*edges(field, flat_source, kinds, cells_x, cells_y), "shard")
+    sweep, columns, column_a, *to_x = first_sweep(
+        mat_real, mat_loss, field, flat_source, kinds, *got_y, cells_x, cells_y
+    )
+    got_x = swap(*to_x, "space")
+    current, currents, pieces = up(
+        (mat_real, mat_loss, field, sweep, columns, column_a, flat_source, kinds, *got_x),
         surface_map,
         weights,
         interp,
         cosine,
         sine,
+        cells_x,
+        cells_y,
         groups,
         slices,
     )
@@ -345,7 +516,7 @@
     spots = offset + jnp.where(offset < 0, below, jnp.where(offset < boxes, 0, above))
     near = near_force(spots, currents, first, second, near_blocks)
     forcing = down(incoming, near, weights, interp, cosine, sine, groups, slices)
-    return (current, forcing)
+    return (current.reshape(volume_field.shape), forcing)
 
 
 def solution(mesh):

time: 108 us -> 75.2 us (0.70)
  other arithmetic: 26.8 us -> 0.61 us
  Pallas kernels: 16.3 us -> 24.2 us
  waiting for transfers between devices: 25 us -> 18.4 us
  local copies, waits for them, and re-layouts: 10.6 us -> 6.55 us
  starting transfers between devices: 27.7 us -> 24.3 us
    ppermute x4 -> x0, waiting for transfers between devices: 10.5 us -> none  [the longest x2 8.09 us: padded_2(): after = lax.ppermute(leading, axis, down_pairs)]
    broadcast_in_dim x2 -> x0, other arithmetic: 10 us -> none  [the longest x1 5.09 us: relax(): diagonal_coef[None]]
    ppermute x4 -> x0, starting transfers between devices: 8.61 us -> none  [the longest x2 5.84 us: padded_2(): before = lax.ppermute(last, axis, up_pairs)]
    pallas_call x1 -> x3, Pallas kernels: 5.95 us -> 13.8 us  [the longest x1 7.75 us: up(): pl.pallas_call(lambda *refs: up_body(*refs, cx=cx, cy=cy, groups=groups,...]
    convert_element_type x1 -> x0, other arithmetic: 6.03 us -> none  [relax(): padded_2(stacked.astype(bf16), (('space', 1), ('shard', 2)), 2).astype(f32)]
    slice x7 -> x0, local copies, waits for them, and re-layouts: 5.19 us -> none  [the longest x1 1.62 us: relax(): diagonal_coef = diagonal_coef + jnp.where(present, mat_real[kind], 0.0)]
    ppermute x2 -> x6, waiting for transfers between devices: 5.45 us -> 9.34 us  [swap(): lax.ppermute(v, axis, swap_pairs(n, k))]
    all_to_all x1, starting transfers between devices: 11.3 us -> 15.1 us  [shards(): lax.all_to_all(pieces, every, split_axis=0, concat_axis=0, tiled=True)]
  transfers between devices with their start and end apart: 8 -> 8, of which waited for: 5 -> 4; matrix products, arithmetic and copies ran while one was open for 3% -> 4% of each run, Pallas kernels for 2% -> 3%
where the time goes in v2:
time: 75.2 us; the launch traced here: 74.8 us
  starting transfers between devices  24.3 us (32%)
  Pallas kernels  24.2 us (32%)
  waiting for transfers between devices  18.4 us (24%)
  local copies, waits for them, and re-layouts  6.55 us (9%)
    all_to_all x1, starting transfers between devices, shards(): lax.all_to_all(pieces, every, split_axis=0, concat_axis=0, tiled=True)  15.1 us
    ppermute x6, waiting for transfers between devices, swap(): lax.ppermute(v, axis, swap_pairs(n, k))  9.34 us
    all_to_all x1, waiting for transfers between devices, shards(): lax.all_to_all(pieces, every, split_axis=0, concat_axis=0, tiled=True)  9.04 us
    pallas_call x1, Pallas kernels, up(): pl.pallas_call(lambda *refs: up_body(*refs, cx=cx, cy=cy, groups=groups,...  7.75 us
    ppermute x6, starting transfers between devices, swap(): lax.ppermute(v, axis, swap_pairs(n, k))  6.67 us
    unnamed x29, local copies, waits for them, and re-layouts  5.65 us
    pallas_call x1, Pallas kernels, far_combine(): pl.pallas_call(far_body, out_shape=jax.ShapeDtypeStruct(sources.shape, bf...  4.07 us
    pallas_call x1, Pallas kernels, down(): pl.pallas_call(lambda *refs: down_body(*refs, groups=groups, slices=slice...  4.03 us
  transfers between devices with their start and end apart: 8, of which 4 were waited for; matrix products, arithmetic and copies ran while one was open for 4% of the time, Pallas kernels for 3%

profile of v2, /device:TPU:0, one launch (start us, length us, event | category | flops | bytes accessed | tf_op | source)
XLA Modules:
  0.0 74.8 jit_solution(1741401084895941519)
XLA Ops:
  0.6 0.0 copy-start.9
  0.6 2.4 %edges.1 = (bf16[400,128]{1,0:T(8,128)(2,1)}, bf16[400,128]{1,0:T(8,128)(2,1)}) custom-call(f32[2048,128]{1,0:T(8,128)} %bitcast.6, f32[2048,128]{1,0:T(8,128)} %bitcast.9, s32[64,128]{1,0:T(8,128)} %bitcast.15), custom_call_target="tpu_custom_call" | custom-call | tf_op jit(solution)/shard_map/edges/pallas_call | solution.py:363
  3.0 3.0 %collective-permute-start = (bf16[400,128]{1,0:T(8,128)(2,1)}, bf16[400,128]{1,0:T(8,128)(2,1)S(1)}, u32[]{:S(2)}, u32[]{:S(2)}) collective-permute-start(bf16[400,128]{1,0:T(8,128)(2,1)} %get-tuple-element.12), channel_id=1, source_target_pairs={{0,1},{1,0},{2,3},{3,2},{4,5},{5,4},{6,7},{7,6},{8,9},{9,8},{10,11... | collective-permute-start | bytes 307208 | tf_op jit(solution)/shard_map/ppermute | solution.py:43
  6.0 0.7 collective-permute-start.1
  6.6 2.4 %collective-permute-done.refs_5_ = bf16[400,128]{1,0:T(8,128)(2,1)S(1)} collective-permute-done((bf16[400,128]{1,0:T(8,128)(2,1)}, bf16[400,128]{1,0:T(8,128)(2,1)S(1)}, u32[]{:S(2)}, u32[]{:S(2)}) %collective-permute-start) | collective-permute-done | bytes 102432 | tf_op jit(solution)/shard_map/ppermute | solution.py:43
  9.1 0.0 copy-start.7
  9.1 0.0 collective-permute-done.1.refs_6_
  9.1 0.6 copy-done.7
  9.7 0.0 copy-start.8
  9.7 0.6 copy-done.8
  10.3 3.7 %first_sweep.1 = (f32[2048,128]{1,0:T(8,128)}, f32[2,128,128]{2,1,0:T(8,128)}, f32[2,8,128]{2,1,0:T(8,128)}, bf16[1104,128]{1,0:T(8,128)(2,1)}, bf16[1104,128]{1,0:T(8,128)(2,1)}) custom-call(f32[8]{0:T(128)} %refs_0_.3, f32[8]{0:T(128)} %refs_1_.3, f32[2048,128]{1,0:T(8,128)} %bitcast.7, f32[2048,128]{1,0:T(8,128)} %bitcast.10, s32[64,128]{1,0:T(8,128)} %bitcast.16, ...), custom_call_target="tpu_custom_call" | custom-call | tf_op jit(solution)/shard_map/first_sweep/pallas_call | solution.py:445
  14.0 0.0 collective-permute-start.2
  14.0 0.7 collective-permute-start.3
  14.7 0.0 copy-done.9
  14.7 0.9 %fusion = (f32[8,2048]{1,0:T(8,128)}, f32[8,2048]{1,0:T(8,128)}) fusion(f32[8,2048]{1,0:T(8,128)S(1)} %copy-done.9), kind=kLoop, calls=%fused_computation.1 | loop fusion | bytes 196608 | tf_op jit(solution)/shard_map/sin | solution.py:482
  15.6 0.2 collective-permute-done.2.refs_8_
  15.8 0.0 copy-start.2
  15.8 0.0 collective-permute-done.3.refs_9_
  15.8 0.7 copy-done.2
  16.5 0.1 copy-done.3
  16.6 0.0 copy-start.10
  16.6 0.0 copy-start.11
  16.6 7.8 %up.1 = (f32[2048,128]{1,0:T(8,128)}, bf16[16,16,256]{2,1,0:T(8,128)(2,1)}, bf16[32,16,256]{2,1,0:T(8,128)(2,1)}) custom-call(f32[8]{0:T(128)} %refs_0_.3, f32[8]{0:T(128)} %refs_1_.3, f32[2048,128]{1,0:T(8,128)} %bitcast.8, f32[2048,128]{1,0:T(8,128)} %get-tuple-element.14.refs_3_, f32[2,128,128]{2,1,0:T(8,128)} %get-tuple-element.15.refs_4_, ...), custom_call_target="tpu_custom_call" | custom-call | tf_op jit(solution)/shard_map/up/pallas_call | solution.py:171
  24.4 0.0 copy-start.12
  24.4 0.0 copy-start.4
  24.4 15.1 %all-to-all-start = ((bf16[32,16,256]{2,1,0:T(8,128)(2,1)}), bf16[32,16,256]{2,1,0:T(8,128)(2,1)S(1)}, u32[]{:S(2)}, u32[]{:S(2)}) async-start(bf16[32,16,256]{2,1,0:T(8,128)(2,1)} %get-tuple-element.20), calls=%async_computation | async-start | bytes 524288 | tf_op jit(solution)/shard_map/all_to_all | solution.py:504
  39.5 0.0 copy-done.10
  39.5 0.7 copy.16.lists
  40.2 0.0 copy-done.11
  40.2 0.7 copy.17.kinds
  40.9 9.0 %all-to-all-done.sources = bf16[32,16,256]{2,1,0:T(8,128)(2,1)S(1)} async-done(((bf16[32,16,256]{2,1,0:T(8,128)(2,1)}), bf16[32,16,256]{2,1,0:T(8,128)(2,1)S(1)}, u32[]{:S(2)}, u32[]{:S(2)}) %all-to-all-start) | async-done | bytes 262176 | tf_op jit(solution)/shard_map/all_to_all | solution.py:504
  49.9 0.7 copy-done.1
  50.6 4.1 %far.1 = bf16[32,16,256]{2,1,0:T(8,128)(2,1)} custom-call(s32[64,8]{1,0:T(8,128)} %copy.16.lists, s32[64,8]{1,0:T(8,128)} %copy.17.kinds, bf16[32,16,256]{2,1,0:T(8,128)(2,1)} %copy-done.1, f32[316,2,256]{2,1,0:T(2,128)} %translate.1), custom_call_target="tpu_custom_call" | custom-call | tf_op jit(solution)/shard_map/far/pallas_call | solution.py:221
  54.7 2.6 %all-to-all-start.1 = ((bf16[32,16,256]{2,1,0:T(8,128)(2,1)}), bf16[32,16,256]{2,1,0:T(8,128)(2,1)S(1)}, u32[]{:S(2)}, u32[]{:S(2)}) async-start(bf16[32,16,256]{2,1,0:T(8,128)(2,1)} %far.1), calls=%async_computation.1 | async-start | bytes 524288 | tf_op jit(solution)/shard_map/all_to_all | solution.py:506
  57.3 0.0 copy-done.12
  57.3 0.1 copy.18
  57.4 0.0 copy-done.4
  57.4 1.7 %collective-permute-start.4 = (bf16[16,16,256]{2,1,0:T(8,128)(2,1)S(1)}, bf16[16,16,256]{2,1,0:T(8,128)(2,1)S(1)}, u32[]{:S(2)}, u32[]{:S(2)}) collective-permute-start(bf16[16,16,256]{2,1,0:T(8,128)(2,1)S(1)} %copy-done.4), channel_id=1, source_target_pairs={{0,1},{1,0},{2,3},{3,2},{4,5},{5,4},{6,7},{7,6},{8,9},{9,8},{10,11... | collective-permute-start | bytes 393224 | tf_op jit(solution)/shard_map/ppermute | solution.py:43
  59.1 0.7 collective-permute-start.5
  59.8 0.6 select_add_fusion.spots
  60.4 6.7 %collective-permute-done.4.first = bf16[16,16,256]{2,1,0:T(8,128)(2,1)S(1)} collective-permute-done((bf16[16,16,256]{2,1,0:T(8,128)(2,1)S(1)}, bf16[16,16,256]{2,1,0:T(8,128)(2,1)S(1)}, u32[]{:S(2)}, u32[]{:S(2)}) %collective-permute-start.4) | collective-permute-done | bytes 131104 | tf_op jit(solution)/shard_map/ppermute | solution.py:43
  67.1 0.0 collective-permute-done.5.second
  67.1 0.6 copy-done.5
  67.7 0.0 copy-done.6
  67.8 2.3 %near.1.refs_1_ = f32[16,16,256]{2,1,0:T(8,128)} custom-call(s32[16,4]{1,0:T(8,128)} %select_add_fusion.spots, bf16[16,16,256]{2,1,0:T(8,128)(2,1)} %get-tuple-element.21.own, bf16[16,16,256]{2,1,0:T(8,128)(2,1)} %copy-done.5, bf16[16,16,256]{2,1,0:T(8,128)(2,1)} %copy-done.6, bf16[1024,256]{1,0:T(8,128)(2,1)} %bitcast.14), custom_call_target="tpu_custom_call" | custom-call | tf_op jit(solution)/shard_map/near/pallas_call | solution.py:248
  70.0 0.0 all-to-all-done.1.refs_0_
  70.0 0.7 copy-done
  70.7 4.0 %down.1 = f32[16,16,256]{2,1,0:T(8,128)} custom-call(bf16[32,16,256]{2,1,0:T(8,128)(2,1)} %copy-done, f32[16,16,256]{2,1,0:T(8,128)} %near.1.refs_1_, bf16[256,512]{1,0:T(8,128)(2,1)} %bitcast.13, bf16[512,2048]{1,0:T(8,128)(2,1)} %refs_3_.1, f32[8,2048]{1,0:T(8,128)} %get-tuple-element.23.refs_13_.refs_4_, f32[8,2048]{1,0:T(8,128)} %get-tuple-element.22.refs_14_.refs_5_), custom_call_target="tpu_custom_call" | custom-call | tf_op jit(solution)/shard_map/down/pallas_call | solution.py:291
  (5 shorter events, 0.0 us)
Async XLA Ops:
  0.6 14.1 %copy-start.9 = (f32[8,2048]{1,0:T(8,128)S(1)}, f32[8,2048]{1,0:T(8,128)}, u32[]{:S(2)}) copy-start(f32[8,2048]{1,0:T(8,128)} %param.24) | copy-start | bytes 196612
  3.0 6.1 %collective-permute-start = (bf16[400,128]{1,0:T(8,128)(2,1)}, bf16[400,128]{1,0:T(8,128)(2,1)S(1)}, u32[]{:S(2)}, u32[]{:S(2)}) collective-permute-start(bf16[400,128]{1,0:T(8,128)(2,1)} %get-tuple-element.12), channel_id=1, source_target_pairs={{0,1},{1,0},{2,3},{3,2},{4,5},{5,4},{6,7},{7,6},{8,9},{9,8},{10,11... | collective-permute-start | bytes 307208 | tf_op jit(solution)/shard_map/ppermute | solution.py:43
  6.0 3.1 %collective-permute-start.1 = (bf16[400,128]{1,0:T(8,128)(2,1)}, bf16[400,128]{1,0:T(8,128)(2,1)S(1)}, u32[]{:S(2)}, u32[]{:S(2)}) collective-permute-start(bf16[400,128]{1,0:T(8,128)(2,1)} %get-tuple-element.13), channel_id=1, source_target_pairs={{1,2},{2,1},{3,4},{4,3},{5,6},{6,5},{9,10},{10,9},{11,12},{12,11},... | collective-permute-start | bytes 307208 | tf_op jit(solution)/shard_map/ppermute | solution.py:43
  9.1 0.6 copy-start.7
  9.7 0.6 copy-start.8
  14.0 1.8 %collective-permute-start.2 = (bf16[1104,128]{1,0:T(8,128)(2,1)}, bf16[1104,128]{1,0:T(8,128)(2,1)S(1)}, u32[]{:S(2)}, u32[]{:S(2)}) collective-permute-start(bf16[1104,128]{1,0:T(8,128)(2,1)} %get-tuple-element.17), channel_id=1, source_target_pairs={{0,8},{8,0},{16,24},{24,16},{1,9},{9,1},{17,25},{25,17},{2,10},{10... | collective-permute-start | bytes 847880 | tf_op jit(solution)/shard_map/ppermute | solution.py:43
  14.0 1.8 %collective-permute-start.3 = (bf16[1104,128]{1,0:T(8,128)(2,1)}, bf16[1104,128]{1,0:T(8,128)(2,1)S(1)}, u32[]{:S(2)}, u32[]{:S(2)}) collective-permute-start(bf16[1104,128]{1,0:T(8,128)(2,1)} %get-tuple-element.18), channel_id=1, source_target_pairs={{8,16},{16,8},{9,17},{17,9},{10,18},{18,10},{11,19},{19,11},{12,20... | collective-permute-start | bytes 847880 | tf_op jit(solution)/shard_map/ppermute | solution.py:43
  15.8 0.7 copy-start.2
  15.8 0.8 %copy-start.3 = (bf16[1104,128]{1,0:T(8,128)(2,1)}, bf16[1104,128]{1,0:T(8,128)(2,1)S(1)}, u32[]{:S(2)}) copy-start(bf16[1104,128]{1,0:T(8,128)(2,1)S(1)} %collective-permute-done.3.refs_9_) | copy-start | bytes 847876
  16.6 22.9 %copy-start.10 = (s32[64,8]{0,1:T(8,128)S(1)}, s32[64,8]{0,1:T(8,128)}, u32[]{:S(2)}) copy-start(s32[64,8]{0,1:T(8,128)} %param.25) | copy-start | bytes 6148
  16.6 23.6 %copy-start.11 = (s32[64,8]{0,1:T(8,128)S(1)}, s32[64,8]{0,1:T(8,128)}, u32[]{:S(2)}) copy-start(s32[64,8]{0,1:T(8,128)} %param.26) | copy-start | bytes 6148
  24.4 32.9 %copy-start.12 = (s32[16,4]{0,1:T(4,128)S(1)}, s32[16,4]{0,1:T(4,128)}, u32[]{:S(2)}) copy-start(s32[16,4]{0,1:T(4,128)} %param.20) | copy-start | bytes 772
  24.4 33.0 %copy-start.4 = (bf16[16,16,256]{2,1,0:T(8,128)(2,1)S(1)}, bf16[16,16,256]{2,1,0:T(8,128)(2,1)}, u32[]{:S(2)}) copy-start(bf16[16,16,256]{2,1,0:T(8,128)(2,1)} %get-tuple-element.21.own) | copy-start | bytes 393220
  24.4 25.5 %all-to-all-start = ((bf16[32,16,256]{2,1,0:T(8,128)(2,1)}), bf16[32,16,256]{2,1,0:T(8,128)(2,1)S(1)}, u32[]{:S(2)}, u32[]{:S(2)}) async-start(bf16[32,16,256]{2,1,0:T(8,128)(2,1)} %get-tuple-element.20), calls=%async_computation | async-start | bytes 524288 | tf_op jit(solution)/shard_map/all_to_all | solution.py:504
  49.9 0.7 copy-start.1
  54.7 15.4 %all-to-all-start.1 = ((bf16[32,16,256]{2,1,0:T(8,128)(2,1)}), bf16[32,16,256]{2,1,0:T(8,128)(2,1)S(1)}, u32[]{:S(2)}, u32[]{:S(2)}) async-start(bf16[32,16,256]{2,1,0:T(8,128)(2,1)} %far.1), calls=%async_computation.1 | async-start | bytes 524288 | tf_op jit(solution)/shard_map/all_to_all | solution.py:506
  57.4 9.7 %collective-permute-start.4 = (bf16[16,16,256]{2,1,0:T(8,128)(2,1)S(1)}, bf16[16,16,256]{2,1,0:T(8,128)(2,1)S(1)}, u32[]{:S(2)}, u32[]{:S(2)}) collective-permute-start(bf16[16,16,256]{2,1,0:T(8,128)(2,1)S(1)} %copy-done.4), channel_id=1, source_target_pairs={{0,1},{1,0},{2,3},{3,2},{4,5},{5,4},{6,7},{7,6},{8,9},{9,8},{10,11... | collective-permute-start | bytes 393224 | tf_op jit(solution)/shard_map/ppermute | solution.py:43
  59.1 8.0 %collective-permute-start.5 = (bf16[16,16,256]{2,1,0:T(8,128)(2,1)S(1)}, bf16[16,16,256]{2,1,0:T(8,128)(2,1)S(1)}, u32[]{:S(2)}, u32[]{:S(2)}) collective-permute-start(bf16[16,16,256]{2,1,0:T(8,128)(2,1)S(1)} %copy-done.4), channel_id=1, source_target_pairs={{1,2},{2,1},{3,4},{4,3},{5,6},{6,5},{9,10},{10,9},{11,12},{12,11},... | collective-permute-start | bytes 393224 | tf_op jit(solution)/shard_map/ppermute | solution.py:43
  67.1 0.7 copy-start.5
  67.1 0.7 copy-start.6
  70.0 0.7 copy-start

commit v3 on v2

--- a/solution.py
+++ b/solution.py
@@ -11,6 +11,18 @@
 CHILDREN = 8
 
 
+def held(*arrays):
+    return [pltpu.with_memory_space_constraint(a, pltpu.VMEM) for a in arrays]
+
+
+def left(*arrays):
+    return [pltpu.with_memory_space_constraint(a, pltpu.HBM) for a in arrays]
+
+
+def params(mib):
+    return pltpu.CompilerParams(vmem_limit_bytes=mib << 20)
+
+
 def dot(a, b):
     return jnp.dot(a, b, preferred_element_type=f32)
 
@@ -31,6 +43,37 @@
     return n.bit_length() - 1
 
 
+def prepare(angle, smap, cx, cy, nz):
+    boxes, unknowns = smap.shape
+
+    def body(angle, smap, cosine, sine, chosen, depth):
+        cosine[...] = jnp.cos(angle[...])
+        sine[...] = jnp.sin(angle[...])
+        level = lax.broadcasted_iota(jnp.int32, (nz, unknowns), 0)
+        for b in range(boxes):
+            key = smap[b : b + 1, :]
+            key_z = key & (nz - 1)
+            key_x = key >> (log2(nz) + log2(cy))
+            lanes = slice(b * unknowns, (b + 1) * unknowns)
+            for x in range(cx):
+                hit = level == jnp.where(key_x == x, key_z, -1)
+                chosen[x * nz : (x + 1) * nz, lanes] = jnp.where(hit, 1.0, 0.0).astype(bf16)
+            depth[:, lanes] = jnp.broadcast_to((key >> log2(nz)) & (cy - 1), (8, unknowns))
+
+    shape = pltpu.VMEM(angle.shape, f32)
+    return pl.pallas_call(
+        body,
+        out_shape=(
+            shape,
+            shape,
+            pltpu.VMEM((cx * nz, boxes * unknowns), bf16),
+            pltpu.VMEM((8, boxes * unknowns), jnp.int32),
+        ),
+        compiler_params=params(6),
+        name="prepare",
+    )(*held(angle, smap))
+
+
 def swap_pairs(n, first):
     pairs = []
     for i in range(first, n - 1, 2):
@@ -40,7 +83,8 @@
 
 def swap(for_even, for_odd, axis):
     n = lax.axis_size(axis)
-    return [lax.ppermute(v, axis, swap_pairs(n, k)) for k, v in enumerate((for_even, for_odd))]
+    far = lax.ppermute(for_odd, axis, swap_pairs(n, 1))
+    return lax.ppermute(for_even, axis, swap_pairs(n, 0)), far
 
 
 def second_sweep(mat_real, mat_loss, field, sweep, columns, column_a, source, kinds, got_first, got_second, out, beside, store, cx, cy):
@@ -97,13 +141,15 @@
 
 def up_body(
     mat_real, mat_loss, field, sweep, columns, column_a, source, kinds, got_first, got_second,
-    smap, radiate, interp, cosine, sine, volume, cur, out, beside, cells, rows, *, cx, cy, groups, slices
+    chosen, depth, radiate, interp, cosine, sine, volume, cur, out, beside, cells, rows, fresh, sem,
+    *, cx, cy, groups, slices
 ):
     nz = field.shape[1]
     channels = field.shape[0] // (cx * cy)
     excite = channels // 2
     group = excite // groups
-    boxes, unknowns = smap.shape
+    boxes = cur.shape[0]
+    unknowns = depth.shape[1] // boxes
 
     def store(t, e, x, value):
         place = (e // group) * 2 * group + t * group + e % group
@@ -112,20 +158,16 @@
 
     second_sweep(
         mat_real, mat_loss, field, sweep, columns, column_a, source, kinds, got_first, got_second,
-        volume, beside, store, cx, cy
+        fresh, beside, store, cx, cy
     )
+    leaving = pltpu.make_async_copy(fresh, volume, sem)
+    leaving.start()
     lhs = jnp.concatenate([cells[x].astype(bf16) for x in range(cx)], axis=1)
     pair = 2
     for b in range(0, boxes, pair):
-        keys = jnp.concatenate([smap[b + j : b + j + 1, :] for j in range(pair)], axis=1)
-        key_z = keys & (nz - 1)
-        key_y = (keys >> log2(nz)) & (cy - 1)
-        key_x = keys >> (log2(nz) + log2(cy))
-        level = lax.broadcasted_iota(jnp.int32, (nz, pair * unknowns), 0)
-        hot = [
-            jnp.where(level == jnp.where(key_x == x, key_z, -1), 1.0, 0.0).astype(bf16) for x in range(cx)
-        ]
-        picked = dot(lhs, jnp.concatenate(hot, axis=0))
+        lanes = slice(b * unknowns, (b + pair) * unknowns)
+        picked = dot(lhs, chosen[:, lanes])
+        key_y = jnp.concatenate([depth[:, lanes]] * (channels // 8), axis=0)
         found = jnp.zeros((channels, pair * unknowns), f32)
         for y in range(cy):
             found = jnp.where(key_y == y, picked[y * channels : (y + 1) * channels], found)
@@ -156,14 +198,15 @@
             piece = jnp.concatenate([whole[p, s] for p in range(parents)], axis=0)
             for k in range(tile // width):
                 out[s * slices + n // width + k] = piece[:, k * width : (k + 1) * width]
-
-
-def up(volume_args, smap, radiate, interp, cosine, sine, cx, cy, groups, slices):
+    leaving.wait()
+
+
+def up(volume_args, chosen, depth, boxes, radiate, interp, cosine, sine, cx, cy, groups, slices):
     field = volume_args[2]
     nz = field.shape[1]
     total = field.shape[0] // cy
     channels = total // cx
-    boxes, unknowns = smap.shape
+    unknowns = depth.shape[1] // boxes
     width = interp.shape[1] // slices
     piece_rows = boxes // CHILDREN * (channels // groups)
     smem = pl.BlockSpec(memory_space=pltpu.SMEM)
@@ -171,23 +214,25 @@
     return pl.pallas_call(
         lambda *refs: up_body(*refs, cx=cx, cy=cy, groups=groups, slices=slices),
         out_shape=(
-            jax.ShapeDtypeStruct(field.shape, f32),
-            jax.ShapeDtypeStruct((boxes, channels // 2, 2 * unknowns), bf16),
-            jax.ShapeDtypeStruct((groups * slices, piece_rows, width), bf16),
+            pltpu.HBM(field.shape, f32),
+            pltpu.VMEM((boxes, channels // 2, 2 * unknowns), bf16),
+            pltpu.VMEM((groups * slices, piece_rows, width), bf16),
         ),
-        in_specs=[smem, smem] + [vmem] * 13,
-        out_specs=(vmem,) * 3,
+        in_specs=[smem, smem] + [vmem] * 14,
+        out_specs=(pl.BlockSpec(memory_space=pltpu.HBM), vmem, vmem),
         scratch_shapes=[
             pltpu.VMEM((2, total, nz), f32),
             pltpu.VMEM((cx, cy * channels, nz), f32),
             pltpu.VMEM((boxes * channels, 2 * unknowns), bf16),
+            pltpu.VMEM(field.shape, f32),
+            pltpu.SemaphoreType.DMA(()),
         ],
-        name="up",
-    )(*volume_args, smap, radiate, interp, cosine, sine)
+        compiler_params=params(16), name="up",
+    )(*volume_args[:2], *held(*volume_args[2:], chosen, depth, radiate, interp, cosine, sine))
 
 
 def far_body(lists, kinds, sources, translate, out, plain, turned):
-    targets, far = lists.shape
+    far, targets = lists.shape
     devices, piece_rows, width = sources.shape
     per = targets // devices
     tile = piece_rows // per
@@ -201,8 +246,8 @@
             t = d * per + j
             total = jnp.zeros((tile, width), f32)
             for f in range(far):
-                p = lists[t, f]
-                k = kinds[t, f]
+                p = lists[f, t]
+                k = kinds[f, t]
                 factor = translate[k]
                 total = total + factor[0:1] * plain[p] + factor[1:2] * turned[p]
             results.append(total)
@@ -213,49 +258,58 @@
 
 
 def far_combine(lists, kinds, sources, translate):
-    targets = lists.shape[0]
+    targets = lists.shape[1]
     devices, piece_rows, width = sources.shape
     tile = piece_rows // (targets // devices)
     smem = pl.BlockSpec(memory_space=pltpu.SMEM)
     vmem = pl.BlockSpec(memory_space=pltpu.VMEM)
     return pl.pallas_call(
         far_body,
-        out_shape=jax.ShapeDtypeStruct(sources.shape, bf16),
+        out_shape=pltpu.VMEM(sources.shape, bf16),
         in_specs=[smem, smem, vmem, vmem],
         out_specs=vmem,
         scratch_shapes=[pltpu.VMEM((targets, tile, width), f32)] * 2,
-        name="far",
-    )(lists, kinds, sources, translate)
-
-
-def near_body(spots, own, first, second, blocks, out, boxes_all, rows):
+        compiler_params=params(8), name="far",
+    )(lists, kinds, *held(sources, translate))
+
+
+def near_body(lists, own, first, second, blocks, angle, out, cosine, sine, boxes_all, rows):
+    cosine[...] = jnp.cos(angle[...])
+    sine[...] = jnp.sin(angle[...])
     boxes, excite, k = own.shape
-    slots = spots.shape[1]
+    slots = lists.shape[0]
+    shard = lax.axis_index("shard")
+    base = (lax.axis_index("space") * lax.axis_size("shard") + shard) * boxes
+    even = lax.rem(shard, 2) == 0
+    above = jnp.where(even, 0, boxes)
+    below = jnp.where(even, 3 * boxes, 2 * boxes)
     boxes_all[0:boxes] = own[...]
     boxes_all[boxes : 2 * boxes] = first[...]
     boxes_all[2 * boxes : 3 * boxes] = second[...]
     for b in range(boxes):
         for s in range(slots):
-            rows[b * excite : (b + 1) * excite, s * k : (s + 1) * k] = boxes_all[spots[b, s]]
+            away = lists[s, b] - base
+            spot = away + jnp.where(away < 0, below, jnp.where(away < boxes, 0, above))
+            rows[b * excite : (b + 1) * excite, s * k : (s + 1) * k] = boxes_all[spot]
     out[...] = dot(rows[...], blocks[...]).reshape(out.shape)
 
 
-def near_force(spots, own, first, second, blocks):
+def near_force(lists, own, first, second, blocks, angle):
     boxes, excite, k = own.shape
-    slots = spots.shape[1]
+    slots = lists.shape[0]
     smem = pl.BlockSpec(memory_space=pltpu.SMEM)
     vmem = pl.BlockSpec(memory_space=pltpu.VMEM)
     return pl.pallas_call(
         near_body,
-        out_shape=jax.ShapeDtypeStruct((boxes, excite, k), f32),
-        in_specs=[smem, vmem, vmem, vmem, vmem],
-        out_specs=vmem,
+        out_shape=(pltpu.VMEM((boxes, excite, k), f32),) + (pltpu.VMEM(angle.shape, f32),) * 2,
+        in_specs=[smem] + [vmem] * 5,
+        out_specs=(vmem,) * 3,
         scratch_shapes=[
             pltpu.VMEM((3 * boxes, excite, k), bf16),
             pltpu.VMEM((boxes * excite, slots * k), bf16),
         ],
-        name="near",
-    )(spots, own, first, second, blocks.reshape(slots * k, k))
+        compiler_params=params(6), name="near",
+    )(lists, *held(own, first, second, blocks.reshape(slots * k, k), angle))
 
 
 def down_body(pieces, near, radiate, interp, cosine, sine, out, shifted, *, groups, slices):
@@ -292,8 +346,8 @@
         lambda *refs: down_body(*refs, groups=groups, slices=slices),
         out_shape=jax.ShapeDtypeStruct(near.shape, f32),
         scratch_shapes=[pltpu.VMEM((boxes * excite * 2, interp.shape[1]), f32)],
-        name="down",
-    )(pieces, near, radiate, interp, cosine, sine)
+        compiler_params=params(16), name="down",
+    )(*held(pieces, near, radiate, interp, cosine, sine))
 
 
 def is_even(axis):
@@ -337,32 +391,47 @@
     )
 
 
-def edge_body(field, source, kinds, first, second, *, cx, cy):
-    total = field.shape[0] // cy
+def edge_body(field, source, kinds, first, second, layers, kind_rows, sem, kind_sem):
+    total, cy, _ = field.shape
+    cx = kinds.shape[0]
     even = is_even("shard")
-
-    def face(inner, outer):
-        def layer(ref, y):
-            return jnp.concatenate(
-                [ref[pl.ds(r * cy + y, 8, stride=cy), :] for r in range(0, total, 8)], axis=0
-            )
-
-        kind = kinds[pl.ds(outer, cx, stride=cy), :].astype(f32) + 1.0
-        kind = jnp.concatenate([kind] * (16 // cx), axis=0)
-        return jnp.concatenate([layer(field, inner), layer(field, outer), layer(source, outer), kind], axis=0)
-
-    high = face(cy - 2, cy - 1)
-    low = face(1, 0)
-    first[...] = jnp.where(even, high, low).astype(bf16)
-    second[...] = jnp.where(even, low, high).astype(bf16)
-
-
-def edges(field, source, kinds, cx, cy):
-    rows = 3 * (field.shape[0] // cy) + 16
-    message = jax.ShapeDtypeStruct((rows, field.shape[1]), bf16)
+    faces = ((cy - 2, cy - 1), (1, 0))
+    copies = []
+    for i, (inner, outer) in enumerate(faces):
+        for k, (ref, y) in enumerate(((field, inner), (field, outer), (source, outer))):
+            copies.append(pltpu.make_async_copy(ref.at[:, y], layers.at[i, k], sem.at[i, k]))
+        copies.append(pltpu.make_async_copy(kinds.at[:, outer], kind_rows.at[i], kind_sem.at[i]))
+    for copy in copies:
+        copy.start()
+    for copy in copies:
+        copy.wait()
+    for k in range(3):
+        rows = slice(k * total, (k + 1) * total)
+        first[rows, :] = jnp.where(even, layers[0, k], layers[1, k]).astype(bf16)
+        second[rows, :] = jnp.where(even, layers[1, k], layers[0, k]).astype(bf16)
+    kind = [jnp.concatenate([kind_rows[i].astype(f32) + 1.0] * (16 // cx), axis=0) for i in range(2)]
+    first[3 * total :, :] = jnp.where(even, kind[0], kind[1]).astype(bf16)
+    second[3 * total :, :] = jnp.where(even, kind[1], kind[0]).astype(bf16)
+
+
+def edges(field, source, kinds):
+    total, _, nz = field.shape
+    cx = kinds.shape[0]
+    message = pltpu.VMEM((3 * total + 16, nz), bf16)
+    anywhere = pl.BlockSpec(memory_space=pl.ANY)
     return pl.pallas_call(
-        lambda *refs: edge_body(*refs, cx=cx, cy=cy), out_shape=(message, message), name="edges"
-    )(field, source, kinds)
+        edge_body,
+        out_shape=(message, message),
+        in_specs=[anywhere] * 3,
+        scratch_shapes=[
+            pltpu.VMEM((2, 3, total, nz), f32),
+            pltpu.VMEM((2, cx, nz), jnp.int32),
+            pltpu.SemaphoreType.DMA((2, 3)),
+            pltpu.SemaphoreType.DMA((2,)),
+        ],
+        compiler_params=params(6),
+        name="edges",
+    )(*left(field, source, kinds))
 
 
 def first_body(
@@ -441,21 +510,21 @@
     channels = total // cx
     smem = pl.BlockSpec(memory_space=pltpu.SMEM)
     vmem = pl.BlockSpec(memory_space=pltpu.VMEM)
-    message = jax.ShapeDtypeStruct((2 * channels * cy + 2 * channels + cy, nz), bf16)
+    message = pltpu.VMEM((2 * channels * cy + 2 * channels + cy, nz), bf16)
     return pl.pallas_call(
         lambda *refs: first_body(*refs, cx=cx, cy=cy),
         out_shape=(
-            jax.ShapeDtypeStruct(field.shape, f32),
-            jax.ShapeDtypeStruct((2, total, nz), f32),
-            jax.ShapeDtypeStruct((2, 8, nz), f32),
+            pltpu.VMEM(field.shape, f32),
+            pltpu.VMEM((2, total, nz), f32),
+            pltpu.VMEM((2, 8, nz), f32),
             message,
             message,
         ),
         in_specs=[smem, smem] + [vmem] * 5,
         out_specs=(vmem,) * 5,
         scratch_shapes=[pltpu.VMEM((2, total, nz), f32)],
-        name="first_sweep",
-    )(mat_real, mat_loss, field, source, kinds, got_first, got_second)
+        compiler_params=params(8), name="first_sweep",
+    )(mat_real, mat_loss, *held(field, source, kinds, got_first, got_second))
 
 
 def shards(
@@ -478,20 +547,22 @@
     groups = lax.axis_size("space")
     slices = lax.axis_size("shard")
     excite, cells_x, cells_y, cells_z = volume_field.shape[1:]
-    cosine = jnp.cos(phase_angle)
-    sine = jnp.sin(phase_angle)
+    cosine, sine, chosen, depth = prepare(phase_angle, surface_map, cells_x, cells_y, cells_z)
     weights = radiate.reshape(2 * radiate.shape[1], radiate.shape[2])
     field = volume_field.reshape(-1, cells_z)
     flat_source = source.reshape(-1, cells_z)
     kinds = material.reshape(-1, cells_z)
-    got_y = swap(*edges(field, flat_source, kinds, cells_x, cells_y), "shard")
+    bricks = (-1, cells_y, cells_z)
+    got_y = swap(*edges(volume_field.reshape(bricks), source.reshape(bricks), material), "shard")
     sweep, columns, column_a, *to_x = first_sweep(
         mat_real, mat_loss, field, flat_source, kinds, *got_y, cells_x, cells_y
     )
     got_x = swap(*to_x, "space")
     current, currents, pieces = up(
         (mat_real, mat_loss, field, sweep, columns, column_a, flat_source, kinds, *got_x),
-        surface_map,
+        chosen,
+        depth,
+        near_boxes.shape[0],
         weights,
         interp,
         cosine,
@@ -502,19 +573,11 @@
         slices,
     )
     directed = lax.all_to_all(pieces, every, split_axis=0, concat_axis=0, tiled=True)
-    combined = far_combine(far_parents, far_kind, directed, translate)
+    first, second = swap(currents, currents, "shard")
+    directed, first, second = lax.optimization_barrier((directed, first, second))
+    combined = far_combine(far_parents.T, far_kind.T, directed, translate)
     incoming = lax.all_to_all(combined, every, split_axis=0, concat_axis=0, tiled=True)
-
-    shard = lax.axis_index("shard")
-    rank = lax.axis_index("space") * slices + shard
-    boxes = near_boxes.shape[0]
-    first, second = swap(currents, currents, "shard")
-    offset = near_boxes - rank * boxes
-    even = shard % 2 == 0
-    above = jnp.where(even, 0, boxes)
-    below = jnp.where(even, 2 * boxes, boxes) + boxes
-    spots = offset + jnp.where(offset < 0, below, jnp.where(offset < boxes, 0, above))
-    near = near_force(spots, currents, first, second, near_blocks)
+    near, cosine, sine = near_force(near_boxes.T, currents, first, second, near_blocks, phase_angle)
     forcing = down(incoming, near, weights, interp, cosine, sine, groups, slices)
     return (current.reshape(volume_field.shape), forcing)
 

time: 75.2 us -> 65.8 us (0.87)
  Pallas kernels: 24.2 us -> 15.4 us
  starting transfers between devices: 24.3 us -> 30.7 us
  waiting for transfers between devices: 18.4 us -> 14.2 us
  local copies, waits for them, and re-layouts: 6.55 us -> 4.21 us
    all_to_all x1, waiting for transfers between devices: 9.04 us -> 0.01 us  [shards(): lax.all_to_all(pieces, every, split_axis=0, concat_axis=0, tiled=True)]
    all_to_all x1, waiting for transfers between devices: 0.01 us -> 6.52 us  [shards(): lax.all_to_all(combined, every, split_axis=0, concat_axis=0, tiled=True)]
    ppermute x6, starting transfers between devices: 6.67 us -> 9.64 us  [the longest x3 7.64 us: swap(): return (lax.ppermute(for_even, axis, swap_pairs(n, 0)), far)]
    all_to_all x1, starting transfers between devices: 2.58 us -> 5.47 us  [shards(): lax.all_to_all(combined, every, split_axis=0, concat_axis=0, tiled=True)]
    pallas_call x1, Pallas kernels: 7.75 us -> 5.3 us  [up(): pl.pallas_call(lambda *refs: up_body(*refs, cx=cx, cy=cy, groups=groups,...]
    pallas_call x3 -> x4, Pallas kernels: 8.7 us -> 6.31 us  [the longest x1 2.97 us: far_combine(): pl.pallas_call(far_body, out_shape=pltpu.VMEM(sources.shape, bf16), in_sp...]
    pallas_call x1, Pallas kernels: 3.67 us -> 1.55 us  [first_sweep(): pl.pallas_call(lambda *refs: first_body(*refs, cx=cx, cy=cy), out_shape=(...]
    pallas_call x1, Pallas kernels: 4.03 us -> 2.26 us  [down(): pl.pallas_call(lambda *refs: down_body(*refs, groups=groups, slices=slice...]
  transfers between devices with their start and end apart: 8 -> 8, of which waited for: 4 -> 3; matrix products, arithmetic and copies ran while one was open for 4% -> 0% of each run, Pallas kernels for 3% -> 3%
where the time goes in v3:
time: 65.8 us; the launch traced here: 65.5 us
  starting transfers between devices  30.7 us (47%)
  Pallas kernels  15.4 us (23%)
  waiting for transfers between devices  14.2 us (22%)
  local copies, waits for them, and re-layouts  4.21 us (6%)
  between operations  0.93 us (1%)
    all_to_all x1, starting transfers between devices, shards(): lax.all_to_all(pieces, every, split_axis=0, concat_axis=0, tiled=True)  15.6 us
    ppermute x3, waiting for transfers between devices, swap(): return (lax.ppermute(for_even, axis, swap_pairs(n, 0)), far)  7.65 us
    ppermute x3, starting transfers between devices, swap(): return (lax.ppermute(for_even, axis, swap_pairs(n, 0)), far)  7.64 us
    all_to_all x1, waiting for transfers between devices, shards(): lax.all_to_all(combined, every, split_axis=0, concat_axis=0, tiled=True)  6.52 us
    all_to_all x1, starting transfers between devices, shards(): lax.all_to_all(combined, every, split_axis=0, concat_axis=0, tiled=True)  5.47 us
    pallas_call x1, Pallas kernels, up(): pl.pallas_call(lambda *refs: up_body(*refs, cx=cx, cy=cy, groups=groups,...  5.3 us
    unnamed x36, local copies, waits for them, and re-layouts  4.21 us
    pallas_call x1, Pallas kernels, far_combine(): pl.pallas_call(far_body, out_shape=pltpu.VMEM(sources.shape, bf16), in_sp...  2.97 us
  transfers between devices with their start and end apart: 8, of which 3 were waited for; matrix products, arithmetic and copies ran while one was open for 0% of the time, Pallas kernels for 3%

profile of v3, /device:TPU:0, one launch (start us, length us, event | category | flops | bytes accessed | tf_op | source)
XLA Modules:
  0.0 65.5 jit_solution(11608393840275530367)
XLA Ops:
  0.6 0.0 copy-start.6
  0.6 0.0 copy-start
  0.7 0.0 copy-start.1
  0.7 0.0 copy-start.17
  0.7 0.0 copy-start.16
  0.7 0.0 copy-start.7
  0.7 0.0 copy-start.12
  0.7 0.0 copy-start.2
  0.7 0.0 copy-start.3
  0.7 1.3 %edges.1 = (bf16[400,128]{1,0:T(8,128)(2,1)S(1)}, bf16[400,128]{1,0:T(8,128)(2,1)S(1)}) custom-call(f32[128,16,128]{2,1,0:T(8,128)} %bitcast.11, f32[128,16,128]{2,1,0:T(8,128)} %bitcast.14, s32[4,16,128]{2,1,0:T(8,128)} %kinds.1), custom_call_target="tpu_custom_call" | custom-call | tf_op jit(solution)/shard_map/edges/pallas_call | solution.py:422
  2.0 3.0 %collective-permute-start = (bf16[400,128]{1,0:T(8,128)(2,1)S(1)}, bf16[400,128]{1,0:T(8,128)(2,1)S(1)}, u32[]{:S(2)}, u32[]{:S(2)}) collective-permute-start(bf16[400,128]{1,0:T(8,128)(2,1)S(1)} %get-tuple-element.22), channel_id=1, source_target_pairs={{0,1},{1,0},{2,3},{3,2},{4,5},{5,4},{6,7},{7,6},{8,9},{9,8},{10,11... | collective-permute-start | bytes 307208 | tf_op jit(solution)/shard_map/ppermute | solution.py:87
  5.1 0.7 %collective-permute-start.1 = (bf16[400,128]{1,0:T(8,128)(2,1)S(1)}, bf16[400,128]{1,0:T(8,128)(2,1)S(1)}, u32[]{:S(2)}, u32[]{:S(2)}) collective-permute-start(bf16[400,128]{1,0:T(8,128)(2,1)S(1)} %get-tuple-element.23), channel_id=1, source_target_pairs={{1,2},{2,1},{3,4},{4,3},{5,6},{6,5},{9,10},{10,9},{11,12},{12,11},... | collective-permute-start | bytes 307208 | tf_op jit(solution)/shard_map/ppermute | solution.py:86
  5.7 2.2 %collective-permute-done.refs_5_ = bf16[400,128]{1,0:T(8,128)(2,1)S(1)} collective-permute-done((bf16[400,128]{1,0:T(8,128)(2,1)S(1)}, bf16[400,128]{1,0:T(8,128)(2,1)S(1)}, u32[]{:S(2)}, u32[]{:S(2)}) %collective-permute-start) | collective-permute-done | bytes 102432 | tf_op jit(solution)/shard_map/ppermute | solution.py:87
  7.9 0.0 collective-permute-done.1.refs_6_
  7.9 0.0 copy-done.6
  7.9 0.0 copy-done
  8.0 1.6 %first_sweep.1 = (f32[2048,128]{1,0:T(8,128)S(1)}, f32[2,128,128]{2,1,0:T(8,128)S(1)}, f32[2,8,128]{2,1,0:T(8,128)S(1)}, bf16[1104,128]{1,0:T(8,128)(2,1)S(1)}, bf16[1104,128]{1,0:T(8,128)(2,1)S(1)}) custom-call(f32[8]{0:T(128)S(1)} %copy-done.16, f32[8]{0:T(128)S(1)} %copy-done.17, f32[2048,128]{1,0:T(8,128)S(1)} %bitcast.12, f32[2048,128]{1,0:T(8,128)S(1)} %bitcast.15, ...), custom_call_target="tpu_custom_call" | custom-call | tf_op jit(solution)/shard_map/first_sweep/pallas_call | solution.py:514
  9.5 0.1 collective-permute-start.2
  9.6 0.7 %collective-permute-start.3 = (bf16[1104,128]{1,0:T(8,128)(2,1)S(1)}, bf16[1104,128]{1,0:T(8,128)(2,1)S(1)}, u32[]{:S(2)}, u32[]{:S(2)}) collective-permute-start(bf16[1104,128]{1,0:T(8,128)(2,1)S(1)} %get-tuple-element.28), channel_id=1, source_target_pairs={{8,16},{16,8},{9,17},{17,9},{10,18},{18,10},{11,19},{19,11},{12,20... | collective-permute-start | bytes 847880 | tf_op jit(solution)/shard_map/ppermute | solution.py:86
  10.3 1.0 %prepare.1 = (f32[8,2048]{1,0:T(8,128)S(1)}, f32[8,2048]{1,0:T(8,128)S(1)}, bf16[512,2048]{1,0:T(8,128)(2,1)S(1)}, s32[8,2048]{1,0:T(8,128)S(1)}) custom-call(f32[8,2048]{1,0:T(8,128)S(1)} %copy-done.7, s32[16,128]{1,0:T(8,128)S(1)} %copy-done.12), custom_call_target="tpu_custom_call" | custom-call | tf_op jit(solution)/shard_map/prepare/pallas_call | solution.py:64
  11.3 0.0 collective-permute-done.2.refs_8_
  11.3 0.0 collective-permute-done.3.refs_9_
  11.4 0.0 copy-done.2
  11.4 0.0 copy-done.3
  11.4 0.0 copy-start.4
  11.4 0.0 copy-start.13
  11.4 0.0 copy-start.14
  11.4 5.3 %up.1 = (f32[2048,128]{1,0:T(8,128)}, bf16[16,16,256]{2,1,0:T(8,128)(2,1)S(1)}, bf16[32,16,256]{2,1,0:T(8,128)(2,1)}) custom-call(f32[8]{0:T(128)S(1)} %copy-done.16, f32[8]{0:T(128)S(1)} %copy-done.17, f32[2048,128]{1,0:T(8,128)S(1)} %bitcast.13, f32[2048,128]{1,0:T(8,128)S(1)} %get-tuple-element.24.refs_3_, f32[2,128,128]{2,1,0:T(8,128)S(1)} %get-tuple-element.25.refs_4_, ...), custom_call_target="tpu_custom_call" | custom-call | tf_op jit(solution)/shard_map/up/pallas_call | solution.py:214
  16.7 0.0 copy-start.15
  16.7 15.6 %all-to-all-start = ((bf16[32,16,256]{2,1,0:T(8,128)(2,1)}), bf16[32,16,256]{2,1,0:T(8,128)(2,1)S(1)}, u32[]{:S(2)}, u32[]{:S(2)}) async-start(bf16[32,16,256]{2,1,0:T(8,128)(2,1)} %get-tuple-element.34), calls=%async_computation | async-start | bytes 524288 | tf_op jit(solution)/shard_map/all_to_all | solution.py:575
  32.4 0.7 %collective-permute-start.5 = (bf16[16,16,256]{2,1,0:T(8,128)(2,1)S(1)}, bf16[16,16,256]{2,1,0:T(8,128)(2,1)S(1)}, u32[]{:S(2)}, u32[]{:S(2)}) collective-permute-start(bf16[16,16,256]{2,1,0:T(8,128)(2,1)S(1)} %get-tuple-element.35.own), channel_id=1, source_target_pairs={{1,2},{2,1},{3,4},{4,3},{5,6},{6,5},{9,10},{10,9},{11,12},{12,11},... | collective-permute-start | bytes 393224 | tf_op jit(solution)/shard_map/ppermute | solution.py:86
  33.0 4.5 %collective-permute-start.4 = (bf16[16,16,256]{2,1,0:T(8,128)(2,1)S(1)}, bf16[16,16,256]{2,1,0:T(8,128)(2,1)S(1)}, u32[]{:S(2)}, u32[]{:S(2)}) collective-permute-start(bf16[16,16,256]{2,1,0:T(8,128)(2,1)S(1)} %get-tuple-element.35.own), channel_id=1, source_target_pairs={{0,1},{1,0},{2,3},{3,2},{4,5},{5,4},{6,7},{7,6},{8,9},{9,8},{10,11... | collective-permute-start | bytes 393224 | tf_op jit(solution)/shard_map/ppermute | solution.py:87
  37.6 0.0 collective-permute-done.5.second
  37.6 0.7 copy-done.8
  38.2 5.4 %collective-permute-done.4.first = bf16[16,16,256]{2,1,0:T(8,128)(2,1)S(1)} collective-permute-done((bf16[16,16,256]{2,1,0:T(8,128)(2,1)S(1)}, bf16[16,16,256]{2,1,0:T(8,128)(2,1)S(1)}, u32[]{:S(2)}, u32[]{:S(2)}) %collective-permute-start.4) | collective-permute-done | bytes 131104 | tf_op jit(solution)/shard_map/ppermute | solution.py:87
  43.7 0.7 copy-done.10
  44.3 0.0 all-to-all-done.sources
  44.3 0.0 copy-done.13
  44.3 3.0 %far.1 = bf16[32,16,256]{2,1,0:T(8,128)(2,1)} custom-call(s32[8,64]{1,0:T(8,128)S(1)} %bitcast.22, s32[8,64]{1,0:T(8,128)S(1)} %bitcast.23, bf16[32,16,256]{2,1,0:T(8,128)(2,1)S(1)} %all-to-all-done.sources, f32[316,2,256]{2,1,0:T(2,128)S(1)} %copy-done.4), custom_call_target="tpu_custom_call" | custom-call | tf_op jit(solution)/shard_map/far/pallas_call | solution.py:266
  47.3 5.5 %all-to-all-start.1 = ((bf16[32,16,256]{2,1,0:T(8,128)(2,1)}), bf16[32,16,256]{2,1,0:T(8,128)(2,1)S(1)}, u32[]{:S(2)}, u32[]{:S(2)}) async-start(bf16[32,16,256]{2,1,0:T(8,128)(2,1)} %far.1), calls=%async_computation.1 | async-start | bytes 524288 | tf_op jit(solution)/shard_map/all_to_all | solution.py:579
  52.8 0.0 copy-done.15
  52.8 0.0 copy-start.5
  52.8 1.0 %copy-done.5 = bf16[4,256,256]{2,1,0:T(8,128)(2,1)S(1)} copy-done((bf16[4,256,256]{2,1,0:T(8,128)(2,1)S(1)}, bf16[4,256,256]{2,1,0:T(8,128)(2,1)}, u32[]{:S(2)}) %copy-start.5) | copy-done | bytes 524312
  53.8 0.9 %copy-done.9 = bf16[16,16,256]{2,1,0:T(8,128)(2,1)S(1)} copy-done((bf16[16,16,256]{2,1,0:T(8,128)(2,1)S(1)}, bf16[16,16,256]{2,1,0:T(8,128)(2,1)}, u32[]{:S(2)}) %copy-start.9) | copy-done | bytes 131096
  54.7 0.9 %copy-done.11 = bf16[16,16,256]{2,1,0:T(8,128)(2,1)S(1)} copy-done((bf16[16,16,256]{2,1,0:T(8,128)(2,1)S(1)}, bf16[16,16,256]{2,1,0:T(8,128)(2,1)}, u32[]{:S(2)}) %copy-start.11) | copy-done | bytes 131096
  55.6 1.0 %near.1 = (f32[16,16,256]{2,1,0:T(8,128)S(1)}, f32[8,2048]{1,0:T(8,128)S(1)}, f32[8,2048]{1,0:T(8,128)S(1)}) custom-call(s32[4,16]{1,0:T(4,128)S(1)} %bitcast.24, bf16[16,16,256]{2,1,0:T(8,128)(2,1)S(1)} %get-tuple-element.35.own, bf16[16,16,256]{2,1,0:T(8,128)(2,1)S(1)} %copy-done.11, bf16[16,16,256]{2,1,0:T(8,128)(2,1)S(1)} %copy-done.9, ...), custom_call_target="tpu_custom_call" | custom-call | tf_op jit(solution)/shard_map/near/pallas_call | solution.py:302
  56.7 6.5 %all-to-all-done.1.refs_0_ = bf16[32,16,256]{2,1,0:T(8,128)(2,1)S(1)} async-done(((bf16[32,16,256]{2,1,0:T(8,128)(2,1)}), bf16[32,16,256]{2,1,0:T(8,128)(2,1)S(1)}, u32[]{:S(2)}, u32[]{:S(2)}) %all-to-all-start.1) | async-done | bytes 262176 | tf_op jit(solution)/shard_map/all_to_all | solution.py:579
  63.2 2.3 %down.1 = f32[16,16,256]{2,1,0:T(8,128)} custom-call(bf16[32,16,256]{2,1,0:T(8,128)(2,1)S(1)} %all-to-all-done.1.refs_0_, f32[16,16,256]{2,1,0:T(8,128)S(1)} %get-tuple-element.39.refs_1_, bf16[256,512]{1,0:T(8,128)(2,1)S(1)} %bitcast.18, bf16[512,2048]{1,0:T(8,128)(2,1)S(1)} %copy-done.2, f32[8,2048]{1,0:T(8,128)S(1)} %get-tuple-element.40.refs_4_, ...), custom_call_target="tpu_custom_call" | custom-call | tf_op jit(solution)/shard_map/down/pallas_call | solution.py:345
  (11 shorter events, 0.0 us)
Async XLA Ops:
  0.6 7.3 %copy-start.6 = (s32[4,16,128]{2,1,0:T(8,128)S(1)}, s32[4,16,128]{2,1,0:T(8,128)}, u32[]{:S(2)}) copy-start(s32[4,16,128]{2,1,0:T(8,128)} %kinds.1) | copy-start | bytes 98308
  0.6 7.3 %copy-start = (f32[2,16,4,16,128]{4,3,2,1,0:T(8,128)S(1)}, f32[2,16,4,16,128]{4,3,2,1,0:T(8,128)}, u32[]{:S(2)}) copy-start(f32[2,16,4,16,128]{4,3,2,1,0:T(8,128)} %param.14) | copy-start | bytes 3145732
  0.7 7.3 %copy-start.1 = (f32[2,16,4,16,128]{4,3,2,1,0:T(8,128)S(1)}, f32[2,16,4,16,128]{4,3,2,1,0:T(8,128)}, u32[]{:S(2)}) copy-start(f32[2,16,4,16,128]{4,3,2,1,0:T(8,128)} %param.15) | copy-start | bytes 3145732
  0.7 7.3 %copy-start.17 = (f32[8]{0:T(128)S(1)}, f32[8]{0:T(128)}, u32[]{:S(2)}) copy-start(f32[8]{0:T(128)} %refs_1_.3) | copy-start | bytes 100
  0.7 7.3 %copy-start.16 = (f32[8]{0:T(128)S(1)}, f32[8]{0:T(128)}, u32[]{:S(2)}) copy-start(f32[8]{0:T(128)} %refs_0_.3) | copy-start | bytes 100
  0.7 9.6 %copy-start.7 = (f32[8,2048]{1,0:T(8,128)S(1)}, f32[8,2048]{1,0:T(8,128)}, u32[]{:S(2)}) copy-start(f32[8,2048]{1,0:T(8,128)} %angle.3) | copy-start | bytes 196612
  0.7 9.6 %copy-start.12 = (s32[16,128]{1,0:T(8,128)S(1)}, s32[16,128]{1,0:T(8,128)}, u32[]{:S(2)}) copy-start(s32[16,128]{1,0:T(8,128)} %smap.1) | copy-start | bytes 24580
  0.7 10.7 %copy-start.2 = (bf16[512,2048]{1,0:T(8,128)(2,1)S(1)}, bf16[512,2048]{1,0:T(8,128)(2,1)}, u32[]{:S(2)}) copy-start(bf16[512,2048]{1,0:T(8,128)(2,1)} %refs_3_.1) | copy-start | bytes 6291460
  0.7 10.7 %copy-start.3 = (bf16[2,128,512]{2,1,0:T(8,128)(2,1)S(1)}, bf16[2,128,512]{2,1,0:T(8,128)(2,1)}, u32[]{:S(2)}) copy-start(bf16[2,128,512]{2,1,0:T(8,128)(2,1)} %param.22) | copy-start | bytes 786436
  2.0 5.9 %collective-permute-start = (bf16[400,128]{1,0:T(8,128)(2,1)S(1)}, bf16[400,128]{1,0:T(8,128)(2,1)S(1)}, u32[]{:S(2)}, u32[]{:S(2)}) collective-permute-start(bf16[400,128]{1,0:T(8,128)(2,1)S(1)} %get-tuple-element.22), channel_id=1, source_target_pairs={{0,1},{1,0},{2,3},{3,2},{4,5},{5,4},{6,7},{7,6},{8,9},{9,8},{10,11... | collective-permute-start | bytes 307208 | tf_op jit(solution)/shard_map/ppermute | solution.py:87
  5.1 2.9 %collective-permute-start.1 = (bf16[400,128]{1,0:T(8,128)(2,1)S(1)}, bf16[400,128]{1,0:T(8,128)(2,1)S(1)}, u32[]{:S(2)}, u32[]{:S(2)}) collective-permute-start(bf16[400,128]{1,0:T(8,128)(2,1)S(1)} %get-tuple-element.23), channel_id=1, source_target_pairs={{1,2},{2,1},{3,4},{4,3},{5,6},{6,5},{9,10},{10,9},{11,12},{12,11},... | collective-permute-start | bytes 307208 | tf_op jit(solution)/shard_map/ppermute | solution.py:86
  9.5 1.8 %collective-permute-start.2 = (bf16[1104,128]{1,0:T(8,128)(2,1)S(1)}, bf16[1104,128]{1,0:T(8,128)(2,1)S(1)}, u32[]{:S(2)}, u32[]{:S(2)}) collective-permute-start(bf16[1104,128]{1,0:T(8,128)(2,1)S(1)} %get-tuple-element.27), channel_id=1, source_target_pairs={{0,8},{8,0},{16,24},{24,16},{1,9},{9,1},{17,25},{25,17},{2,10},{10... | collective-permute-start | bytes 847880 | tf_op jit(solution)/shard_map/ppermute | solution.py:87
  9.6 1.7 %collective-permute-start.3 = (bf16[1104,128]{1,0:T(8,128)(2,1)S(1)}, bf16[1104,128]{1,0:T(8,128)(2,1)S(1)}, u32[]{:S(2)}, u32[]{:S(2)}) collective-permute-start(bf16[1104,128]{1,0:T(8,128)(2,1)S(1)} %get-tuple-element.28), channel_id=1, source_target_pairs={{8,16},{16,8},{9,17},{17,9},{10,18},{18,10},{11,19},{19,11},{12,20... | collective-permute-start | bytes 847880 | tf_op jit(solution)/shard_map/ppermute | solution.py:86
  11.4 32.9 %copy-start.4 = (f32[316,2,256]{2,1,0:T(2,128)S(1)}, f32[316,2,256]{2,1,0:T(2,128)}, u32[]{:S(2)}) copy-start(f32[316,2,256]{2,1,0:T(2,128)} %translate.1) | copy-start | bytes 1941508
  11.4 32.9 %copy-start.13 = (s32[64,8]{0,1:T(8,128)S(1)}, s32[64,8]{0,1:T(8,128)}, u32[]{:S(2)}) copy-start(s32[64,8]{0,1:T(8,128)} %param.25) | copy-start | bytes 6148
  11.4 32.9 %copy-start.14 = (s32[64,8]{0,1:T(8,128)S(1)}, s32[64,8]{0,1:T(8,128)}, u32[]{:S(2)}) copy-start(s32[64,8]{0,1:T(8,128)} %param.26) | copy-start | bytes 6148
  16.7 36.1 %copy-start.15 = (s32[16,4]{0,1:T(4,128)S(1)}, s32[16,4]{0,1:T(4,128)}, u32[]{:S(2)}) copy-start(s32[16,4]{0,1:T(4,128)} %param.20) | copy-start | bytes 772
  16.7 27.6 %all-to-all-start = ((bf16[32,16,256]{2,1,0:T(8,128)(2,1)}), bf16[32,16,256]{2,1,0:T(8,128)(2,1)S(1)}, u32[]{:S(2)}, u32[]{:S(2)}) async-start(bf16[32,16,256]{2,1,0:T(8,128)(2,1)} %get-tuple-element.34), calls=%async_computation | async-start | bytes 524288 | tf_op jit(solution)/shard_map/all_to_all | solution.py:575
  32.4 5.2 %collective-permute-start.5 = (bf16[16,16,256]{2,1,0:T(8,128)(2,1)S(1)}, bf16[16,16,256]{2,1,0:T(8,128)(2,1)S(1)}, u32[]{:S(2)}, u32[]{:S(2)}) collective-permute-start(bf16[16,16,256]{2,1,0:T(8,128)(2,1)S(1)} %get-tuple-element.35.own), channel_id=1, source_target_pairs={{1,2},{2,1},{3,4},{4,3},{5,6},{6,5},{9,10},{10,9},{11,12},{12,11},... | collective-permute-start | bytes 393224 | tf_op jit(solution)/shard_map/ppermute | solution.py:86
  33.0 10.6 %collective-permute-start.4 = (bf16[16,16,256]{2,1,0:T(8,128)(2,1)S(1)}, bf16[16,16,256]{2,1,0:T(8,128)(2,1)S(1)}, u32[]{:S(2)}, u32[]{:S(2)}) collective-permute-start(bf16[16,16,256]{2,1,0:T(8,128)(2,1)S(1)} %get-tuple-element.35.own), channel_id=1, source_target_pairs={{0,1},{1,0},{2,3},{3,2},{4,5},{5,4},{6,7},{7,6},{8,9},{9,8},{10,11... | collective-permute-start | bytes 393224 | tf_op jit(solution)/shard_map/ppermute | solution.py:87
  37.6 0.7 copy-start.8
  43.7 0.7 copy-start.10
  47.3 15.9 %all-to-all-start.1 = ((bf16[32,16,256]{2,1,0:T(8,128)(2,1)}), bf16[32,16,256]{2,1,0:T(8,128)(2,1)S(1)}, u32[]{:S(2)}, u32[]{:S(2)}) async-start(bf16[32,16,256]{2,1,0:T(8,128)(2,1)} %far.1), calls=%async_computation.1 | async-start | bytes 524288 | tf_op jit(solution)/shard_map/all_to_all | solution.py:579
  52.8 1.0 %copy-start.5 = (bf16[4,256,256]{2,1,0:T(8,128)(2,1)S(1)}, bf16[4,256,256]{2,1,0:T(8,128)(2,1)}, u32[]{:S(2)}) copy-start(bf16[4,256,256]{2,1,0:T(8,128)(2,1)} %param.21) | copy-start | bytes 1572868
  53.8 0.9 %copy-start.9 = (bf16[16,16,256]{2,1,0:T(8,128)(2,1)S(1)}, bf16[16,16,256]{2,1,0:T(8,128)(2,1)}, u32[]{:S(2)}) copy-start(bf16[16,16,256]{2,1,0:T(8,128)(2,1)} %copy-done.8) | copy-start | bytes 393220
  54.7 0.9 %copy-start.11 = (bf16[16,16,256]{2,1,0:T(8,128)(2,1)S(1)}, bf16[16,16,256]{2,1,0:T(8,128)(2,1)}, u32[]{:S(2)}) copy-start(bf16[16,16,256]{2,1,0:T(8,128)(2,1)} %copy-done.10) | copy-start | bytes 393220

commit v4 on v3

--- a/solution.py
+++ b/solution.py
@@ -4,6 +4,7 @@
 from jax.experimental import pallas as pl
 from jax.experimental.pallas import tpu as pltpu
 from jax.sharding import PartitionSpec as P
+
 
 relaxation = 0.8
 f32 = jnp.float32
@@ -83,8 +84,10 @@
 
 def swap(for_even, for_odd, axis):
     n = lax.axis_size(axis)
-    far = lax.ppermute(for_odd, axis, swap_pairs(n, 1))
-    return lax.ppermute(for_even, axis, swap_pairs(n, 0)), far
+    received = []
+    for k, value in enumerate((for_even, for_odd)):
+        received.append(lax.ppermute(value, axis, swap_pairs(n, k)))
+    return received
 
 
 def second_sweep(mat_real, mat_loss, field, sweep, columns, column_a, source, kinds, got_first, got_second, out, beside, store, cx, cy):
@@ -144,7 +147,6 @@
     chosen, depth, radiate, interp, cosine, sine, volume, cur, out, beside, cells, rows, fresh, sem,
     *, cx, cy, groups, slices
 ):
-    nz = field.shape[1]
     channels = field.shape[0] // (cx * cy)
     excite = channels // 2
     group = excite // groups
@@ -231,30 +233,29 @@
     )(*volume_args[:2], *held(*volume_args[2:], chosen, depth, radiate, interp, cosine, sine))
 
 
-def far_body(lists, kinds, sources, translate, out, plain, turned):
+def far_body(lists, kinds, sources, translate, out, plain):
     far, targets = lists.shape
     devices, piece_rows, width = sources.shape
     per = targets // devices
     tile = piece_rows // per
-    wide = sources[...].astype(f32).reshape(targets, tile, width)
-    plain[...] = wide
-    turned[...] = half_turn(wide)
+    plain[...] = sources[...].astype(f32).reshape(targets, tile, width)
 
     def one(d, _):
         results = []
         for j in range(per):
             t = d * per + j
-            total = jnp.zeros((tile, width), f32)
+            along = jnp.zeros((tile, width), f32)
+            across = jnp.zeros((tile, width), f32)
             for f in range(far):
-                p = lists[f, t]
-                k = kinds[f, t]
-                factor = translate[k]
-                total = total + factor[0:1] * plain[p] + factor[1:2] * turned[p]
-            results.append(total)
+                source = plain[lists[f, t]]
+                factor = translate[kinds[f, t]]
+                along = along + factor[0:1] * source
+                across = across + factor[1:2] * source
+            results.append(along + half_turn(across))
         out[d] = jnp.concatenate(results, axis=0).astype(bf16)
         return 0
 
-    lax.fori_loop(0, devices, one, 0)
+    lax.fori_loop(0, devices, one, 0, unroll=4)
 
 
 def far_combine(lists, kinds, sources, translate):
@@ -268,8 +269,9 @@
         out_shape=pltpu.VMEM(sources.shape, bf16),
         in_specs=[smem, smem, vmem, vmem],
         out_specs=vmem,
-        scratch_shapes=[pltpu.VMEM((targets, tile, width), f32)] * 2,
-        compiler_params=params(8), name="far",
+        scratch_shapes=[pltpu.VMEM((targets, tile, width), f32)],
+        compiler_params=params(8),
+        name="far",
     )(lists, kinds, *held(sources, translate))
 
 
@@ -313,7 +315,7 @@
 
 
 def down_body(pieces, near, radiate, interp, cosine, sine, out, shifted, *, groups, slices):
-    _, piece_rows, width = pieces.shape
+    _, _, width = pieces.shape
     boxes, excite, both = out.shape
     unknowns = both // 2
     group = excite // groups
@@ -341,7 +343,7 @@
 
 
 def down(pieces, near, radiate, interp, cosine, sine, groups, slices):
-    boxes, excite, both = near.shape
+    boxes, excite, _ = near.shape
     return pl.pallas_call(
         lambda *refs: down_body(*refs, groups=groups, slices=slices),
         out_shape=jax.ShapeDtypeStruct(near.shape, f32),
@@ -527,7 +529,7 @@
     )(mat_real, mat_loss, *held(field, source, kinds, got_first, got_second))
 
 
-def shards(
+def steps(
     volume_field,
     source,
     material,
@@ -546,7 +548,7 @@
     every = ("space", "shard")
     groups = lax.axis_size("space")
     slices = lax.axis_size("shard")
-    excite, cells_x, cells_y, cells_z = volume_field.shape[1:]
+    _, cells_x, cells_y, cells_z = volume_field.shape[1:]
     cosine, sine, chosen, depth = prepare(phase_angle, surface_map, cells_x, cells_y, cells_z)
     weights = radiate.reshape(2 * radiate.shape[1], radiate.shape[2])
     field = volume_field.reshape(-1, cells_z)
@@ -574,7 +576,6 @@
     )
     directed = lax.all_to_all(pieces, every, split_axis=0, concat_axis=0, tiled=True)
     first, second = swap(currents, currents, "shard")
-    directed, first, second = lax.optimization_barrier((directed, first, second))
     combined = far_combine(far_parents.T, far_kind.T, directed, translate)
     incoming = lax.all_to_all(combined, every, split_axis=0, concat_axis=0, tiled=True)
     near, cosine, sine = near_force(near_boxes.T, currents, first, second, near_blocks, phase_angle)
@@ -584,7 +585,7 @@
 
 def solution(mesh):
     return jax.shard_map(
-        shards,
+        steps,
         mesh=mesh,
         in_specs=(
             P(None, None, "space", "shard", None),

time: 65.8 us -> 64.4 us (0.979)
  blocking collectives: 0 us -> 25.9 us
  starting transfers between devices: 30.7 us -> 12.2 us
  waiting for transfers between devices: 14.2 us -> 8.32 us
  local copies, waits for them, and re-layouts: 4.21 us -> 2.43 us
  Pallas kernels: 15.4 us -> 14.4 us
    all_to_all x0 -> x1, blocking collectives: none -> 25.9 us  [steps(): lax.all_to_all(pieces, every, split_axis=0, concat_axis=0, tiled=True)]
    all_to_all x2 -> x1, starting transfers between devices: 21.1 us -> 2.59 us  [steps(): lax.all_to_all(combined, every, split_axis=0, concat_axis=0, tiled=True)]
    all_to_all x2 -> x1, waiting for transfers between devices: 6.53 us -> 0.01 us  [steps(): lax.all_to_all(combined, every, split_axis=0, concat_axis=0, tiled=True)]
    unnamed x36, local copies, waits for them, and re-layouts: 4.21 us -> 2.43 us
    pallas_call x1, Pallas kernels: 5.3 us -> 4.58 us  [up(): pl.pallas_call(lambda *refs: up_body(*refs, cx=cx, cy=cy, groups=groups,...]
    ppermute x6, waiting for transfers between devices: 7.66 us -> 8.32 us  [swap(): received.append(lax.ppermute(value, axis, swap_pairs(n, k)))]
  transfers between devices with their start and end apart: 8 -> 7, of which waited for: 3 -> 2; matrix products, arithmetic and copies ran while one was open for 0% -> 0% of each run, Pallas kernels for 3% -> 3%
where the time goes in v4:
time: 64.4 us; the launch traced here: 64.1 us
  blocking collectives  25.9 us (40%)
  Pallas kernels  14.4 us (22%)
  starting transfers between devices  12.2 us (19%)
  waiting for transfers between devices  8.32 us (13%)
  local copies, waits for them, and re-layouts  2.43 us (4%)
  between operations  0.93 us (1%)
    all_to_all x1, blocking collectives, steps(): lax.all_to_all(pieces, every, split_axis=0, concat_axis=0, tiled=True)  25.9 us
    ppermute x6, starting transfers between devices, swap(): received.append(lax.ppermute(value, axis, swap_pairs(n, k)))  9.59 us
    ppermute x6, waiting for transfers between devices, swap(): received.append(lax.ppermute(value, axis, swap_pairs(n, k)))  8.32 us
    pallas_call x1, Pallas kernels, up(): pl.pallas_call(lambda *refs: up_body(*refs, cx=cx, cy=cy, groups=groups,...  4.58 us
    pallas_call x1, Pallas kernels, far_combine(): pl.pallas_call(far_body, out_shape=pltpu.VMEM(sources.shape, bf16), in_sp...  2.65 us
    all_to_all x1, starting transfers between devices, steps(): lax.all_to_all(combined, every, split_axis=0, concat_axis=0, tiled=True)  2.59 us
    unnamed x36, local copies, waits for them, and re-layouts  2.43 us
    pallas_call x1, Pallas kernels, down(): pl.pallas_call(lambda *refs: down_body(*refs, groups=groups, slices=slice...  2.26 us
  transfers between devices with their start and end apart: 7, of which 2 were waited for; matrix products, arithmetic and copies ran while one was open for 0% of the time, Pallas kernels for 3%

profile of v4, /device:TPU:0, one launch (start us, length us, event | category | flops | bytes accessed | tf_op | source)
XLA Modules:
  0.0 64.1 jit_solution(7244581160913199560)
XLA Ops:
  0.6 0.0 copy-start.6
  0.6 0.0 copy-start
  0.7 0.0 copy-start.1
  0.7 0.0 copy-start.17
  0.7 0.0 copy-start.16
  0.7 0.0 copy-start.7
  0.7 0.0 copy-start.12
  0.7 0.0 copy-start.2
  0.7 0.0 copy-start.3
  0.7 1.3 %edges.1 = (bf16[400,128]{1,0:T(8,128)(2,1)S(1)}, bf16[400,128]{1,0:T(8,128)(2,1)S(1)}) custom-call(f32[128,16,128]{2,1,0:T(8,128)} %bitcast.11, f32[128,16,128]{2,1,0:T(8,128)} %bitcast.14, s32[4,16,128]{2,1,0:T(8,128)} %kinds.1), custom_call_target="tpu_custom_call" | custom-call | tf_op jit(solution)/shard_map/edges/pallas_call | solution.py:424
  2.0 3.0 %collective-permute-start = (bf16[400,128]{1,0:T(8,128)(2,1)S(1)}, bf16[400,128]{1,0:T(8,128)(2,1)S(1)}, u32[]{:S(2)}, u32[]{:S(2)}) collective-permute-start(bf16[400,128]{1,0:T(8,128)(2,1)S(1)} %get-tuple-element.19), channel_id=1, source_target_pairs={{0,1},{1,0},{2,3},{3,2},{4,5},{5,4},{6,7},{7,6},{8,9},{9,8},{10,11... | collective-permute-start | bytes 307208 | tf_op jit(solution)/shard_map/ppermute | solution.py:89
  5.1 0.7 %collective-permute-start.1 = (bf16[400,128]{1,0:T(8,128)(2,1)S(1)}, bf16[400,128]{1,0:T(8,128)(2,1)S(1)}, u32[]{:S(2)}, u32[]{:S(2)}) collective-permute-start(bf16[400,128]{1,0:T(8,128)(2,1)S(1)} %get-tuple-element.20), channel_id=1, source_target_pairs={{1,2},{2,1},{3,4},{4,3},{5,6},{6,5},{9,10},{10,9},{11,12},{12,11},... | collective-permute-start | bytes 307208 | tf_op jit(solution)/shard_map/ppermute | solution.py:89
  5.7 2.2 %collective-permute-done.refs_5_ = bf16[400,128]{1,0:T(8,128)(2,1)S(1)} collective-permute-done((bf16[400,128]{1,0:T(8,128)(2,1)S(1)}, bf16[400,128]{1,0:T(8,128)(2,1)S(1)}, u32[]{:S(2)}, u32[]{:S(2)}) %collective-permute-start) | collective-permute-done | bytes 102432 | tf_op jit(solution)/shard_map/ppermute | solution.py:89
  7.9 0.0 collective-permute-done.1.refs_6_
  7.9 0.0 copy-done.6
  7.9 0.0 copy-done
  7.9 0.0 copy-done.1
  8.0 0.0 copy-done.17
  8.0 0.0 copy-done.16
  8.0 1.6 %first_sweep.1 = (f32[2048,128]{1,0:T(8,128)S(1)}, f32[2,128,128]{2,1,0:T(8,128)S(1)}, f32[2,8,128]{2,1,0:T(8,128)S(1)}, bf16[1104,128]{1,0:T(8,128)(2,1)S(1)}, bf16[1104,128]{1,0:T(8,128)(2,1)S(1)}) custom-call(f32[8]{0:T(128)S(1)} %copy-done.16, f32[8]{0:T(128)S(1)} %copy-done.17, f32[2048,128]{1,0:T(8,128)S(1)} %bitcast.12, f32[2048,128]{1,0:T(8,128)S(1)} %bitcast.15, ...), custom_call_target="tpu_custom_call" | custom-call | tf_op jit(solution)/shard_map/first_sweep/pallas_call | solution.py:516
  9.5 0.1 collective-permute-start.2
  9.6 0.7 %collective-permute-start.3 = (bf16[1104,128]{1,0:T(8,128)(2,1)S(1)}, bf16[1104,128]{1,0:T(8,128)(2,1)S(1)}, u32[]{:S(2)}, u32[]{:S(2)}) collective-permute-start(bf16[1104,128]{1,0:T(8,128)(2,1)S(1)} %get-tuple-element.25), channel_id=1, source_target_pairs={{8,16},{16,8},{9,17},{17,9},{10,18},{18,10},{11,19},{19,11},{12,20... | collective-permute-start | bytes 847880 | tf_op jit(solution)/shard_map/ppermute | solution.py:89
  10.3 0.0 copy-done.7
  10.3 0.0 copy-done.12
  10.3 1.0 %prepare.1 = (f32[8,2048]{1,0:T(8,128)S(1)}, f32[8,2048]{1,0:T(8,128)S(1)}, bf16[512,2048]{1,0:T(8,128)(2,1)S(1)}, s32[8,2048]{1,0:T(8,128)S(1)}) custom-call(f32[8,2048]{1,0:T(8,128)S(1)} %copy-done.7, s32[16,128]{1,0:T(8,128)S(1)} %copy-done.12), custom_call_target="tpu_custom_call" | custom-call | tf_op jit(solution)/shard_map/prepare/pallas_call | solution.py:65
  11.3 0.0 collective-permute-done.2.refs_8_
  11.3 0.0 collective-permute-done.3.refs_9_
  11.4 0.0 copy-done.2
  11.4 0.0 copy-start.4
  11.4 0.0 copy-start.13
  11.4 0.0 copy-start.14
  11.4 4.6 %up.1 = (f32[2048,128]{1,0:T(8,128)}, bf16[16,16,256]{2,1,0:T(8,128)(2,1)S(1)}, bf16[32,16,256]{2,1,0:T(8,128)(2,1)S(1)}) custom-call(f32[8]{0:T(128)S(1)} %copy-done.16, f32[8]{0:T(128)S(1)} %copy-done.17, f32[2048,128]{1,0:T(8,128)S(1)} %bitcast.13, f32[2048,128]{1,0:T(8,128)S(1)} %get-tuple-element.21.refs_3_, ...), custom_call_target="tpu_custom_call" | custom-call | tf_op jit(solution)/shard_map/up/pallas_call | solution.py:216
  16.0 0.0 copy-start.5
  16.0 0.0 copy-start.15
  16.0 25.9 %all_to_all.10.sources = bf16[32,16,256]{2,1,0:T(8,128)(2,1)S(1)} all-to-all(bf16[32,16,256]{2,1,0:T(8,128)(2,1)S(1)} %get-tuple-element.31), channel_id=1, replica_groups=mesh['space'=4,'shard'=8] {'space','shard'}, dimensions={0} | all-to-all | bytes 524288 | tf_op jit(solution)/shard_map/all_to_all | solution.py:577
  41.9 0.0 copy-done.4
  41.9 2.6 %far.1 = bf16[32,16,256]{2,1,0:T(8,128)(2,1)} custom-call(s32[8,64]{1,0:T(8,128)S(1)} %bitcast.22, s32[8,64]{1,0:T(8,128)S(1)} %bitcast.23, bf16[32,16,256]{2,1,0:T(8,128)(2,1)S(1)} %all_to_all.10.sources, f32[316,2,256]{2,1,0:T(2,128)S(1)} %copy-done.4), custom_call_target="tpu_custom_call" | custom-call | tf_op jit(solution)/shard_map/far/pallas_call | solution.py:267
  44.6 2.6 %all-to-all-start.1 = ((bf16[32,16,256]{2,1,0:T(8,128)(2,1)}), bf16[32,16,256]{2,1,0:T(8,128)(2,1)S(1)}, u32[]{:S(2)}, u32[]{:S(2)}) async-start(bf16[32,16,256]{2,1,0:T(8,128)(2,1)} %far.1), calls=%async_computation.1 | async-start | bytes 524288 | tf_op jit(solution)/shard_map/all_to_all | solution.py:580
  47.1 0.7 %collective-permute-start.5 = (bf16[16,16,256]{2,1,0:T(8,128)(2,1)S(1)}, bf16[16,16,256]{2,1,0:T(8,128)(2,1)S(1)}, u32[]{:S(2)}, u32[]{:S(2)}) collective-permute-start(bf16[16,16,256]{2,1,0:T(8,128)(2,1)S(1)} %get-tuple-element.32.own), channel_id=1, source_target_pairs={{1,2},{2,1},{3,4},{4,3},{5,6},{6,5},{9,10},{10,9},{11,12},{12,11},... | collective-permute-start | bytes 393224 | tf_op jit(solution)/shard_map/ppermute | solution.py:89
  47.8 4.5 %collective-permute-start.4 = (bf16[16,16,256]{2,1,0:T(8,128)(2,1)S(1)}, bf16[16,16,256]{2,1,0:T(8,128)(2,1)S(1)}, u32[]{:S(2)}, u32[]{:S(2)}) collective-permute-start(bf16[16,16,256]{2,1,0:T(8,128)(2,1)S(1)} %get-tuple-element.32.own), channel_id=1, source_target_pairs={{0,1},{1,0},{2,3},{3,2},{4,5},{5,4},{6,7},{7,6},{8,9},{9,8},{10,11... | collective-permute-start | bytes 393224 | tf_op jit(solution)/shard_map/ppermute | solution.py:89
  52.3 0.0 collective-permute-done.5.second
  52.3 6.1 %collective-permute-done.4.first = bf16[16,16,256]{2,1,0:T(8,128)(2,1)S(1)} collective-permute-done((bf16[16,16,256]{2,1,0:T(8,128)(2,1)S(1)}, bf16[16,16,256]{2,1,0:T(8,128)(2,1)S(1)}, u32[]{:S(2)}, u32[]{:S(2)}) %collective-permute-start.4) | collective-permute-done | bytes 131104 | tf_op jit(solution)/shard_map/ppermute | solution.py:89
  58.4 0.9 %copy-done.9 = bf16[16,16,256]{2,1,0:T(8,128)(2,1)S(1)} copy-done((bf16[16,16,256]{2,1,0:T(8,128)(2,1)S(1)}, bf16[16,16,256]{2,1,0:T(8,128)(2,1)}, u32[]{:S(2)}) %copy-start.9) | copy-done | bytes 131096
  59.3 1.0 %near.1 = (f32[16,16,256]{2,1,0:T(8,128)S(1)}, f32[8,2048]{1,0:T(8,128)S(1)}, f32[8,2048]{1,0:T(8,128)S(1)}) custom-call(s32[4,16]{1,0:T(4,128)S(1)} %bitcast.24, bf16[16,16,256]{2,1,0:T(8,128)(2,1)S(1)} %copy-done.9, bf16[16,16,256]{2,1,0:T(8,128)(2,1)S(1)} %collective-permute-done.4.first, bf16[16,16,256]{2,1,0:T(8,128)(2,1)S(1)} %collective-permute-done.5.second, ...), custom_call_target="tpu_custom_call" | custom-call | tf_op jit(solution)/shard_map/near/pallas_call | solution.py:304
  60.4 0.6 copy-done.10
  61.0 0.0 all-to-all-done.1.refs_0_
  61.0 0.8 %copy-done.11 = f32[8,2048]{1,0:T(8,128)S(1)} copy-done((f32[8,2048]{1,0:T(8,128)S(1)}, f32[8,2048]{1,0:T(8,128)}, u32[]{:S(2)}) %copy-start.11) | copy-done | bytes 65560
  61.8 2.3 %down.1 = f32[16,16,256]{2,1,0:T(8,128)} custom-call(bf16[32,16,256]{2,1,0:T(8,128)(2,1)S(1)} %all-to-all-done.1.refs_0_, f32[16,16,256]{2,1,0:T(8,128)S(1)} %get-tuple-element.33.refs_1_, bf16[256,512]{1,0:T(8,128)(2,1)S(1)} %bitcast.18, bf16[512,2048]{1,0:T(8,128)(2,1)S(1)} %copy-done.2, f32[8,2048]{1,0:T(8,128)S(1)} %get-tuple-element.34.refs_4_, ...), custom_call_target="tpu_custom_call" | custom-call | tf_op jit(solution)/shard_map/down/pallas_call | solution.py:347
  (10 shorter events, 0.0 us)
Async XLA Ops:
  0.6 7.3 %copy-start.6 = (s32[4,16,128]{2,1,0:T(8,128)S(1)}, s32[4,16,128]{2,1,0:T(8,128)}, u32[]{:S(2)}) copy-start(s32[4,16,128]{2,1,0:T(8,128)} %kinds.1) | copy-start | bytes 98308
  0.6 7.3 %copy-start = (f32[2,16,4,16,128]{4,3,2,1,0:T(8,128)S(1)}, f32[2,16,4,16,128]{4,3,2,1,0:T(8,128)}, u32[]{:S(2)}) copy-start(f32[2,16,4,16,128]{4,3,2,1,0:T(8,128)} %param.14) | copy-start | bytes 3145732
  0.7 7.3 %copy-start.1 = (f32[2,16,4,16,128]{4,3,2,1,0:T(8,128)S(1)}, f32[2,16,4,16,128]{4,3,2,1,0:T(8,128)}, u32[]{:S(2)}) copy-start(f32[2,16,4,16,128]{4,3,2,1,0:T(8,128)} %param.15) | copy-start | bytes 3145732
  0.7 7.3 %copy-start.17 = (f32[8]{0:T(128)S(1)}, f32[8]{0:T(128)}, u32[]{:S(2)}) copy-start(f32[8]{0:T(128)} %refs_1_.3) | copy-start | bytes 100
  0.7 7.3 %copy-start.16 = (f32[8]{0:T(128)S(1)}, f32[8]{0:T(128)}, u32[]{:S(2)}) copy-start(f32[8]{0:T(128)} %refs_0_.3) | copy-start | bytes 100
  0.7 9.6 %copy-start.7 = (f32[8,2048]{1,0:T(8,128)S(1)}, f32[8,2048]{1,0:T(8,128)}, u32[]{:S(2)}) copy-start(f32[8,2048]{1,0:T(8,128)} %angle.3) | copy-start | bytes 196612
  0.7 9.6 %copy-start.12 = (s32[16,128]{1,0:T(8,128)S(1)}, s32[16,128]{1,0:T(8,128)}, u32[]{:S(2)}) copy-start(s32[16,128]{1,0:T(8,128)} %smap.1) | copy-start | bytes 24580
  0.7 10.7 %copy-start.2 = (bf16[512,2048]{1,0:T(8,128)(2,1)S(1)}, bf16[512,2048]{1,0:T(8,128)(2,1)}, u32[]{:S(2)}) copy-start(bf16[512,2048]{1,0:T(8,128)(2,1)} %refs_3_.1) | copy-start | bytes 6291460
  0.7 10.7 %copy-start.3 = (bf16[2,128,512]{2,1,0:T(8,128)(2,1)S(1)}, bf16[2,128,512]{2,1,0:T(8,128)(2,1)}, u32[]{:S(2)}) copy-start(bf16[2,128,512]{2,1,0:T(8,128)(2,1)} %param.22) | copy-start | bytes 786436
  2.0 5.9 %collective-permute-start = (bf16[400,128]{1,0:T(8,128)(2,1)S(1)}, bf16[400,128]{1,0:T(8,128)(2,1)S(1)}, u32[]{:S(2)}, u32[]{:S(2)}) collective-permute-start(bf16[400,128]{1,0:T(8,128)(2,1)S(1)} %get-tuple-element.19), channel_id=1, source_target_pairs={{0,1},{1,0},{2,3},{3,2},{4,5},{5,4},{6,7},{7,6},{8,9},{9,8},{10,11... | collective-permute-start | bytes 307208 | tf_op jit(solution)/shard_map/ppermute | solution.py:89
  5.1 2.9 %collective-permute-start.1 = (bf16[400,128]{1,0:T(8,128)(2,1)S(1)}, bf16[400,128]{1,0:T(8,128)(2,1)S(1)}, u32[]{:S(2)}, u32[]{:S(2)}) collective-permute-start(bf16[400,128]{1,0:T(8,128)(2,1)S(1)} %get-tuple-element.20), channel_id=1, source_target_pairs={{1,2},{2,1},{3,4},{4,3},{5,6},{6,5},{9,10},{10,9},{11,12},{12,11},... | collective-permute-start | bytes 307208 | tf_op jit(solution)/shard_map/ppermute | solution.py:89
  9.5 1.8 %collective-permute-start.2 = (bf16[1104,128]{1,0:T(8,128)(2,1)S(1)}, bf16[1104,128]{1,0:T(8,128)(2,1)S(1)}, u32[]{:S(2)}, u32[]{:S(2)}) collective-permute-start(bf16[1104,128]{1,0:T(8,128)(2,1)S(1)} %get-tuple-element.24), channel_id=1, source_target_pairs={{0,8},{8,0},{16,24},{24,16},{1,9},{9,1},{17,25},{25,17},{2,10},{10... | collective-permute-start | bytes 847880 | tf_op jit(solution)/shard_map/ppermute | solution.py:89
  9.6 1.7 %collective-permute-start.3 = (bf16[1104,128]{1,0:T(8,128)(2,1)S(1)}, bf16[1104,128]{1,0:T(8,128)(2,1)S(1)}, u32[]{:S(2)}, u32[]{:S(2)}) collective-permute-start(bf16[1104,128]{1,0:T(8,128)(2,1)S(1)} %get-tuple-element.25), channel_id=1, source_target_pairs={{8,16},{16,8},{9,17},{17,9},{10,18},{18,10},{11,19},{19,11},{12,20... | collective-permute-start | bytes 847880 | tf_op jit(solution)/shard_map/ppermute | solution.py:89
  11.4 30.5 %copy-start.4 = (f32[316,2,256]{2,1,0:T(2,128)S(1)}, f32[316,2,256]{2,1,0:T(2,128)}, u32[]{:S(2)}) copy-start(f32[316,2,256]{2,1,0:T(2,128)} %translate.1) | copy-start | bytes 1941508
  11.4 30.5 %copy-start.13 = (s32[64,8]{0,1:T(8,128)S(1)}, s32[64,8]{0,1:T(8,128)}, u32[]{:S(2)}) copy-start(s32[64,8]{0,1:T(8,128)} %param.25) | copy-start | bytes 6148
  11.4 30.5 %copy-start.14 = (s32[64,8]{0,1:T(8,128)S(1)}, s32[64,8]{0,1:T(8,128)}, u32[]{:S(2)}) copy-start(s32[64,8]{0,1:T(8,128)} %param.26) | copy-start | bytes 6148
  16.0 42.4 %copy-start.8 = (bf16[16,16,256]{2,1,0:T(8,128)(2,1)}, bf16[16,16,256]{2,1,0:T(8,128)(2,1)S(1)}, u32[]{:S(2)}) copy-start(bf16[16,16,256]{2,1,0:T(8,128)(2,1)S(1)} %get-tuple-element.32.own) | copy-start | bytes 393220
  16.0 42.4 %copy-start.5 = (bf16[4,256,256]{2,1,0:T(8,128)(2,1)S(1)}, bf16[4,256,256]{2,1,0:T(8,128)(2,1)}, u32[]{:S(2)}) copy-start(bf16[4,256,256]{2,1,0:T(8,128)(2,1)} %param.21) | copy-start | bytes 1572868
  16.0 42.4 %copy-start.15 = (s32[16,4]{0,1:T(4,128)S(1)}, s32[16,4]{0,1:T(4,128)}, u32[]{:S(2)}) copy-start(s32[16,4]{0,1:T(4,128)} %param.20) | copy-start | bytes 772
  44.6 16.4 %all-to-all-start.1 = ((bf16[32,16,256]{2,1,0:T(8,128)(2,1)}), bf16[32,16,256]{2,1,0:T(8,128)(2,1)S(1)}, u32[]{:S(2)}, u32[]{:S(2)}) async-start(bf16[32,16,256]{2,1,0:T(8,128)(2,1)} %far.1), calls=%async_computation.1 | async-start | bytes 524288 | tf_op jit(solution)/shard_map/all_to_all | solution.py:580
  47.1 5.2 %collective-permute-start.5 = (bf16[16,16,256]{2,1,0:T(8,128)(2,1)S(1)}, bf16[16,16,256]{2,1,0:T(8,128)(2,1)S(1)}, u32[]{:S(2)}, u32[]{:S(2)}) collective-permute-start(bf16[16,16,256]{2,1,0:T(8,128)(2,1)S(1)} %get-tuple-element.32.own), channel_id=1, source_target_pairs={{1,2},{2,1},{3,4},{4,3},{5,6},{6,5},{9,10},{10,9},{11,12},{12,11},... | collective-permute-start | bytes 393224 | tf_op jit(solution)/shard_map/ppermute | solution.py:89
  47.8 10.6 %collective-permute-start.4 = (bf16[16,16,256]{2,1,0:T(8,128)(2,1)S(1)}, bf16[16,16,256]{2,1,0:T(8,128)(2,1)S(1)}, u32[]{:S(2)}, u32[]{:S(2)}) collective-permute-start(bf16[16,16,256]{2,1,0:T(8,128)(2,1)S(1)} %get-tuple-element.32.own), channel_id=1, source_target_pairs={{0,1},{1,0},{2,3},{3,2},{4,5},{5,4},{6,7},{7,6},{8,9},{9,8},{10,11... | collective-permute-start | bytes 393224 | tf_op jit(solution)/shard_map/ppermute | solution.py:89
  58.4 0.9 %copy-start.9 = (bf16[16,16,256]{2,1,0:T(8,128)(2,1)S(1)}, bf16[16,16,256]{2,1,0:T(8,128)(2,1)}, u32[]{:S(2)}) copy-start(bf16[16,16,256]{2,1,0:T(8,128)(2,1)} %copy-done.8) | copy-start | bytes 393220
  60.4 0.6 copy-start.10
  61.0 0.8 %copy-start.11 = (f32[8,2048]{1,0:T(8,128)S(1)}, f32[8,2048]{1,0:T(8,128)}, u32[]{:S(2)}) copy-start(f32[8,2048]{1,0:T(8,128)} %copy-done.10) | copy-start | bytes 196612

commit v5 on v4

--- a/solution.py
+++ b/solution.py
@@ -90,61 +90,68 @@
     return received
 
 
-def second_sweep(mat_real, mat_loss, field, sweep, columns, column_a, source, kinds, got_first, got_second, out, beside, store, cx, cy):
+def second_sweep(
+    mat_real, mat_loss, field, sweep, columns, column_a, source, kinds, early_first, early_second,
+    late_first, late_second, out, beside, a_all, b_all, store, cx, cy
+):
     total = field.shape[0] // cy
     channels = total // cx
     excite = channels // 2
     plane = channels * cy
-    even = is_even("space")
-    a, b = coefficients(kinds[...], mat_real, mat_loss, 0)
-
-    def halo(side, start, size):
-        one = got_first[start : start + size, :].astype(f32)
-        two = got_second[start : start + size, :].astype(f32)
-        return jnp.where(even, two, one) if side == 0 else jnp.where(even, one, two)
-
-    faces = (0, cx - 1)
-    for y_side in range(2):
-        beside[y_side] = columns[y_side]
-        for x_side, x in enumerate(faces):
-            corner = halo(x_side, 2 * plane + y_side * channels, channels)
-            factor = column_a[y_side, x : x + 1, :]
-            for c in range(0, channels, 8):
-                rows = pl.ds(c * cx + x, 8, stride=cx)
-                beside.at[y_side][rows, :] = beside.at[y_side][rows, :] + factor * corner[c : c + 8]
-    face_a = []
-    for x_side in range(2):
-        kind = halo(x_side, 2 * plane + 2 * channels, cy).astype(jnp.int32)
-        face_a.append(coefficients(kind, mat_real, mat_loss, 1)[0])
-    for e in range(excite):
-        v = []
-        for p in range(2):
-            c = p * excite + e
-            own = [sweep[(c * cx + x) * cy : (c * cx + x + 1) * cy, :] for x in range(cx)]
-            outer = []
-            for x_side, x in enumerate(faces):
-                own[x] = own[x] + a[x * cy : (x + 1) * cy] * halo(x_side, c * cy, cy)
-                before = field[(c * cx + x) * cy : (c * cx + x + 1) * cy, :]
-                outer.append(halo(x_side, plane + c * cy, cy) + face_a[x_side] * before)
-            v.append([outer[0]] + own + [outer[1]])
-        for x in range(cx):
-            sums = []
+    a_all[...], b_all[...] = coefficients(kinds[...], mat_real, mat_loss, 0)
+    ends = (0, cx - 1)
+
+    def run(*got):
+        for y_side in range(2):
+            beside[y_side] = columns[y_side]
+            for x_side, x in enumerate(ends):
+                at = plane + y_side * channels
+                corner = got[x_side][1][at : at + channels, :].astype(f32)
+                factor = column_a[y_side, x : x + 1, :]
+                for c in range(0, channels, 8):
+                    rows = pl.ds(c * cx + x, 8, stride=cx)
+                    beside.at[y_side][rows, :] = beside.at[y_side][rows, :] + factor * corner[c : c + 8]
+        face_a = [
+            coefficients(got[side][0][plane:, :].astype(f32).astype(jnp.int32), mat_real, mat_loss, 1)[0]
+            for side in range(2)
+        ]
+
+        def one(e, _):
+            values = []
             for p in range(2):
-                at = (p * excite + e) * cx + x
-                w = v[p][x + 1]
-                n = source[at * cy : (at + 1) * cy, :] + along_z(w)
-                n = n + along_y(w, beside[0, at : at + 1, :], beside[1, at : at + 1, :])
-                sums.append(n + v[p][x] + v[p][x + 2])
-            new = relaxed((v[0][x + 1], v[1][x + 1]), sums, a[x * cy : (x + 1) * cy], b[x * cy : (x + 1) * cy])
-            for p in range(2):
-                at = (p * excite + e) * cx + x
-                out[at * cy : (at + 1) * cy, :] = new[p]
-                store(p, e, x, new[p])
+                c = p * excite + e
+                own = [tiles_at(sweep, (c * cx + x) * cy, cy) for x in range(cx)]
+                outer = []
+                for side, x in enumerate(ends):
+                    raw = wide_tiles_at(got[side][0], c * cy, cy)
+                    own[x] = [
+                        t + a_all[x * cy + i * 8 : x * cy + i * 8 + 8, :] * h
+                        for i, (t, h) in enumerate(zip(own[x], raw))
+                    ]
+                    part = wide_tiles_at(got[side][1], c * cy, cy)
+                    before = tiles_at(field, (c * cx + x) * cy, cy)
+                    outer.append(
+                        [q + face_a[side][i * 8 : i * 8 + 8] * t for i, (q, t) in enumerate(zip(part, before))]
+                    )
+                values.append([outer[0]] + own + [outer[1]])
+
+            def emit(p, x, i, value):
+                at = ((p * excite + e) * cx + x) * cy + i
+                out[pl.ds(pl.multiple_of(at, 8), 8), :] = value
+                store(p, e, x, i, value)
+
+            sweep_brick(values, e, excite, cx, cy, source, beside, a_all, b_all, emit)
+            return 0
+
+        lax.fori_loop(0, excite, one, 0)
+
+    by_parity("space", run, (early_first, late_first), (early_second, late_second))
 
 
 def up_body(
-    mat_real, mat_loss, field, sweep, columns, column_a, source, kinds, got_first, got_second,
-    chosen, depth, radiate, interp, cosine, sine, volume, cur, out, beside, cells, rows, fresh, sem,
+    mat_real, mat_loss, field, sweep, columns, column_a, source, kinds, early_first, early_second,
+    late_first, late_second, chosen, depth, radiate, interp, cosine, sine, volume, cur, out,
+    beside, cells, rows, fresh, a_all, b_all, sem,
     *, cx, cy, groups, slices
 ):
     channels = field.shape[0] // (cx * cy)
@@ -153,14 +160,13 @@
     boxes = cur.shape[0]
     unknowns = depth.shape[1] // boxes
 
-    def store(t, e, x, value):
+    def store(t, e, x, y, value):
         place = (e // group) * 2 * group + t * group + e % group
-        for y in range(0, cy, 8):
-            cells.at[x][pl.ds(y * channels + place, 8, stride=channels), :] = value[y : y + 8]
+        cells.at[x][pl.ds(y * channels + place, 8, stride=channels), :] = value
 
     second_sweep(
-        mat_real, mat_loss, field, sweep, columns, column_a, source, kinds, got_first, got_second,
-        fresh, beside, store, cx, cy
+        mat_real, mat_loss, field, sweep, columns, column_a, source, kinds, early_first, early_second,
+        late_first, late_second, fresh, beside, a_all, b_all, store, cx, cy
     )
     leaving = pltpu.make_async_copy(fresh, volume, sem)
     leaving.start()
@@ -220,22 +226,51 @@
             pltpu.VMEM((boxes, channels // 2, 2 * unknowns), bf16),
             pltpu.VMEM((groups * slices, piece_rows, width), bf16),
         ),
-        in_specs=[smem, smem] + [vmem] * 14,
+        in_specs=[smem, smem] + [vmem] * 16,
         out_specs=(pl.BlockSpec(memory_space=pltpu.HBM), vmem, vmem),
         scratch_shapes=[
             pltpu.VMEM((2, total, nz), f32),
             pltpu.VMEM((cx, cy * channels, nz), f32),
             pltpu.VMEM((boxes * channels, 2 * unknowns), bf16),
             pltpu.VMEM(field.shape, f32),
+            pltpu.VMEM((cx * cy, nz), f32),
+            pltpu.VMEM((cx * cy, nz), f32),
             pltpu.SemaphoreType.DMA(()),
         ],
         compiler_params=params(16), name="up",
     )(*volume_args[:2], *held(*volume_args[2:], chosen, depth, radiate, interp, cosine, sine))
 
 
-def far_body(lists, kinds, sources, translate, out, plain):
+def tables(lists, kinds, translate):
     far, targets = lists.shape
+
+    def body(lists, kinds, translate, factors, order):
+        def one(t, _):
+            for f in range(far):
+                order[t * far + f] = lists[f, t]
+                factors[t * far + f] = translate[kinds[f, t]]
+            return 0
+
+        lax.fori_loop(0, targets, one, 0, unroll=2)
+
+    smem = pl.BlockSpec(memory_space=pltpu.SMEM)
+    vmem = pl.BlockSpec(memory_space=pltpu.VMEM)
+    return pl.pallas_call(
+        body,
+        out_shape=(
+            pltpu.VMEM((targets * far,) + translate.shape[1:], f32),
+            jax.ShapeDtypeStruct((targets * far,), jnp.int32),
+        ),
+        in_specs=[smem, smem, vmem],
+        out_specs=(vmem, smem),
+        compiler_params=params(8),
+        name="tables",
+    )(lists, kinds, *held(translate))
+
+
+def far_body(order, sources, factors, out, plain, *, targets):
     devices, piece_rows, width = sources.shape
+    far = order.shape[0] // targets
     per = targets // devices
     tile = piece_rows // per
     plain[...] = sources[...].astype(f32).reshape(targets, tile, width)
@@ -243,12 +278,12 @@
     def one(d, _):
         results = []
         for j in range(per):
-            t = d * per + j
             along = jnp.zeros((tile, width), f32)
             across = jnp.zeros((tile, width), f32)
             for f in range(far):
-                source = plain[lists[f, t]]
-                factor = translate[kinds[f, t]]
+                pair = d * (per * far) + (j * far + f)
+                source = plain[order[pair]]
+                factor = factors[pair]
                 along = along + factor[0:1] * source
                 across = across + factor[1:2] * source
             results.append(along + half_turn(across))
@@ -258,21 +293,20 @@
     lax.fori_loop(0, devices, one, 0, unroll=4)
 
 
-def far_combine(lists, kinds, sources, translate):
-    targets = lists.shape[1]
+def far_combine(order, sources, factors, targets):
     devices, piece_rows, width = sources.shape
     tile = piece_rows // (targets // devices)
     smem = pl.BlockSpec(memory_space=pltpu.SMEM)
     vmem = pl.BlockSpec(memory_space=pltpu.VMEM)
     return pl.pallas_call(
-        far_body,
+        lambda *refs: far_body(*refs, targets=targets),
         out_shape=pltpu.VMEM(sources.shape, bf16),
-        in_specs=[smem, smem, vmem, vmem],
+        in_specs=[smem, vmem, vmem],
         out_specs=vmem,
         scratch_shapes=[pltpu.VMEM((targets, tile, width), f32)],
         compiler_params=params(8),
         name="far",
-    )(lists, kinds, *held(sources, translate))
+    )(order, *held(sources, factors))
 
 
 def near_body(lists, own, first, second, blocks, angle, out, cosine, sine, boxes_all, rows):
@@ -323,15 +357,16 @@
     parents = boxes // CHILDREN
     for h in range(slices):
         lanes = slice(h * width, (h + 1) * width)
-        for s in range(groups):
-            incoming = pieces[s * slices + h].astype(f32).reshape(parents, tile, width)
-            turned = half_turn(incoming)
+        for s in range(0, groups, 2):
+            pair = [pieces[(s + k) * slices + h].astype(f32) for k in range(2)]
             for p in range(parents):
-                for child in range(0, CHILDREN):
+                incoming = jnp.concatenate([v[p * tile : (p + 1) * tile] for v in pair], axis=0)
+                turned = half_turn(incoming.reshape(2, tile, width)).reshape(2 * tile, width)
+                for child in range(CHILDREN):
                     row = ((p * CHILDREN + child) * groups + s) * tile
-                    value = cosine[child : child + 1, lanes] * incoming[p] - sine[child : child + 1, lanes] * turned[p]
-                    shifted[row : row + tile, lanes] = value
-    leaf_in = dot_t(shifted[...].astype(bf16), interp[...]).astype(bf16)
+                    value = cosine[child : child + 1, lanes] * incoming - sine[child : child + 1, lanes] * turned
+                    shifted[row : row + 2 * tile, lanes] = value.astype(bf16)
+    leaf_in = dot_t(shifted[...], interp[...]).astype(bf16)
     back = dot_t(leaf_in, radiate[...]).reshape(boxes, groups, tile, both)
     own = back[..., :unknowns] - half_turn(back[..., unknowns:])
     for b in range(boxes):
@@ -347,7 +382,7 @@
     return pl.pallas_call(
         lambda *refs: down_body(*refs, groups=groups, slices=slices),
         out_shape=jax.ShapeDtypeStruct(near.shape, f32),
-        scratch_shapes=[pltpu.VMEM((boxes * excite * 2, interp.shape[1]), f32)],
+        scratch_shapes=[pltpu.VMEM((boxes * excite * 2, interp.shape[1]), bf16)],
         compiler_params=params(16), name="down",
     )(*held(pieces, near, radiate, interp, cosine, sine))
 
@@ -377,12 +412,14 @@
     return lower + upper
 
 
-def along_y(v, low, high):
-    rows = v.shape[0]
-    row = lax.broadcasted_iota(jnp.int32, v.shape, 0)
-    lower = jnp.where(row == 0, low, pltpu.roll(v, 1, 0))
-    upper = jnp.where(row == rows - 1, high, pltpu.roll(v, rows - 1, 0))
-    return lower + upper
+def along_y(tiles, low, high):
+    row = lax.broadcasted_iota(jnp.int32, tiles[0].shape, 0)
+    lower = [low] + [pltpu.roll(t, 1, 0) for t in tiles]
+    upper = [pltpu.roll(t, 7, 0) for t in tiles] + [high]
+    return [
+        jnp.where(row == 0, lower[i], lower[i + 1]) + jnp.where(row == 7, upper[i + 1], upper[i])
+        for i in range(len(tiles))
+    ]
 
 
 def relaxed(v, total, a, b):
@@ -393,8 +430,52 @@
     )
 
 
-def edge_body(field, source, kinds, first, second, layers, kind_rows, sem, kind_sem):
-    total, cy, _ = field.shape
+def tiles_at(ref, at, rows):
+    return [ref[pl.ds(pl.multiple_of(at + i, 8), 8), :] for i in range(0, rows, 8)]
+
+
+def wide_tiles_at(ref, at, rows):
+    wide = ref[pl.ds(pl.multiple_of(at, 16), rows), :].astype(f32)
+    return [wide[i : i + 8] for i in range(0, rows, 8)]
+
+
+def sweep_brick(values, e, excite, cx, cy, source, beside, a, b, emit):
+    for x in range(cx):
+        sums = []
+        for p in range(2):
+            at = (p * excite + e) * cx + x
+            edge = [jnp.broadcast_to(beside[side, pl.ds(at, 1), :], (8, source.shape[1])) for side in range(2)]
+            here = values[p][x + 1]
+            total = [n + along_z(t) + y for n, t, y in zip(tiles_at(source, at * cy, cy), here, along_y(here, *edge))]
+            for other in (values[p][x], values[p][x + 2]):
+                if other is not None:
+                    total = [n + t for n, t in zip(total, other)]
+            sums.append(total)
+        for i in range(cy // 8):
+            rows = slice(x * cy + i * 8, x * cy + i * 8 + 8)
+            new = relaxed(
+                (values[0][x + 1][i], values[1][x + 1][i]), (sums[0][i], sums[1][i]), a[rows, :], b[rows, :]
+            )
+            for p in range(2):
+                emit(p, x, i * 8, new[p])
+
+
+def by_parity(axis, run, first, second):
+    even = is_even(axis)
+
+    @pl.when(even)
+    def _():
+        run(second, first)
+
+    @pl.when(jnp.logical_not(even))
+    def _():
+        run(first, second)
+
+
+def edge_body(
+    mat_real, mat_loss, field, source, kinds, first, second, layers, kind_rows, sem, kind_sem
+):
+    total, cy, nz = field.shape
     cx = kinds.shape[0]
     even = is_even("shard")
     faces = ((cy - 2, cy - 1), (1, 0))
@@ -402,109 +483,127 @@
     for i, (inner, outer) in enumerate(faces):
         for k, (ref, y) in enumerate(((field, inner), (field, outer), (source, outer))):
             copies.append(pltpu.make_async_copy(ref.at[:, y], layers.at[i, k], sem.at[i, k]))
-        copies.append(pltpu.make_async_copy(kinds.at[:, outer], kind_rows.at[i], kind_sem.at[i]))
+        for k in range(2):
+            copies.append(
+                pltpu.make_async_copy(kinds.at[:, outer], kind_rows.at[i, pl.ds(k * cx, cx)], kind_sem.at[i, k])
+            )
     for copy in copies:
         copy.start()
     for copy in copies:
         copy.wait()
-    for k in range(3):
-        rows = slice(k * total, (k + 1) * total)
+    row = lax.broadcasted_iota(jnp.int32, (8, nz), 0) & (cx - 1)
+    for i in range(2):
+        a, b = coefficients(kind_rows[i], mat_real, mat_loss, 0)
+        for j in range(0, total // 2, 8):
+            v, sums = [], []
+            for part in range(2):
+                rows = slice(part * (total // 2) + j, part * (total // 2) + j + 8)
+                here = layers[i, 1, rows, :]
+                n = layers[i, 0, rows, :] + layers[i, 2, rows, :] + along_z(here)
+                n = n + jnp.where(row == 0, 0.0, pltpu.roll(here, 1, 0))
+                n = n + jnp.where(row == cx - 1, 0.0, pltpu.roll(here, 7, 0))
+                v.append(here)
+                sums.append(n)
+            new = relaxed(v, sums, a, b)
+            for part in range(2):
+                layers[i, 2, part * (total // 2) + j : part * (total // 2) + j + 8, :] = new[part]
+    for place, k in ((0, 1), (1, 2)):
+        rows = slice(place * total, (place + 1) * total)
         first[rows, :] = jnp.where(even, layers[0, k], layers[1, k]).astype(bf16)
         second[rows, :] = jnp.where(even, layers[1, k], layers[0, k]).astype(bf16)
-    kind = [jnp.concatenate([kind_rows[i].astype(f32) + 1.0] * (16 // cx), axis=0) for i in range(2)]
-    first[3 * total :, :] = jnp.where(even, kind[0], kind[1]).astype(bf16)
-    second[3 * total :, :] = jnp.where(even, kind[1], kind[0]).astype(bf16)
-
-
-def edges(field, source, kinds):
+    kind = [jnp.concatenate([kind_rows[i].astype(f32) + 1.0] * 2, axis=0) for i in range(2)]
+    first[2 * total :, :] = jnp.where(even, kind[0], kind[1]).astype(bf16)
+    second[2 * total :, :] = jnp.where(even, kind[1], kind[0]).astype(bf16)
+
+
+def edges(mat_real, mat_loss, field, source, kinds):
     total, _, nz = field.shape
-    cx = kinds.shape[0]
-    message = pltpu.VMEM((3 * total + 16, nz), bf16)
+    assert 2 * kinds.shape[0] == 8
+    message = pltpu.VMEM((2 * total + 16, nz), bf16)
     anywhere = pl.BlockSpec(memory_space=pl.ANY)
+    smem = pl.BlockSpec(memory_space=pltpu.SMEM)
     return pl.pallas_call(
         edge_body,
         out_shape=(message, message),
-        in_specs=[anywhere] * 3,
+        in_specs=[smem, smem] + [anywhere] * 3,
         scratch_shapes=[
             pltpu.VMEM((2, 3, total, nz), f32),
-            pltpu.VMEM((2, cx, nz), jnp.int32),
+            pltpu.VMEM((2, 8, nz), jnp.int32),
             pltpu.SemaphoreType.DMA((2, 3)),
-            pltpu.SemaphoreType.DMA((2,)),
+            pltpu.SemaphoreType.DMA((2, 2)),
         ],
         compiler_params=params(6),
         name="edges",
-    )(*left(field, source, kinds))
+    )(mat_real, mat_loss, *left(field, source, kinds))
+
+
+def faces(field, kinds, cx, cy):
+    channels = field.shape[0] // (cx * cy)
+
+    def body(field, kinds, first, second):
+        even = is_even("space")
+        for message, x in ((first, jnp.where(even, cx - 1, 0)), (second, jnp.where(even, 0, cx - 1))):
+            for c in range(channels):
+                rows = pl.ds(pl.multiple_of((c * cx + x) * cy, cy), cy)
+                message[c * cy : (c + 1) * cy, :] = field[rows, :].astype(bf16)
+            kind = kinds[pl.ds(pl.multiple_of(x * cy, cy), cy), :].astype(f32) + 1.0
+            message[channels * cy :, :] = kind.astype(bf16)
+
+    message = pltpu.VMEM((channels * cy + cy, field.shape[1]), bf16)
+    return pl.pallas_call(body, out_shape=(message, message), compiler_params=params(6), name="faces")(
+        *held(field, kinds)
+    )
 
 
 def first_body(
     mat_real, mat_loss, field, source, kinds, got_first, got_second,
-    sweep, columns, column_a, to_first, to_second, near, *, cx, cy
+    sweep, columns, column_a, to_first, to_second, near, a_all, b_all, *, cx, cy
 ):
     total = field.shape[0] // cy
     channels = total // cx
     excite = channels // 2
-    even_y = is_even("shard")
-    a, b = coefficients(kinds[...], mat_real, mat_loss, 0)
-    row = lax.broadcasted_iota(jnp.int32, (8, field.shape[1]), 0) & (cx - 1)
-    one = got_first[...].astype(f32)
-    two = got_second[...].astype(f32)
-    for side, own_y in ((0, 0), (1, cy - 1)):
-        halo = jnp.where(even_y, two, one) if side == 0 else jnp.where(even_y, one, two)
-        kind = halo[3 * total : 3 * total + 8].astype(jnp.int32)
-        col_a, col_b = coefficients(kind, mat_real, mat_loss, 1)
-        column_a[side] = col_a
-        near[side] = halo[total : 2 * total]
-        for j in range(0, total // 2, 8):
-            v, sums = [], []
-            for part in range(2):
-                at = part * (total // 2) + j
-                beside = halo[total + at : total + at + 8]
-                nbr = halo[at : at + 8] + halo[2 * total + at : 2 * total + at + 8] + along_z(beside)
-                nbr = nbr + field[pl.ds(at * cy + own_y, 8, stride=cy), :]
-                nbr = nbr + jnp.where(row == 0, 0.0, pltpu.roll(beside, 1, 0))
-                nbr = nbr + jnp.where(row == cx - 1, 0.0, pltpu.roll(beside, 7, 0))
-                v.append(beside)
-                sums.append(nbr)
-            new = relaxed(v, sums, col_a, col_b)
-            for part in range(2):
-                at = part * (total // 2) + j
-                columns[side, at : at + 8] = new[part]
-    for e in range(excite):
-        v = [
-            [field[at * cy : (at + 1) * cy, :] for at in range((p * excite + e) * cx, (p * excite + e + 1) * cx)]
+    a_all[...], b_all[...] = coefficients(kinds[...], mat_real, mat_loss, 0)
+
+    def columns_from(*got):
+        for side, own_y in ((0, 0), (1, cy - 1)):
+            halo = got[side]
+            kind = halo[2 * total :, :].astype(f32)[0:8].astype(jnp.int32)
+            col_a = coefficients(kind, mat_real, mat_loss, 1)[0]
+            column_a[side] = col_a
+            near[side] = halo[0:total, :].astype(f32)
+            part = halo[total : 2 * total, :].astype(f32)
+            for j in range(0, total, 8):
+                own = field[pl.ds(j * cy + own_y, 8, stride=cy), :]
+                columns[side, j : j + 8] = part[j : j + 8] + col_a * own
+
+    by_parity("shard", columns_from, got_first, got_second)
+
+    def one(e, _):
+        values = [
+            [None] + [tiles_at(field, ((p * excite + e) * cx + x) * cy, cy) for x in range(cx)] + [None]
             for p in range(2)
         ]
-        for x in range(cx):
-            sums = []
-            for p in range(2):
-                at = (p * excite + e) * cx + x
-                n = source[at * cy : (at + 1) * cy, :] + along_z(v[p][x])
-                n = n + along_y(v[p][x], near[0, at : at + 1, :], near[1, at : at + 1, :])
-                if x > 0:
-                    n = n + v[p][x - 1]
-                if x < cx - 1:
-                    n = n + v[p][x + 1]
-                sums.append(n)
-            new = relaxed((v[0][x], v[1][x]), sums, a[x * cy : (x + 1) * cy], b[x * cy : (x + 1) * cy])
-            for p in range(2):
-                at = (p * excite + e) * cx + x
-                sweep[at * cy : (at + 1) * cy, :] = new[p]
+
+        def emit(p, x, i, value):
+            at = ((p * excite + e) * cx + x) * cy + i
+            sweep[pl.ds(pl.multiple_of(at, 8), 8), :] = value
+
+        sweep_brick(values, e, excite, cx, cy, source, near, a_all, b_all, emit)
+        return 0
+
+    lax.fori_loop(0, excite, one, 0, unroll=2)
     even_x = is_even("space")
     plane = channels * cy
     for message, x in ((to_first, jnp.where(even_x, cx - 1, 0)), (to_second, jnp.where(even_x, 0, cx - 1))):
         for c in range(channels):
             rows = pl.ds(pl.multiple_of((c * cx + x) * cy, cy), cy)
-            message[c * cy : (c + 1) * cy, :] = field[rows, :].astype(bf16)
-            message[plane + c * cy : plane + (c + 1) * cy, :] = sweep[rows, :].astype(bf16)
+            message[c * cy : (c + 1) * cy, :] = sweep[rows, :].astype(bf16)
         for side in range(2):
             corner = jnp.concatenate(
                 [near.at[side][pl.ds(c * cx + x, 8, stride=cx), :] for c in range(0, channels, 8)], axis=0
             )
-            at = 2 * plane + side * channels
+            at = plane + side * channels
             message[at : at + channels, :] = corner.astype(bf16)
-        at = 2 * plane + 2 * channels
-        kind = kinds[pl.ds(pl.multiple_of(x * cy, cy), cy), :].astype(f32) + 1.0
-        message[at : at + cy, :] = kind.astype(bf16)
 
 
 def first_sweep(mat_real, mat_loss, field, source, kinds, got_first, got_second, cx, cy):
@@ -512,7 +611,7 @@
     channels = total // cx
     smem = pl.BlockSpec(memory_space=pltpu.SMEM)
     vmem = pl.BlockSpec(memory_space=pltpu.VMEM)
-    message = pltpu.VMEM((2 * channels * cy + 2 * channels + cy, nz), bf16)
+    message = pltpu.VMEM((channels * cy + 2 * channels, nz), bf16)
     return pl.pallas_call(
         lambda *refs: first_body(*refs, cx=cx, cy=cy),
         out_shape=(
@@ -524,8 +623,9 @@
         ),
         in_specs=[smem, smem] + [vmem] * 5,
         out_specs=(vmem,) * 5,
-        scratch_shapes=[pltpu.VMEM((2, total, nz), f32)],
-        compiler_params=params(8), name="first_sweep",
+        scratch_shapes=[pltpu.VMEM((2, total, nz), f32)] + [pltpu.VMEM((cx * cy, nz), f32)] * 2,
+        compiler_params=params(8),
+        name="first_sweep",
     )(mat_real, mat_loss, *held(field, source, kinds, got_first, got_second))
 
 
@@ -555,13 +655,15 @@
     flat_source = source.reshape(-1, cells_z)
     kinds = material.reshape(-1, cells_z)
     bricks = (-1, cells_y, cells_z)
-    got_y = swap(*edges(volume_field.reshape(bricks), source.reshape(bricks), material), "shard")
+    to_y = edges(mat_real, mat_loss, volume_field.reshape(bricks), source.reshape(bricks), material)
+    got_y = swap(*to_y, "shard")
+    got_early = swap(*faces(field, kinds, cells_x, cells_y), "space")
     sweep, columns, column_a, *to_x = first_sweep(
         mat_real, mat_loss, field, flat_source, kinds, *got_y, cells_x, cells_y
     )
-    got_x = swap(*to_x, "space")
+    got_late = swap(*to_x, "space")
     current, currents, pieces = up(
-        (mat_real, mat_loss, field, sweep, columns, column_a, flat_source, kinds, *got_x),
+        (mat_real, mat_loss, field, sweep, columns, column_a, flat_source, kinds, *got_early, *got_late),
         chosen,
         depth,
         near_boxes.shape[0],
@@ -576,7 +678,8 @@
     )
     directed = lax.all_to_all(pieces, every, split_axis=0, concat_axis=0, tiled=True)
     first, second = swap(currents, currents, "shard")
-    combined = far_combine(far_parents.T, far_kind.T, directed, translate)
+    factors, order = tables(far_parents.T, far_kind.T, translate)
+    combined = far_combine(order, directed, factors, far_parents.shape[0])
     incoming = lax.all_to_all(combined, every, split_axis=0, concat_axis=0, tiled=True)
     near, cosine, sine = near_force(near_boxes.T, currents, first, second, near_blocks, phase_angle)
     forcing = down(incoming, near, weights, interp, cosine, sine, groups, slices)

time: 64.4 us -> 68.3 us (1.061)
  the two profiles are of different devices: /device:TPU:0 before, /device:TPU:17 now
where the time goes in v5:
time: 68.3 us; the launch traced here: 67.8 us
  starting transfers between devices  23.4 us (34%)
  Pallas kernels  18.9 us (28%)
  waiting for transfers between devices  18.7 us (27%)
  local copies, waits for them, and re-layouts  5.88 us (9%)
  between operations  0.94 us (1%)
    ppermute x8, starting transfers between devices, swap(): received.append(lax.ppermute(value, axis, swap_pairs(n, k)))  14.6 us
    ppermute x8, waiting for transfers between devices, swap(): received.append(lax.ppermute(value, axis, swap_pairs(n, k)))  14 us
    pallas_call x1, Pallas kernels, up(): pl.pallas_call(lambda *refs: up_body(*refs, cx=cx, cy=cy, groups=groups,...  6.37 us
    unnamed x38, local copies, waits for them, and re-layouts  5.88 us
    all_to_all x1, waiting for transfers between devices, steps(): lax.all_to_all(pieces, every, split_axis=0, concat_axis=0, tiled=True)  4.77 us
    all_to_all x1, starting transfers between devices, steps(): lax.all_to_all(combined, every, split_axis=0, concat_axis=0, tiled=True)  4.64 us
    all_to_all x1, starting transfers between devices, steps(): lax.all_to_all(pieces, every, split_axis=0, concat_axis=0, tiled=True)  4.13 us
    pallas_call x1, Pallas kernels, tables(): pl.pallas_call(body, out_shape=(pltpu.VMEM((targets * far,) + translate.s...  2.54 us
  transfers between devices with their start and end apart: 10, of which 5 were waited for; matrix products, arithmetic and copies ran while one was open for 0% of the time, Pallas kernels for 7%

profile of v5, /device:TPU:17, one launch (start us, length us, event | category | flops | bytes accessed | tf_op | source)
XLA Modules:
  0.0 67.8 jit_solution(2232234508841595465)
XLA Ops:
  0.6 0.0 copy-start.6
  0.6 0.0 copy-start
  0.7 0.0 copy-start.1
  0.7 0.0 copy-start.12
  0.7 0.8 %copy-done.12 = f32[8]{0:T(128)S(1)} copy-done((f32[8]{0:T(128)S(1)}, f32[8]{0:T(128)}, u32[]{:S(2)}) %copy-start.12) | copy-done | bytes 56
  1.5 0.7 copy-done.14
  2.1 1.9 %edges.1 = (bf16[272,128]{1,0:T(8,128)(2,1)S(1)}, bf16[272,128]{1,0:T(8,128)(2,1)S(1)}) custom-call(f32[8]{0:T(128)S(1)} %copy-done.12, f32[8]{0:T(128)S(1)} %copy-done.14, f32[128,16,128]{2,1,0:T(8,128)} %bitcast.11, f32[128,16,128]{2,1,0:T(8,128)} %bitcast.15, s32[4,16,128]{2,1,0:T(8,128)} %kinds.1), custom_call_target="tpu_custom_call" | custom-call | tf_op jit(solution)/shard_map/edges/pallas_call | solution.py:525
  4.0 0.0 copy-start.8
  4.0 0.0 copy-start.11
  4.0 0.0 copy-start.2
  4.0 0.0 copy-start.3
  4.1 1.3 %collective-permute-start = (bf16[272,128]{1,0:T(8,128)(2,1)S(1)}, bf16[272,128]{1,0:T(8,128)(2,1)S(1)}, u32[]{:S(2)}, u32[]{:S(2)}) collective-permute-start(bf16[272,128]{1,0:T(8,128)(2,1)S(1)} %get-tuple-element.23), channel_id=1, source_target_pairs={{0,1},{1,0},{2,3},{3,2},{4,5},{5,4},{6,7},{7,6},{8,9},{9,8},{10,11... | collective-permute-start | bytes 208904 | tf_op jit(solution)/shard_map/ppermute | solution.py:89
  5.3 2.2 %collective-permute-start.1 = (bf16[272,128]{1,0:T(8,128)(2,1)S(1)}, bf16[272,128]{1,0:T(8,128)(2,1)S(1)}, u32[]{:S(2)}, u32[]{:S(2)}) collective-permute-start(bf16[272,128]{1,0:T(8,128)(2,1)S(1)} %get-tuple-element.24), channel_id=1, source_target_pairs={{1,2},{2,1},{3,4},{4,3},{5,6},{6,5},{9,10},{10,9},{11,12},{12,11},... | collective-permute-start | bytes 208904 | tf_op jit(solution)/shard_map/ppermute | solution.py:89
  7.5 0.0 collective-permute-done.refs_5_
  7.5 3.8 %collective-permute-done.1.refs_6_ = bf16[272,128]{1,0:T(8,128)(2,1)S(1)} collective-permute-done((bf16[272,128]{1,0:T(8,128)(2,1)S(1)}, bf16[272,128]{1,0:T(8,128)(2,1)S(1)}, u32[]{:S(2)}, u32[]{:S(2)}) %collective-permute-start.1) | collective-permute-done | bytes 69664 | tf_op jit(solution)/shard_map/ppermute | solution.py:89
  11.3 1.9 %first_sweep.1 = (f32[2048,128]{1,0:T(8,128)S(1)}, f32[2,128,128]{2,1,0:T(8,128)S(1)}, f32[2,8,128]{2,1,0:T(8,128)S(1)}, bf16[576,128]{1,0:T(8,128)(2,1)S(1)}, bf16[576,128]{1,0:T(8,128)(2,1)S(1)}) custom-call(f32[8]{0:T(128)S(1)} %copy-done.13, f32[8]{0:T(128)S(1)} %copy-done.15, f32[2048,128]{1,0:T(8,128)S(1)} %bitcast.12, f32[2048,128]{1,0:T(8,128)S(1)} %bitcast.16, ...), custom_call_target="tpu_custom_call" | custom-call | tf_op jit(solution)/shard_map/first_sweep/pallas_call | solution.py:615
  13.2 2.2 %collective-permute-start.4 = (bf16[576,128]{1,0:T(8,128)(2,1)S(1)}, bf16[576,128]{1,0:T(8,128)(2,1)S(1)}, u32[]{:S(2)}, u32[]{:S(2)}) collective-permute-start(bf16[576,128]{1,0:T(8,128)(2,1)S(1)} %get-tuple-element.30), channel_id=1, source_target_pairs={{0,8},{8,0},{16,24},{24,16},{1,9},{9,1},{17,25},{25,17},{2,10},{10... | collective-permute-start | bytes 442376 | tf_op jit(solution)/shard_map/ppermute | solution.py:89
  15.4 3.0 %collective-permute-start.5 = (bf16[576,128]{1,0:T(8,128)(2,1)S(1)}, bf16[576,128]{1,0:T(8,128)(2,1)S(1)}, u32[]{:S(2)}, u32[]{:S(2)}) collective-permute-start(bf16[576,128]{1,0:T(8,128)(2,1)S(1)} %get-tuple-element.31), channel_id=1, source_target_pairs={{8,16},{16,8},{9,17},{17,9},{10,18},{18,10},{11,19},{19,11},{12,20... | collective-permute-start | bytes 442376 | tf_op jit(solution)/shard_map/ppermute | solution.py:89
  18.4 0.1 faces.1
  18.5 0.1 collective-permute-start.2
  18.5 2.5 %collective-permute-start.3 = (bf16[528,128]{1,0:T(8,128)(2,1)S(1)}, bf16[528,128]{1,0:T(8,128)(2,1)S(1)}, u32[]{:S(2)}, u32[]{:S(2)}) collective-permute-start(bf16[528,128]{1,0:T(8,128)(2,1)S(1)} %get-tuple-element.29), channel_id=1, source_target_pairs={{8,16},{16,8},{9,17},{17,9},{10,18},{18,10},{11,19},{19,11},{12,20... | collective-permute-start | bytes 405512 | tf_op jit(solution)/shard_map/ppermute | solution.py:89
  21.1 1.0 %prepare.1 = (f32[8,2048]{1,0:T(8,128)S(1)}, f32[8,2048]{1,0:T(8,128)S(1)}, bf16[512,2048]{1,0:T(8,128)(2,1)S(1)}, s32[8,2048]{1,0:T(8,128)S(1)}) custom-call(f32[8,2048]{1,0:T(8,128)S(1)} %copy-done.8, s32[16,128]{1,0:T(8,128)S(1)} %copy-done.11), custom_call_target="tpu_custom_call" | custom-call | tf_op jit(solution)/shard_map/prepare/pallas_call | solution.py:65
  22.1 0.0 collective-permute-done.2.refs_8_
  22.1 2.8 %collective-permute-done.3.refs_9_ = bf16[528,128]{1,0:T(8,128)(2,1)S(1)} collective-permute-done((bf16[528,128]{1,0:T(8,128)(2,1)S(1)}, bf16[528,128]{1,0:T(8,128)(2,1)S(1)}, u32[]{:S(2)}, u32[]{:S(2)}) %collective-permute-start.3) | collective-permute-done | bytes 135200 | tf_op jit(solution)/shard_map/ppermute | solution.py:89
  24.9 0.0 collective-permute-done.4.refs_10_
  24.9 0.0 collective-permute-done.5.refs_11_
  24.9 0.0 copy-start.16
  24.9 0.0 copy-start.17
  24.9 6.4 %up.1 = (f32[2048,128]{1,0:T(8,128)}, bf16[16,16,256]{2,1,0:T(8,128)(2,1)S(1)}, bf16[32,16,256]{2,1,0:T(8,128)(2,1)}) custom-call(f32[8]{0:T(128)S(1)} %copy-done.13, f32[8]{0:T(128)S(1)} %copy-done.15, f32[2048,128]{1,0:T(8,128)S(1)} %bitcast.14, f32[2048,128]{1,0:T(8,128)S(1)} %get-tuple-element.25.refs_3_, f32[2,128,128]{2,1,0:T(8,128)S(1)} %get-tuple-element.26.refs_4_, ...), custom_call_target="tpu_custom_call" | custom-call | tf_op jit(solution)/shard_map/up/pallas_call | solution.py:222
  31.3 0.6 copy-done.9
  32.0 4.1 %all-to-all-start = ((bf16[32,16,256]{2,1,0:T(8,128)(2,1)}), bf16[32,16,256]{2,1,0:T(8,128)(2,1)}, u32[]{:S(2)}, u32[]{:S(2)}) async-start(bf16[32,16,256]{2,1,0:T(8,128)(2,1)} %get-tuple-element.38), calls=%async_computation | async-start | bytes 524288 | tf_op jit(solution)/shard_map/all_to_all | solution.py:679
  36.1 0.0 copy-start.5
  36.1 1.1 %copy-done.5 = f32[316,2,256]{2,1,0:T(2,128)S(1)} copy-done((f32[316,2,256]{2,1,0:T(2,128)S(1)}, f32[316,2,256]{2,1,0:T(2,128)}, u32[]{:S(2)}) %copy-start.5) | copy-done | bytes 647192
  37.2 2.5 %tables.1 = (f32[512,2,256]{2,1,0:T(2,128)S(1)}, s32[512]{0:T(512)S(1)}) custom-call(s32[8,64]{1,0:T(8,128)S(1)} %bitcast.24, s32[8,64]{1,0:T(8,128)S(1)} %bitcast.25, f32[316,2,256]{2,1,0:T(2,128)S(1)} %copy-done.5), custom_call_target="tpu_custom_call" | custom-call | tf_op jit(solution)/shard_map/tables/pallas_call | solution.py:258
  39.7 4.8 %all-to-all-done.refs_1_ = bf16[32,16,256]{2,1,0:T(8,128)(2,1)} async-done(((bf16[32,16,256]{2,1,0:T(8,128)(2,1)}), bf16[32,16,256]{2,1,0:T(8,128)(2,1)}, u32[]{:S(2)}, u32[]{:S(2)}) %all-to-all-start) | async-done | bytes 262176 | tf_op jit(solution)/shard_map/all_to_all | solution.py:679
  44.5 1.8 %far.1 = bf16[32,16,256]{2,1,0:T(8,128)(2,1)S(1)} custom-call(s32[512]{0:T(512)S(1)} %get-tuple-element.37.refs_0_, bf16[32,16,256]{2,1,0:T(8,128)(2,1)} %all-to-all-done.refs_1_, f32[512,2,256]{2,1,0:T(2,128)S(1)} %get-tuple-element.39.refs_2_), custom_call_target="tpu_custom_call" | custom-call | tf_op jit(solution)/shard_map/far/pallas_call | solution.py:301
  46.4 0.0 copy-start.4
  46.4 0.7 %copy-done.4 = bf16[32,16,256]{2,1,0:T(8,128)(2,1)} copy-done((bf16[32,16,256]{2,1,0:T(8,128)(2,1)}, bf16[32,16,256]{2,1,0:T(8,128)(2,1)S(1)}, u32[]{:S(2)}) %copy-start.4) | copy-done | bytes 262168
  47.1 4.6 %all-to-all-start.1 = ((bf16[32,16,256]{2,1,0:T(8,128)(2,1)}), bf16[32,16,256]{2,1,0:T(8,128)(2,1)S(1)}, u32[]{:S(2)}, u32[]{:S(2)}) async-start(bf16[32,16,256]{2,1,0:T(8,128)(2,1)} %copy-done.4), calls=%async_computation.1 | async-start | bytes 524288 | tf_op jit(solution)/shard_map/all_to_all | solution.py:683
  51.7 1.3 %collective-permute-start.6 = (bf16[16,16,256]{2,1,0:T(8,128)(2,1)}, bf16[16,16,256]{2,1,0:T(8,128)(2,1)S(1)}, u32[]{:S(2)}, u32[]{:S(2)}) collective-permute-start(bf16[16,16,256]{2,1,0:T(8,128)(2,1)} %copy-done.9), channel_id=1, source_target_pairs={{0,1},{1,0},{2,3},{3,2},{4,5},{5,4},{6,7},{7,6},{8,9},{9,8},{10,11... | collective-permute-start | bytes 393224 | tf_op jit(solution)/shard_map/ppermute | solution.py:89
  53.0 2.1 %collective-permute-start.7 = (bf16[16,16,256]{2,1,0:T(8,128)(2,1)}, bf16[16,16,256]{2,1,0:T(8,128)(2,1)S(1)}, u32[]{:S(2)}, u32[]{:S(2)}) collective-permute-start(bf16[16,16,256]{2,1,0:T(8,128)(2,1)} %copy-done.9), channel_id=1, source_target_pairs={{1,2},{2,1},{3,4},{4,3},{5,6},{6,5},{9,10},{10,9},{11,12},{12,11},... | collective-permute-start | bytes 393224 | tf_op jit(solution)/shard_map/ppermute | solution.py:89
  55.1 4.5 %collective-permute-done.6.first = bf16[16,16,256]{2,1,0:T(8,128)(2,1)S(1)} collective-permute-done((bf16[16,16,256]{2,1,0:T(8,128)(2,1)}, bf16[16,16,256]{2,1,0:T(8,128)(2,1)S(1)}, u32[]{:S(2)}, u32[]{:S(2)}) %collective-permute-start.6) | collective-permute-done | bytes 131104 | tf_op jit(solution)/shard_map/ppermute | solution.py:89
  59.6 3.0 %collective-permute-done.7.second = bf16[16,16,256]{2,1,0:T(8,128)(2,1)S(1)} collective-permute-done((bf16[16,16,256]{2,1,0:T(8,128)(2,1)}, bf16[16,16,256]{2,1,0:T(8,128)(2,1)S(1)}, u32[]{:S(2)}, u32[]{:S(2)}) %collective-permute-start.7) | collective-permute-done | bytes 131104 | tf_op jit(solution)/shard_map/ppermute | solution.py:89
  62.5 1.0 %copy-done.7 = bf16[4,256,256]{2,1,0:T(8,128)(2,1)S(1)} copy-done((bf16[4,256,256]{2,1,0:T(8,128)(2,1)S(1)}, bf16[4,256,256]{2,1,0:T(8,128)(2,1)}, u32[]{:S(2)}) %copy-start.7) | copy-done | bytes 524312
  63.6 0.9 %copy-done.10 = bf16[16,16,256]{2,1,0:T(8,128)(2,1)S(1)} copy-done((bf16[16,16,256]{2,1,0:T(8,128)(2,1)S(1)}, bf16[16,16,256]{2,1,0:T(8,128)(2,1)}, u32[]{:S(2)}) %copy-start.10) | copy-done | bytes 131096
  64.5 1.0 %near.1 = (f32[16,16,256]{2,1,0:T(8,128)S(1)}, f32[8,2048]{1,0:T(8,128)S(1)}, f32[8,2048]{1,0:T(8,128)S(1)}) custom-call(s32[4,16]{1,0:T(4,128)S(1)} %bitcast.26, bf16[16,16,256]{2,1,0:T(8,128)(2,1)S(1)} %copy-done.10, bf16[16,16,256]{2,1,0:T(8,128)(2,1)S(1)} %collective-permute-done.6.first, bf16[16,16,256]{2,1,0:T(8,128)(2,1)S(1)} %collective-permute-done.7.second, ...), custom_call_target="tpu_custom_call" | custom-call | tf_op jit(solution)/shard_map/near/pallas_call | solution.py:338
  65.5 0.0 all-to-all-done.1.refs_0_
  65.5 2.3 %down.1 = f32[16,16,256]{2,1,0:T(8,128)} custom-call(bf16[32,16,256]{2,1,0:T(8,128)(2,1)S(1)} %all-to-all-done.1.refs_0_, f32[16,16,256]{2,1,0:T(8,128)S(1)} %get-tuple-element.41.refs_1_, bf16[256,512]{1,0:T(8,128)(2,1)S(1)} %bitcast.19, bf16[512,2048]{1,0:T(8,128)(2,1)S(1)} %copy-done.2, f32[8,2048]{1,0:T(8,128)S(1)} %get-tuple-element.42.refs_4_, ...), custom_call_target="tpu_custom_call" | custom-call | tf_op jit(solution)/shard_map/down/pallas_call | solution.py:382
  (19 shorter events, 0.0 us)
Async XLA Ops:
  0.6 10.6 %copy-start.6 = (s32[4,16,128]{2,1,0:T(8,128)S(1)}, s32[4,16,128]{2,1,0:T(8,128)}, u32[]{:S(2)}) copy-start(s32[4,16,128]{2,1,0:T(8,128)} %kinds.1) | copy-start | bytes 98308
  0.6 10.6 %copy-start = (f32[2,16,4,16,128]{4,3,2,1,0:T(8,128)S(1)}, f32[2,16,4,16,128]{4,3,2,1,0:T(8,128)}, u32[]{:S(2)}) copy-start(f32[2,16,4,16,128]{4,3,2,1,0:T(8,128)} %param.14) | copy-start | bytes 3145732
  0.7 10.6 %copy-start.1 = (f32[2,16,4,16,128]{4,3,2,1,0:T(8,128)S(1)}, f32[2,16,4,16,128]{4,3,2,1,0:T(8,128)}, u32[]{:S(2)}) copy-start(f32[2,16,4,16,128]{4,3,2,1,0:T(8,128)} %param.15) | copy-start | bytes 3145732
  0.7 0.8 %copy-start.12 = (f32[8]{0:T(128)S(1)}, f32[8]{0:T(128)}, u32[]{:S(2)}) copy-start(f32[8]{0:T(128)} %refs_0_.3) | copy-start | bytes 100
  1.5 0.7 copy-start.14
  2.1 9.2 %copy-start.13 = (f32[8]{0:T(128)S(1)}, f32[8]{0:T(128)}, u32[]{:S(2)}) copy-start(f32[8]{0:T(128)} %refs_0_.3) | copy-start | bytes 100
  2.1 9.2 %copy-start.15 = (f32[8]{0:T(128)S(1)}, f32[8]{0:T(128)}, u32[]{:S(2)}) copy-start(f32[8]{0:T(128)} %refs_1_.3) | copy-start | bytes 100
  4.0 17.1 %copy-start.8 = (f32[8,2048]{1,0:T(8,128)S(1)}, f32[8,2048]{1,0:T(8,128)}, u32[]{:S(2)}) copy-start(f32[8,2048]{1,0:T(8,128)} %angle.3) | copy-start | bytes 196612
  4.0 17.1 %copy-start.11 = (s32[16,128]{1,0:T(8,128)S(1)}, s32[16,128]{1,0:T(8,128)}, u32[]{:S(2)}) copy-start(s32[16,128]{1,0:T(8,128)} %smap.1) | copy-start | bytes 24580
  4.0 20.9 %copy-start.2 = (bf16[512,2048]{1,0:T(8,128)(2,1)S(1)}, bf16[512,2048]{1,0:T(8,128)(2,1)}, u32[]{:S(2)}) copy-start(bf16[512,2048]{1,0:T(8,128)(2,1)} %refs_3_.1) | copy-start | bytes 6291460
  4.0 20.9 %copy-start.3 = (bf16[2,128,512]{2,1,0:T(8,128)(2,1)S(1)}, bf16[2,128,512]{2,1,0:T(8,128)(2,1)}, u32[]{:S(2)}) copy-start(bf16[2,128,512]{2,1,0:T(8,128)(2,1)} %param.22) | copy-start | bytes 786436
  4.1 3.5 %collective-permute-start = (bf16[272,128]{1,0:T(8,128)(2,1)S(1)}, bf16[272,128]{1,0:T(8,128)(2,1)S(1)}, u32[]{:S(2)}, u32[]{:S(2)}) collective-permute-start(bf16[272,128]{1,0:T(8,128)(2,1)S(1)} %get-tuple-element.23), channel_id=1, source_target_pairs={{0,1},{1,0},{2,3},{3,2},{4,5},{5,4},{6,7},{7,6},{8,9},{9,8},{10,11... | collective-permute-start | bytes 208904 | tf_op jit(solution)/shard_map/ppermute | solution.py:89
  5.3 5.9 %collective-permute-start.1 = (bf16[272,128]{1,0:T(8,128)(2,1)S(1)}, bf16[272,128]{1,0:T(8,128)(2,1)S(1)}, u32[]{:S(2)}, u32[]{:S(2)}) collective-permute-start(bf16[272,128]{1,0:T(8,128)(2,1)S(1)} %get-tuple-element.24), channel_id=1, source_target_pairs={{1,2},{2,1},{3,4},{4,3},{5,6},{6,5},{9,10},{10,9},{11,12},{12,11},... | collective-permute-start | bytes 208904 | tf_op jit(solution)/shard_map/ppermute | solution.py:89
  13.2 11.7 %collective-permute-start.4 = (bf16[576,128]{1,0:T(8,128)(2,1)S(1)}, bf16[576,128]{1,0:T(8,128)(2,1)S(1)}, u32[]{:S(2)}, u32[]{:S(2)}) collective-permute-start(bf16[576,128]{1,0:T(8,128)(2,1)S(1)} %get-tuple-element.30), channel_id=1, source_target_pairs={{0,8},{8,0},{16,24},{24,16},{1,9},{9,1},{17,25},{25,17},{2,10},{10... | collective-permute-start | bytes 442376 | tf_op jit(solution)/shard_map/ppermute | solution.py:89
  15.4 9.5 %collective-permute-start.5 = (bf16[576,128]{1,0:T(8,128)(2,1)S(1)}, bf16[576,128]{1,0:T(8,128)(2,1)S(1)}, u32[]{:S(2)}, u32[]{:S(2)}) collective-permute-start(bf16[576,128]{1,0:T(8,128)(2,1)S(1)} %get-tuple-element.31), channel_id=1, source_target_pairs={{8,16},{16,8},{9,17},{17,9},{10,18},{18,10},{11,19},{19,11},{12,20... | collective-permute-start | bytes 442376 | tf_op jit(solution)/shard_map/ppermute | solution.py:89
  18.5 3.6 %collective-permute-start.2 = (bf16[528,128]{1,0:T(8,128)(2,1)S(1)}, bf16[528,128]{1,0:T(8,128)(2,1)S(1)}, u32[]{:S(2)}, u32[]{:S(2)}) collective-permute-start(bf16[528,128]{1,0:T(8,128)(2,1)S(1)} %get-tuple-element.28), channel_id=1, source_target_pairs={{0,8},{8,0},{16,24},{24,16},{1,9},{9,1},{17,25},{25,17},{2,10},{10... | collective-permute-start | bytes 405512 | tf_op jit(solution)/shard_map/ppermute | solution.py:89
  18.5 6.3 %collective-permute-start.3 = (bf16[528,128]{1,0:T(8,128)(2,1)S(1)}, bf16[528,128]{1,0:T(8,128)(2,1)S(1)}, u32[]{:S(2)}, u32[]{:S(2)}) collective-permute-start(bf16[528,128]{1,0:T(8,128)(2,1)S(1)} %get-tuple-element.29), channel_id=1, source_target_pairs={{8,16},{16,8},{9,17},{17,9},{10,18},{18,10},{11,19},{19,11},{12,20... | collective-permute-start | bytes 405512 | tf_op jit(solution)/shard_map/ppermute | solution.py:89
  24.9 11.2 %copy-start.16 = (s32[64,8]{0,1:T(8,128)S(1)}, s32[64,8]{0,1:T(8,128)}, u32[]{:S(2)}) copy-start(s32[64,8]{0,1:T(8,128)} %param.25) | copy-start | bytes 6148
  24.9 11.2 %copy-start.17 = (s32[64,8]{0,1:T(8,128)S(1)}, s32[64,8]{0,1:T(8,128)}, u32[]{:S(2)}) copy-start(s32[64,8]{0,1:T(8,128)} %param.26) | copy-start | bytes 6148
  31.3 0.7 copy-start.9
  32.0 30.6 %copy-start.18 = (s32[16,4]{0,1:T(4,128)S(1)}, s32[16,4]{0,1:T(4,128)}, u32[]{:S(2)}) copy-start(s32[16,4]{0,1:T(4,128)} %param.20) | copy-start | bytes 772
  32.0 12.6 %all-to-all-start = ((bf16[32,16,256]{2,1,0:T(8,128)(2,1)}), bf16[32,16,256]{2,1,0:T(8,128)(2,1)}, u32[]{:S(2)}, u32[]{:S(2)}) async-start(bf16[32,16,256]{2,1,0:T(8,128)(2,1)} %get-tuple-element.38), calls=%async_computation | async-start | bytes 524288 | tf_op jit(solution)/shard_map/all_to_all | solution.py:679
  36.1 1.1 %copy-start.5 = (f32[316,2,256]{2,1,0:T(2,128)S(1)}, f32[316,2,256]{2,1,0:T(2,128)}, u32[]{:S(2)}) copy-start(f32[316,2,256]{2,1,0:T(2,128)} %translate.1) | copy-start | bytes 1941508
  46.4 0.7 %copy-start.4 = (bf16[32,16,256]{2,1,0:T(8,128)(2,1)}, bf16[32,16,256]{2,1,0:T(8,128)(2,1)S(1)}, u32[]{:S(2)}) copy-start(bf16[32,16,256]{2,1,0:T(8,128)(2,1)S(1)} %far.1) | copy-start | bytes 786436
  47.1 18.5 %all-to-all-start.1 = ((bf16[32,16,256]{2,1,0:T(8,128)(2,1)}), bf16[32,16,256]{2,1,0:T(8,128)(2,1)S(1)}, u32[]{:S(2)}, u32[]{:S(2)}) async-start(bf16[32,16,256]{2,1,0:T(8,128)(2,1)} %copy-done.4), calls=%async_computation.1 | async-start | bytes 524288 | tf_op jit(solution)/shard_map/all_to_all | solution.py:683
  51.7 7.8 %collective-permute-start.6 = (bf16[16,16,256]{2,1,0:T(8,128)(2,1)}, bf16[16,16,256]{2,1,0:T(8,128)(2,1)S(1)}, u32[]{:S(2)}, u32[]{:S(2)}) collective-permute-start(bf16[16,16,256]{2,1,0:T(8,128)(2,1)} %copy-done.9), channel_id=1, source_target_pairs={{0,1},{1,0},{2,3},{3,2},{4,5},{5,4},{6,7},{7,6},{8,9},{9,8},{10,11... | collective-permute-start | bytes 393224 | tf_op jit(solution)/shard_map/ppermute | solution.py:89
  53.0 9.5 %collective-permute-start.7 = (bf16[16,16,256]{2,1,0:T(8,128)(2,1)}, bf16[16,16,256]{2,1,0:T(8,128)(2,1)S(1)}, u32[]{:S(2)}, u32[]{:S(2)}) collective-permute-start(bf16[16,16,256]{2,1,0:T(8,128)(2,1)} %copy-done.9), channel_id=1, source_target_pairs={{1,2},{2,1},{3,4},{4,3},{5,6},{6,5},{9,10},{10,9},{11,12},{12,11},... | collective-permute-start | bytes 393224 | tf_op jit(solution)/shard_map/ppermute | solution.py:89
  62.5 1.0 %copy-start.7 = (bf16[4,256,256]{2,1,0:T(8,128)(2,1)S(1)}, bf16[4,256,256]{2,1,0:T(8,128)(2,1)}, u32[]{:S(2)}) copy-start(bf16[4,256,256]{2,1,0:T(8,128)(2,1)} %param.21) | copy-start | bytes 1572868
  63.5 0.9 %copy-start.10 = (bf16[16,16,256]{2,1,0:T(8,128)(2,1)S(1)}, bf16[16,16,256]{2,1,0:T(8,128)(2,1)}, u32[]{:S(2)}) copy-start(bf16[16,16,256]{2,1,0:T(8,128)(2,1)} %copy-done.9) | copy-start | bytes 393220

commit v6 on v5

--- a/solution.py
+++ b/solution.py
@@ -91,94 +91,108 @@
 
 
 def second_sweep(
-    mat_real, mat_loss, field, sweep, columns, column_a, source, kinds, early_first, early_second,
-    late_first, late_second, out, beside, a_all, b_all, store, cx, cy
+    mat_real, mat_loss, field, sweep, columns, column_a, source, kinds, got_first, got_second,
+    out, beside, a_all, b_all, store, cx, cy
 ):
     total = field.shape[0] // cy
     channels = total // cx
     excite = channels // 2
     plane = channels * cy
     a_all[...], b_all[...] = coefficients(kinds[...], mat_real, mat_loss, 0)
+    got = below_above("space", got_first, got_second)
     ends = (0, cx - 1)
-
-    def run(*got):
-        for y_side in range(2):
-            beside[y_side] = columns[y_side]
-            for x_side, x in enumerate(ends):
-                at = plane + y_side * channels
-                corner = got[x_side][1][at : at + channels, :].astype(f32)
-                factor = column_a[y_side, x : x + 1, :]
-                for c in range(0, channels, 8):
-                    rows = pl.ds(c * cx + x, 8, stride=cx)
-                    beside.at[y_side][rows, :] = beside.at[y_side][rows, :] + factor * corner[c : c + 8]
-        face_a = [
-            coefficients(got[side][0][plane:, :].astype(f32).astype(jnp.int32), mat_real, mat_loss, 1)[0]
-            for side in range(2)
-        ]
-
-        def one(e, _):
-            values = []
-            for p in range(2):
-                c = p * excite + e
-                own = [tiles_at(sweep, (c * cx + x) * cy, cy) for x in range(cx)]
-                outer = []
-                for side, x in enumerate(ends):
-                    raw = wide_tiles_at(got[side][0], c * cy, cy)
-                    own[x] = [
-                        t + a_all[x * cy + i * 8 : x * cy + i * 8 + 8, :] * h
-                        for i, (t, h) in enumerate(zip(own[x], raw))
-                    ]
-                    part = wide_tiles_at(got[side][1], c * cy, cy)
-                    before = tiles_at(field, (c * cx + x) * cy, cy)
-                    outer.append(
-                        [q + face_a[side][i * 8 : i * 8 + 8] * t for i, (q, t) in enumerate(zip(part, before))]
-                    )
-                values.append([outer[0]] + own + [outer[1]])
-
-            def emit(p, x, i, value):
-                at = ((p * excite + e) * cx + x) * cy + i
-                out[pl.ds(pl.multiple_of(at, 8), 8), :] = value
-                store(p, e, x, i, value)
-
-            sweep_brick(values, e, excite, cx, cy, source, beside, a_all, b_all, emit)
-            return 0
-
-        lax.fori_loop(0, excite, one, 0)
-
-    by_parity("space", run, (early_first, late_first), (early_second, late_second))
+    for y_side in range(2):
+        beside[y_side] = columns[y_side]
+        for x_side, x in enumerate(ends):
+            corner = got[x_side](2 * plane + y_side * channels, channels)
+            factor = column_a[y_side, x : x + 1, :]
+            for c in range(0, channels, 8):
+                rows = pl.ds(c * cx + x, 8, stride=cx)
+                beside.at[y_side][rows, :] = beside.at[y_side][rows, :] + factor * corner[c : c + 8]
+    face_a = [
+        coefficients(got[side](2 * plane + 2 * channels, cy).astype(jnp.int32), mat_real, mat_loss, 1)[0]
+        for side in range(2)
+    ]
+    for e in range(excite):
+        values = []
+        for p in range(2):
+            c = p * excite + e
+            own = [tiles_at(sweep, (c * cx + x) * cy, cy) for x in range(cx)]
+            outer = []
+            for side, x in enumerate(ends):
+                raw = tiles_of(got[side](c * cy, cy))
+                factors = tiles_at(a_all, x * cy, cy)
+                own[x] = [t + f * h for t, f, h in zip(own[x], factors, raw)]
+                part = tiles_of(got[side](plane + c * cy, cy))
+                before = tiles_at(field, (c * cx + x) * cy, cy)
+                outer.append([q + f * t for q, f, t in zip(part, tiles_of(face_a[side]), before)])
+            values.append([outer[0]] + own + [outer[1]])
+
+        def emit(p, x, new, e=e):
+            at = ((p * excite + e) * cx + x) * cy
+            whole = jnp.concatenate(new, axis=0)
+            out[at : at + cy, :] = whole
+            store(p * excite + e, x, whole)
+
+        sweep_brick(values, e, excite, cx, cy, source, beside, a_all, b_all, emit)
+
+
+def gather_rows(parts):
+    row = lax.broadcasted_iota(jnp.int32, parts[0].shape, 0)
+    upper = row < 4
+    fours = [
+        jnp.where(upper, parts[r], parts[r + 4]) + pltpu.roll(jnp.where(upper, parts[r + 4], parts[r]), 4, 0)
+        for r in range(4)
+    ]
+    second = (row & 2) == 0
+    twos = [
+        jnp.where(second, fours[r] + pltpu.roll(fours[r], 6, 0), fours[r + 2] + pltpu.roll(fours[r + 2], 2, 0))
+        for r in range(2)
+    ]
+    first = (row & 1) == 0
+    return jnp.where(first, twos[0] + pltpu.roll(twos[0], 7, 0), twos[1] + pltpu.roll(twos[1], 1, 0))
 
 
 def up_body(
-    mat_real, mat_loss, field, sweep, columns, column_a, source, kinds, early_first, early_second,
-    late_first, late_second, chosen, depth, radiate, interp, cosine, sine, volume, cur, out,
-    beside, cells, rows, fresh, a_all, b_all, sem,
-    *, cx, cy, groups, slices
+    mat_real, mat_loss, field, sweep, columns, column_a, source, kinds, got_first, got_second,
+    chosen, depth, radiate, interp, cosine, sine, volume, cur, out,
+    beside, cells, rows, fresh, a_all, b_all, sem, *, cx, cy, groups, slices
 ):
+    nz = field.shape[1]
     channels = field.shape[0] // (cx * cy)
     excite = channels // 2
     group = excite // groups
+    assert 2 * group == 8 and cy % 8 == 0
     boxes = cur.shape[0]
     unknowns = depth.shape[1] // boxes
 
-    def store(t, e, x, y, value):
-        place = (e // group) * 2 * group + t * group + e % group
-        cells.at[x][pl.ds(y * channels + place, 8, stride=channels), :] = value
+    def store(c, x, value):
+        cells[c * cy : (c + 1) * cy, x * nz : (x + 1) * nz] = value.astype(bf16)
 
     second_sweep(
-        mat_real, mat_loss, field, sweep, columns, column_a, source, kinds, early_first, early_second,
-        late_first, late_second, fresh, beside, a_all, b_all, store, cx, cy
+        mat_real, mat_loss, field, sweep, columns, column_a, source, kinds, got_first, got_second,
+        fresh, beside, a_all, b_all, store, cx, cy
     )
     leaving = pltpu.make_async_copy(fresh, volume, sem)
     leaving.start()
-    lhs = jnp.concatenate([cells[x].astype(bf16) for x in range(cx)], axis=1)
     pair = 2
     for b in range(0, boxes, pair):
         lanes = slice(b * unknowns, (b + pair) * unknowns)
-        picked = dot(lhs, chosen[:, lanes])
-        key_y = jnp.concatenate([depth[:, lanes]] * (channels // 8), axis=0)
-        found = jnp.zeros((channels, pair * unknowns), f32)
-        for y in range(cy):
-            found = jnp.where(key_y == y, picked[y * channels : (y + 1) * channels], found)
+        picked = dot(cells[...], chosen[:, lanes])
+        key_y = depth[:, lanes]
+        row = lax.broadcasted_iota(jnp.int32, key_y.shape, 0)
+        hits = [key_y == row + y for y in range(0, cy, 8)]
+        found = []
+        for s in range(groups):
+            parts = []
+            for r in range(2 * group):
+                c = (r // group) * excite + s * group + r % group
+                kept = jnp.zeros(key_y.shape, f32)
+                for i, hit in enumerate(hits):
+                    kept = jnp.where(hit, picked[c * cy + i * 8 : c * cy + i * 8 + 8], kept)
+                parts.append(kept)
+            found.append(gather_rows(parts))
+        found = jnp.concatenate(found, axis=0)
         for j in range(pair):
             own = found[:, j * unknowns : (j + 1) * unknowns].reshape(groups, 2 * group, unknowns)
             turned = half_turn(own)
@@ -224,13 +238,13 @@
         out_shape=(
             pltpu.HBM(field.shape, f32),
             pltpu.VMEM((boxes, channels // 2, 2 * unknowns), bf16),
-            pltpu.VMEM((groups * slices, piece_rows, width), bf16),
+            jax.ShapeDtypeStruct((groups * slices, piece_rows, width), bf16),
         ),
-        in_specs=[smem, smem] + [vmem] * 16,
+        in_specs=[smem, smem] + [vmem] * 14,
         out_specs=(pl.BlockSpec(memory_space=pltpu.HBM), vmem, vmem),
         scratch_shapes=[
             pltpu.VMEM((2, total, nz), f32),
-            pltpu.VMEM((cx, cy * channels, nz), f32),
+            pltpu.VMEM((channels * cy, cx * nz), bf16),
             pltpu.VMEM((boxes * channels, 2 * unknowns), bf16),
             pltpu.VMEM(field.shape, f32),
             pltpu.VMEM((cx * cy, nz), f32),
@@ -241,10 +255,13 @@
     )(*volume_args[:2], *held(*volume_args[2:], chosen, depth, radiate, interp, cosine, sine))
 
 
-def tables(lists, kinds, translate):
+def tables(lists, kinds, translate, angle):
     far, targets = lists.shape
 
-    def body(lists, kinds, translate, factors, order):
+    def body(lists, kinds, translate, angle, factors, order, cosine, sine):
+        cosine[...] = jnp.cos(angle[...])
+        sine[...] = jnp.sin(angle[...])
+
         def one(t, _):
             for f in range(far):
                 order[t * far + f] = lists[f, t]
@@ -260,12 +277,14 @@
         out_shape=(
             pltpu.VMEM((targets * far,) + translate.shape[1:], f32),
             jax.ShapeDtypeStruct((targets * far,), jnp.int32),
+            pltpu.VMEM(angle.shape, f32),
+            pltpu.VMEM(angle.shape, f32),
         ),
-        in_specs=[smem, smem, vmem],
-        out_specs=(vmem, smem),
+        in_specs=[smem, smem, vmem, vmem],
+        out_specs=(vmem, smem, vmem, vmem),
         compiler_params=params(8),
         name="tables",
-    )(lists, kinds, *held(translate))
+    )(lists, kinds, *held(translate, angle))
 
 
 def far_body(order, sources, factors, out, plain, *, targets):
@@ -300,7 +319,7 @@
     vmem = pl.BlockSpec(memory_space=pltpu.VMEM)
     return pl.pallas_call(
         lambda *refs: far_body(*refs, targets=targets),
-        out_shape=pltpu.VMEM(sources.shape, bf16),
+        out_shape=jax.ShapeDtypeStruct(sources.shape, bf16),
         in_specs=[smem, vmem, vmem],
         out_specs=vmem,
         scratch_shapes=[pltpu.VMEM((targets, tile, width), f32)],
@@ -309,9 +328,7 @@
     )(order, *held(sources, factors))
 
 
-def near_body(lists, own, first, second, blocks, angle, out, cosine, sine, boxes_all, rows):
-    cosine[...] = jnp.cos(angle[...])
-    sine[...] = jnp.sin(angle[...])
+def near_body(lists, own, first, second, blocks, out, boxes_all, rows):
     boxes, excite, k = own.shape
     slots = lists.shape[0]
     shard = lax.axis_index("shard")
@@ -330,22 +347,22 @@
     out[...] = dot(rows[...], blocks[...]).reshape(out.shape)
 
 
-def near_force(lists, own, first, second, blocks, angle):
+def near_force(lists, own, first, second, blocks):
     boxes, excite, k = own.shape
     slots = lists.shape[0]
     smem = pl.BlockSpec(memory_space=pltpu.SMEM)
     vmem = pl.BlockSpec(memory_space=pltpu.VMEM)
     return pl.pallas_call(
         near_body,
-        out_shape=(pltpu.VMEM((boxes, excite, k), f32),) + (pltpu.VMEM(angle.shape, f32),) * 2,
-        in_specs=[smem] + [vmem] * 5,
-        out_specs=(vmem,) * 3,
+        out_shape=pltpu.VMEM((boxes, excite, k), f32),
+        in_specs=[smem] + [vmem] * 4,
+        out_specs=vmem,
         scratch_shapes=[
             pltpu.VMEM((3 * boxes, excite, k), bf16),
             pltpu.VMEM((boxes * excite, slots * k), bf16),
         ],
         compiler_params=params(6), name="near",
-    )(lists, *held(own, first, second, blocks.reshape(slots * k, k), angle))
+    )(lists, *held(own, first, second, blocks.reshape(slots * k, k)))
 
 
 def down_body(pieces, near, radiate, interp, cosine, sine, out, shifted, *, groups, slices):
@@ -430,13 +447,12 @@
     )
 
 
+def tiles_of(value):
+    return [value[i : i + 8] for i in range(0, value.shape[0], 8)]
+
+
 def tiles_at(ref, at, rows):
-    return [ref[pl.ds(pl.multiple_of(at + i, 8), 8), :] for i in range(0, rows, 8)]
-
-
-def wide_tiles_at(ref, at, rows):
-    wide = ref[pl.ds(pl.multiple_of(at, 16), rows), :].astype(f32)
-    return [wide[i : i + 8] for i in range(0, rows, 8)]
+    return [ref[i : i + 8, :] for i in range(at, at + rows, 8)]
 
 
 def sweep_brick(values, e, excite, cx, cy, source, beside, a, b, emit):
@@ -444,42 +460,47 @@
         sums = []
         for p in range(2):
             at = (p * excite + e) * cx + x
-            edge = [jnp.broadcast_to(beside[side, pl.ds(at, 1), :], (8, source.shape[1])) for side in range(2)]
+            edge = [jnp.broadcast_to(beside[side, at : at + 1, :], (8, source.shape[1])) for side in range(2)]
             here = values[p][x + 1]
             total = [n + along_z(t) + y for n, t, y in zip(tiles_at(source, at * cy, cy), here, along_y(here, *edge))]
             for other in (values[p][x], values[p][x + 2]):
                 if other is not None:
                     total = [n + t for n, t in zip(total, other)]
             sums.append(total)
+        new = []
         for i in range(cy // 8):
             rows = slice(x * cy + i * 8, x * cy + i * 8 + 8)
-            new = relaxed(
-                (values[0][x + 1][i], values[1][x + 1][i]), (sums[0][i], sums[1][i]), a[rows, :], b[rows, :]
+            new.append(
+                relaxed((values[0][x + 1][i], values[1][x + 1][i]), (sums[0][i], sums[1][i]), a[rows, :], b[rows, :])
             )
-            for p in range(2):
-                emit(p, x, i * 8, new[p])
-
-
-def by_parity(axis, run, first, second):
+        for p in range(2):
+            emit(p, x, [pair[p] for pair in new])
+
+
+def below_above(axis, first, second):
     even = is_even(axis)
 
-    @pl.when(even)
-    def _():
-        run(second, first)
-
-    @pl.when(jnp.logical_not(even))
-    def _():
-        run(first, second)
+    def pick(one, two):
+        def rows(at, size):
+            return jnp.where(even, one[at : at + size, :].astype(f32), two[at : at + size, :].astype(f32))
+
+        return rows
+
+    return pick(second, first), pick(first, second)
 
 
 def edge_body(
-    mat_real, mat_loss, field, source, kinds, first, second, layers, kind_rows, sem, kind_sem
+    real_table, loss_table, field, source, kinds, first, second, layers, kind_rows, mat_real, mat_loss,
+    sem, kind_sem, table_sem
 ):
     total, cy, nz = field.shape
     cx = kinds.shape[0]
     even = is_even("shard")
     faces = ((cy - 2, cy - 1), (1, 0))
-    copies = []
+    copies = [
+        pltpu.make_async_copy(real_table, mat_real, table_sem.at[0]),
+        pltpu.make_async_copy(loss_table, mat_loss, table_sem.at[1]),
+    ]
     for i, (inner, outer) in enumerate(faces):
         for k, (ref, y) in enumerate(((field, inner), (field, outer), (source, outer))):
             copies.append(pltpu.make_async_copy(ref.at[:, y], layers.at[i, k], sem.at[i, k]))
@@ -521,38 +542,22 @@
     assert 2 * kinds.shape[0] == 8
     message = pltpu.VMEM((2 * total + 16, nz), bf16)
     anywhere = pl.BlockSpec(memory_space=pl.ANY)
-    smem = pl.BlockSpec(memory_space=pltpu.SMEM)
     return pl.pallas_call(
         edge_body,
         out_shape=(message, message),
-        in_specs=[smem, smem] + [anywhere] * 3,
+        in_specs=[anywhere] * 5,
         scratch_shapes=[
             pltpu.VMEM((2, 3, total, nz), f32),
             pltpu.VMEM((2, 8, nz), jnp.int32),
+            pltpu.SMEM(mat_real.shape, f32),
+            pltpu.SMEM(mat_loss.shape, f32),
             pltpu.SemaphoreType.DMA((2, 3)),
             pltpu.SemaphoreType.DMA((2, 2)),
+            pltpu.SemaphoreType.DMA((2,)),
         ],
         compiler_params=params(6),
         name="edges",
-    )(mat_real, mat_loss, *left(field, source, kinds))
-
-
-def faces(field, kinds, cx, cy):
-    channels = field.shape[0] // (cx * cy)
-
-    def body(field, kinds, first, second):
-        even = is_even("space")
-        for message, x in ((first, jnp.where(even, cx - 1, 0)), (second, jnp.where(even, 0, cx - 1))):
-            for c in range(channels):
-                rows = pl.ds(pl.multiple_of((c * cx + x) * cy, cy), cy)
-                message[c * cy : (c + 1) * cy, :] = field[rows, :].astype(bf16)
-            kind = kinds[pl.ds(pl.multiple_of(x * cy, cy), cy), :].astype(f32) + 1.0
-            message[channels * cy :, :] = kind.astype(bf16)
-
-    message = pltpu.VMEM((channels * cy + cy, field.shape[1]), bf16)
-    return pl.pallas_call(body, out_shape=(message, message), compiler_params=params(6), name="faces")(
-        *held(field, kinds)
-    )
+    )(*left(mat_real, mat_loss, field, source, kinds))
 
 
 def first_body(
@@ -564,46 +569,42 @@
     excite = channels // 2
     a_all[...], b_all[...] = coefficients(kinds[...], mat_real, mat_loss, 0)
 
-    def columns_from(*got):
-        for side, own_y in ((0, 0), (1, cy - 1)):
-            halo = got[side]
-            kind = halo[2 * total :, :].astype(f32)[0:8].astype(jnp.int32)
-            col_a = coefficients(kind, mat_real, mat_loss, 1)[0]
-            column_a[side] = col_a
-            near[side] = halo[0:total, :].astype(f32)
-            part = halo[total : 2 * total, :].astype(f32)
-            for j in range(0, total, 8):
-                own = field[pl.ds(j * cy + own_y, 8, stride=cy), :]
-                columns[side, j : j + 8] = part[j : j + 8] + col_a * own
-
-    by_parity("shard", columns_from, got_first, got_second)
-
-    def one(e, _):
+    for side, (halo, own_y) in enumerate(zip(below_above("shard", got_first, got_second), (0, cy - 1))):
+        kind = halo(2 * total, 16)[0:8].astype(jnp.int32)
+        col_a = coefficients(kind, mat_real, mat_loss, 1)[0]
+        column_a[side] = col_a
+        near[side] = halo(0, total)
+        for j in range(0, total, 16):
+            part = halo(total + j, 16)
+            for k in (0, 8):
+                own = field[pl.ds((j + k) * cy + own_y, 8, stride=cy), :]
+                columns[side, j + k : j + k + 8] = part[k : k + 8] + col_a * own
+    for e in range(excite):
         values = [
             [None] + [tiles_at(field, ((p * excite + e) * cx + x) * cy, cy) for x in range(cx)] + [None]
             for p in range(2)
         ]
 
-        def emit(p, x, i, value):
-            at = ((p * excite + e) * cx + x) * cy + i
-            sweep[pl.ds(pl.multiple_of(at, 8), 8), :] = value
+        def emit(p, x, new, e=e):
+            at = ((p * excite + e) * cx + x) * cy
+            sweep[at : at + cy, :] = jnp.concatenate(new, axis=0)
 
         sweep_brick(values, e, excite, cx, cy, source, near, a_all, b_all, emit)
-        return 0
-
-    lax.fori_loop(0, excite, one, 0, unroll=2)
     even_x = is_even("space")
     plane = channels * cy
     for message, x in ((to_first, jnp.where(even_x, cx - 1, 0)), (to_second, jnp.where(even_x, 0, cx - 1))):
         for c in range(channels):
             rows = pl.ds(pl.multiple_of((c * cx + x) * cy, cy), cy)
-            message[c * cy : (c + 1) * cy, :] = sweep[rows, :].astype(bf16)
+            message[c * cy : (c + 1) * cy, :] = field[rows, :].astype(bf16)
+            message[plane + c * cy : plane + (c + 1) * cy, :] = sweep[rows, :].astype(bf16)
         for side in range(2):
             corner = jnp.concatenate(
                 [near.at[side][pl.ds(c * cx + x, 8, stride=cx), :] for c in range(0, channels, 8)], axis=0
             )
-            at = plane + side * channels
+            at = 2 * plane + side * channels
             message[at : at + channels, :] = corner.astype(bf16)
+        kind = kinds[pl.ds(pl.multiple_of(x * cy, cy), cy), :].astype(f32) + 1.0
+        message[2 * plane + 2 * channels :, :] = kind.astype(bf16)
 
 
 def first_sweep(mat_real, mat_loss, field, source, kinds, got_first, got_second, cx, cy):
@@ -611,7 +612,7 @@
     channels = total // cx
     smem = pl.BlockSpec(memory_space=pltpu.SMEM)
     vmem = pl.BlockSpec(memory_space=pltpu.VMEM)
-    message = pltpu.VMEM((channels * cy + 2 * channels, nz), bf16)
+    message = pltpu.VMEM((2 * channels * cy + 2 * channels + cy, nz), bf16)
     return pl.pallas_call(
         lambda *refs: first_body(*refs, cx=cx, cy=cy),
         out_shape=(
@@ -657,13 +658,12 @@
     bricks = (-1, cells_y, cells_z)
     to_y = edges(mat_real, mat_loss, volume_field.reshape(bricks), source.reshape(bricks), material)
     got_y = swap(*to_y, "shard")
-    got_early = swap(*faces(field, kinds, cells_x, cells_y), "space")
     sweep, columns, column_a, *to_x = first_sweep(
         mat_real, mat_loss, field, flat_source, kinds, *got_y, cells_x, cells_y
     )
-    got_late = swap(*to_x, "space")
+    got_x = swap(*to_x, "space")
     current, currents, pieces = up(
-        (mat_real, mat_loss, field, sweep, columns, column_a, flat_source, kinds, *got_early, *got_late),
+        (mat_real, mat_loss, field, sweep, columns, column_a, flat_source, kinds, *got_x),
         chosen,
         depth,
         near_boxes.shape[0],
@@ -678,10 +678,10 @@
     )
     directed = lax.all_to_all(pieces, every, split_axis=0, concat_axis=0, tiled=True)
     first, second = swap(currents, currents, "shard")
-    factors, order = tables(far_parents.T, far_kind.T, translate)
+    factors, order, cosine, sine = tables(far_parents.T, far_kind.T, translate, phase_angle)
     combined = far_combine(order, directed, factors, far_parents.shape[0])
     incoming = lax.all_to_all(combined, every, split_axis=0, concat_axis=0, tiled=True)
-    near, cosine, sine = near_force(near_boxes.T, currents, first, second, near_blocks, phase_angle)
+    near = near_force(near_boxes.T, currents, first, second, near_blocks)
     forcing = down(incoming, near, weights, interp, cosine, sine, groups, slices)
     return (current.reshape(volume_field.shape), forcing)
 

time: 68.3 us -> 66.6 us (0.975)
  the two profiles are of different devices: /device:TPU:17 before, /device:TPU:0 now
where the time goes in v6:
time: 66.6 us; the launch traced here: 66 us
  starting transfers between devices  23.9 us (36%)
  Pallas kernels  16.5 us (25%)
  waiting for transfers between devices  14 us (21%)
  local copies, waits for them, and re-layouts  10.6 us (16%)
  between operations  0.93 us (1%)
    all_to_all x1, starting transfers between devices, steps(): lax.all_to_all(pieces, every, split_axis=0, concat_axis=0, tiled=True)  14.5 us
    unnamed x48, local copies, waits for them, and re-layouts  10.6 us
    ppermute x6, waiting for transfers between devices, swap(): received.append(lax.ppermute(value, axis, swap_pairs(n, k)))  8.96 us
    ppermute x6, starting transfers between devices, swap(): received.append(lax.ppermute(value, axis, swap_pairs(n, k)))  6.87 us
    all_to_all x1, waiting for transfers between devices, steps(): lax.all_to_all(pieces, every, split_axis=0, concat_axis=0, tiled=True)  5.08 us
    pallas_call x1, Pallas kernels, up(): pl.pallas_call(lambda *refs: up_body(*refs, cx=cx, cy=cy, groups=groups,...  4.75 us
    pallas_call x1, Pallas kernels, tables(): pl.pallas_call(body, out_shape=(pltpu.VMEM((targets * far,) + translate.s...  2.96 us
    all_to_all x1, starting transfers between devices, steps(): lax.all_to_all(combined, every, split_axis=0, concat_axis=0, tiled=True)  2.59 us
  transfers between devices with their start and end apart: 8, of which 3 were waited for; matrix products, arithmetic and copies ran while one was open for 0% of the time, Pallas kernels for 7%

profile of v6, /device:TPU:0, one launch (start us, length us, event | category | flops | bytes accessed | tf_op | source)
XLA Modules:
  0.0 66.0 jit_solution(13004880338666038307)
XLA Ops:
  0.6 0.0 copy-start
  0.6 0.0 copy-start.1
  0.7 0.0 copy-start.7
  0.7 0.0 copy-start.2
  0.7 0.0 copy-start.3
  0.7 1.5 %edges.1 = (bf16[272,128]{1,0:T(8,128)(2,1)S(1)}, bf16[272,128]{1,0:T(8,128)(2,1)S(1)}) custom-call(f32[8]{0:T(128)} %refs_0_.3, f32[8]{0:T(128)} %refs_1_.3, f32[128,16,128]{2,1,0:T(8,128)} %bitcast.11, f32[128,16,128]{2,1,0:T(8,128)} %bitcast.14, s32[4,16,128]{2,1,0:T(8,128)} %kinds.1), custom_call_target="tpu_custom_call" | custom-call | tf_op jit(solution)/shard_map/edges/pallas_call | solution.py:545
  2.1 3.0 %collective-permute-start = (bf16[272,128]{1,0:T(8,128)(2,1)S(1)}, bf16[272,128]{1,0:T(8,128)(2,1)S(1)}, u32[]{:S(2)}, u32[]{:S(2)}) collective-permute-start(bf16[272,128]{1,0:T(8,128)(2,1)S(1)} %get-tuple-element.20), channel_id=1, source_target_pairs={{0,1},{1,0},{2,3},{3,2},{4,5},{5,4},{6,7},{7,6},{8,9},{9,8},{10,11... | collective-permute-start | bytes 208904 | tf_op jit(solution)/shard_map/ppermute | solution.py:89
  5.2 0.7 collective-permute-start.1
  5.8 1.6 %collective-permute-done.refs_5_ = bf16[272,128]{1,0:T(8,128)(2,1)S(1)} collective-permute-done((bf16[272,128]{1,0:T(8,128)(2,1)S(1)}, bf16[272,128]{1,0:T(8,128)(2,1)S(1)}, u32[]{:S(2)}, u32[]{:S(2)}) %collective-permute-start) | collective-permute-done | bytes 69664 | tf_op jit(solution)/shard_map/ppermute | solution.py:89
  7.5 0.0 collective-permute-done.1.refs_6_
  7.5 0.0 copy-start.17
  7.5 0.6 copy-done.17
  8.2 0.7 copy-done.19
  8.8 1.4 %first_sweep.1 = (f32[2048,128]{1,0:T(8,128)S(1)}, f32[2,128,128]{2,1,0:T(8,128)S(1)}, f32[2,8,128]{2,1,0:T(8,128)S(1)}, bf16[1104,128]{1,0:T(8,128)(2,1)S(1)}, bf16[1104,128]{1,0:T(8,128)(2,1)S(1)}) custom-call(f32[8]{0:T(128)S(1)} %copy-done.17, f32[8]{0:T(128)S(1)} %copy-done.19, f32[2048,128]{1,0:T(8,128)S(1)} %bitcast.12, f32[2048,128]{1,0:T(8,128)S(1)} %bitcast.15, ...), custom_call_target="tpu_custom_call" | custom-call | tf_op jit(solution)/shard_map/first_sweep/pallas_call | solution.py:616
  10.2 0.1 collective-permute-start.2
  10.3 0.7 %collective-permute-start.3 = (bf16[1104,128]{1,0:T(8,128)(2,1)S(1)}, bf16[1104,128]{1,0:T(8,128)(2,1)S(1)}, u32[]{:S(2)}, u32[]{:S(2)}) collective-permute-start(bf16[1104,128]{1,0:T(8,128)(2,1)S(1)} %get-tuple-element.26), channel_id=1, source_target_pairs={{8,16},{16,8},{9,17},{17,9},{10,18},{18,10},{11,19},{19,11},{12,20... | collective-permute-start | bytes 847880 | tf_op jit(solution)/shard_map/ppermute | solution.py:89
  11.0 0.0 copy-start.8
  11.0 0.8 %copy-done.8 = f32[8,2048]{1,0:T(8,128)S(1)} copy-done((f32[8,2048]{1,0:T(8,128)S(1)}, f32[8,2048]{1,0:T(8,128)}, u32[]{:S(2)}) %copy-start.8) | copy-done | bytes 65560
  11.8 0.7 %copy-done.16 = s32[16,128]{1,0:T(8,128)S(1)} copy-done((s32[16,128]{1,0:T(8,128)S(1)}, s32[16,128]{1,0:T(8,128)}, u32[]{:S(2)}) %copy-start.16) | copy-done | bytes 8216
  12.5 1.0 %prepare.1 = (f32[8,2048]{1,0:T(8,128)S(1)}, f32[8,2048]{1,0:T(8,128)S(1)}, bf16[512,2048]{1,0:T(8,128)(2,1)S(1)}, s32[8,2048]{1,0:T(8,128)S(1)}) custom-call(f32[8,2048]{1,0:T(8,128)S(1)} %copy-done.8, s32[16,128]{1,0:T(8,128)S(1)} %copy-done.16), custom_call_target="tpu_custom_call" | custom-call | tf_op jit(solution)/shard_map/prepare/pallas_call | solution.py:65
  13.5 0.0 collective-permute-done.2.refs_8_
  13.5 0.0 collective-permute-done.3.refs_9_
  13.5 0.0 copy-start.18
  13.6 0.6 copy-done.18
  14.2 0.7 copy-done.20
  14.9 4.7 %up.1 = (f32[2048,128]{1,0:T(8,128)}, bf16[16,16,256]{2,1,0:T(8,128)(2,1)S(1)}, bf16[32,16,256]{2,1,0:T(8,128)(2,1)}) custom-call(f32[8]{0:T(128)S(1)} %copy-done.18, f32[8]{0:T(128)S(1)} %copy-done.20, f32[2048,128]{1,0:T(8,128)S(1)} %bitcast.13, f32[2048,128]{1,0:T(8,128)S(1)} %get-tuple-element.22.refs_3_, f32[2,128,128]{2,1,0:T(8,128)S(1)} %get-tuple-element.23.refs_4_, ...), custom_call_target="tpu_custom_call" | custom-call | tf_op jit(solution)/shard_map/up/pallas_call | solution.py:236
  19.6 0.6 copy-done.10
  20.3 14.5 %all-to-all-start = ((bf16[32,16,256]{2,1,0:T(8,128)(2,1)}), bf16[32,16,256]{2,1,0:T(8,128)(2,1)}, u32[]{:S(2)}, u32[]{:S(2)}) async-start(bf16[32,16,256]{2,1,0:T(8,128)(2,1)} %get-tuple-element.33), calls=%async_computation | async-start | bytes 524288 | tf_op jit(solution)/shard_map/all_to_all | solution.py:679
  34.8 0.0 copy-start.5
  34.8 1.1 %copy-done.5 = f32[316,2,256]{2,1,0:T(2,128)S(1)} copy-done((f32[316,2,256]{2,1,0:T(2,128)S(1)}, f32[316,2,256]{2,1,0:T(2,128)}, u32[]{:S(2)}) %copy-start.5) | copy-done | bytes 647192
  35.9 3.0 %tables.1 = (f32[512,2,256]{2,1,0:T(2,128)S(1)}, s32[512]{0:T(512)S(1)}, f32[8,2048]{1,0:T(8,128)S(1)}, f32[8,2048]{1,0:T(8,128)S(1)}) custom-call(s32[8,64]{1,0:T(8,128)S(1)} %bitcast.22, s32[8,64]{1,0:T(8,128)S(1)} %bitcast.23, f32[316,2,256]{2,1,0:T(2,128)S(1)} %copy-done.5, f32[8,2048]{1,0:T(8,128)S(1)} %copy-done.9), custom_call_target="tpu_custom_call" | custom-call | tf_op jit(solution)/shard_map/tables/pallas_call | solution.py:275
  38.9 0.6 copy-done.12
  39.5 0.6 copy-done.14
  40.1 5.1 %all-to-all-done.refs_1_ = bf16[32,16,256]{2,1,0:T(8,128)(2,1)} async-done(((bf16[32,16,256]{2,1,0:T(8,128)(2,1)}), bf16[32,16,256]{2,1,0:T(8,128)(2,1)}, u32[]{:S(2)}, u32[]{:S(2)}) %all-to-all-start) | async-done | bytes 262176 | tf_op jit(solution)/shard_map/all_to_all | solution.py:679
  45.2 1.8 %far.1 = bf16[32,16,256]{2,1,0:T(8,128)(2,1)S(1)} custom-call(s32[512]{0:T(512)S(1)} %get-tuple-element.32.refs_0_, bf16[32,16,256]{2,1,0:T(8,128)(2,1)} %all-to-all-done.refs_1_, f32[512,2,256]{2,1,0:T(2,128)S(1)} %get-tuple-element.34.refs_2_), custom_call_target="tpu_custom_call" | custom-call | tf_op jit(solution)/shard_map/far/pallas_call | solution.py:320
  47.0 0.0 copy-start.4
  47.0 0.7 %copy-done.4 = bf16[32,16,256]{2,1,0:T(8,128)(2,1)} copy-done((bf16[32,16,256]{2,1,0:T(8,128)(2,1)}, bf16[32,16,256]{2,1,0:T(8,128)(2,1)S(1)}, u32[]{:S(2)}) %copy-start.4) | copy-done | bytes 262168
  47.7 2.6 %all-to-all-start.1 = ((bf16[32,16,256]{2,1,0:T(8,128)(2,1)}), bf16[32,16,256]{2,1,0:T(8,128)(2,1)S(1)}, u32[]{:S(2)}, u32[]{:S(2)}) async-start(bf16[32,16,256]{2,1,0:T(8,128)(2,1)} %copy-done.4), calls=%async_computation.1 | async-start | bytes 524288 | tf_op jit(solution)/shard_map/all_to_all | solution.py:683
  50.3 1.8 %collective-permute-start.4 = (bf16[16,16,256]{2,1,0:T(8,128)(2,1)S(1)}, bf16[16,16,256]{2,1,0:T(8,128)(2,1)S(1)}, u32[]{:S(2)}, u32[]{:S(2)}) collective-permute-start(bf16[16,16,256]{2,1,0:T(8,128)(2,1)S(1)} %copy-done.11), channel_id=1, source_target_pairs={{0,1},{1,0},{2,3},{3,2},{4,5},{5,4},{6,7},{7,6},{8,9},{9,8},{10,11... | collective-permute-start | bytes 393224 | tf_op jit(solution)/shard_map/ppermute | solution.py:89
  52.1 0.7 collective-permute-start.5
  52.8 7.3 %collective-permute-done.4.first = bf16[16,16,256]{2,1,0:T(8,128)(2,1)S(1)} collective-permute-done((bf16[16,16,256]{2,1,0:T(8,128)(2,1)S(1)}, bf16[16,16,256]{2,1,0:T(8,128)(2,1)S(1)}, u32[]{:S(2)}, u32[]{:S(2)}) %collective-permute-start.4) | collective-permute-done | bytes 131104 | tf_op jit(solution)/shard_map/ppermute | solution.py:89
  60.1 0.0 collective-permute-done.5.second
  60.1 1.0 %copy-done.6 = bf16[4,256,256]{2,1,0:T(8,128)(2,1)S(1)} copy-done((bf16[4,256,256]{2,1,0:T(8,128)(2,1)S(1)}, bf16[4,256,256]{2,1,0:T(8,128)(2,1)}, u32[]{:S(2)}) %copy-start.6) | copy-done | bytes 524312
  61.1 0.9 %near.1.refs_1_ = f32[16,16,256]{2,1,0:T(8,128)S(1)} custom-call(s32[4,16]{1,0:T(4,128)S(1)} %bitcast.24, bf16[16,16,256]{2,1,0:T(8,128)(2,1)S(1)} %copy-done.11, bf16[16,16,256]{2,1,0:T(8,128)(2,1)S(1)} %collective-permute-done.4.first, bf16[16,16,256]{2,1,0:T(8,128)(2,1)S(1)} %collective-permute-done.5.second, bf16[1024,256]{1,0:T(8,128)(2,1)S(1)} %bitcast.19), custom_call_target="tpu_custom_call" | custom-call | tf_op jit(solution)/shard_map/near/pallas_call | solution.py:355
  62.0 0.0 all-to-all-done.1.refs_0_
  62.1 0.8 %copy-done.13 = f32[8,2048]{1,0:T(8,128)S(1)} copy-done((f32[8,2048]{1,0:T(8,128)S(1)}, f32[8,2048]{1,0:T(8,128)}, u32[]{:S(2)}) %copy-start.13) | copy-done | bytes 65560
  62.9 0.8 %copy-done.15 = f32[8,2048]{1,0:T(8,128)S(1)} copy-done((f32[8,2048]{1,0:T(8,128)S(1)}, f32[8,2048]{1,0:T(8,128)}, u32[]{:S(2)}) %copy-start.15) | copy-done | bytes 65560
  63.7 2.3 %down.1 = f32[16,16,256]{2,1,0:T(8,128)} custom-call(bf16[32,16,256]{2,1,0:T(8,128)(2,1)S(1)} %all-to-all-done.1.refs_0_, f32[16,16,256]{2,1,0:T(8,128)S(1)} %near.1.refs_1_, bf16[256,512]{1,0:T(8,128)(2,1)S(1)} %bitcast.18, bf16[512,2048]{1,0:T(8,128)(2,1)S(1)} %copy-done.2, f32[8,2048]{1,0:T(8,128)S(1)} %copy-done.13, f32[8,2048]{1,0:T(8,128)S(1)} %copy-done.15), custom_call_target="tpu_custom_call" | custom-call | tf_op jit(solution)/shard_map/down/pallas_call | solution.py:399
  (24 shorter events, 0.0 us)
Async XLA Ops:
  0.6 6.8 %copy-start = (f32[2,16,4,16,128]{4,3,2,1,0:T(8,128)S(1)}, f32[2,16,4,16,128]{4,3,2,1,0:T(8,128)}, u32[]{:S(2)}) copy-start(f32[2,16,4,16,128]{4,3,2,1,0:T(8,128)} %param.14) | copy-start | bytes 3145732
  0.6 6.8 %copy-start.1 = (f32[2,16,4,16,128]{4,3,2,1,0:T(8,128)S(1)}, f32[2,16,4,16,128]{4,3,2,1,0:T(8,128)}, u32[]{:S(2)}) copy-start(f32[2,16,4,16,128]{4,3,2,1,0:T(8,128)} %param.15) | copy-start | bytes 3145732
  0.7 6.8 %copy-start.7 = (s32[4,16,128]{2,1,0:T(8,128)S(1)}, s32[4,16,128]{2,1,0:T(8,128)}, u32[]{:S(2)}) copy-start(s32[4,16,128]{2,1,0:T(8,128)} %kinds.1) | copy-start | bytes 98308
  0.7 12.9 %copy-start.2 = (bf16[512,2048]{1,0:T(8,128)(2,1)S(1)}, bf16[512,2048]{1,0:T(8,128)(2,1)}, u32[]{:S(2)}) copy-start(bf16[512,2048]{1,0:T(8,128)(2,1)} %refs_3_.1) | copy-start | bytes 6291460
  0.7 12.9 %copy-start.3 = (bf16[2,128,512]{2,1,0:T(8,128)(2,1)S(1)}, bf16[2,128,512]{2,1,0:T(8,128)(2,1)}, u32[]{:S(2)}) copy-start(bf16[2,128,512]{2,1,0:T(8,128)(2,1)} %param.22) | copy-start | bytes 786436
  2.1 5.3 %collective-permute-start = (bf16[272,128]{1,0:T(8,128)(2,1)S(1)}, bf16[272,128]{1,0:T(8,128)(2,1)S(1)}, u32[]{:S(2)}, u32[]{:S(2)}) collective-permute-start(bf16[272,128]{1,0:T(8,128)(2,1)S(1)} %get-tuple-element.20), channel_id=1, source_target_pairs={{0,1},{1,0},{2,3},{3,2},{4,5},{5,4},{6,7},{7,6},{8,9},{9,8},{10,11... | collective-permute-start | bytes 208904 | tf_op jit(solution)/shard_map/ppermute | solution.py:89
  5.2 2.3 %collective-permute-start.1 = (bf16[272,128]{1,0:T(8,128)(2,1)S(1)}, bf16[272,128]{1,0:T(8,128)(2,1)S(1)}, u32[]{:S(2)}, u32[]{:S(2)}) collective-permute-start(bf16[272,128]{1,0:T(8,128)(2,1)S(1)} %get-tuple-element.21), channel_id=1, source_target_pairs={{1,2},{2,1},{3,4},{4,3},{5,6},{6,5},{9,10},{10,9},{11,12},{12,11},... | collective-permute-start | bytes 208904 | tf_op jit(solution)/shard_map/ppermute | solution.py:89
  7.5 0.7 copy-start.17
  8.2 0.7 copy-start.19
  10.2 3.3 %collective-permute-start.2 = (bf16[1104,128]{1,0:T(8,128)(2,1)S(1)}, bf16[1104,128]{1,0:T(8,128)(2,1)S(1)}, u32[]{:S(2)}, u32[]{:S(2)}) collective-permute-start(bf16[1104,128]{1,0:T(8,128)(2,1)S(1)} %get-tuple-element.25), channel_id=1, source_target_pairs={{0,8},{8,0},{16,24},{24,16},{1,9},{9,1},{17,25},{25,17},{2,10},{10... | collective-permute-start | bytes 847880 | tf_op jit(solution)/shard_map/ppermute | solution.py:89
  10.3 3.2 %collective-permute-start.3 = (bf16[1104,128]{1,0:T(8,128)(2,1)S(1)}, bf16[1104,128]{1,0:T(8,128)(2,1)S(1)}, u32[]{:S(2)}, u32[]{:S(2)}) collective-permute-start(bf16[1104,128]{1,0:T(8,128)(2,1)S(1)} %get-tuple-element.26), channel_id=1, source_target_pairs={{8,16},{16,8},{9,17},{17,9},{10,18},{18,10},{11,19},{19,11},{12,20... | collective-permute-start | bytes 847880 | tf_op jit(solution)/shard_map/ppermute | solution.py:89
  11.0 0.8 %copy-start.8 = (f32[8,2048]{1,0:T(8,128)S(1)}, f32[8,2048]{1,0:T(8,128)}, u32[]{:S(2)}) copy-start(f32[8,2048]{1,0:T(8,128)} %angle.3) | copy-start | bytes 196612
  11.8 0.7 %copy-start.16 = (s32[16,128]{1,0:T(8,128)S(1)}, s32[16,128]{1,0:T(8,128)}, u32[]{:S(2)}) copy-start(s32[16,128]{1,0:T(8,128)} %smap.1) | copy-start | bytes 24580
  13.5 0.7 copy-start.18
  14.2 0.7 copy-start.20
  14.9 19.9 %copy-start.9 = (f32[8,2048]{1,0:T(8,128)S(1)}, f32[8,2048]{1,0:T(8,128)}, u32[]{:S(2)}) copy-start(f32[8,2048]{1,0:T(8,128)} %angle.3) | copy-start | bytes 196612
  14.9 19.9 %copy-start.21 = (s32[64,8]{0,1:T(8,128)S(1)}, s32[64,8]{0,1:T(8,128)}, u32[]{:S(2)}) copy-start(s32[64,8]{0,1:T(8,128)} %param.25) | copy-start | bytes 6148
  14.9 19.9 %copy-start.22 = (s32[64,8]{0,1:T(8,128)S(1)}, s32[64,8]{0,1:T(8,128)}, u32[]{:S(2)}) copy-start(s32[64,8]{0,1:T(8,128)} %param.26) | copy-start | bytes 6148
  19.6 0.7 copy-start.10
  20.3 39.8 %copy-start.23 = (s32[16,4]{0,1:T(4,128)S(1)}, s32[16,4]{0,1:T(4,128)}, u32[]{:S(2)}) copy-start(s32[16,4]{0,1:T(4,128)} %param.20) | copy-start | bytes 772
  20.3 24.9 %all-to-all-start = ((bf16[32,16,256]{2,1,0:T(8,128)(2,1)}), bf16[32,16,256]{2,1,0:T(8,128)(2,1)}, u32[]{:S(2)}, u32[]{:S(2)}) async-start(bf16[32,16,256]{2,1,0:T(8,128)(2,1)} %get-tuple-element.33), calls=%async_computation | async-start | bytes 524288 | tf_op jit(solution)/shard_map/all_to_all | solution.py:679
  34.8 1.1 %copy-start.5 = (f32[316,2,256]{2,1,0:T(2,128)S(1)}, f32[316,2,256]{2,1,0:T(2,128)}, u32[]{:S(2)}) copy-start(f32[316,2,256]{2,1,0:T(2,128)} %translate.1) | copy-start | bytes 1941508
  38.9 0.6 copy-start.12
  39.5 0.6 copy-start.14
  40.1 10.2 %copy-start.11 = (bf16[16,16,256]{2,1,0:T(8,128)(2,1)S(1)}, bf16[16,16,256]{2,1,0:T(8,128)(2,1)}, u32[]{:S(2)}) copy-start(bf16[16,16,256]{2,1,0:T(8,128)(2,1)} %copy-done.10) | copy-start | bytes 393220
  47.0 0.7 %copy-start.4 = (bf16[32,16,256]{2,1,0:T(8,128)(2,1)}, bf16[32,16,256]{2,1,0:T(8,128)(2,1)S(1)}, u32[]{:S(2)}) copy-start(bf16[32,16,256]{2,1,0:T(8,128)(2,1)S(1)} %far.1) | copy-start | bytes 786436
  47.7 14.3 %all-to-all-start.1 = ((bf16[32,16,256]{2,1,0:T(8,128)(2,1)}), bf16[32,16,256]{2,1,0:T(8,128)(2,1)S(1)}, u32[]{:S(2)}, u32[]{:S(2)}) async-start(bf16[32,16,256]{2,1,0:T(8,128)(2,1)} %copy-done.4), calls=%async_computation.1 | async-start | bytes 524288 | tf_op jit(solution)/shard_map/all_to_all | solution.py:683
  50.3 9.8 %collective-permute-start.4 = (bf16[16,16,256]{2,1,0:T(8,128)(2,1)S(1)}, bf16[16,16,256]{2,1,0:T(8,128)(2,1)S(1)}, u32[]{:S(2)}, u32[]{:S(2)}) collective-permute-start(bf16[16,16,256]{2,1,0:T(8,128)(2,1)S(1)} %copy-done.11), channel_id=1, source_target_pairs={{0,1},{1,0},{2,3},{3,2},{4,5},{5,4},{6,7},{7,6},{8,9},{9,8},{10,11... | collective-permute-start | bytes 393224 | tf_op jit(solution)/shard_map/ppermute | solution.py:89
  52.1 8.0 %collective-permute-start.5 = (bf16[16,16,256]{2,1,0:T(8,128)(2,1)S(1)}, bf16[16,16,256]{2,1,0:T(8,128)(2,1)S(1)}, u32[]{:S(2)}, u32[]{:S(2)}) collective-permute-start(bf16[16,16,256]{2,1,0:T(8,128)(2,1)S(1)} %copy-done.11), channel_id=1, source_target_pairs={{1,2},{2,1},{3,4},{4,3},{5,6},{6,5},{9,10},{10,9},{11,12},{12,11},... | collective-permute-start | bytes 393224 | tf_op jit(solution)/shard_map/ppermute | solution.py:89
  60.1 1.0 %copy-start.6 = (bf16[4,256,256]{2,1,0:T(8,128)(2,1)S(1)}, bf16[4,256,256]{2,1,0:T(8,128)(2,1)}, u32[]{:S(2)}) copy-start(bf16[4,256,256]{2,1,0:T(8,128)(2,1)} %param.21) | copy-start | bytes 1572868
  62.0 0.8 %copy-start.13 = (f32[8,2048]{1,0:T(8,128)S(1)}, f32[8,2048]{1,0:T(8,128)}, u32[]{:S(2)}) copy-start(f32[8,2048]{1,0:T(8,128)} %copy-done.12) | copy-start | bytes 196612
  62.9 0.8 %copy-start.15 = (f32[8,2048]{1,0:T(8,128)S(1)}, f32[8,2048]{1,0:T(8,128)}, u32[]{:S(2)}) copy-start(f32[8,2048]{1,0:T(8,128)} %copy-done.14) | copy-start | bytes 196612

commit v7 on v6

--- a/solution.py
+++ b/solution.py
@@ -91,14 +91,14 @@
 
 
 def second_sweep(
-    mat_real, mat_loss, field, sweep, columns, column_a, source, kinds, got_first, got_second,
+    table, field, sweep, columns, column_a, source, kinds, got_first, got_second,
     out, beside, a_all, b_all, store, cx, cy
 ):
     total = field.shape[0] // cy
     channels = total // cx
     excite = channels // 2
     plane = channels * cy
-    a_all[...], b_all[...] = coefficients(kinds[...], mat_real, mat_loss, 0)
+    a_all[...], b_all[...] = coefficients(kinds[...], table, 0)
     got = below_above("space", got_first, got_second)
     ends = (0, cx - 1)
     for y_side in range(2):
@@ -110,7 +110,7 @@
                 rows = pl.ds(c * cx + x, 8, stride=cx)
                 beside.at[y_side][rows, :] = beside.at[y_side][rows, :] + factor * corner[c : c + 8]
     face_a = [
-        coefficients(got[side](2 * plane + 2 * channels, cy).astype(jnp.int32), mat_real, mat_loss, 1)[0]
+        coefficients(got[side](2 * plane + 2 * channels, cy).astype(jnp.int32), table, 1)[0]
         for side in range(2)
     ]
     for e in range(excite):
@@ -154,7 +154,7 @@
 
 
 def up_body(
-    mat_real, mat_loss, field, sweep, columns, column_a, source, kinds, got_first, got_second,
+    table, field, sweep, columns, column_a, source, kinds, got_first, got_second,
     chosen, depth, radiate, interp, cosine, sine, volume, cur, out,
     beside, cells, rows, fresh, a_all, b_all, sem, *, cx, cy, groups, slices
 ):
@@ -170,7 +170,7 @@
         cells[c * cy : (c + 1) * cy, x * nz : (x + 1) * nz] = value.astype(bf16)
 
     second_sweep(
-        mat_real, mat_loss, field, sweep, columns, column_a, source, kinds, got_first, got_second,
+        table, field, sweep, columns, column_a, source, kinds, got_first, got_second,
         fresh, beside, a_all, b_all, store, cx, cy
     )
     leaving = pltpu.make_async_copy(fresh, volume, sem)
@@ -224,23 +224,22 @@
 
 
 def up(volume_args, chosen, depth, boxes, radiate, interp, cosine, sine, cx, cy, groups, slices):
-    field = volume_args[2]
+    field = volume_args[1]
     nz = field.shape[1]
     total = field.shape[0] // cy
     channels = total // cx
     unknowns = depth.shape[1] // boxes
     width = interp.shape[1] // slices
     piece_rows = boxes // CHILDREN * (channels // groups)
-    smem = pl.BlockSpec(memory_space=pltpu.SMEM)
     vmem = pl.BlockSpec(memory_space=pltpu.VMEM)
     return pl.pallas_call(
         lambda *refs: up_body(*refs, cx=cx, cy=cy, groups=groups, slices=slices),
         out_shape=(
             pltpu.HBM(field.shape, f32),
             pltpu.VMEM((boxes, channels // 2, 2 * unknowns), bf16),
-            jax.ShapeDtypeStruct((groups * slices, piece_rows, width), bf16),
+            pltpu.HBM((groups * slices, piece_rows, width), bf16),
         ),
-        in_specs=[smem, smem] + [vmem] * 14,
+        in_specs=[vmem] * 15,
         out_specs=(pl.BlockSpec(memory_space=pltpu.HBM), vmem, vmem),
         scratch_shapes=[
             pltpu.VMEM((2, total, nz), f32),
@@ -252,16 +251,13 @@
             pltpu.SemaphoreType.DMA(()),
         ],
         compiler_params=params(16), name="up",
-    )(*volume_args[:2], *held(*volume_args[2:], chosen, depth, radiate, interp, cosine, sine))
-
-
-def tables(lists, kinds, translate, angle):
+    )(*held(*volume_args, chosen, depth, radiate, interp, cosine, sine))
+
+
+def tables(lists, kinds, translate):
     far, targets = lists.shape
 
-    def body(lists, kinds, translate, angle, factors, order, cosine, sine):
-        cosine[...] = jnp.cos(angle[...])
-        sine[...] = jnp.sin(angle[...])
-
+    def body(lists, kinds, translate, factors, order):
         def one(t, _):
             for f in range(far):
                 order[t * far + f] = lists[f, t]
@@ -277,14 +273,12 @@
         out_shape=(
             pltpu.VMEM((targets * far,) + translate.shape[1:], f32),
             jax.ShapeDtypeStruct((targets * far,), jnp.int32),
-            pltpu.VMEM(angle.shape, f32),
-            pltpu.VMEM(angle.shape, f32),
         ),
-        in_specs=[smem, smem, vmem, vmem],
-        out_specs=(vmem, smem, vmem, vmem),
+        in_specs=[smem, smem, vmem],
+        out_specs=(vmem, smem),
         compiler_params=params(8),
         name="tables",
-    )(lists, kinds, *held(translate, angle))
+    )(lists, kinds, *held(translate))
 
 
 def far_body(order, sources, factors, out, plain, *, targets):
@@ -319,7 +313,7 @@
     vmem = pl.BlockSpec(memory_space=pltpu.VMEM)
     return pl.pallas_call(
         lambda *refs: far_body(*refs, targets=targets),
-        out_shape=jax.ShapeDtypeStruct(sources.shape, bf16),
+        out_shape=pltpu.HBM(sources.shape, bf16),
         in_specs=[smem, vmem, vmem],
         out_specs=vmem,
         scratch_shapes=[pltpu.VMEM((targets, tile, width), f32)],
@@ -328,7 +322,9 @@
     )(order, *held(sources, factors))
 
 
-def near_body(lists, own, first, second, blocks, out, boxes_all, rows):
+def near_body(lists, own, first, second, blocks, angle, out, cosine, sine, boxes_all, rows):
+    cosine[...] = jnp.cos(angle[...])
+    sine[...] = jnp.sin(angle[...])
     boxes, excite, k = own.shape
     slots = lists.shape[0]
     shard = lax.axis_index("shard")
@@ -347,22 +343,22 @@
     out[...] = dot(rows[...], blocks[...]).reshape(out.shape)
 
 
-def near_force(lists, own, first, second, blocks):
+def near_force(lists, own, first, second, blocks, angle):
     boxes, excite, k = own.shape
     slots = lists.shape[0]
     smem = pl.BlockSpec(memory_space=pltpu.SMEM)
     vmem = pl.BlockSpec(memory_space=pltpu.VMEM)
     return pl.pallas_call(
         near_body,
-        out_shape=pltpu.VMEM((boxes, excite, k), f32),
-        in_specs=[smem] + [vmem] * 4,
-        out_specs=vmem,
+        out_shape=(pltpu.VMEM((boxes, excite, k), f32),) + (pltpu.VMEM(angle.shape, f32),) * 2,
+        in_specs=[smem] + [vmem] * 5,
+        out_specs=(vmem,) * 3,
         scratch_shapes=[
             pltpu.VMEM((3 * boxes, excite, k), bf16),
             pltpu.VMEM((boxes * excite, slots * k), bf16),
         ],
         compiler_params=params(6), name="near",
-    )(lists, *held(own, first, second, blocks.reshape(slots * k, k)))
+    )(lists, *held(own, first, second, blocks.reshape(slots * k, k), angle))
 
 
 def down_body(pieces, near, radiate, interp, cosine, sine, out, shifted, *, groups, slices):
@@ -408,13 +404,14 @@
     return lax.rem(lax.axis_index(axis), 2) == 0
 
 
-def coefficients(kinds, mat_real, mat_loss, base):
+def coefficients(kinds, table, base):
+    mats = table.shape[0] // 2
     diagonal = jnp.full(kinds.shape, 6.0, f32)
     loss = jnp.zeros(kinds.shape, f32)
-    for k in range(mat_real.shape[0]):
+    for k in range(mats):
         present = kinds == k + base
-        diagonal = jnp.where(present, 6.0 + mat_real[k], diagonal)
-        loss = jnp.where(present, mat_loss[k], loss)
+        diagonal = jnp.where(present, 6.0 + table[k : k + 1, :], diagonal)
+        loss = jnp.where(present, table[mats + k : mats + k + 1, :], loss)
     a = relaxation / diagonal
     if base > 0:
         a = jnp.where(kinds < base, 0.0, a)
@@ -490,7 +487,7 @@
 
 
 def edge_body(
-    real_table, loss_table, field, source, kinds, first, second, layers, kind_rows, mat_real, mat_loss,
+    real_table, loss_table, field, source, kinds, first, second, table, layers, kind_rows, mat_real, mat_loss,
     sem, kind_sem, table_sem
 ):
     total, cy, nz = field.shape
@@ -512,9 +509,12 @@
         copy.start()
     for copy in copies:
         copy.wait()
+    for k in range(mat_real.shape[0]):
+        table[k : k + 1, :] = jnp.full((1, nz), mat_real[k], f32)
+        table[mat_real.shape[0] + k : mat_real.shape[0] + k + 1, :] = jnp.full((1, nz), mat_loss[k], f32)
     row = lax.broadcasted_iota(jnp.int32, (8, nz), 0) & (cx - 1)
     for i in range(2):
-        a, b = coefficients(kind_rows[i], mat_real, mat_loss, 0)
+        a, b = coefficients(kind_rows[i], table, 0)
         for j in range(0, total // 2, 8):
             v, sums = [], []
             for part in range(2):
@@ -544,7 +544,7 @@
     anywhere = pl.BlockSpec(memory_space=pl.ANY)
     return pl.pallas_call(
         edge_body,
-        out_shape=(message, message),
+        out_shape=(message, message, pltpu.VMEM((2 * mat_real.shape[0], nz), f32)),
         in_specs=[anywhere] * 5,
         scratch_shapes=[
             pltpu.VMEM((2, 3, total, nz), f32),
@@ -561,17 +561,17 @@
 
 
 def first_body(
-    mat_real, mat_loss, field, source, kinds, got_first, got_second,
+    table, field, source, kinds, got_first, got_second,
     sweep, columns, column_a, to_first, to_second, near, a_all, b_all, *, cx, cy
 ):
     total = field.shape[0] // cy
     channels = total // cx
     excite = channels // 2
-    a_all[...], b_all[...] = coefficients(kinds[...], mat_real, mat_loss, 0)
+    a_all[...], b_all[...] = coefficients(kinds[...], table, 0)
 
     for side, (halo, own_y) in enumerate(zip(below_above("shard", got_first, got_second), (0, cy - 1))):
         kind = halo(2 * total, 16)[0:8].astype(jnp.int32)
-        col_a = coefficients(kind, mat_real, mat_loss, 1)[0]
+        col_a = coefficients(kind, table, 1)[0]
         column_a[side] = col_a
         near[side] = halo(0, total)
         for j in range(0, total, 16):
@@ -607,10 +607,9 @@
         message[2 * plane + 2 * channels :, :] = kind.astype(bf16)
 
 
-def first_sweep(mat_real, mat_loss, field, source, kinds, got_first, got_second, cx, cy):
+def first_sweep(table, field, source, kinds, got_first, got_second, cx, cy):
     total, nz = field.shape[0] // cy, field.shape[1]
     channels = total // cx
-    smem = pl.BlockSpec(memory_space=pltpu.SMEM)
     vmem = pl.BlockSpec(memory_space=pltpu.VMEM)
     message = pltpu.VMEM((2 * channels * cy + 2 * channels + cy, nz), bf16)
     return pl.pallas_call(
@@ -622,12 +621,12 @@
             message,
             message,
         ),
-        in_specs=[smem, smem] + [vmem] * 5,
+        in_specs=[vmem] * 6,
         out_specs=(vmem,) * 5,
         scratch_shapes=[pltpu.VMEM((2, total, nz), f32)] + [pltpu.VMEM((cx * cy, nz), f32)] * 2,
         compiler_params=params(8),
         name="first_sweep",
-    )(mat_real, mat_loss, *held(field, source, kinds, got_first, got_second))
+    )(*held(table, field, source, kinds, got_first, got_second))
 
 
 def steps(
@@ -656,14 +655,14 @@
     flat_source = source.reshape(-1, cells_z)
     kinds = material.reshape(-1, cells_z)
     bricks = (-1, cells_y, cells_z)
-    to_y = edges(mat_real, mat_loss, volume_field.reshape(bricks), source.reshape(bricks), material)
+    *to_y, table = edges(mat_real, mat_loss, volume_field.reshape(bricks), source.reshape(bricks), material)
     got_y = swap(*to_y, "shard")
     sweep, columns, column_a, *to_x = first_sweep(
-        mat_real, mat_loss, field, flat_source, kinds, *got_y, cells_x, cells_y
+        table, field, flat_source, kinds, *got_y, cells_x, cells_y
     )
     got_x = swap(*to_x, "space")
     current, currents, pieces = up(
-        (mat_real, mat_loss, field, sweep, columns, column_a, flat_source, kinds, *got_x),
+        (table, field, sweep, columns, column_a, flat_source, kinds, *got_x),
         chosen,
         depth,
         near_boxes.shape[0],
@@ -678,10 +677,10 @@
     )
     directed = lax.all_to_all(pieces, every, split_axis=0, concat_axis=0, tiled=True)
     first, second = swap(currents, currents, "shard")
-    factors, order, cosine, sine = tables(far_parents.T, far_kind.T, translate, phase_angle)
+    factors, order = tables(far_parents.T, far_kind.T, translate)
     combined = far_combine(order, directed, factors, far_parents.shape[0])
     incoming = lax.all_to_all(combined, every, split_axis=0, concat_axis=0, tiled=True)
-    near = near_force(near_boxes.T, currents, first, second, near_blocks)
+    near, cosine, sine = near_force(near_boxes.T, currents, first, second, near_blocks, phase_angle)
     forcing = down(incoming, near, weights, interp, cosine, sine, groups, slices)
     return (current.reshape(volume_field.shape), forcing)
 

time: 66.6 us -> 62.3 us (0.935)
  the two profiles are of different devices: /device:TPU:0 before, /device:TPU:17 now
where the time goes in v7:
time: 62.3 us; the launch traced here: 61.7 us
  starting transfers between devices  21.3 us (34%)
  waiting for transfers between devices  18.4 us (30%)
  Pallas kernels  16 us (26%)
  local copies, waits for them, and re-layouts  5.23 us (8%)
  between operations  0.84 us (1%)
    ppermute x6, waiting for transfers between devices, swap(): received.append(lax.ppermute(value, axis, swap_pairs(n, k)))  13.6 us
    ppermute x6, starting transfers between devices, swap(): received.append(lax.ppermute(value, axis, swap_pairs(n, k)))  11.9 us
    unnamed x30, local copies, waits for them, and re-layouts  5.23 us
    all_to_all x1, waiting for transfers between devices, steps(): lax.all_to_all(pieces, every, split_axis=0, concat_axis=0, tiled=True)  4.77 us
    all_to_all x1, starting transfers between devices, steps(): lax.all_to_all(pieces, every, split_axis=0, concat_axis=0, tiled=True)  4.69 us
    all_to_all x1, starting transfers between devices, steps(): lax.all_to_all(combined, every, split_axis=0, concat_axis=0, tiled=True)  4.64 us
    pallas_call x1, Pallas kernels, up(): pl.pallas_call(lambda *refs: up_body(*refs, cx=cx, cy=cy, groups=groups,...  4.28 us
    pallas_call x1, Pallas kernels, far_combine(): pl.pallas_call(lambda *refs: far_body(*refs, targets=targets), out_shape=...  2.56 us
  transfers between devices with their start and end apart: 8, of which 5 were waited for; matrix products, arithmetic and copies ran while one was open for 0% of the time, Pallas kernels for 7%

profile of v7, /device:TPU:17, one launch (start us, length us, event | category | flops | bytes accessed | tf_op | source)
XLA Modules:
  0.0 61.7 jit_solution(12290036712060841800)
XLA Ops:
  0.6 0.0 copy-start
  0.6 0.0 copy-start.1
  0.7 0.0 copy-start.6
  0.7 0.0 copy-start.2
  0.7 0.0 copy-start.3
  0.7 1.5 %edges.1 = (bf16[272,128]{1,0:T(8,128)(2,1)S(1)}, bf16[272,128]{1,0:T(8,128)(2,1)S(1)}, f32[16,128]{1,0:T(8,128)S(1)}) custom-call(f32[8]{0:T(128)} %real_table.1, f32[8]{0:T(128)} %loss_table.1, f32[128,16,128]{2,1,0:T(8,128)} %bitcast.11, f32[128,16,128]{2,1,0:T(8,128)} %bitcast.14, s32[4,16,128]{2,1,0:T(8,128)} %kinds.1), custom_call_target="tpu_custom_call" | custom-call | tf_op jit(solution)/shard_map/edges/pallas_call | solution.py:545
  2.2 1.3 %collective-permute-start = (bf16[272,128]{1,0:T(8,128)(2,1)S(1)}, bf16[272,128]{1,0:T(8,128)(2,1)S(1)}, u32[]{:S(2)}, u32[]{:S(2)}) collective-permute-start(bf16[272,128]{1,0:T(8,128)(2,1)S(1)} %get-tuple-element.23), channel_id=1, source_target_pairs={{0,1},{1,0},{2,3},{3,2},{4,5},{5,4},{6,7},{7,6},{8,9},{9,8},{10,11... | collective-permute-start | bytes 208904 | tf_op jit(solution)/shard_map/ppermute | solution.py:89
  3.4 2.0 %collective-permute-start.1 = (bf16[272,128]{1,0:T(8,128)(2,1)S(1)}, bf16[272,128]{1,0:T(8,128)(2,1)S(1)}, u32[]{:S(2)}, u32[]{:S(2)}) collective-permute-start(bf16[272,128]{1,0:T(8,128)(2,1)S(1)} %get-tuple-element.24), channel_id=1, source_target_pairs={{1,2},{2,1},{3,4},{4,3},{5,6},{6,5},{9,10},{10,9},{11,12},{12,11},... | collective-permute-start | bytes 208904 | tf_op jit(solution)/shard_map/ppermute | solution.py:89
  5.5 0.0 collective-permute-done.refs_4_
  5.5 3.9 %collective-permute-done.1.refs_5_ = bf16[272,128]{1,0:T(8,128)(2,1)S(1)} collective-permute-done((bf16[272,128]{1,0:T(8,128)(2,1)S(1)}, bf16[272,128]{1,0:T(8,128)(2,1)S(1)}, u32[]{:S(2)}, u32[]{:S(2)}) %collective-permute-start.1) | collective-permute-done | bytes 69664 | tf_op jit(solution)/shard_map/ppermute | solution.py:89
  9.4 0.0 copy-done
  9.4 0.0 copy-done.1
  9.4 0.0 copy-done.6
  9.4 0.8 %first_sweep.1 = (f32[2048,128]{1,0:T(8,128)S(1)}, f32[2,128,128]{2,1,0:T(8,128)S(1)}, f32[2,8,128]{2,1,0:T(8,128)S(1)}, bf16[1104,128]{1,0:T(8,128)(2,1)S(1)}, bf16[1104,128]{1,0:T(8,128)(2,1)S(1)}) custom-call(f32[16,128]{1,0:T(8,128)S(1)} %get-tuple-element.22.refs_0_, f32[2048,128]{1,0:T(8,128)S(1)} %bitcast.12, f32[2048,128]{1,0:T(8,128)S(1)} %bitcast.15, ...), custom_call_target="tpu_custom_call" | custom-call | tf_op jit(solution)/shard_map/first_sweep/pallas_call | solution.py:615
  10.2 2.2 %collective-permute-start.2 = (bf16[1104,128]{1,0:T(8,128)(2,1)S(1)}, bf16[1104,128]{1,0:T(8,128)(2,1)S(1)}, u32[]{:S(2)}, u32[]{:S(2)}) collective-permute-start(bf16[1104,128]{1,0:T(8,128)(2,1)S(1)} %get-tuple-element.28), channel_id=1, source_target_pairs={{0,8},{8,0},{16,24},{24,16},{1,9},{9,1},{17,25},{25,17},{2,10},{10... | collective-permute-start | bytes 847880 | tf_op jit(solution)/shard_map/ppermute | solution.py:89
  12.4 3.0 %collective-permute-start.3 = (bf16[1104,128]{1,0:T(8,128)(2,1)S(1)}, bf16[1104,128]{1,0:T(8,128)(2,1)S(1)}, u32[]{:S(2)}, u32[]{:S(2)}) collective-permute-start(bf16[1104,128]{1,0:T(8,128)(2,1)S(1)} %get-tuple-element.29), channel_id=1, source_target_pairs={{8,16},{16,8},{9,17},{17,9},{10,18},{18,10},{11,19},{19,11},{12,20... | collective-permute-start | bytes 847880 | tf_op jit(solution)/shard_map/ppermute | solution.py:89
  15.5 0.0 copy-start.7
  15.5 0.8 %copy-done.7 = f32[8,2048]{1,0:T(8,128)S(1)} copy-done((f32[8,2048]{1,0:T(8,128)S(1)}, f32[8,2048]{1,0:T(8,128)}, u32[]{:S(2)}) %copy-start.7) | copy-done | bytes 65560
  16.3 0.0 copy-start.11
  16.3 0.7 %copy-done.11 = s32[16,128]{1,0:T(8,128)S(1)} copy-done((s32[16,128]{1,0:T(8,128)S(1)}, s32[16,128]{1,0:T(8,128)}, u32[]{:S(2)}) %copy-start.11) | copy-done | bytes 8216
  17.0 1.0 %prepare.1 = (f32[8,2048]{1,0:T(8,128)S(1)}, f32[8,2048]{1,0:T(8,128)S(1)}, bf16[512,2048]{1,0:T(8,128)(2,1)S(1)}, s32[8,2048]{1,0:T(8,128)S(1)}) custom-call(f32[8,2048]{1,0:T(8,128)S(1)} %copy-done.7, s32[16,128]{1,0:T(8,128)S(1)} %copy-done.11), custom_call_target="tpu_custom_call" | custom-call | tf_op jit(solution)/shard_map/prepare/pallas_call | solution.py:65
  18.0 0.0 collective-permute-done.2.refs_7_
  18.0 2.3 %collective-permute-done.3.refs_8_ = bf16[1104,128]{1,0:T(8,128)(2,1)S(1)} collective-permute-done((bf16[1104,128]{1,0:T(8,128)(2,1)S(1)}, bf16[1104,128]{1,0:T(8,128)(2,1)S(1)}, u32[]{:S(2)}, u32[]{:S(2)}) %collective-permute-start.3) | collective-permute-done | bytes 282656 | tf_op jit(solution)/shard_map/ppermute | solution.py:89
  20.3 0.0 copy-done.2
  20.3 0.0 copy-done.3
  20.3 4.3 %up.1 = (f32[2048,128]{1,0:T(8,128)}, bf16[16,16,256]{2,1,0:T(8,128)(2,1)S(1)}, bf16[32,16,256]{2,1,0:T(8,128)(2,1)}) custom-call(f32[16,128]{1,0:T(8,128)S(1)} %get-tuple-element.22.refs_0_, f32[2048,128]{1,0:T(8,128)S(1)} %bitcast.13, f32[2048,128]{1,0:T(8,128)S(1)} %get-tuple-element.25.refs_2_, f32[2,128,128]{2,1,0:T(8,128)S(1)} %get-tuple-element.26.refs_3_, ...), custom_call_target="tpu_custom_call" | custom-call | tf_op jit(solution)/shard_map/up/pallas_call | solution.py:235
  24.6 0.0 copy-start.9
  24.6 0.6 %copy-done.9 = bf16[16,16,256]{2,1,0:T(8,128)(2,1)} copy-done((bf16[16,16,256]{2,1,0:T(8,128)(2,1)}, bf16[16,16,256]{2,1,0:T(8,128)(2,1)S(1)}, u32[]{:S(2)}) %copy-start.9) | copy-done | bytes 131096
  25.3 4.7 %all-to-all-start = ((bf16[32,16,256]{2,1,0:T(8,128)(2,1)}), bf16[32,16,256]{2,1,0:T(8,128)(2,1)}, u32[]{:S(2)}, u32[]{:S(2)}) async-start(bf16[32,16,256]{2,1,0:T(8,128)(2,1)} %get-tuple-element.36), calls=%async_computation | async-start | bytes 524288 | tf_op jit(solution)/shard_map/all_to_all | solution.py:678
  30.0 0.0 copy-done.12
  30.0 0.0 copy-done.13
  30.0 0.0 copy-start.4
  30.0 1.1 %copy-done.4 = f32[316,2,256]{2,1,0:T(2,128)S(1)} copy-done((f32[316,2,256]{2,1,0:T(2,128)S(1)}, f32[316,2,256]{2,1,0:T(2,128)}, u32[]{:S(2)}) %copy-start.4) | copy-done | bytes 647192
  31.1 2.5 %tables.1 = (f32[512,2,256]{2,1,0:T(2,128)S(1)}, s32[512]{0:T(512)S(1)}) custom-call(s32[8,64]{1,0:T(8,128)S(1)} %bitcast.22, s32[8,64]{1,0:T(8,128)S(1)} %bitcast.23, f32[316,2,256]{2,1,0:T(2,128)S(1)} %copy-done.4), custom_call_target="tpu_custom_call" | custom-call | tf_op jit(solution)/shard_map/tables/pallas_call | solution.py:271
  33.6 4.8 %all-to-all-done.refs_1_ = bf16[32,16,256]{2,1,0:T(8,128)(2,1)} async-done(((bf16[32,16,256]{2,1,0:T(8,128)(2,1)}), bf16[32,16,256]{2,1,0:T(8,128)(2,1)}, u32[]{:S(2)}, u32[]{:S(2)}) %all-to-all-start) | async-done | bytes 262176 | tf_op jit(solution)/shard_map/all_to_all | solution.py:678
  38.4 2.6 %far.1 = bf16[32,16,256]{2,1,0:T(8,128)(2,1)} custom-call(s32[512]{0:T(512)S(1)} %get-tuple-element.35.refs_0_, bf16[32,16,256]{2,1,0:T(8,128)(2,1)} %all-to-all-done.refs_1_, f32[512,2,256]{2,1,0:T(2,128)S(1)} %get-tuple-element.37.refs_2_), custom_call_target="tpu_custom_call" | custom-call | tf_op jit(solution)/shard_map/far/pallas_call | solution.py:314
  41.0 4.6 %all-to-all-start.1 = ((bf16[32,16,256]{2,1,0:T(8,128)(2,1)}), bf16[32,16,256]{2,1,0:T(8,128)(2,1)S(1)}, u32[]{:S(2)}, u32[]{:S(2)}) async-start(bf16[32,16,256]{2,1,0:T(8,128)(2,1)} %far.1), calls=%async_computation.1 | async-start | bytes 524288 | tf_op jit(solution)/shard_map/all_to_all | solution.py:682
  45.6 1.3 %collective-permute-start.4 = (bf16[16,16,256]{2,1,0:T(8,128)(2,1)}, bf16[16,16,256]{2,1,0:T(8,128)(2,1)S(1)}, u32[]{:S(2)}, u32[]{:S(2)}) collective-permute-start(bf16[16,16,256]{2,1,0:T(8,128)(2,1)} %copy-done.9), channel_id=1, source_target_pairs={{0,1},{1,0},{2,3},{3,2},{4,5},{5,4},{6,7},{7,6},{8,9},{9,8},{10,11... | collective-permute-start | bytes 393224 | tf_op jit(solution)/shard_map/ppermute | solution.py:89
  46.9 2.1 %collective-permute-start.5 = (bf16[16,16,256]{2,1,0:T(8,128)(2,1)}, bf16[16,16,256]{2,1,0:T(8,128)(2,1)S(1)}, u32[]{:S(2)}, u32[]{:S(2)}) collective-permute-start(bf16[16,16,256]{2,1,0:T(8,128)(2,1)} %copy-done.9), channel_id=1, source_target_pairs={{1,2},{2,1},{3,4},{4,3},{5,6},{6,5},{9,10},{10,9},{11,12},{12,11},... | collective-permute-start | bytes 393224 | tf_op jit(solution)/shard_map/ppermute | solution.py:89
  49.0 4.5 %collective-permute-done.4.first = bf16[16,16,256]{2,1,0:T(8,128)(2,1)S(1)} collective-permute-done((bf16[16,16,256]{2,1,0:T(8,128)(2,1)}, bf16[16,16,256]{2,1,0:T(8,128)(2,1)S(1)}, u32[]{:S(2)}, u32[]{:S(2)}) %collective-permute-start.4) | collective-permute-done | bytes 131104 | tf_op jit(solution)/shard_map/ppermute | solution.py:89
  53.4 3.0 %collective-permute-done.5.second = bf16[16,16,256]{2,1,0:T(8,128)(2,1)S(1)} collective-permute-done((bf16[16,16,256]{2,1,0:T(8,128)(2,1)}, bf16[16,16,256]{2,1,0:T(8,128)(2,1)S(1)}, u32[]{:S(2)}, u32[]{:S(2)}) %collective-permute-start.5) | collective-permute-done | bytes 131104 | tf_op jit(solution)/shard_map/ppermute | solution.py:89
  56.4 0.0 copy-done.8
  56.4 0.0 copy-done.14
  56.4 1.0 %copy-done.5 = bf16[4,256,256]{2,1,0:T(8,128)(2,1)S(1)} copy-done((bf16[4,256,256]{2,1,0:T(8,128)(2,1)S(1)}, bf16[4,256,256]{2,1,0:T(8,128)(2,1)}, u32[]{:S(2)}) %copy-start.5) | copy-done | bytes 524312
  57.4 0.9 %copy-done.10 = bf16[16,16,256]{2,1,0:T(8,128)(2,1)S(1)} copy-done((bf16[16,16,256]{2,1,0:T(8,128)(2,1)S(1)}, bf16[16,16,256]{2,1,0:T(8,128)(2,1)}, u32[]{:S(2)}) %copy-start.10) | copy-done | bytes 131096
  58.4 1.0 %near.1 = (f32[16,16,256]{2,1,0:T(8,128)S(1)}, f32[8,2048]{1,0:T(8,128)S(1)}, f32[8,2048]{1,0:T(8,128)S(1)}) custom-call(s32[4,16]{1,0:T(4,128)S(1)} %bitcast.24, bf16[16,16,256]{2,1,0:T(8,128)(2,1)S(1)} %copy-done.10, bf16[16,16,256]{2,1,0:T(8,128)(2,1)S(1)} %collective-permute-done.4.first, bf16[16,16,256]{2,1,0:T(8,128)(2,1)S(1)} %collective-permute-done.5.second, ...), custom_call_target="tpu_custom_call" | custom-call | tf_op jit(solution)/shard_map/near/pallas_call | solution.py:351
  59.4 0.0 all-to-all-done.1.refs_0_
  59.4 2.3 %down.1 = f32[16,16,256]{2,1,0:T(8,128)} custom-call(bf16[32,16,256]{2,1,0:T(8,128)(2,1)S(1)} %all-to-all-done.1.refs_0_, f32[16,16,256]{2,1,0:T(8,128)S(1)} %get-tuple-element.39.refs_1_, bf16[256,512]{1,0:T(8,128)(2,1)S(1)} %bitcast.18, bf16[512,2048]{1,0:T(8,128)(2,1)S(1)} %copy-done.2, f32[8,2048]{1,0:T(8,128)S(1)} %get-tuple-element.40.refs_4_, ...), custom_call_target="tpu_custom_call" | custom-call | tf_op jit(solution)/shard_map/down/pallas_call | solution.py:395
  (6 shorter events, 0.0 us)
Async XLA Ops:
  0.6 8.7 %copy-start = (f32[2,16,4,16,128]{4,3,2,1,0:T(8,128)S(1)}, f32[2,16,4,16,128]{4,3,2,1,0:T(8,128)}, u32[]{:S(2)}) copy-start(f32[2,16,4,16,128]{4,3,2,1,0:T(8,128)} %param.14) | copy-start | bytes 3145732
  0.6 8.7 %copy-start.1 = (f32[2,16,4,16,128]{4,3,2,1,0:T(8,128)S(1)}, f32[2,16,4,16,128]{4,3,2,1,0:T(8,128)}, u32[]{:S(2)}) copy-start(f32[2,16,4,16,128]{4,3,2,1,0:T(8,128)} %param.15) | copy-start | bytes 3145732
  0.7 8.7 %copy-start.6 = (s32[4,16,128]{2,1,0:T(8,128)S(1)}, s32[4,16,128]{2,1,0:T(8,128)}, u32[]{:S(2)}) copy-start(s32[4,16,128]{2,1,0:T(8,128)} %kinds.1) | copy-start | bytes 98308
  0.7 19.6 %copy-start.2 = (bf16[512,2048]{1,0:T(8,128)(2,1)S(1)}, bf16[512,2048]{1,0:T(8,128)(2,1)}, u32[]{:S(2)}) copy-start(bf16[512,2048]{1,0:T(8,128)(2,1)} %refs_3_.1) | copy-start | bytes 6291460
  0.7 19.6 %copy-start.3 = (bf16[2,128,512]{2,1,0:T(8,128)(2,1)S(1)}, bf16[2,128,512]{2,1,0:T(8,128)(2,1)}, u32[]{:S(2)}) copy-start(bf16[2,128,512]{2,1,0:T(8,128)(2,1)} %param.22) | copy-start | bytes 786436
  2.2 3.3 %collective-permute-start = (bf16[272,128]{1,0:T(8,128)(2,1)S(1)}, bf16[272,128]{1,0:T(8,128)(2,1)S(1)}, u32[]{:S(2)}, u32[]{:S(2)}) collective-permute-start(bf16[272,128]{1,0:T(8,128)(2,1)S(1)} %get-tuple-element.23), channel_id=1, source_target_pairs={{0,1},{1,0},{2,3},{3,2},{4,5},{5,4},{6,7},{7,6},{8,9},{9,8},{10,11... | collective-permute-start | bytes 208904 | tf_op jit(solution)/shard_map/ppermute | solution.py:89
  3.4 5.9 %collective-permute-start.1 = (bf16[272,128]{1,0:T(8,128)(2,1)S(1)}, bf16[272,128]{1,0:T(8,128)(2,1)S(1)}, u32[]{:S(2)}, u32[]{:S(2)}) collective-permute-start(bf16[272,128]{1,0:T(8,128)(2,1)S(1)} %get-tuple-element.24), channel_id=1, source_target_pairs={{1,2},{2,1},{3,4},{4,3},{5,6},{6,5},{9,10},{10,9},{11,12},{12,11},... | collective-permute-start | bytes 208904 | tf_op jit(solution)/shard_map/ppermute | solution.py:89
  10.2 7.8 %collective-permute-start.2 = (bf16[1104,128]{1,0:T(8,128)(2,1)S(1)}, bf16[1104,128]{1,0:T(8,128)(2,1)S(1)}, u32[]{:S(2)}, u32[]{:S(2)}) collective-permute-start(bf16[1104,128]{1,0:T(8,128)(2,1)S(1)} %get-tuple-element.28), channel_id=1, source_target_pairs={{0,8},{8,0},{16,24},{24,16},{1,9},{9,1},{17,25},{25,17},{2,10},{10... | collective-permute-start | bytes 847880 | tf_op jit(solution)/shard_map/ppermute | solution.py:89
  12.4 7.9 %collective-permute-start.3 = (bf16[1104,128]{1,0:T(8,128)(2,1)S(1)}, bf16[1104,128]{1,0:T(8,128)(2,1)S(1)}, u32[]{:S(2)}, u32[]{:S(2)}) collective-permute-start(bf16[1104,128]{1,0:T(8,128)(2,1)S(1)} %get-tuple-element.29), channel_id=1, source_target_pairs={{8,16},{16,8},{9,17},{17,9},{10,18},{18,10},{11,19},{19,11},{12,20... | collective-permute-start | bytes 847880 | tf_op jit(solution)/shard_map/ppermute | solution.py:89
  15.5 0.8 %copy-start.7 = (f32[8,2048]{1,0:T(8,128)S(1)}, f32[8,2048]{1,0:T(8,128)}, u32[]{:S(2)}) copy-start(f32[8,2048]{1,0:T(8,128)} %angle.3) | copy-start | bytes 196612
  16.3 0.7 %copy-start.11 = (s32[16,128]{1,0:T(8,128)S(1)}, s32[16,128]{1,0:T(8,128)}, u32[]{:S(2)}) copy-start(s32[16,128]{1,0:T(8,128)} %smap.1) | copy-start | bytes 24580
  20.3 9.7 %copy-start.12 = (s32[64,8]{0,1:T(8,128)S(1)}, s32[64,8]{0,1:T(8,128)}, u32[]{:S(2)}) copy-start(s32[64,8]{0,1:T(8,128)} %param.25) | copy-start | bytes 6148
  20.3 9.7 %copy-start.13 = (s32[64,8]{0,1:T(8,128)S(1)}, s32[64,8]{0,1:T(8,128)}, u32[]{:S(2)}) copy-start(s32[64,8]{0,1:T(8,128)} %param.26) | copy-start | bytes 6148
  24.6 0.7 %copy-start.9 = (bf16[16,16,256]{2,1,0:T(8,128)(2,1)}, bf16[16,16,256]{2,1,0:T(8,128)(2,1)S(1)}, u32[]{:S(2)}) copy-start(bf16[16,16,256]{2,1,0:T(8,128)(2,1)S(1)} %get-tuple-element.38.own) | copy-start | bytes 393220
  25.3 31.1 %copy-start.8 = (f32[8,2048]{1,0:T(8,128)S(1)}, f32[8,2048]{1,0:T(8,128)}, u32[]{:S(2)}) copy-start(f32[8,2048]{1,0:T(8,128)} %angle.3) | copy-start | bytes 196612
  25.3 31.1 %copy-start.14 = (s32[16,4]{0,1:T(4,128)S(1)}, s32[16,4]{0,1:T(4,128)}, u32[]{:S(2)}) copy-start(s32[16,4]{0,1:T(4,128)} %param.20) | copy-start | bytes 772
  25.3 13.1 %all-to-all-start = ((bf16[32,16,256]{2,1,0:T(8,128)(2,1)}), bf16[32,16,256]{2,1,0:T(8,128)(2,1)}, u32[]{:S(2)}, u32[]{:S(2)}) async-start(bf16[32,16,256]{2,1,0:T(8,128)(2,1)} %get-tuple-element.36), calls=%async_computation | async-start | bytes 524288 | tf_op jit(solution)/shard_map/all_to_all | solution.py:678
  30.0 1.1 %copy-start.4 = (f32[316,2,256]{2,1,0:T(2,128)S(1)}, f32[316,2,256]{2,1,0:T(2,128)}, u32[]{:S(2)}) copy-start(f32[316,2,256]{2,1,0:T(2,128)} %translate.1) | copy-start | bytes 1941508
  41.0 18.5 %all-to-all-start.1 = ((bf16[32,16,256]{2,1,0:T(8,128)(2,1)}), bf16[32,16,256]{2,1,0:T(8,128)(2,1)S(1)}, u32[]{:S(2)}, u32[]{:S(2)}) async-start(bf16[32,16,256]{2,1,0:T(8,128)(2,1)} %far.1), calls=%async_computation.1 | async-start | bytes 524288 | tf_op jit(solution)/shard_map/all_to_all | solution.py:682
  45.6 7.8 %collective-permute-start.4 = (bf16[16,16,256]{2,1,0:T(8,128)(2,1)}, bf16[16,16,256]{2,1,0:T(8,128)(2,1)S(1)}, u32[]{:S(2)}, u32[]{:S(2)}) collective-permute-start(bf16[16,16,256]{2,1,0:T(8,128)(2,1)} %copy-done.9), channel_id=1, source_target_pairs={{0,1},{1,0},{2,3},{3,2},{4,5},{5,4},{6,7},{7,6},{8,9},{9,8},{10,11... | collective-permute-start | bytes 393224 | tf_op jit(solution)/shard_map/ppermute | solution.py:89
  46.9 9.5 %collective-permute-start.5 = (bf16[16,16,256]{2,1,0:T(8,128)(2,1)}, bf16[16,16,256]{2,1,0:T(8,128)(2,1)S(1)}, u32[]{:S(2)}, u32[]{:S(2)}) collective-permute-start(bf16[16,16,256]{2,1,0:T(8,128)(2,1)} %copy-done.9), channel_id=1, source_target_pairs={{1,2},{2,1},{3,4},{4,3},{5,6},{6,5},{9,10},{10,9},{11,12},{12,11},... | collective-permute-start | bytes 393224 | tf_op jit(solution)/shard_map/ppermute | solution.py:89
  56.4 1.0 %copy-start.5 = (bf16[4,256,256]{2,1,0:T(8,128)(2,1)S(1)}, bf16[4,256,256]{2,1,0:T(8,128)(2,1)}, u32[]{:S(2)}) copy-start(bf16[4,256,256]{2,1,0:T(8,128)(2,1)} %param.21) | copy-start | bytes 1572868
  57.4 0.9 %copy-start.10 = (bf16[16,16,256]{2,1,0:T(8,128)(2,1)S(1)}, bf16[16,16,256]{2,1,0:T(8,128)(2,1)}, u32[]{:S(2)}) copy-start(bf16[16,16,256]{2,1,0:T(8,128)(2,1)} %copy-done.9) | copy-start | bytes 393220

commit v8 on v7

--- a/solution.py
+++ b/solution.py
@@ -91,7 +91,7 @@
 
 
 def second_sweep(
-    table, field, sweep, columns, column_a, source, kinds, got_first, got_second,
+    table, field, sweep, columns, column_a, source, kinds, early_first, early_second, late_first, late_second,
     out, beside, a_all, b_all, store, cx, cy
 ):
     total = field.shape[0] // cy
@@ -99,18 +99,19 @@
     excite = channels // 2
     plane = channels * cy
     a_all[...], b_all[...] = coefficients(kinds[...], table, 0)
-    got = below_above("space", got_first, got_second)
+    early = below_above("space", early_first, early_second)
+    late = below_above("space", late_first, late_second)
     ends = (0, cx - 1)
     for y_side in range(2):
         beside[y_side] = columns[y_side]
         for x_side, x in enumerate(ends):
-            corner = got[x_side](2 * plane + y_side * channels, channels)
+            corner = late[x_side](plane + y_side * channels, channels)
             factor = column_a[y_side, x : x + 1, :]
             for c in range(0, channels, 8):
                 rows = pl.ds(c * cx + x, 8, stride=cx)
                 beside.at[y_side][rows, :] = beside.at[y_side][rows, :] + factor * corner[c : c + 8]
     face_a = [
-        coefficients(got[side](2 * plane + 2 * channels, cy).astype(jnp.int32), table, 1)[0]
+        coefficients(early[side](plane, cy).astype(jnp.int32), table, 1)[0]
         for side in range(2)
     ]
     for e in range(excite):
@@ -120,10 +121,10 @@
             own = [tiles_at(sweep, (c * cx + x) * cy, cy) for x in range(cx)]
             outer = []
             for side, x in enumerate(ends):
-                raw = tiles_of(got[side](c * cy, cy))
+                raw = tiles_of(early[side](c * cy, cy))
                 factors = tiles_at(a_all, x * cy, cy)
                 own[x] = [t + f * h for t, f, h in zip(own[x], factors, raw)]
-                part = tiles_of(got[side](plane + c * cy, cy))
+                part = tiles_of(late[side](c * cy, cy))
                 before = tiles_at(field, (c * cx + x) * cy, cy)
                 outer.append([q + f * t for q, f, t in zip(part, tiles_of(face_a[side]), before)])
             values.append([outer[0]] + own + [outer[1]])
@@ -154,9 +155,9 @@
 
 
 def up_body(
-    table, field, sweep, columns, column_a, source, kinds, got_first, got_second,
+    table, field, sweep, columns, column_a, source, kinds, early_first, early_second, late_first, late_second,
     chosen, depth, radiate, interp, cosine, sine, volume, cur, out,
-    beside, cells, rows, fresh, a_all, b_all, sem, *, cx, cy, groups, slices
+    beside, cells, rows, fresh, a_all, b_all, sent, sem, sent_sem, *, cx, cy, groups, slices
 ):
     nz = field.shape[1]
     channels = field.shape[0] // (cx * cy)
@@ -170,11 +171,12 @@
         cells[c * cy : (c + 1) * cy, x * nz : (x + 1) * nz] = value.astype(bf16)
 
     second_sweep(
-        table, field, sweep, columns, column_a, source, kinds, got_first, got_second,
+        table, field, sweep, columns, column_a, source, kinds, early_first, early_second, late_first, late_second,
         fresh, beside, a_all, b_all, store, cx, cy
     )
     leaving = pltpu.make_async_copy(fresh, volume, sem)
     leaving.start()
+    moves = [leaving]
     pair = 2
     for b in range(0, boxes, pair):
         lanes = slice(b * unknowns, (b + pair) * unknowns)
@@ -219,8 +221,12 @@
         for s in range(groups):
             piece = jnp.concatenate([whole[p, s] for p in range(parents)], axis=0)
             for k in range(tile // width):
-                out[s * slices + n // width + k] = piece[:, k * width : (k + 1) * width]
-    leaving.wait()
+                sent[s, n // width + k] = piece[:, k * width : (k + 1) * width]
+        some = pl.ds(n // width, tile // width)
+        moves.append(pltpu.make_async_copy(sent.at[:, some], out.at[:, some], sent_sem.at[n // tile]))
+        moves[-1].start()
+    for move in moves:
+        move.wait()
 
 
 def up(volume_args, chosen, depth, boxes, radiate, interp, cosine, sine, cx, cy, groups, slices):
@@ -232,15 +238,16 @@
     width = interp.shape[1] // slices
     piece_rows = boxes // CHILDREN * (channels // groups)
     vmem = pl.BlockSpec(memory_space=pltpu.VMEM)
+    hbm = pl.BlockSpec(memory_space=pltpu.HBM)
     return pl.pallas_call(
         lambda *refs: up_body(*refs, cx=cx, cy=cy, groups=groups, slices=slices),
         out_shape=(
             pltpu.HBM(field.shape, f32),
             pltpu.VMEM((boxes, channels // 2, 2 * unknowns), bf16),
-            pltpu.HBM((groups * slices, piece_rows, width), bf16),
+            pltpu.HBM((groups, slices, piece_rows, width), bf16),
         ),
-        in_specs=[vmem] * 15,
-        out_specs=(pl.BlockSpec(memory_space=pltpu.HBM), vmem, vmem),
+        in_specs=[vmem] * 17,
+        out_specs=(hbm, vmem, hbm),
         scratch_shapes=[
             pltpu.VMEM((2, total, nz), f32),
             pltpu.VMEM((channels * cy, cx * nz), bf16),
@@ -248,7 +255,9 @@
             pltpu.VMEM(field.shape, f32),
             pltpu.VMEM((cx * cy, nz), f32),
             pltpu.VMEM((cx * cy, nz), f32),
+            pltpu.VMEM((groups, slices, piece_rows, width), bf16),
             pltpu.SemaphoreType.DMA(()),
+            pltpu.SemaphoreType.DMA((interp.shape[1] // max(width, 256),)),
         ],
         compiler_params=params(16), name="up",
     )(*held(*volume_args, chosen, depth, radiate, interp, cosine, sine))
@@ -281,7 +290,7 @@
     )(lists, kinds, *held(translate))
 
 
-def far_body(order, sources, factors, out, plain, *, targets):
+def far_body(order, sources, factors, out, plain, sent, sem, *, targets):
     devices, piece_rows, width = sources.shape
     far = order.shape[0] // targets
     per = targets // devices
@@ -300,10 +309,19 @@
                 along = along + factor[0:1] * source
                 across = across + factor[1:2] * source
             results.append(along + half_turn(across))
-        out[d] = jnp.concatenate(results, axis=0).astype(bf16)
+        sent[d] = jnp.concatenate(results, axis=0).astype(bf16)
         return 0
 
-    lax.fori_loop(0, devices, one, 0, unroll=4)
+    parts = sem.shape[0]
+    moves = []
+    for part in range(parts):
+        first = part * (devices // parts)
+        lax.fori_loop(first, first + devices // parts, one, 0, unroll=4)
+        some = pl.ds(first, devices // parts)
+        moves.append(pltpu.make_async_copy(sent.at[some], out.at[some], sem.at[part]))
+        moves[-1].start()
+    for move in moves:
+        move.wait()
 
 
 def far_combine(order, sources, factors, targets):
@@ -315,8 +333,12 @@
         lambda *refs: far_body(*refs, targets=targets),
         out_shape=pltpu.HBM(sources.shape, bf16),
         in_specs=[smem, vmem, vmem],
-        out_specs=vmem,
-        scratch_shapes=[pltpu.VMEM((targets, tile, width), f32)],
+        out_specs=pl.BlockSpec(memory_space=pltpu.HBM),
+        scratch_shapes=[
+            pltpu.VMEM((targets, tile, width), f32),
+            pltpu.VMEM(sources.shape, bf16),
+            pltpu.SemaphoreType.DMA((4,)),
+        ],
         compiler_params=params(8),
         name="far",
     )(order, *held(sources, factors))
@@ -361,7 +383,7 @@
     )(lists, *held(own, first, second, blocks.reshape(slots * k, k), angle))
 
 
-def down_body(pieces, near, radiate, interp, cosine, sine, out, shifted, *, groups, slices):
+def down_body(pieces, near, radiate, interp, cosine, sine, out, shifted, sent, sem, *, groups, slices):
     _, _, width = pieces.shape
     boxes, excite, both = out.shape
     unknowns = both // 2
@@ -380,23 +402,43 @@
                     value = cosine[child : child + 1, lanes] * incoming - sine[child : child + 1, lanes] * turned
                     shifted[row : row + 2 * tile, lanes] = value.astype(bf16)
     leaf_in = dot_t(shifted[...], interp[...]).astype(bf16)
-    back = dot_t(leaf_in, radiate[...]).reshape(boxes, groups, tile, both)
-    own = back[..., :unknowns] - half_turn(back[..., unknowns:])
-    for b in range(boxes):
-        parts = [
-            jnp.concatenate([own[b, s, t * group : (t + 1) * group] for s in range(groups)], axis=0)
-            for t in range(2)
-        ]
-        out[b] = jnp.concatenate(parts, axis=1) + near[b]
+    parts = sem.shape[0]
+    count = boxes // parts
+    box_rows = groups * tile
+    moves = []
+    for part in range(parts):
+        first = part * count
+        some = leaf_in[first * box_rows : (first + count) * box_rows]
+        back = dot_t(some, radiate[...]).reshape(count, groups, tile, both)
+        own = back[..., :unknowns] - half_turn(back[..., unknowns:])
+        for b in range(count):
+            halves = [
+                jnp.concatenate([own[b, s, t * group : (t + 1) * group] for s in range(groups)], axis=0)
+                for t in range(2)
+            ]
+            sent[first + b] = jnp.concatenate(halves, axis=1) + near[first + b]
+        some = pl.ds(first, count)
+        moves.append(pltpu.make_async_copy(sent.at[some], out.at[some], sem.at[part]))
+        moves[-1].start()
+    for move in moves:
+        move.wait()
 
 
 def down(pieces, near, radiate, interp, cosine, sine, groups, slices):
     boxes, excite, _ = near.shape
+    vmem = pl.BlockSpec(memory_space=pltpu.VMEM)
     return pl.pallas_call(
         lambda *refs: down_body(*refs, groups=groups, slices=slices),
-        out_shape=jax.ShapeDtypeStruct(near.shape, f32),
-        scratch_shapes=[pltpu.VMEM((boxes * excite * 2, interp.shape[1]), bf16)],
-        compiler_params=params(16), name="down",
+        out_shape=pltpu.HBM(near.shape, f32),
+        in_specs=[vmem] * 6,
+        out_specs=pl.BlockSpec(memory_space=pltpu.HBM),
+        scratch_shapes=[
+            pltpu.VMEM((boxes * excite * 2, interp.shape[1]), bf16),
+            pltpu.VMEM(near.shape, f32),
+            pltpu.SemaphoreType.DMA((4,)),
+        ],
+        compiler_params=params(16),
+        name="down",
     )(*held(pieces, near, radiate, interp, cosine, sine))
 
 
@@ -560,6 +602,24 @@
     )(*left(mat_real, mat_loss, field, source, kinds))
 
 
+def faces(field, kinds, cx, cy):
+    channels = field.shape[0] // (cx * cy)
+
+    def body(field, kinds, first, second):
+        even = is_even("space")
+        for message, x in ((first, jnp.where(even, cx - 1, 0)), (second, jnp.where(even, 0, cx - 1))):
+            for c in range(channels):
+                rows = pl.ds(pl.multiple_of((c * cx + x) * cy, cy), cy)
+                message[c * cy : (c + 1) * cy, :] = field[rows, :].astype(bf16)
+            kind = kinds[pl.ds(pl.multiple_of(x * cy, cy), cy), :].astype(f32) + 1.0
+            message[channels * cy :, :] = kind.astype(bf16)
+
+    message = pltpu.VMEM((channels * cy + cy, field.shape[1]), bf16)
+    return pl.pallas_call(body, out_shape=(message, message), compiler_params=params(6), name="faces")(
+        *held(field, kinds)
+    )
+
+
 def first_body(
     table, field, source, kinds, got_first, got_second,
     sweep, columns, column_a, to_first, to_second, near, a_all, b_all, *, cx, cy
@@ -595,23 +655,20 @@
     for message, x in ((to_first, jnp.where(even_x, cx - 1, 0)), (to_second, jnp.where(even_x, 0, cx - 1))):
         for c in range(channels):
             rows = pl.ds(pl.multiple_of((c * cx + x) * cy, cy), cy)
-            message[c * cy : (c + 1) * cy, :] = field[rows, :].astype(bf16)
-            message[plane + c * cy : plane + (c + 1) * cy, :] = sweep[rows, :].astype(bf16)
+            message[c * cy : (c + 1) * cy, :] = sweep[rows, :].astype(bf16)
         for side in range(2):
             corner = jnp.concatenate(
                 [near.at[side][pl.ds(c * cx + x, 8, stride=cx), :] for c in range(0, channels, 8)], axis=0
             )
-            at = 2 * plane + side * channels
+            at = plane + side * channels
             message[at : at + channels, :] = corner.astype(bf16)
-        kind = kinds[pl.ds(pl.multiple_of(x * cy, cy), cy), :].astype(f32) + 1.0
-        message[2 * plane + 2 * channels :, :] = kind.astype(bf16)
 
 
 def first_sweep(table, field, source, kinds, got_first, got_second, cx, cy):
     total, nz = field.shape[0] // cy, field.shape[1]
     channels = total // cx
     vmem = pl.BlockSpec(memory_space=pltpu.VMEM)
-    message = pltpu.VMEM((2 * channels * cy + 2 * channels + cy, nz), bf16)
+    message = pltpu.VMEM((channels * cy + 2 * channels, nz), bf16)
     return pl.pallas_call(
         lambda *refs: first_body(*refs, cx=cx, cy=cy),
         out_shape=(
@@ -656,13 +713,15 @@
     kinds = material.reshape(-1, cells_z)
     bricks = (-1, cells_y, cells_z)
     *to_y, table = edges(mat_real, mat_loss, volume_field.reshape(bricks), source.reshape(bricks), material)
+    field, flat_source, interp, kinds, *to_y = lax.optimization_barrier((field, flat_source, interp, kinds, *to_y))
     got_y = swap(*to_y, "shard")
+    got_early = swap(*faces(field, kinds, cells_x, cells_y), "space")
     sweep, columns, column_a, *to_x = first_sweep(
         table, field, flat_source, kinds, *got_y, cells_x, cells_y
     )
-    got_x = swap(*to_x, "space")
+    got_late = swap(*to_x, "space")
     current, currents, pieces = up(
-        (table, field, sweep, columns, column_a, flat_source, kinds, *got_x),
+        (table, field, sweep, columns, column_a, flat_source, kinds, *got_early, *got_late),
         chosen,
         depth,
         near_boxes.shape[0],
@@ -675,7 +734,7 @@
         groups,
         slices,
     )
-    directed = lax.all_to_all(pieces, every, split_axis=0, concat_axis=0, tiled=True)
+    directed = lax.all_to_all(pieces.reshape((groups * slices,) + pieces.shape[2:]), every, split_axis=0, concat_axis=0, tiled=True)
     first, second = swap(currents, currents, "shard")
     factors, order = tables(far_parents.T, far_kind.T, translate)
     combined = far_combine(order, directed, factors, far_parents.shape[0])

time: 62.3 us -> 63.2 us (1.014)
  starting transfers between devices: 21.3 us -> 23.4 us
  local copies, waits for them, and re-layouts: 5.23 us -> 3.74 us
    ppermute x6 -> x8, starting transfers between devices: 11.9 us -> 14.6 us  [swap(): received.append(lax.ppermute(value, axis, swap_pairs(n, k)))]
    unnamed x30 -> x28, local copies, waits for them, and re-layouts: 5.23 us -> 3.74 us
    ppermute x6 -> x8, waiting for transfers between devices: 13.6 us -> 14 us  [swap(): received.append(lax.ppermute(value, axis, swap_pairs(n, k)))]
  transfers between devices with their start and end apart: 8 -> 10, of which waited for: 5 -> 5; matrix products, arithmetic and copies ran while one was open for 0% -> 0% of each run, Pallas kernels for 7% -> 7%
where the time goes in v8:
time: 63.2 us; the launch traced here: 62.7 us
  starting transfers between devices  23.4 us (37%)
  waiting for transfers between devices  18.7 us (30%)
  Pallas kernels  15.9 us (25%)
  local copies, waits for them, and re-layouts  3.74 us (6%)
  between operations  0.92 us (1%)
    ppermute x8, starting transfers between devices, swap(): received.append(lax.ppermute(value, axis, swap_pairs(n, k)))  14.6 us
    ppermute x8, waiting for transfers between devices, swap(): received.append(lax.ppermute(value, axis, swap_pairs(n, k)))  14 us
    all_to_all x1, waiting for transfers between devices, steps(): lax.all_to_all(pieces.reshape((groups * slices,) + pieces.shape[2:]), eve...  4.77 us
    all_to_all x1, starting transfers between devices, steps(): lax.all_to_all(combined, every, split_axis=0, concat_axis=0, tiled=True)  4.66 us
    pallas_call x1, Pallas kernels, up(): pl.pallas_call(lambda *refs: up_body(*refs, cx=cx, cy=cy, groups=groups,...  4.23 us
    all_to_all x1, starting transfers between devices, steps(): lax.all_to_all(pieces.reshape((groups * slices,) + pieces.shape[2:]), eve...  4.14 us
    unnamed x28, local copies, waits for them, and re-layouts  3.74 us
    pallas_call x1, Pallas kernels, tables(): pl.pallas_call(body, out_shape=(pltpu.VMEM((targets * far,) + translate.s...  2.54 us
  transfers between devices with their start and end apart: 10, of which 5 were waited for; matrix products, arithmetic and copies ran while one was open for 0% of the time, Pallas kernels for 7%

profile of v8, /device:TPU:17, one launch (start us, length us, event | category | flops | bytes accessed | tf_op | source)
XLA Modules:
  0.0 62.7 jit_solution(7379732438882555383)
XLA Ops:
  0.6 0.0 copy-start
  0.6 0.0 copy-start.1
  0.7 0.0 copy-start.5
  0.7 1.5 %edges.1 = (bf16[272,128]{1,0:T(8,128)(2,1)S(1)}, bf16[272,128]{1,0:T(8,128)(2,1)S(1)}, f32[16,128]{1,0:T(8,128)S(1)}) custom-call(f32[8]{0:T(128)} %real_table.1, f32[8]{0:T(128)} %loss_table.1, f32[128,16,128]{2,1,0:T(8,128)} %bitcast.12, f32[128,16,128]{2,1,0:T(8,128)} %bitcast.16, s32[4,16,128]{2,1,0:T(8,128)} %kinds.1), custom_call_target="tpu_custom_call" | custom-call | tf_op jit(solution)/shard_map/edges/pallas_call | solution.py:587
  2.1 0.0 copy-start.7
  2.2 0.0 copy-start.10
  2.2 0.0 copy-start.2
  2.2 0.0 copy-start.3
  2.2 1.3 %collective-permute-start = (bf16[272,128]{1,0:T(8,128)(2,1)S(1)}, bf16[272,128]{1,0:T(8,128)(2,1)S(1)}, u32[]{:S(2)}, u32[]{:S(2)}) collective-permute-start(bf16[272,128]{1,0:T(8,128)(2,1)S(1)} %get-tuple-element.36), channel_id=1, source_target_pairs={{0,1},{1,0},{2,3},{3,2},{4,5},{5,4},{6,7},{7,6},{8,9},{9,8},{10,11... | collective-permute-start | bytes 208904 | tf_op jit(solution)/shard_map/ppermute | solution.py:89
  3.5 2.2 %collective-permute-start.1 = (bf16[272,128]{1,0:T(8,128)(2,1)S(1)}, bf16[272,128]{1,0:T(8,128)(2,1)S(1)}, u32[]{:S(2)}, u32[]{:S(2)}) collective-permute-start(bf16[272,128]{1,0:T(8,128)(2,1)S(1)} %get-tuple-element.37), channel_id=1, source_target_pairs={{1,2},{2,1},{3,4},{4,3},{5,6},{6,5},{9,10},{10,9},{11,12},{12,11},... | collective-permute-start | bytes 208904 | tf_op jit(solution)/shard_map/ppermute | solution.py:89
  5.7 0.0 collective-permute-done.refs_4_
  5.7 3.8 %collective-permute-done.1.refs_5_ = bf16[272,128]{1,0:T(8,128)(2,1)S(1)} collective-permute-done((bf16[272,128]{1,0:T(8,128)(2,1)S(1)}, bf16[272,128]{1,0:T(8,128)(2,1)S(1)}, u32[]{:S(2)}, u32[]{:S(2)}) %collective-permute-start.1) | collective-permute-done | bytes 69664 | tf_op jit(solution)/shard_map/ppermute | solution.py:89
  9.4 0.0 copy-done
  9.4 0.0 copy-done.1
  9.4 0.0 copy-done.5
  9.4 0.9 %first_sweep.1 = (f32[2048,128]{1,0:T(8,128)S(1)}, f32[2,128,128]{2,1,0:T(8,128)S(1)}, f32[2,8,128]{2,1,0:T(8,128)S(1)}, bf16[576,128]{1,0:T(8,128)(2,1)S(1)}, bf16[576,128]{1,0:T(8,128)(2,1)S(1)}) custom-call(f32[16,128]{1,0:T(8,128)S(1)} %get-tuple-element.30.refs_0_, f32[2048,128]{1,0:T(8,128)S(1)} %bitcast.13, f32[2048,128]{1,0:T(8,128)S(1)} %bitcast.17, ...), custom_call_target="tpu_custom_call" | custom-call | tf_op jit(solution)/shard_map/first_sweep/pallas_call | solution.py:672
  10.3 2.2 %collective-permute-start.4 = (bf16[576,128]{1,0:T(8,128)(2,1)S(1)}, bf16[576,128]{1,0:T(8,128)(2,1)S(1)}, u32[]{:S(2)}, u32[]{:S(2)}) collective-permute-start(bf16[576,128]{1,0:T(8,128)(2,1)S(1)} %get-tuple-element.43), channel_id=1, source_target_pairs={{0,8},{8,0},{16,24},{24,16},{1,9},{9,1},{17,25},{25,17},{2,10},{10... | collective-permute-start | bytes 442376 | tf_op jit(solution)/shard_map/ppermute | solution.py:89
  12.5 3.0 %collective-permute-start.5 = (bf16[576,128]{1,0:T(8,128)(2,1)S(1)}, bf16[576,128]{1,0:T(8,128)(2,1)S(1)}, u32[]{:S(2)}, u32[]{:S(2)}) collective-permute-start(bf16[576,128]{1,0:T(8,128)(2,1)S(1)} %get-tuple-element.44), channel_id=1, source_target_pairs={{8,16},{16,8},{9,17},{17,9},{10,18},{18,10},{11,19},{19,11},{12,20... | collective-permute-start | bytes 442376 | tf_op jit(solution)/shard_map/ppermute | solution.py:89
  15.5 0.1 faces.1
  15.6 0.1 collective-permute-start.2
  15.7 2.5 %collective-permute-start.3 = (bf16[528,128]{1,0:T(8,128)(2,1)S(1)}, bf16[528,128]{1,0:T(8,128)(2,1)S(1)}, u32[]{:S(2)}, u32[]{:S(2)}) collective-permute-start(bf16[528,128]{1,0:T(8,128)(2,1)S(1)} %get-tuple-element.42), channel_id=1, source_target_pairs={{8,16},{16,8},{9,17},{17,9},{10,18},{18,10},{11,19},{19,11},{12,20... | collective-permute-start | bytes 405512 | tf_op jit(solution)/shard_map/ppermute | solution.py:89
  18.2 1.0 %prepare.1 = (f32[8,2048]{1,0:T(8,128)S(1)}, f32[8,2048]{1,0:T(8,128)S(1)}, bf16[512,2048]{1,0:T(8,128)(2,1)S(1)}, s32[8,2048]{1,0:T(8,128)S(1)}) custom-call(f32[8,2048]{1,0:T(8,128)S(1)} %copy-done.7, s32[16,128]{1,0:T(8,128)S(1)} %copy-done.10), custom_call_target="tpu_custom_call" | custom-call | tf_op jit(solution)/shard_map/prepare/pallas_call | solution.py:65
  19.2 0.0 collective-permute-done.2.refs_7_
  19.2 2.8 %collective-permute-done.3.refs_8_ = bf16[528,128]{1,0:T(8,128)(2,1)S(1)} collective-permute-done((bf16[528,128]{1,0:T(8,128)(2,1)S(1)}, bf16[528,128]{1,0:T(8,128)(2,1)S(1)}, u32[]{:S(2)}, u32[]{:S(2)}) %collective-permute-start.3) | collective-permute-done | bytes 135200 | tf_op jit(solution)/shard_map/ppermute | solution.py:89
  22.0 0.0 collective-permute-done.4.refs_9_
  22.0 0.0 collective-permute-done.5.refs_10_
  22.0 0.0 copy-start.11
  22.0 0.0 copy-start.12
  22.0 4.2 %up.1 = (f32[2048,128]{1,0:T(8,128)}, bf16[16,16,256]{2,1,0:T(8,128)(2,1)S(1)}, bf16[4,8,16,256]{3,2,1,0:T(8,128)(2,1)}) custom-call(f32[16,128]{1,0:T(8,128)S(1)} %get-tuple-element.30.refs_0_, f32[2048,128]{1,0:T(8,128)S(1)} %bitcast.15, f32[2048,128]{1,0:T(8,128)S(1)} %get-tuple-element.38.refs_2_, f32[2,128,128]{2,1,0:T(8,128)S(1)} %get-tuple-element.39.refs_3_, ...), custom_call_target="tpu_custom_call" | custom-call | tf_op jit(solution)/shard_map/up/pallas_call | solution.py:242
  26.3 0.7 %copy-done.8 = bf16[16,16,256]{2,1,0:T(8,128)(2,1)} copy-done((bf16[16,16,256]{2,1,0:T(8,128)(2,1)}, bf16[16,16,256]{2,1,0:T(8,128)(2,1)S(1)}, u32[]{:S(2)}) %copy-start.8) | copy-done | bytes 131096
  26.9 4.1 %all-to-all-start = ((bf16[32,16,256]{2,1,0:T(8,128)(2,1)}), bf16[32,16,256]{2,1,0:T(8,128)(2,1)}, u32[]{:S(2)}, u32[]{:S(2)}) async-start(bf16[32,16,256]{2,1,0:T(8,128)(2,1)} %bitcast.28), calls=%async_computation | async-start | bytes 524288 | tf_op jit(solution)/shard_map/all_to_all | solution.py:737
  31.1 0.0 copy-done.11
  31.1 0.0 copy-done.12
  31.1 0.0 copy-start.4
  31.1 1.1 %copy-done.4 = f32[316,2,256]{2,1,0:T(2,128)S(1)} copy-done((f32[316,2,256]{2,1,0:T(2,128)S(1)}, f32[316,2,256]{2,1,0:T(2,128)}, u32[]{:S(2)}) %copy-start.4) | copy-done | bytes 647192
  32.2 2.5 %tables.1 = (f32[512,2,256]{2,1,0:T(2,128)S(1)}, s32[512]{0:T(512)S(1)}) custom-call(s32[8,64]{1,0:T(8,128)S(1)} %bitcast.25, s32[8,64]{1,0:T(8,128)S(1)} %bitcast.26, f32[316,2,256]{2,1,0:T(2,128)S(1)} %copy-done.4), custom_call_target="tpu_custom_call" | custom-call | tf_op jit(solution)/shard_map/tables/pallas_call | solution.py:280
  34.8 4.8 %all-to-all-done.refs_1_ = bf16[32,16,256]{2,1,0:T(8,128)(2,1)} async-done(((bf16[32,16,256]{2,1,0:T(8,128)(2,1)}), bf16[32,16,256]{2,1,0:T(8,128)(2,1)}, u32[]{:S(2)}, u32[]{:S(2)}) %all-to-all-start) | async-done | bytes 262176 | tf_op jit(solution)/shard_map/all_to_all | solution.py:737
  39.5 2.5 %far.1 = bf16[32,16,256]{2,1,0:T(8,128)(2,1)} custom-call(s32[512]{0:T(512)S(1)} %get-tuple-element.51.refs_0_, bf16[32,16,256]{2,1,0:T(8,128)(2,1)} %all-to-all-done.refs_1_, f32[512,2,256]{2,1,0:T(2,128)S(1)} %get-tuple-element.53.refs_2_), custom_call_target="tpu_custom_call" | custom-call | tf_op jit(solution)/shard_map/far/pallas_call | solution.py:332
  42.0 4.7 %all-to-all-start.1 = ((bf16[32,16,256]{2,1,0:T(8,128)(2,1)}), bf16[32,16,256]{2,1,0:T(8,128)(2,1)S(1)}, u32[]{:S(2)}, u32[]{:S(2)}) async-start(bf16[32,16,256]{2,1,0:T(8,128)(2,1)} %far.1), calls=%async_computation.1 | async-start | bytes 524288 | tf_op jit(solution)/shard_map/all_to_all | solution.py:741
  46.7 1.3 %collective-permute-start.6 = (bf16[16,16,256]{2,1,0:T(8,128)(2,1)}, bf16[16,16,256]{2,1,0:T(8,128)(2,1)S(1)}, u32[]{:S(2)}, u32[]{:S(2)}) collective-permute-start(bf16[16,16,256]{2,1,0:T(8,128)(2,1)} %copy-done.8), channel_id=1, source_target_pairs={{0,1},{1,0},{2,3},{3,2},{4,5},{5,4},{6,7},{7,6},{8,9},{9,8},{10,11... | collective-permute-start | bytes 393224 | tf_op jit(solution)/shard_map/ppermute | solution.py:89
  48.0 2.1 %collective-permute-start.7 = (bf16[16,16,256]{2,1,0:T(8,128)(2,1)}, bf16[16,16,256]{2,1,0:T(8,128)(2,1)S(1)}, u32[]{:S(2)}, u32[]{:S(2)}) collective-permute-start(bf16[16,16,256]{2,1,0:T(8,128)(2,1)} %copy-done.8), channel_id=1, source_target_pairs={{1,2},{2,1},{3,4},{4,3},{5,6},{6,5},{9,10},{10,9},{11,12},{12,11},... | collective-permute-start | bytes 393224 | tf_op jit(solution)/shard_map/ppermute | solution.py:89
  50.1 4.5 %collective-permute-done.6.first = bf16[16,16,256]{2,1,0:T(8,128)(2,1)S(1)} collective-permute-done((bf16[16,16,256]{2,1,0:T(8,128)(2,1)}, bf16[16,16,256]{2,1,0:T(8,128)(2,1)S(1)}, u32[]{:S(2)}, u32[]{:S(2)}) %collective-permute-start.6) | collective-permute-done | bytes 131104 | tf_op jit(solution)/shard_map/ppermute | solution.py:89
  54.5 2.9 %collective-permute-done.7.second = bf16[16,16,256]{2,1,0:T(8,128)(2,1)S(1)} collective-permute-done((bf16[16,16,256]{2,1,0:T(8,128)(2,1)}, bf16[16,16,256]{2,1,0:T(8,128)(2,1)S(1)}, u32[]{:S(2)}, u32[]{:S(2)}) %collective-permute-start.7) | collective-permute-done | bytes 131104 | tf_op jit(solution)/shard_map/ppermute | solution.py:89
  57.5 1.0 %copy-done.6 = bf16[4,256,256]{2,1,0:T(8,128)(2,1)S(1)} copy-done((bf16[4,256,256]{2,1,0:T(8,128)(2,1)S(1)}, bf16[4,256,256]{2,1,0:T(8,128)(2,1)}, u32[]{:S(2)}) %copy-start.6) | copy-done | bytes 524312
  58.5 0.9 %copy-done.9 = bf16[16,16,256]{2,1,0:T(8,128)(2,1)S(1)} copy-done((bf16[16,16,256]{2,1,0:T(8,128)(2,1)S(1)}, bf16[16,16,256]{2,1,0:T(8,128)(2,1)}, u32[]{:S(2)}) %copy-start.9) | copy-done | bytes 131096
  59.4 1.0 %near.1 = (f32[16,16,256]{2,1,0:T(8,128)S(1)}, f32[8,2048]{1,0:T(8,128)S(1)}, f32[8,2048]{1,0:T(8,128)S(1)}) custom-call(s32[4,16]{1,0:T(4,128)S(1)} %bitcast.27, bf16[16,16,256]{2,1,0:T(8,128)(2,1)S(1)} %copy-done.9, bf16[16,16,256]{2,1,0:T(8,128)(2,1)S(1)} %collective-permute-done.6.first, bf16[16,16,256]{2,1,0:T(8,128)(2,1)S(1)} %collective-permute-done.7.second, ...), custom_call_target="tpu_custom_call" | custom-call | tf_op jit(solution)/shard_map/near/pallas_call | solution.py:373
  60.5 0.0 all-to-all-done.1.refs_0_
  60.5 2.2 %down.1 = f32[16,16,256]{2,1,0:T(8,128)} custom-call(bf16[32,16,256]{2,1,0:T(8,128)(2,1)S(1)} %all-to-all-done.1.refs_0_, f32[16,16,256]{2,1,0:T(8,128)S(1)} %get-tuple-element.55.refs_1_, bf16[256,512]{1,0:T(8,128)(2,1)S(1)} %bitcast.20, bf16[512,2048]{1,0:T(8,128)(2,1)S(1)} %copy-done.2, f32[8,2048]{1,0:T(8,128)S(1)} %get-tuple-element.56.refs_4_, ...), custom_call_target="tpu_custom_call" | custom-call | tf_op jit(solution)/shard_map/down/pallas_call | solution.py:430
  (9 shorter events, 0.0 us)
Async XLA Ops:
  0.6 8.8 %copy-start = (f32[2,16,4,16,128]{4,3,2,1,0:T(8,128)S(1)}, f32[2,16,4,16,128]{4,3,2,1,0:T(8,128)}, u32[]{:S(2)}) copy-start(f32[2,16,4,16,128]{4,3,2,1,0:T(8,128)} %param.14) | copy-start | bytes 3145732
  0.6 8.8 %copy-start.1 = (f32[2,16,4,16,128]{4,3,2,1,0:T(8,128)S(1)}, f32[2,16,4,16,128]{4,3,2,1,0:T(8,128)}, u32[]{:S(2)}) copy-start(f32[2,16,4,16,128]{4,3,2,1,0:T(8,128)} %param.15) | copy-start | bytes 3145732
  0.7 8.8 %copy-start.5 = (s32[4,16,128]{2,1,0:T(8,128)S(1)}, s32[4,16,128]{2,1,0:T(8,128)}, u32[]{:S(2)}) copy-start(s32[4,16,128]{2,1,0:T(8,128)} %kinds.1) | copy-start | bytes 98308
  2.1 16.0 %copy-start.7 = (f32[8,2048]{1,0:T(8,128)S(1)}, f32[8,2048]{1,0:T(8,128)}, u32[]{:S(2)}) copy-start(f32[8,2048]{1,0:T(8,128)} %angle.3) | copy-start | bytes 196612
  2.2 16.0 %copy-start.10 = (s32[16,128]{1,0:T(8,128)S(1)}, s32[16,128]{1,0:T(8,128)}, u32[]{:S(2)}) copy-start(s32[16,128]{1,0:T(8,128)} %smap.1) | copy-start | bytes 24580
  2.2 19.8 %copy-start.2 = (bf16[512,2048]{1,0:T(8,128)(2,1)S(1)}, bf16[512,2048]{1,0:T(8,128)(2,1)}, u32[]{:S(2)}) copy-start(bf16[512,2048]{1,0:T(8,128)(2,1)} %refs_3_) | copy-start | bytes 6291460
  2.2 19.8 %copy-start.3 = (bf16[2,128,512]{2,1,0:T(8,128)(2,1)S(1)}, bf16[2,128,512]{2,1,0:T(8,128)(2,1)}, u32[]{:S(2)}) copy-start(bf16[2,128,512]{2,1,0:T(8,128)(2,1)} %param.22) | copy-start | bytes 786436
  2.2 3.5 %collective-permute-start = (bf16[272,128]{1,0:T(8,128)(2,1)S(1)}, bf16[272,128]{1,0:T(8,128)(2,1)S(1)}, u32[]{:S(2)}, u32[]{:S(2)}) collective-permute-start(bf16[272,128]{1,0:T(8,128)(2,1)S(1)} %get-tuple-element.36), channel_id=1, source_target_pairs={{0,1},{1,0},{2,3},{3,2},{4,5},{5,4},{6,7},{7,6},{8,9},{9,8},{10,11... | collective-permute-start | bytes 208904 | tf_op jit(solution)/shard_map/ppermute | solution.py:89
  3.5 5.9 %collective-permute-start.1 = (bf16[272,128]{1,0:T(8,128)(2,1)S(1)}, bf16[272,128]{1,0:T(8,128)(2,1)S(1)}, u32[]{:S(2)}, u32[]{:S(2)}) collective-permute-start(bf16[272,128]{1,0:T(8,128)(2,1)S(1)} %get-tuple-element.37), channel_id=1, source_target_pairs={{1,2},{2,1},{3,4},{4,3},{5,6},{6,5},{9,10},{10,9},{11,12},{12,11},... | collective-permute-start | bytes 208904 | tf_op jit(solution)/shard_map/ppermute | solution.py:89
  10.3 11.7 %collective-permute-start.4 = (bf16[576,128]{1,0:T(8,128)(2,1)S(1)}, bf16[576,128]{1,0:T(8,128)(2,1)S(1)}, u32[]{:S(2)}, u32[]{:S(2)}) collective-permute-start(bf16[576,128]{1,0:T(8,128)(2,1)S(1)} %get-tuple-element.43), channel_id=1, source_target_pairs={{0,8},{8,0},{16,24},{24,16},{1,9},{9,1},{17,25},{25,17},{2,10},{10... | collective-permute-start | bytes 442376 | tf_op jit(solution)/shard_map/ppermute | solution.py:89
  12.5 9.5 %collective-permute-start.5 = (bf16[576,128]{1,0:T(8,128)(2,1)S(1)}, bf16[576,128]{1,0:T(8,128)(2,1)S(1)}, u32[]{:S(2)}, u32[]{:S(2)}) collective-permute-start(bf16[576,128]{1,0:T(8,128)(2,1)S(1)} %get-tuple-element.44), channel_id=1, source_target_pairs={{8,16},{16,8},{9,17},{17,9},{10,18},{18,10},{11,19},{19,11},{12,20... | collective-permute-start | bytes 442376 | tf_op jit(solution)/shard_map/ppermute | solution.py:89
  15.6 3.6 %collective-permute-start.2 = (bf16[528,128]{1,0:T(8,128)(2,1)S(1)}, bf16[528,128]{1,0:T(8,128)(2,1)S(1)}, u32[]{:S(2)}, u32[]{:S(2)}) collective-permute-start(bf16[528,128]{1,0:T(8,128)(2,1)S(1)} %get-tuple-element.41), channel_id=1, source_target_pairs={{0,8},{8,0},{16,24},{24,16},{1,9},{9,1},{17,25},{25,17},{2,10},{10... | collective-permute-start | bytes 405512 | tf_op jit(solution)/shard_map/ppermute | solution.py:89
  15.7 6.3 %collective-permute-start.3 = (bf16[528,128]{1,0:T(8,128)(2,1)S(1)}, bf16[528,128]{1,0:T(8,128)(2,1)S(1)}, u32[]{:S(2)}, u32[]{:S(2)}) collective-permute-start(bf16[528,128]{1,0:T(8,128)(2,1)S(1)} %get-tuple-element.42), channel_id=1, source_target_pairs={{8,16},{16,8},{9,17},{17,9},{10,18},{18,10},{11,19},{19,11},{12,20... | collective-permute-start | bytes 405512 | tf_op jit(solution)/shard_map/ppermute | solution.py:89
  22.0 9.1 %copy-start.11 = (s32[64,8]{0,1:T(8,128)S(1)}, s32[64,8]{0,1:T(8,128)}, u32[]{:S(2)}) copy-start(s32[64,8]{0,1:T(8,128)} %param.25) | copy-start | bytes 6148
  22.0 9.1 %copy-start.12 = (s32[64,8]{0,1:T(8,128)S(1)}, s32[64,8]{0,1:T(8,128)}, u32[]{:S(2)}) copy-start(s32[64,8]{0,1:T(8,128)} %param.26) | copy-start | bytes 6148
  26.3 0.7 %copy-start.8 = (bf16[16,16,256]{2,1,0:T(8,128)(2,1)}, bf16[16,16,256]{2,1,0:T(8,128)(2,1)S(1)}, u32[]{:S(2)}) copy-start(bf16[16,16,256]{2,1,0:T(8,128)(2,1)S(1)} %get-tuple-element.54.own) | copy-start | bytes 393220
  26.9 30.5 %copy-start.13 = (s32[16,4]{0,1:T(4,128)S(1)}, s32[16,4]{0,1:T(4,128)}, u32[]{:S(2)}) copy-start(s32[16,4]{0,1:T(4,128)} %param.20) | copy-start | bytes 772
  26.9 12.6 %all-to-all-start = ((bf16[32,16,256]{2,1,0:T(8,128)(2,1)}), bf16[32,16,256]{2,1,0:T(8,128)(2,1)}, u32[]{:S(2)}, u32[]{:S(2)}) async-start(bf16[32,16,256]{2,1,0:T(8,128)(2,1)} %bitcast.28), calls=%async_computation | async-start | bytes 524288 | tf_op jit(solution)/shard_map/all_to_all | solution.py:737
  31.1 1.1 %copy-start.4 = (f32[316,2,256]{2,1,0:T(2,128)S(1)}, f32[316,2,256]{2,1,0:T(2,128)}, u32[]{:S(2)}) copy-start(f32[316,2,256]{2,1,0:T(2,128)} %translate.1) | copy-start | bytes 1941508
  42.0 18.5 %all-to-all-start.1 = ((bf16[32,16,256]{2,1,0:T(8,128)(2,1)}), bf16[32,16,256]{2,1,0:T(8,128)(2,1)S(1)}, u32[]{:S(2)}, u32[]{:S(2)}) async-start(bf16[32,16,256]{2,1,0:T(8,128)(2,1)} %far.1), calls=%async_computation.1 | async-start | bytes 524288 | tf_op jit(solution)/shard_map/all_to_all | solution.py:741
  46.7 7.9 %collective-permute-start.6 = (bf16[16,16,256]{2,1,0:T(8,128)(2,1)}, bf16[16,16,256]{2,1,0:T(8,128)(2,1)S(1)}, u32[]{:S(2)}, u32[]{:S(2)}) collective-permute-start(bf16[16,16,256]{2,1,0:T(8,128)(2,1)} %copy-done.8), channel_id=1, source_target_pairs={{0,1},{1,0},{2,3},{3,2},{4,5},{5,4},{6,7},{7,6},{8,9},{9,8},{10,11... | collective-permute-start | bytes 393224 | tf_op jit(solution)/shard_map/ppermute | solution.py:89
  48.0 9.5 %collective-permute-start.7 = (bf16[16,16,256]{2,1,0:T(8,128)(2,1)}, bf16[16,16,256]{2,1,0:T(8,128)(2,1)S(1)}, u32[]{:S(2)}, u32[]{:S(2)}) collective-permute-start(bf16[16,16,256]{2,1,0:T(8,128)(2,1)} %copy-done.8), channel_id=1, source_target_pairs={{1,2},{2,1},{3,4},{4,3},{5,6},{6,5},{9,10},{10,9},{11,12},{12,11},... | collective-permute-start | bytes 393224 | tf_op jit(solution)/shard_map/ppermute | solution.py:89
  57.5 1.0 %copy-start.6 = (bf16[4,256,256]{2,1,0:T(8,128)(2,1)S(1)}, bf16[4,256,256]{2,1,0:T(8,128)(2,1)}, u32[]{:S(2)}) copy-start(bf16[4,256,256]{2,1,0:T(8,128)(2,1)} %param.21) | copy-start | bytes 1572868
  58.5 0.9 %copy-start.9 = (bf16[16,16,256]{2,1,0:T(8,128)(2,1)S(1)}, bf16[16,16,256]{2,1,0:T(8,128)(2,1)}, u32[]{:S(2)}) copy-start(bf16[16,16,256]{2,1,0:T(8,128)(2,1)} %copy-done.8) | copy-start | bytes 393220

commit v9 on v8

--- a/solution.py
+++ b/solution.py
@@ -221,10 +221,7 @@
         for s in range(groups):
             piece = jnp.concatenate([whole[p, s] for p in range(parents)], axis=0)
             for k in range(tile // width):
-                sent[s, n // width + k] = piece[:, k * width : (k + 1) * width]
-        some = pl.ds(n // width, tile // width)
-        moves.append(pltpu.make_async_copy(sent.at[:, some], out.at[:, some], sent_sem.at[n // tile]))
-        moves[-1].start()
+                out[s, n // width + k] = piece[:, k * width : (k + 1) * width]
     for move in moves:
         move.wait()
 
@@ -247,7 +244,7 @@
             pltpu.HBM((groups, slices, piece_rows, width), bf16),
         ),
         in_specs=[vmem] * 17,
-        out_specs=(hbm, vmem, hbm),
+        out_specs=(hbm, vmem, vmem),
         scratch_shapes=[
             pltpu.VMEM((2, total, nz), f32),
             pltpu.VMEM((channels * cy, cx * nz), bf16),

time: 63.2 us -> 63.3 us (level)
  no operation moved by 1% of the time
where the time goes in v9:
time: 63.3 us; the launch traced here: 62.8 us
  starting transfers between devices  23.4 us (37%)
  waiting for transfers between devices  18.7 us (30%)
  Pallas kernels  16 us (25%)
  local copies, waits for them, and re-layouts  3.74 us (6%)
  between operations  0.92 us (1%)
    ppermute x8, starting transfers between devices, swap(): received.append(lax.ppermute(value, axis, swap_pairs(n, k)))  14.6 us
    ppermute x8, waiting for transfers between devices, swap(): received.append(lax.ppermute(value, axis, swap_pairs(n, k)))  14 us
    all_to_all x1, waiting for transfers between devices, steps(): lax.all_to_all(pieces.reshape((groups * slices,) + pieces.shape[2:]), eve...  4.77 us
    all_to_all x1, starting transfers between devices, steps(): lax.all_to_all(combined, every, split_axis=0, concat_axis=0, tiled=True)  4.66 us
    pallas_call x1, Pallas kernels, up(): pl.pallas_call(lambda *refs: up_body(*refs, cx=cx, cy=cy, groups=groups,...  4.31 us
    all_to_all x1, starting transfers between devices, steps(): lax.all_to_all(pieces.reshape((groups * slices,) + pieces.shape[2:]), eve...  4.14 us
    unnamed x28, local copies, waits for them, and re-layouts  3.74 us
    pallas_call x1, Pallas kernels, tables(): pl.pallas_call(body, out_shape=(pltpu.VMEM((targets * far,) + translate.s...  2.54 us
  transfers between devices with their start and end apart: 10, of which 5 were waited for; matrix products, arithmetic and copies ran while one was open for 0% of the time, Pallas kernels for 7%

profile of v9, /device:TPU:17, one launch (start us, length us, event | category | flops | bytes accessed | tf_op | source)
XLA Modules:
  0.0 62.8 jit_solution(8649534613966146945)
XLA Ops:
  0.6 0.0 copy-start
  0.6 0.0 copy-start.1
  0.7 0.0 copy-start.5
  0.7 1.5 %edges.1 = (bf16[272,128]{1,0:T(8,128)(2,1)S(1)}, bf16[272,128]{1,0:T(8,128)(2,1)S(1)}, f32[16,128]{1,0:T(8,128)S(1)}) custom-call(f32[8]{0:T(128)} %real_table.1, f32[8]{0:T(128)} %loss_table.1, f32[128,16,128]{2,1,0:T(8,128)} %bitcast.12, f32[128,16,128]{2,1,0:T(8,128)} %bitcast.16, s32[4,16,128]{2,1,0:T(8,128)} %kinds.1), custom_call_target="tpu_custom_call" | custom-call | tf_op jit(solution)/shard_map/edges/pallas_call | solution.py:584
  2.1 0.0 copy-start.7
  2.2 0.0 copy-start.10
  2.2 0.0 copy-start.2
  2.2 0.0 copy-start.3
  2.2 1.3 %collective-permute-start = (bf16[272,128]{1,0:T(8,128)(2,1)S(1)}, bf16[272,128]{1,0:T(8,128)(2,1)S(1)}, u32[]{:S(2)}, u32[]{:S(2)}) collective-permute-start(bf16[272,128]{1,0:T(8,128)(2,1)S(1)} %get-tuple-element.36), channel_id=1, source_target_pairs={{0,1},{1,0},{2,3},{3,2},{4,5},{5,4},{6,7},{7,6},{8,9},{9,8},{10,11... | collective-permute-start | bytes 208904 | tf_op jit(solution)/shard_map/ppermute | solution.py:89
  3.5 2.2 %collective-permute-start.1 = (bf16[272,128]{1,0:T(8,128)(2,1)S(1)}, bf16[272,128]{1,0:T(8,128)(2,1)S(1)}, u32[]{:S(2)}, u32[]{:S(2)}) collective-permute-start(bf16[272,128]{1,0:T(8,128)(2,1)S(1)} %get-tuple-element.37), channel_id=1, source_target_pairs={{1,2},{2,1},{3,4},{4,3},{5,6},{6,5},{9,10},{10,9},{11,12},{12,11},... | collective-permute-start | bytes 208904 | tf_op jit(solution)/shard_map/ppermute | solution.py:89
  5.7 0.0 collective-permute-done.refs_4_
  5.7 3.8 %collective-permute-done.1.refs_5_ = bf16[272,128]{1,0:T(8,128)(2,1)S(1)} collective-permute-done((bf16[272,128]{1,0:T(8,128)(2,1)S(1)}, bf16[272,128]{1,0:T(8,128)(2,1)S(1)}, u32[]{:S(2)}, u32[]{:S(2)}) %collective-permute-start.1) | collective-permute-done | bytes 69664 | tf_op jit(solution)/shard_map/ppermute | solution.py:89
  9.4 0.0 copy-done
  9.4 0.0 copy-done.1
  9.4 0.0 copy-done.5
  9.4 0.9 %first_sweep.1 = (f32[2048,128]{1,0:T(8,128)S(1)}, f32[2,128,128]{2,1,0:T(8,128)S(1)}, f32[2,8,128]{2,1,0:T(8,128)S(1)}, bf16[576,128]{1,0:T(8,128)(2,1)S(1)}, bf16[576,128]{1,0:T(8,128)(2,1)S(1)}) custom-call(f32[16,128]{1,0:T(8,128)S(1)} %get-tuple-element.30.refs_0_, f32[2048,128]{1,0:T(8,128)S(1)} %bitcast.13, f32[2048,128]{1,0:T(8,128)S(1)} %bitcast.17, ...), custom_call_target="tpu_custom_call" | custom-call | tf_op jit(solution)/shard_map/first_sweep/pallas_call | solution.py:669
  10.3 2.2 %collective-permute-start.4 = (bf16[576,128]{1,0:T(8,128)(2,1)S(1)}, bf16[576,128]{1,0:T(8,128)(2,1)S(1)}, u32[]{:S(2)}, u32[]{:S(2)}) collective-permute-start(bf16[576,128]{1,0:T(8,128)(2,1)S(1)} %get-tuple-element.43), channel_id=1, source_target_pairs={{0,8},{8,0},{16,24},{24,16},{1,9},{9,1},{17,25},{25,17},{2,10},{10... | collective-permute-start | bytes 442376 | tf_op jit(solution)/shard_map/ppermute | solution.py:89
  12.5 3.0 %collective-permute-start.5 = (bf16[576,128]{1,0:T(8,128)(2,1)S(1)}, bf16[576,128]{1,0:T(8,128)(2,1)S(1)}, u32[]{:S(2)}, u32[]{:S(2)}) collective-permute-start(bf16[576,128]{1,0:T(8,128)(2,1)S(1)} %get-tuple-element.44), channel_id=1, source_target_pairs={{8,16},{16,8},{9,17},{17,9},{10,18},{18,10},{11,19},{19,11},{12,20... | collective-permute-start | bytes 442376 | tf_op jit(solution)/shard_map/ppermute | solution.py:89
  15.5 0.1 faces.1
  15.6 0.1 collective-permute-start.2
  15.7 2.5 %collective-permute-start.3 = (bf16[528,128]{1,0:T(8,128)(2,1)S(1)}, bf16[528,128]{1,0:T(8,128)(2,1)S(1)}, u32[]{:S(2)}, u32[]{:S(2)}) collective-permute-start(bf16[528,128]{1,0:T(8,128)(2,1)S(1)} %get-tuple-element.42), channel_id=1, source_target_pairs={{8,16},{16,8},{9,17},{17,9},{10,18},{18,10},{11,19},{19,11},{12,20... | collective-permute-start | bytes 405512 | tf_op jit(solution)/shard_map/ppermute | solution.py:89
  18.2 0.0 copy-done.7
  18.2 1.0 %prepare.1 = (f32[8,2048]{1,0:T(8,128)S(1)}, f32[8,2048]{1,0:T(8,128)S(1)}, bf16[512,2048]{1,0:T(8,128)(2,1)S(1)}, s32[8,2048]{1,0:T(8,128)S(1)}) custom-call(f32[8,2048]{1,0:T(8,128)S(1)} %copy-done.7, s32[16,128]{1,0:T(8,128)S(1)} %copy-done.10), custom_call_target="tpu_custom_call" | custom-call | tf_op jit(solution)/shard_map/prepare/pallas_call | solution.py:65
  19.2 0.0 collective-permute-done.2.refs_7_
  19.2 2.8 %collective-permute-done.3.refs_8_ = bf16[528,128]{1,0:T(8,128)(2,1)S(1)} collective-permute-done((bf16[528,128]{1,0:T(8,128)(2,1)S(1)}, bf16[528,128]{1,0:T(8,128)(2,1)S(1)}, u32[]{:S(2)}, u32[]{:S(2)}) %collective-permute-start.3) | collective-permute-done | bytes 135200 | tf_op jit(solution)/shard_map/ppermute | solution.py:89
  22.0 0.0 collective-permute-done.4.refs_9_
  22.0 0.0 collective-permute-done.5.refs_10_
  22.0 0.0 copy-start.11
  22.0 0.0 copy-start.12
  22.0 4.3 %up.1 = (f32[2048,128]{1,0:T(8,128)}, bf16[16,16,256]{2,1,0:T(8,128)(2,1)S(1)}, bf16[4,8,16,256]{3,2,1,0:T(8,128)(2,1)}) custom-call(f32[16,128]{1,0:T(8,128)S(1)} %get-tuple-element.30.refs_0_, f32[2048,128]{1,0:T(8,128)S(1)} %bitcast.15, f32[2048,128]{1,0:T(8,128)S(1)} %get-tuple-element.38.refs_2_, f32[2,128,128]{2,1,0:T(8,128)S(1)} %get-tuple-element.39.refs_3_, ...), custom_call_target="tpu_custom_call" | custom-call | tf_op jit(solution)/shard_map/up/pallas_call | solution.py:239
  26.4 0.7 %copy-done.8 = bf16[16,16,256]{2,1,0:T(8,128)(2,1)} copy-done((bf16[16,16,256]{2,1,0:T(8,128)(2,1)}, bf16[16,16,256]{2,1,0:T(8,128)(2,1)S(1)}, u32[]{:S(2)}) %copy-start.8) | copy-done | bytes 131096
  27.0 4.1 %all-to-all-start = ((bf16[32,16,256]{2,1,0:T(8,128)(2,1)}), bf16[32,16,256]{2,1,0:T(8,128)(2,1)}, u32[]{:S(2)}, u32[]{:S(2)}) async-start(bf16[32,16,256]{2,1,0:T(8,128)(2,1)} %bitcast.28), calls=%async_computation | async-start | bytes 524288 | tf_op jit(solution)/shard_map/all_to_all | solution.py:734
  31.2 0.0 copy-start.4
  31.2 1.1 %copy-done.4 = f32[316,2,256]{2,1,0:T(2,128)S(1)} copy-done((f32[316,2,256]{2,1,0:T(2,128)S(1)}, f32[316,2,256]{2,1,0:T(2,128)}, u32[]{:S(2)}) %copy-start.4) | copy-done | bytes 647192
  32.3 2.5 %tables.1 = (f32[512,2,256]{2,1,0:T(2,128)S(1)}, s32[512]{0:T(512)S(1)}) custom-call(s32[8,64]{1,0:T(8,128)S(1)} %bitcast.25, s32[8,64]{1,0:T(8,128)S(1)} %bitcast.26, f32[316,2,256]{2,1,0:T(2,128)S(1)} %copy-done.4), custom_call_target="tpu_custom_call" | custom-call | tf_op jit(solution)/shard_map/tables/pallas_call | solution.py:277
  34.8 4.8 %all-to-all-done.refs_1_ = bf16[32,16,256]{2,1,0:T(8,128)(2,1)} async-done(((bf16[32,16,256]{2,1,0:T(8,128)(2,1)}), bf16[32,16,256]{2,1,0:T(8,128)(2,1)}, u32[]{:S(2)}, u32[]{:S(2)}) %all-to-all-start) | async-done | bytes 262176 | tf_op jit(solution)/shard_map/all_to_all | solution.py:734
  39.6 2.5 %far.1 = bf16[32,16,256]{2,1,0:T(8,128)(2,1)} custom-call(s32[512]{0:T(512)S(1)} %get-tuple-element.51.refs_0_, bf16[32,16,256]{2,1,0:T(8,128)(2,1)} %all-to-all-done.refs_1_, f32[512,2,256]{2,1,0:T(2,128)S(1)} %get-tuple-element.53.refs_2_), custom_call_target="tpu_custom_call" | custom-call | tf_op jit(solution)/shard_map/far/pallas_call | solution.py:329
  42.1 4.7 %all-to-all-start.1 = ((bf16[32,16,256]{2,1,0:T(8,128)(2,1)}), bf16[32,16,256]{2,1,0:T(8,128)(2,1)S(1)}, u32[]{:S(2)}, u32[]{:S(2)}) async-start(bf16[32,16,256]{2,1,0:T(8,128)(2,1)} %far.1), calls=%async_computation.1 | async-start | bytes 524288 | tf_op jit(solution)/shard_map/all_to_all | solution.py:738
  46.8 1.3 %collective-permute-start.6 = (bf16[16,16,256]{2,1,0:T(8,128)(2,1)}, bf16[16,16,256]{2,1,0:T(8,128)(2,1)S(1)}, u32[]{:S(2)}, u32[]{:S(2)}) collective-permute-start(bf16[16,16,256]{2,1,0:T(8,128)(2,1)} %copy-done.8), channel_id=1, source_target_pairs={{0,1},{1,0},{2,3},{3,2},{4,5},{5,4},{6,7},{7,6},{8,9},{9,8},{10,11... | collective-permute-start | bytes 393224 | tf_op jit(solution)/shard_map/ppermute | solution.py:89
  48.0 2.1 %collective-permute-start.7 = (bf16[16,16,256]{2,1,0:T(8,128)(2,1)}, bf16[16,16,256]{2,1,0:T(8,128)(2,1)S(1)}, u32[]{:S(2)}, u32[]{:S(2)}) collective-permute-start(bf16[16,16,256]{2,1,0:T(8,128)(2,1)} %copy-done.8), channel_id=1, source_target_pairs={{1,2},{2,1},{3,4},{4,3},{5,6},{6,5},{9,10},{10,9},{11,12},{12,11},... | collective-permute-start | bytes 393224 | tf_op jit(solution)/shard_map/ppermute | solution.py:89
  50.2 4.5 %collective-permute-done.6.first = bf16[16,16,256]{2,1,0:T(8,128)(2,1)S(1)} collective-permute-done((bf16[16,16,256]{2,1,0:T(8,128)(2,1)}, bf16[16,16,256]{2,1,0:T(8,128)(2,1)S(1)}, u32[]{:S(2)}, u32[]{:S(2)}) %collective-permute-start.6) | collective-permute-done | bytes 131104 | tf_op jit(solution)/shard_map/ppermute | solution.py:89
  54.6 2.9 %collective-permute-done.7.second = bf16[16,16,256]{2,1,0:T(8,128)(2,1)S(1)} collective-permute-done((bf16[16,16,256]{2,1,0:T(8,128)(2,1)}, bf16[16,16,256]{2,1,0:T(8,128)(2,1)S(1)}, u32[]{:S(2)}, u32[]{:S(2)}) %collective-permute-start.7) | collective-permute-done | bytes 131104 | tf_op jit(solution)/shard_map/ppermute | solution.py:89
  57.6 0.0 copy-done.13
  57.6 1.0 %copy-done.6 = bf16[4,256,256]{2,1,0:T(8,128)(2,1)S(1)} copy-done((bf16[4,256,256]{2,1,0:T(8,128)(2,1)S(1)}, bf16[4,256,256]{2,1,0:T(8,128)(2,1)}, u32[]{:S(2)}) %copy-start.6) | copy-done | bytes 524312
  58.6 0.9 %copy-done.9 = bf16[16,16,256]{2,1,0:T(8,128)(2,1)S(1)} copy-done((bf16[16,16,256]{2,1,0:T(8,128)(2,1)S(1)}, bf16[16,16,256]{2,1,0:T(8,128)(2,1)}, u32[]{:S(2)}) %copy-start.9) | copy-done | bytes 131096
  59.5 1.0 %near.1 = (f32[16,16,256]{2,1,0:T(8,128)S(1)}, f32[8,2048]{1,0:T(8,128)S(1)}, f32[8,2048]{1,0:T(8,128)S(1)}) custom-call(s32[4,16]{1,0:T(4,128)S(1)} %bitcast.27, bf16[16,16,256]{2,1,0:T(8,128)(2,1)S(1)} %copy-done.9, bf16[16,16,256]{2,1,0:T(8,128)(2,1)S(1)} %collective-permute-done.6.first, bf16[16,16,256]{2,1,0:T(8,128)(2,1)S(1)} %collective-permute-done.7.second, ...), custom_call_target="tpu_custom_call" | custom-call | tf_op jit(solution)/shard_map/near/pallas_call | solution.py:370
  60.6 0.0 all-to-all-done.1.refs_0_
  60.6 2.2 %down.1 = f32[16,16,256]{2,1,0:T(8,128)} custom-call(bf16[32,16,256]{2,1,0:T(8,128)(2,1)S(1)} %all-to-all-done.1.refs_0_, f32[16,16,256]{2,1,0:T(8,128)S(1)} %get-tuple-element.55.refs_1_, bf16[256,512]{1,0:T(8,128)(2,1)S(1)} %bitcast.20, bf16[512,2048]{1,0:T(8,128)(2,1)S(1)} %copy-done.2, f32[8,2048]{1,0:T(8,128)S(1)} %get-tuple-element.56.refs_4_, ...), custom_call_target="tpu_custom_call" | custom-call | tf_op jit(solution)/shard_map/down/pallas_call | solution.py:427
  (9 shorter events, 0.0 us)
Async XLA Ops:
  0.6 8.8 %copy-start = (f32[2,16,4,16,128]{4,3,2,1,0:T(8,128)S(1)}, f32[2,16,4,16,128]{4,3,2,1,0:T(8,128)}, u32[]{:S(2)}) copy-start(f32[2,16,4,16,128]{4,3,2,1,0:T(8,128)} %param.14) | copy-start | bytes 3145732
  0.6 8.8 %copy-start.1 = (f32[2,16,4,16,128]{4,3,2,1,0:T(8,128)S(1)}, f32[2,16,4,16,128]{4,3,2,1,0:T(8,128)}, u32[]{:S(2)}) copy-start(f32[2,16,4,16,128]{4,3,2,1,0:T(8,128)} %param.15) | copy-start | bytes 3145732
  0.7 8.8 %copy-start.5 = (s32[4,16,128]{2,1,0:T(8,128)S(1)}, s32[4,16,128]{2,1,0:T(8,128)}, u32[]{:S(2)}) copy-start(s32[4,16,128]{2,1,0:T(8,128)} %kinds.1) | copy-start | bytes 98308
  2.1 16.0 %copy-start.7 = (f32[8,2048]{1,0:T(8,128)S(1)}, f32[8,2048]{1,0:T(8,128)}, u32[]{:S(2)}) copy-start(f32[8,2048]{1,0:T(8,128)} %angle.3) | copy-start | bytes 196612
  2.2 16.0 %copy-start.10 = (s32[16,128]{1,0:T(8,128)S(1)}, s32[16,128]{1,0:T(8,128)}, u32[]{:S(2)}) copy-start(s32[16,128]{1,0:T(8,128)} %smap.1) | copy-start | bytes 24580
  2.2 19.8 %copy-start.2 = (bf16[512,2048]{1,0:T(8,128)(2,1)S(1)}, bf16[512,2048]{1,0:T(8,128)(2,1)}, u32[]{:S(2)}) copy-start(bf16[512,2048]{1,0:T(8,128)(2,1)} %refs_3_) | copy-start | bytes 6291460
  2.2 19.8 %copy-start.3 = (bf16[2,128,512]{2,1,0:T(8,128)(2,1)S(1)}, bf16[2,128,512]{2,1,0:T(8,128)(2,1)}, u32[]{:S(2)}) copy-start(bf16[2,128,512]{2,1,0:T(8,128)(2,1)} %param.22) | copy-start | bytes 786436
  2.2 3.5 %collective-permute-start = (bf16[272,128]{1,0:T(8,128)(2,1)S(1)}, bf16[272,128]{1,0:T(8,128)(2,1)S(1)}, u32[]{:S(2)}, u32[]{:S(2)}) collective-permute-start(bf16[272,128]{1,0:T(8,128)(2,1)S(1)} %get-tuple-element.36), channel_id=1, source_target_pairs={{0,1},{1,0},{2,3},{3,2},{4,5},{5,4},{6,7},{7,6},{8,9},{9,8},{10,11... | collective-permute-start | bytes 208904 | tf_op jit(solution)/shard_map/ppermute | solution.py:89
  3.5 5.9 %collective-permute-start.1 = (bf16[272,128]{1,0:T(8,128)(2,1)S(1)}, bf16[272,128]{1,0:T(8,128)(2,1)S(1)}, u32[]{:S(2)}, u32[]{:S(2)}) collective-permute-start(bf16[272,128]{1,0:T(8,128)(2,1)S(1)} %get-tuple-element.37), channel_id=1, source_target_pairs={{1,2},{2,1},{3,4},{4,3},{5,6},{6,5},{9,10},{10,9},{11,12},{12,11},... | collective-permute-start | bytes 208904 | tf_op jit(solution)/shard_map/ppermute | solution.py:89
  10.3 11.7 %collective-permute-start.4 = (bf16[576,128]{1,0:T(8,128)(2,1)S(1)}, bf16[576,128]{1,0:T(8,128)(2,1)S(1)}, u32[]{:S(2)}, u32[]{:S(2)}) collective-permute-start(bf16[576,128]{1,0:T(8,128)(2,1)S(1)} %get-tuple-element.43), channel_id=1, source_target_pairs={{0,8},{8,0},{16,24},{24,16},{1,9},{9,1},{17,25},{25,17},{2,10},{10... | collective-permute-start | bytes 442376 | tf_op jit(solution)/shard_map/ppermute | solution.py:89
  12.5 9.5 %collective-permute-start.5 = (bf16[576,128]{1,0:T(8,128)(2,1)S(1)}, bf16[576,128]{1,0:T(8,128)(2,1)S(1)}, u32[]{:S(2)}, u32[]{:S(2)}) collective-permute-start(bf16[576,128]{1,0:T(8,128)(2,1)S(1)} %get-tuple-element.44), channel_id=1, source_target_pairs={{8,16},{16,8},{9,17},{17,9},{10,18},{18,10},{11,19},{19,11},{12,20... | collective-permute-start | bytes 442376 | tf_op jit(solution)/shard_map/ppermute | solution.py:89
  15.6 3.6 %collective-permute-start.2 = (bf16[528,128]{1,0:T(8,128)(2,1)S(1)}, bf16[528,128]{1,0:T(8,128)(2,1)S(1)}, u32[]{:S(2)}, u32[]{:S(2)}) collective-permute-start(bf16[528,128]{1,0:T(8,128)(2,1)S(1)} %get-tuple-element.41), channel_id=1, source_target_pairs={{0,8},{8,0},{16,24},{24,16},{1,9},{9,1},{17,25},{25,17},{2,10},{10... | collective-permute-start | bytes 405512 | tf_op jit(solution)/shard_map/ppermute | solution.py:89
  15.7 6.3 %collective-permute-start.3 = (bf16[528,128]{1,0:T(8,128)(2,1)S(1)}, bf16[528,128]{1,0:T(8,128)(2,1)S(1)}, u32[]{:S(2)}, u32[]{:S(2)}) collective-permute-start(bf16[528,128]{1,0:T(8,128)(2,1)S(1)} %get-tuple-element.42), channel_id=1, source_target_pairs={{8,16},{16,8},{9,17},{17,9},{10,18},{18,10},{11,19},{19,11},{12,20... | collective-permute-start | bytes 405512 | tf_op jit(solution)/shard_map/ppermute | solution.py:89
  22.0 9.2 %copy-start.11 = (s32[64,8]{0,1:T(8,128)S(1)}, s32[64,8]{0,1:T(8,128)}, u32[]{:S(2)}) copy-start(s32[64,8]{0,1:T(8,128)} %param.25) | copy-start | bytes 6148
  22.0 9.2 %copy-start.12 = (s32[64,8]{0,1:T(8,128)S(1)}, s32[64,8]{0,1:T(8,128)}, u32[]{:S(2)}) copy-start(s32[64,8]{0,1:T(8,128)} %param.26) | copy-start | bytes 6148
  26.4 0.7 %copy-start.8 = (bf16[16,16,256]{2,1,0:T(8,128)(2,1)}, bf16[16,16,256]{2,1,0:T(8,128)(2,1)S(1)}, u32[]{:S(2)}) copy-start(bf16[16,16,256]{2,1,0:T(8,128)(2,1)S(1)} %get-tuple-element.54.own) | copy-start | bytes 393220
  27.0 30.5 %copy-start.13 = (s32[16,4]{0,1:T(4,128)S(1)}, s32[16,4]{0,1:T(4,128)}, u32[]{:S(2)}) copy-start(s32[16,4]{0,1:T(4,128)} %param.20) | copy-start | bytes 772
  27.0 12.6 %all-to-all-start = ((bf16[32,16,256]{2,1,0:T(8,128)(2,1)}), bf16[32,16,256]{2,1,0:T(8,128)(2,1)}, u32[]{:S(2)}, u32[]{:S(2)}) async-start(bf16[32,16,256]{2,1,0:T(8,128)(2,1)} %bitcast.28), calls=%async_computation | async-start | bytes 524288 | tf_op jit(solution)/shard_map/all_to_all | solution.py:734
  31.2 1.1 %copy-start.4 = (f32[316,2,256]{2,1,0:T(2,128)S(1)}, f32[316,2,256]{2,1,0:T(2,128)}, u32[]{:S(2)}) copy-start(f32[316,2,256]{2,1,0:T(2,128)} %translate.1) | copy-start | bytes 1941508
  42.1 18.5 %all-to-all-start.1 = ((bf16[32,16,256]{2,1,0:T(8,128)(2,1)}), bf16[32,16,256]{2,1,0:T(8,128)(2,1)S(1)}, u32[]{:S(2)}, u32[]{:S(2)}) async-start(bf16[32,16,256]{2,1,0:T(8,128)(2,1)} %far.1), calls=%async_computation.1 | async-start | bytes 524288 | tf_op jit(solution)/shard_map/all_to_all | solution.py:738
  46.8 7.9 %collective-permute-start.6 = (bf16[16,16,256]{2,1,0:T(8,128)(2,1)}, bf16[16,16,256]{2,1,0:T(8,128)(2,1)S(1)}, u32[]{:S(2)}, u32[]{:S(2)}) collective-permute-start(bf16[16,16,256]{2,1,0:T(8,128)(2,1)} %copy-done.8), channel_id=1, source_target_pairs={{0,1},{1,0},{2,3},{3,2},{4,5},{5,4},{6,7},{7,6},{8,9},{9,8},{10,11... | collective-permute-start | bytes 393224 | tf_op jit(solution)/shard_map/ppermute | solution.py:89
  48.0 9.5 %collective-permute-start.7 = (bf16[16,16,256]{2,1,0:T(8,128)(2,1)}, bf16[16,16,256]{2,1,0:T(8,128)(2,1)S(1)}, u32[]{:S(2)}, u32[]{:S(2)}) collective-permute-start(bf16[16,16,256]{2,1,0:T(8,128)(2,1)} %copy-done.8), channel_id=1, source_target_pairs={{1,2},{2,1},{3,4},{4,3},{5,6},{6,5},{9,10},{10,9},{11,12},{12,11},... | collective-permute-start | bytes 393224 | tf_op jit(solution)/shard_map/ppermute | solution.py:89
  57.6 1.0 %copy-start.6 = (bf16[4,256,256]{2,1,0:T(8,128)(2,1)S(1)}, bf16[4,256,256]{2,1,0:T(8,128)(2,1)}, u32[]{:S(2)}) copy-start(bf16[4,256,256]{2,1,0:T(8,128)(2,1)} %param.21) | copy-start | bytes 1572868
  58.6 0.9 %copy-start.9 = (bf16[16,16,256]{2,1,0:T(8,128)(2,1)S(1)}, bf16[16,16,256]{2,1,0:T(8,128)(2,1)}, u32[]{:S(2)}) copy-start(bf16[16,16,256]{2,1,0:T(8,128)(2,1)} %copy-done.8) | copy-start | bytes 393220

commit v10 on v9

--- a/solution.py
+++ b/solution.py
@@ -240,7 +240,7 @@
         lambda *refs: up_body(*refs, cx=cx, cy=cy, groups=groups, slices=slices),
         out_shape=(
             pltpu.HBM(field.shape, f32),
-            pltpu.VMEM((boxes, channels // 2, 2 * unknowns), bf16),
+            pltpu.HBM((boxes, channels // 2, 2 * unknowns), bf16),
             pltpu.HBM((groups, slices, piece_rows, width), bf16),
         ),
         in_specs=[vmem] * 17,
@@ -341,7 +341,11 @@
     )(order, *held(sources, factors))
 
 
-def near_body(lists, own, first, second, blocks, angle, out, cosine, sine, boxes_all, rows):
+def near_body(
+    lists, own, first, second, blocks, angle, radiate, out, cosine, sine, weights, boxes_all, rows, sem
+):
+    fetch = pltpu.make_async_copy(radiate, weights, sem)
+    fetch.start()
     cosine[...] = jnp.cos(angle[...])
     sine[...] = jnp.sin(angle[...])
     boxes, excite, k = own.shape
@@ -360,24 +364,32 @@
             spot = away + jnp.where(away < 0, below, jnp.where(away < boxes, 0, above))
             rows[b * excite : (b + 1) * excite, s * k : (s + 1) * k] = boxes_all[spot]
     out[...] = dot(rows[...], blocks[...]).reshape(out.shape)
-
-
-def near_force(lists, own, first, second, blocks, angle):
+    fetch.wait()
+
+
+def near_force(lists, own, first, second, blocks, angle, radiate):
     boxes, excite, k = own.shape
     slots = lists.shape[0]
     smem = pl.BlockSpec(memory_space=pltpu.SMEM)
     vmem = pl.BlockSpec(memory_space=pltpu.VMEM)
     return pl.pallas_call(
         near_body,
-        out_shape=(pltpu.VMEM((boxes, excite, k), f32),) + (pltpu.VMEM(angle.shape, f32),) * 2,
-        in_specs=[smem] + [vmem] * 5,
-        out_specs=(vmem,) * 3,
+        out_shape=(
+            pltpu.VMEM((boxes, excite, k), f32),
+            pltpu.VMEM(angle.shape, f32),
+            pltpu.VMEM(angle.shape, f32),
+            pltpu.VMEM(radiate.shape, radiate.dtype),
+        ),
+        in_specs=[smem] + [vmem] * 5 + [pl.BlockSpec(memory_space=pltpu.HBM)],
+        out_specs=(vmem,) * 4,
         scratch_shapes=[
             pltpu.VMEM((3 * boxes, excite, k), bf16),
             pltpu.VMEM((boxes * excite, slots * k), bf16),
+            pltpu.SemaphoreType.DMA(()),
         ],
-        compiler_params=params(6), name="near",
-    )(lists, *held(own, first, second, blocks.reshape(slots * k, k), angle))
+        compiler_params=params(6),
+        name="near",
+    )(lists, *left(own, first, second), *held(blocks.reshape(slots * k, k), angle), *left(radiate))
 
 
 def down_body(pieces, near, radiate, interp, cosine, sine, out, shifted, sent, sem, *, groups, slices):
@@ -736,7 +748,9 @@
     factors, order = tables(far_parents.T, far_kind.T, translate)
     combined = far_combine(order, directed, factors, far_parents.shape[0])
     incoming = lax.all_to_all(combined, every, split_axis=0, concat_axis=0, tiled=True)
-    near, cosine, sine = near_force(near_boxes.T, currents, first, second, near_blocks, phase_angle)
+    near, cosine, sine, weights = near_force(
+        near_boxes.T, currents, first, second, near_blocks, phase_angle, weights
+    )
     forcing = down(incoming, near, weights, interp, cosine, sine, groups, slices)
     return (current.reshape(volume_field.shape), forcing)
 

time: 63.3 us -> 63.3 us (level)
  the two profiles are of different devices: /device:TPU:17 before, /device:TPU:8 now
where the time goes in v10:
time: 63.3 us; the launch traced here: 62.8 us
  starting transfers between devices  23.4 us (37%)
  waiting for transfers between devices  18.5 us (29%)
  Pallas kernels  17 us (27%)
  local copies, waits for them, and re-layouts  2.88 us (5%)
  between operations  0.93 us (1%)
    ppermute x8, waiting for transfers between devices, swap(): received.append(lax.ppermute(value, axis, swap_pairs(n, k)))  12.4 us
    ppermute x8, starting transfers between devices, swap(): received.append(lax.ppermute(value, axis, swap_pairs(n, k)))  11.6 us
    all_to_all x1, starting transfers between devices, steps(): lax.all_to_all(pieces.reshape((groups * slices,) + pieces.shape[2:]), eve...  8.69 us
    all_to_all x1, waiting for transfers between devices, steps(): lax.all_to_all(pieces.reshape((groups * slices,) + pieces.shape[2:]), eve...  6.15 us
    pallas_call x1, Pallas kernels, up(): pl.pallas_call(lambda *refs: up_body(*refs, cx=cx, cy=cy, groups=groups,...  4.35 us
    all_to_all x1, starting transfers between devices, steps(): lax.all_to_all(combined, every, split_axis=0, concat_axis=0, tiled=True)  3.17 us
    unnamed x28, local copies, waits for them, and re-layouts  2.88 us
    pallas_call x1, Pallas kernels, tables(): pl.pallas_call(body, out_shape=(pltpu.VMEM((targets * far,) + translate.s...  2.54 us
  transfers between devices with their start and end apart: 10, of which 4 were waited for; matrix products, arithmetic and copies ran while one was open for 0% of the time, Pallas kernels for 9%

profile of v10, /device:TPU:8, one launch (start us, length us, event | category | flops | bytes accessed | tf_op | source)
XLA Modules:
  0.0 62.8 jit_solution(7672106755010025958)
XLA Ops:
  0.6 0.0 copy-start
  0.6 0.0 copy-start.1
  0.7 0.0 copy-start.5
  0.7 1.5 %edges.1 = (bf16[272,128]{1,0:T(8,128)(2,1)S(1)}, bf16[272,128]{1,0:T(8,128)(2,1)S(1)}, f32[16,128]{1,0:T(8,128)S(1)}) custom-call(f32[8]{0:T(128)} %real_table.1, f32[8]{0:T(128)} %loss_table.1, f32[128,16,128]{2,1,0:T(8,128)} %bitcast.12, f32[128,16,128]{2,1,0:T(8,128)} %bitcast.16, s32[4,16,128]{2,1,0:T(8,128)} %kinds.1), custom_call_target="tpu_custom_call" | custom-call | tf_op jit(solution)/shard_map/edges/pallas_call | solution.py:596
  2.1 0.0 copy-start.7
  2.2 0.0 copy-start.8
  2.2 0.0 copy-start.2
  2.2 0.0 copy-start.3
  2.2 1.6 %collective-permute-start = (bf16[272,128]{1,0:T(8,128)(2,1)S(1)}, bf16[272,128]{1,0:T(8,128)(2,1)S(1)}, u32[]{:S(2)}, u32[]{:S(2)}) collective-permute-start(bf16[272,128]{1,0:T(8,128)(2,1)S(1)} %get-tuple-element.37), channel_id=1, source_target_pairs={{0,1},{1,0},{2,3},{3,2},{4,5},{5,4},{6,7},{7,6},{8,9},{9,8},{10,11... | collective-permute-start | bytes 208904 | tf_op jit(solution)/shard_map/ppermute | solution.py:89
  3.8 1.9 %collective-permute-start.1 = (bf16[272,128]{1,0:T(8,128)(2,1)S(1)}, bf16[272,128]{1,0:T(8,128)(2,1)S(1)}, u32[]{:S(2)}, u32[]{:S(2)}) collective-permute-start(bf16[272,128]{1,0:T(8,128)(2,1)S(1)} %get-tuple-element.38), channel_id=1, source_target_pairs={{1,2},{2,1},{3,4},{4,3},{5,6},{6,5},{9,10},{10,9},{11,12},{12,11},... | collective-permute-start | bytes 208904 | tf_op jit(solution)/shard_map/ppermute | solution.py:89
  5.7 0.9 %collective-permute-done.refs_4_ = bf16[272,128]{1,0:T(8,128)(2,1)S(1)} collective-permute-done((bf16[272,128]{1,0:T(8,128)(2,1)S(1)}, bf16[272,128]{1,0:T(8,128)(2,1)S(1)}, u32[]{:S(2)}, u32[]{:S(2)}) %collective-permute-start) | collective-permute-done | bytes 69664 | tf_op jit(solution)/shard_map/ppermute | solution.py:89
  6.6 4.3 %collective-permute-done.1.refs_5_ = bf16[272,128]{1,0:T(8,128)(2,1)S(1)} collective-permute-done((bf16[272,128]{1,0:T(8,128)(2,1)S(1)}, bf16[272,128]{1,0:T(8,128)(2,1)S(1)}, u32[]{:S(2)}, u32[]{:S(2)}) %collective-permute-start.1) | collective-permute-done | bytes 69664 | tf_op jit(solution)/shard_map/ppermute | solution.py:89
  10.8 0.0 copy-done
  10.9 0.9 %first_sweep.1 = (f32[2048,128]{1,0:T(8,128)S(1)}, f32[2,128,128]{2,1,0:T(8,128)S(1)}, f32[2,8,128]{2,1,0:T(8,128)S(1)}, bf16[576,128]{1,0:T(8,128)(2,1)S(1)}, bf16[576,128]{1,0:T(8,128)(2,1)S(1)}) custom-call(f32[16,128]{1,0:T(8,128)S(1)} %get-tuple-element.31.refs_0_, f32[2048,128]{1,0:T(8,128)S(1)} %bitcast.13, f32[2048,128]{1,0:T(8,128)S(1)} %bitcast.17, ...), custom_call_target="tpu_custom_call" | custom-call | tf_op jit(solution)/shard_map/first_sweep/pallas_call | solution.py:681
  11.7 0.1 collective-permute-start.4
  11.8 0.7 %collective-permute-start.5 = (bf16[576,128]{1,0:T(8,128)(2,1)S(1)}, bf16[576,128]{1,0:T(8,128)(2,1)S(1)}, u32[]{:S(2)}, u32[]{:S(2)}) collective-permute-start(bf16[576,128]{1,0:T(8,128)(2,1)S(1)} %get-tuple-element.45), channel_id=1, source_target_pairs={{8,16},{16,8},{9,17},{17,9},{10,18},{18,10},{11,19},{19,11},{12,20... | collective-permute-start | bytes 442376 | tf_op jit(solution)/shard_map/ppermute | solution.py:89
  12.5 0.1 faces.1
  12.6 2.9 %collective-permute-start.2 = (bf16[528,128]{1,0:T(8,128)(2,1)S(1)}, bf16[528,128]{1,0:T(8,128)(2,1)S(1)}, u32[]{:S(2)}, u32[]{:S(2)}) collective-permute-start(bf16[528,128]{1,0:T(8,128)(2,1)S(1)} %get-tuple-element.42), channel_id=1, source_target_pairs={{0,8},{8,0},{16,24},{24,16},{1,9},{9,1},{17,25},{25,17},{2,10},{10... | collective-permute-start | bytes 405512 | tf_op jit(solution)/shard_map/ppermute | solution.py:89
  15.5 0.7 %collective-permute-start.3 = (bf16[528,128]{1,0:T(8,128)(2,1)S(1)}, bf16[528,128]{1,0:T(8,128)(2,1)S(1)}, u32[]{:S(2)}, u32[]{:S(2)}) collective-permute-start(bf16[528,128]{1,0:T(8,128)(2,1)S(1)} %get-tuple-element.43), channel_id=1, source_target_pairs={{8,16},{16,8},{9,17},{17,9},{10,18},{18,10},{11,19},{19,11},{12,20... | collective-permute-start | bytes 405512 | tf_op jit(solution)/shard_map/ppermute | solution.py:89
  16.2 0.0 copy-done.7
  16.2 0.0 copy-done.8
  16.2 1.0 %prepare.1 = (f32[8,2048]{1,0:T(8,128)S(1)}, f32[8,2048]{1,0:T(8,128)S(1)}, bf16[512,2048]{1,0:T(8,128)(2,1)S(1)}, s32[8,2048]{1,0:T(8,128)S(1)}) custom-call(f32[8,2048]{1,0:T(8,128)S(1)} %copy-done.7, s32[16,128]{1,0:T(8,128)S(1)} %copy-done.8), custom_call_target="tpu_custom_call" | custom-call | tf_op jit(solution)/shard_map/prepare/pallas_call | solution.py:65
  17.2 0.0 collective-permute-done.2.refs_7_
  17.2 0.0 collective-permute-done.3.refs_8_
  17.2 0.0 collective-permute-done.4.refs_9_
  17.2 0.0 collective-permute-done.5.refs_10_
  17.2 0.0 copy-start.9
  17.3 0.0 copy-start.10
  17.3 4.4 %up.1 = (f32[2048,128]{1,0:T(8,128)}, bf16[16,16,256]{2,1,0:T(8,128)(2,1)}, bf16[4,8,16,256]{3,2,1,0:T(8,128)(2,1)}) custom-call(f32[16,128]{1,0:T(8,128)S(1)} %get-tuple-element.31.refs_0_, f32[2048,128]{1,0:T(8,128)S(1)} %bitcast.15, f32[2048,128]{1,0:T(8,128)S(1)} %get-tuple-element.39.refs_2_, f32[2,128,128]{2,1,0:T(8,128)S(1)} %get-tuple-element.40.refs_3_, ...), custom_call_target="tpu_custom_call" | custom-call | tf_op jit(solution)/shard_map/up/pallas_call | solution.py:239
  21.6 0.0 copy-start.11
  21.6 8.7 %all-to-all-start = ((bf16[32,16,256]{2,1,0:T(8,128)(2,1)}), bf16[32,16,256]{2,1,0:T(8,128)(2,1)S(1)}, u32[]{:S(2)}, u32[]{:S(2)}) async-start(bf16[32,16,256]{2,1,0:T(8,128)(2,1)} %bitcast.28), calls=%async_computation | async-start | bytes 524288 | tf_op jit(solution)/shard_map/all_to_all | solution.py:746
  30.4 0.0 copy-start.4
  30.4 1.1 %copy-done.4 = f32[316,2,256]{2,1,0:T(2,128)S(1)} copy-done((f32[316,2,256]{2,1,0:T(2,128)S(1)}, f32[316,2,256]{2,1,0:T(2,128)}, u32[]{:S(2)}) %copy-start.4) | copy-done | bytes 647192
  31.5 2.5 %tables.1 = (f32[512,2,256]{2,1,0:T(2,128)S(1)}, s32[512]{0:T(512)S(1)}) custom-call(s32[8,64]{1,0:T(8,128)S(1)} %bitcast.25, s32[8,64]{1,0:T(8,128)S(1)} %bitcast.26, f32[316,2,256]{2,1,0:T(2,128)S(1)} %copy-done.4), custom_call_target="tpu_custom_call" | custom-call | tf_op jit(solution)/shard_map/tables/pallas_call | solution.py:277
  34.0 6.1 %all-to-all-done.refs_1_ = bf16[32,16,256]{2,1,0:T(8,128)(2,1)S(1)} async-done(((bf16[32,16,256]{2,1,0:T(8,128)(2,1)}), bf16[32,16,256]{2,1,0:T(8,128)(2,1)S(1)}, u32[]{:S(2)}, u32[]{:S(2)}) %all-to-all-start) | async-done | bytes 262176 | tf_op jit(solution)/shard_map/all_to_all | solution.py:746
  40.1 2.1 %far.1 = bf16[32,16,256]{2,1,0:T(8,128)(2,1)} custom-call(s32[512]{0:T(512)S(1)} %get-tuple-element.52.refs_0_, bf16[32,16,256]{2,1,0:T(8,128)(2,1)S(1)} %all-to-all-done.refs_1_, f32[512,2,256]{2,1,0:T(2,128)S(1)} %get-tuple-element.54.refs_2_), custom_call_target="tpu_custom_call" | custom-call | tf_op jit(solution)/shard_map/far/pallas_call | solution.py:329
  42.3 3.2 %all-to-all-start.1 = ((bf16[32,16,256]{2,1,0:T(8,128)(2,1)}), bf16[32,16,256]{2,1,0:T(8,128)(2,1)S(1)}, u32[]{:S(2)}, u32[]{:S(2)}) async-start(bf16[32,16,256]{2,1,0:T(8,128)(2,1)} %far.1), calls=%async_computation.1 | async-start | bytes 524288 | tf_op jit(solution)/shard_map/all_to_all | solution.py:750
  45.4 1.5 %collective-permute-start.6 = (bf16[16,16,256]{2,1,0:T(8,128)(2,1)}, bf16[16,16,256]{2,1,0:T(8,128)(2,1)S(1)}, u32[]{:S(2)}, u32[]{:S(2)}) collective-permute-start(bf16[16,16,256]{2,1,0:T(8,128)(2,1)} %get-tuple-element.55.own), channel_id=1, source_target_pairs={{0,1},{1,0},{2,3},{3,2},{4,5},{5,4},{6,7},{7,6},{8,9},{9,8},{10,11... | collective-permute-start | bytes 393224 | tf_op jit(solution)/shard_map/ppermute | solution.py:89
  47.0 2.2 %collective-permute-start.7 = (bf16[16,16,256]{2,1,0:T(8,128)(2,1)}, bf16[16,16,256]{2,1,0:T(8,128)(2,1)S(1)}, u32[]{:S(2)}, u32[]{:S(2)}) collective-permute-start(bf16[16,16,256]{2,1,0:T(8,128)(2,1)} %get-tuple-element.55.own), channel_id=1, source_target_pairs={{1,2},{2,1},{3,4},{4,3},{5,6},{6,5},{9,10},{10,9},{11,12},{12,11},... | collective-permute-start | bytes 393224 | tf_op jit(solution)/shard_map/ppermute | solution.py:89
  49.2 7.2 %collective-permute-done.6.first = bf16[16,16,256]{2,1,0:T(8,128)(2,1)S(1)} collective-permute-done((bf16[16,16,256]{2,1,0:T(8,128)(2,1)}, bf16[16,16,256]{2,1,0:T(8,128)(2,1)S(1)}, u32[]{:S(2)}, u32[]{:S(2)}) %collective-permute-start.6) | collective-permute-done | bytes 131104 | tf_op jit(solution)/shard_map/ppermute | solution.py:89
  56.4 0.0 collective-permute-done.7.second
  56.4 0.6 %copy-done.12 = bf16[16,16,256]{2,1,0:T(8,128)(2,1)} copy-done((bf16[16,16,256]{2,1,0:T(8,128)(2,1)}, bf16[16,16,256]{2,1,0:T(8,128)(2,1)S(1)}, u32[]{:S(2)}) %copy-start.12) | copy-done | bytes 131096
  57.1 0.1 copy-done.13
  57.1 0.0 copy-done.11
  57.1 1.0 %copy-done.6 = bf16[4,256,256]{2,1,0:T(8,128)(2,1)S(1)} copy-done((bf16[4,256,256]{2,1,0:T(8,128)(2,1)S(1)}, bf16[4,256,256]{2,1,0:T(8,128)(2,1)}, u32[]{:S(2)}) %copy-start.6) | copy-done | bytes 524312
  58.2 2.4 %near.1 = (f32[16,16,256]{2,1,0:T(8,128)S(1)}, f32[8,2048]{1,0:T(8,128)S(1)}, f32[8,2048]{1,0:T(8,128)S(1)}, bf16[256,512]{1,0:T(8,128)(2,1)S(1)}) custom-call(s32[4,16]{1,0:T(4,128)S(1)} %bitcast.27, bf16[16,16,256]{2,1,0:T(8,128)(2,1)} %get-tuple-element.55.own, bf16[16,16,256]{2,1,0:T(8,128)(2,1)} %copy-done.12, bf16[16,16,256]{2,1,0:T(8,128)(2,1)} %copy-done.13, ...), custom_call_target="tpu_custom_call" | custom-call | tf_op jit(solution)/shard_map/near/pallas_call | solution.py:375
  60.5 0.0 all-to-all-done.1.refs_0_
  60.5 2.2 %down.1 = f32[16,16,256]{2,1,0:T(8,128)} custom-call(bf16[32,16,256]{2,1,0:T(8,128)(2,1)S(1)} %all-to-all-done.1.refs_0_, f32[16,16,256]{2,1,0:T(8,128)S(1)} %get-tuple-element.56.refs_1_, bf16[256,512]{1,0:T(8,128)(2,1)S(1)} %get-tuple-element.57.refs_2_, bf16[512,2048]{1,0:T(8,128)(2,1)S(1)} %copy-done.2, f32[8,2048]{1,0:T(8,128)S(1)} %get-tuple-element.58.refs_4_, ...), custom_call_target="tpu_custom_call" | custom-call | tf_op jit(solution)/shard_map/down/pallas_call | solution.py:439
  (9 shorter events, 0.0 us)
Async XLA Ops:
  0.6 10.2 %copy-start = (f32[2,16,4,16,128]{4,3,2,1,0:T(8,128)S(1)}, f32[2,16,4,16,128]{4,3,2,1,0:T(8,128)}, u32[]{:S(2)}) copy-start(f32[2,16,4,16,128]{4,3,2,1,0:T(8,128)} %param.14) | copy-start | bytes 3145732
  0.6 10.2 %copy-start.1 = (f32[2,16,4,16,128]{4,3,2,1,0:T(8,128)S(1)}, f32[2,16,4,16,128]{4,3,2,1,0:T(8,128)}, u32[]{:S(2)}) copy-start(f32[2,16,4,16,128]{4,3,2,1,0:T(8,128)} %param.15) | copy-start | bytes 3145732
  0.7 10.2 %copy-start.5 = (s32[4,16,128]{2,1,0:T(8,128)S(1)}, s32[4,16,128]{2,1,0:T(8,128)}, u32[]{:S(2)}) copy-start(s32[4,16,128]{2,1,0:T(8,128)} %kinds.1) | copy-start | bytes 98308
  2.1 14.0 %copy-start.7 = (f32[8,2048]{1,0:T(8,128)S(1)}, f32[8,2048]{1,0:T(8,128)}, u32[]{:S(2)}) copy-start(f32[8,2048]{1,0:T(8,128)} %angle.3) | copy-start | bytes 196612
  2.2 14.0 %copy-start.8 = (s32[16,128]{1,0:T(8,128)S(1)}, s32[16,128]{1,0:T(8,128)}, u32[]{:S(2)}) copy-start(s32[16,128]{1,0:T(8,128)} %smap.1) | copy-start | bytes 24580
  2.2 15.1 %copy-start.2 = (bf16[512,2048]{1,0:T(8,128)(2,1)S(1)}, bf16[512,2048]{1,0:T(8,128)(2,1)}, u32[]{:S(2)}) copy-start(bf16[512,2048]{1,0:T(8,128)(2,1)} %refs_3_) | copy-start | bytes 6291460
  2.2 15.1 %copy-start.3 = (bf16[2,128,512]{2,1,0:T(8,128)(2,1)S(1)}, bf16[2,128,512]{2,1,0:T(8,128)(2,1)}, u32[]{:S(2)}) copy-start(bf16[2,128,512]{2,1,0:T(8,128)(2,1)} %param.22) | copy-start | bytes 786436
  2.2 4.4 %collective-permute-start = (bf16[272,128]{1,0:T(8,128)(2,1)S(1)}, bf16[272,128]{1,0:T(8,128)(2,1)S(1)}, u32[]{:S(2)}, u32[]{:S(2)}) collective-permute-start(bf16[272,128]{1,0:T(8,128)(2,1)S(1)} %get-tuple-element.37), channel_id=1, source_target_pairs={{0,1},{1,0},{2,3},{3,2},{4,5},{5,4},{6,7},{7,6},{8,9},{9,8},{10,11... | collective-permute-start | bytes 208904 | tf_op jit(solution)/shard_map/ppermute | solution.py:89
  3.8 7.1 %collective-permute-start.1 = (bf16[272,128]{1,0:T(8,128)(2,1)S(1)}, bf16[272,128]{1,0:T(8,128)(2,1)S(1)}, u32[]{:S(2)}, u32[]{:S(2)}) collective-permute-start(bf16[272,128]{1,0:T(8,128)(2,1)S(1)} %get-tuple-element.38), channel_id=1, source_target_pairs={{1,2},{2,1},{3,4},{4,3},{5,6},{6,5},{9,10},{10,9},{11,12},{12,11},... | collective-permute-start | bytes 208904 | tf_op jit(solution)/shard_map/ppermute | solution.py:89
  11.7 5.5 %collective-permute-start.4 = (bf16[576,128]{1,0:T(8,128)(2,1)S(1)}, bf16[576,128]{1,0:T(8,128)(2,1)S(1)}, u32[]{:S(2)}, u32[]{:S(2)}) collective-permute-start(bf16[576,128]{1,0:T(8,128)(2,1)S(1)} %get-tuple-element.44), channel_id=1, source_target_pairs={{0,8},{8,0},{16,24},{24,16},{1,9},{9,1},{17,25},{25,17},{2,10},{10... | collective-permute-start | bytes 442376 | tf_op jit(solution)/shard_map/ppermute | solution.py:89
  11.8 5.4 %collective-permute-start.5 = (bf16[576,128]{1,0:T(8,128)(2,1)S(1)}, bf16[576,128]{1,0:T(8,128)(2,1)S(1)}, u32[]{:S(2)}, u32[]{:S(2)}) collective-permute-start(bf16[576,128]{1,0:T(8,128)(2,1)S(1)} %get-tuple-element.45), channel_id=1, source_target_pairs={{8,16},{16,8},{9,17},{17,9},{10,18},{18,10},{11,19},{19,11},{12,20... | collective-permute-start | bytes 442376 | tf_op jit(solution)/shard_map/ppermute | solution.py:89
  12.6 4.6 %collective-permute-start.2 = (bf16[528,128]{1,0:T(8,128)(2,1)S(1)}, bf16[528,128]{1,0:T(8,128)(2,1)S(1)}, u32[]{:S(2)}, u32[]{:S(2)}) collective-permute-start(bf16[528,128]{1,0:T(8,128)(2,1)S(1)} %get-tuple-element.42), channel_id=1, source_target_pairs={{0,8},{8,0},{16,24},{24,16},{1,9},{9,1},{17,25},{25,17},{2,10},{10... | collective-permute-start | bytes 405512 | tf_op jit(solution)/shard_map/ppermute | solution.py:89
  15.5 1.7 %collective-permute-start.3 = (bf16[528,128]{1,0:T(8,128)(2,1)S(1)}, bf16[528,128]{1,0:T(8,128)(2,1)S(1)}, u32[]{:S(2)}, u32[]{:S(2)}) collective-permute-start(bf16[528,128]{1,0:T(8,128)(2,1)S(1)} %get-tuple-element.43), channel_id=1, source_target_pairs={{8,16},{16,8},{9,17},{17,9},{10,18},{18,10},{11,19},{19,11},{12,20... | collective-permute-start | bytes 405512 | tf_op jit(solution)/shard_map/ppermute | solution.py:89
  17.2 13.1 %copy-start.9 = (s32[64,8]{0,1:T(8,128)S(1)}, s32[64,8]{0,1:T(8,128)}, u32[]{:S(2)}) copy-start(s32[64,8]{0,1:T(8,128)} %param.25) | copy-start | bytes 6148
  17.3 13.1 %copy-start.10 = (s32[64,8]{0,1:T(8,128)S(1)}, s32[64,8]{0,1:T(8,128)}, u32[]{:S(2)}) copy-start(s32[64,8]{0,1:T(8,128)} %param.26) | copy-start | bytes 6148
  21.6 35.5 %copy-start.11 = (s32[16,4]{0,1:T(4,128)S(1)}, s32[16,4]{0,1:T(4,128)}, u32[]{:S(2)}) copy-start(s32[16,4]{0,1:T(4,128)} %param.20) | copy-start | bytes 772
  21.6 18.5 %all-to-all-start = ((bf16[32,16,256]{2,1,0:T(8,128)(2,1)}), bf16[32,16,256]{2,1,0:T(8,128)(2,1)S(1)}, u32[]{:S(2)}, u32[]{:S(2)}) async-start(bf16[32,16,256]{2,1,0:T(8,128)(2,1)} %bitcast.28), calls=%async_computation | async-start | bytes 524288 | tf_op jit(solution)/shard_map/all_to_all | solution.py:746
  30.4 1.1 %copy-start.4 = (f32[316,2,256]{2,1,0:T(2,128)S(1)}, f32[316,2,256]{2,1,0:T(2,128)}, u32[]{:S(2)}) copy-start(f32[316,2,256]{2,1,0:T(2,128)} %translate.1) | copy-start | bytes 1941508
  42.3 18.3 %all-to-all-start.1 = ((bf16[32,16,256]{2,1,0:T(8,128)(2,1)}), bf16[32,16,256]{2,1,0:T(8,128)(2,1)S(1)}, u32[]{:S(2)}, u32[]{:S(2)}) async-start(bf16[32,16,256]{2,1,0:T(8,128)(2,1)} %far.1), calls=%async_computation.1 | async-start | bytes 524288 | tf_op jit(solution)/shard_map/all_to_all | solution.py:750
  45.4 11.0 %collective-permute-start.6 = (bf16[16,16,256]{2,1,0:T(8,128)(2,1)}, bf16[16,16,256]{2,1,0:T(8,128)(2,1)S(1)}, u32[]{:S(2)}, u32[]{:S(2)}) collective-permute-start(bf16[16,16,256]{2,1,0:T(8,128)(2,1)} %get-tuple-element.55.own), channel_id=1, source_target_pairs={{0,1},{1,0},{2,3},{3,2},{4,5},{5,4},{6,7},{7,6},{8,9},{9,8},{10,11... | collective-permute-start | bytes 393224 | tf_op jit(solution)/shard_map/ppermute | solution.py:89
  47.0 9.4 %collective-permute-start.7 = (bf16[16,16,256]{2,1,0:T(8,128)(2,1)}, bf16[16,16,256]{2,1,0:T(8,128)(2,1)S(1)}, u32[]{:S(2)}, u32[]{:S(2)}) collective-permute-start(bf16[16,16,256]{2,1,0:T(8,128)(2,1)} %get-tuple-element.55.own), channel_id=1, source_target_pairs={{1,2},{2,1},{3,4},{4,3},{5,6},{6,5},{9,10},{10,9},{11,12},{12,11},... | collective-permute-start | bytes 393224 | tf_op jit(solution)/shard_map/ppermute | solution.py:89
  56.4 0.7 %copy-start.12 = (bf16[16,16,256]{2,1,0:T(8,128)(2,1)}, bf16[16,16,256]{2,1,0:T(8,128)(2,1)S(1)}, u32[]{:S(2)}) copy-start(bf16[16,16,256]{2,1,0:T(8,128)(2,1)S(1)} %collective-permute-done.6.first) | copy-start | bytes 393220
  56.4 0.7 %copy-start.13 = (bf16[16,16,256]{2,1,0:T(8,128)(2,1)}, bf16[16,16,256]{2,1,0:T(8,128)(2,1)S(1)}, u32[]{:S(2)}) copy-start(bf16[16,16,256]{2,1,0:T(8,128)(2,1)S(1)} %collective-permute-done.7.second) | copy-start | bytes 393220
  57.1 1.0 %copy-start.6 = (bf16[4,256,256]{2,1,0:T(8,128)(2,1)S(1)}, bf16[4,256,256]{2,1,0:T(8,128)(2,1)}, u32[]{:S(2)}) copy-start(bf16[4,256,256]{2,1,0:T(8,128)(2,1)} %param.21) | copy-start | bytes 1572868

commit v11 on v10

--- a/solution.py
+++ b/solution.py
@@ -177,7 +177,7 @@
     leaving = pltpu.make_async_copy(fresh, volume, sem)
     leaving.start()
     moves = [leaving]
-    pair = 2
+    pair = 4
     for b in range(0, boxes, pair):
         lanes = slice(b * unknowns, (b + pair) * unknowns)
         picked = dot(cells[...], chosen[:, lanes])
@@ -208,7 +208,7 @@
     leaf = dot(rows[...], radiate[...]).astype(bf16)
     directions = interp.shape[1]
     width = directions // slices
-    tile = max(width, 256)
+    tile = max(width, 512)
     parents = boxes // CHILDREN
     for n in range(0, directions, tile):
         spread = dot(leaf, interp[:, n : n + tile]).reshape(parents, CHILDREN, groups, 2 * group, tile)
@@ -313,7 +313,7 @@
     moves = []
     for part in range(parts):
         first = part * (devices // parts)
-        lax.fori_loop(first, first + devices // parts, one, 0, unroll=4)
+        lax.fori_loop(first, first + devices // parts, one, 0, unroll=8)
         some = pl.ds(first, devices // parts)
         moves.append(pltpu.make_async_copy(sent.at[some], out.at[some], sem.at[part]))
         moves[-1].start()

time: 63.3 us -> 63.2 us (level)
  no operation moved by 1% of the time
where the time goes in v11:
time: 63.2 us; the launch traced here: 62.7 us
  starting transfers between devices  23.4 us (37%)
  waiting for transfers between devices  18.5 us (29%)
  Pallas kernels  16.9 us (27%)
  local copies, waits for them, and re-layouts  2.88 us (5%)
  between operations  0.93 us (1%)
    ppermute x8, waiting for transfers between devices, swap(): received.append(lax.ppermute(value, axis, swap_pairs(n, k)))  12.4 us
    ppermute x8, starting transfers between devices, swap(): received.append(lax.ppermute(value, axis, swap_pairs(n, k)))  11.6 us
    all_to_all x1, starting transfers between devices, steps(): lax.all_to_all(pieces.reshape((groups * slices,) + pieces.shape[2:]), eve...  8.69 us
    all_to_all x1, waiting for transfers between devices, steps(): lax.all_to_all(pieces.reshape((groups * slices,) + pieces.shape[2:]), eve...  6.15 us
    pallas_call x1, Pallas kernels, up(): pl.pallas_call(lambda *refs: up_body(*refs, cx=cx, cy=cy, groups=groups,...  4.35 us
    all_to_all x1, starting transfers between devices, steps(): lax.all_to_all(combined, every, split_axis=0, concat_axis=0, tiled=True)  3.17 us
    unnamed x28, local copies, waits for them, and re-layouts  2.88 us
    pallas_call x1, Pallas kernels, tables(): pl.pallas_call(body, out_shape=(pltpu.VMEM((targets * far,) + translate.s...  2.54 us
  transfers between devices with their start and end apart: 10, of which 4 were waited for; matrix products, arithmetic and copies ran while one was open for 0% of the time, Pallas kernels for 9%

profile of v11, /device:TPU:8, one launch (start us, length us, event | category | flops | bytes accessed | tf_op | source)
XLA Modules:
  0.0 62.7 jit_solution(12405417640198055391)
XLA Ops:
  0.6 0.0 copy-start
  0.6 0.0 copy-start.1
  0.7 0.0 copy-start.5
  0.7 1.5 %edges.1 = (bf16[272,128]{1,0:T(8,128)(2,1)S(1)}, bf16[272,128]{1,0:T(8,128)(2,1)S(1)}, f32[16,128]{1,0:T(8,128)S(1)}) custom-call(f32[8]{0:T(128)} %real_table.1, f32[8]{0:T(128)} %loss_table.1, f32[128,16,128]{2,1,0:T(8,128)} %bitcast.12, f32[128,16,128]{2,1,0:T(8,128)} %bitcast.16, s32[4,16,128]{2,1,0:T(8,128)} %kinds.1), custom_call_target="tpu_custom_call" | custom-call | tf_op jit(solution)/shard_map/edges/pallas_call | solution.py:596
  2.1 0.0 copy-start.7
  2.2 0.0 copy-start.8
  2.2 0.0 copy-start.2
  2.2 0.0 copy-start.3
  2.2 1.6 %collective-permute-start = (bf16[272,128]{1,0:T(8,128)(2,1)S(1)}, bf16[272,128]{1,0:T(8,128)(2,1)S(1)}, u32[]{:S(2)}, u32[]{:S(2)}) collective-permute-start(bf16[272,128]{1,0:T(8,128)(2,1)S(1)} %get-tuple-element.37), channel_id=1, source_target_pairs={{0,1},{1,0},{2,3},{3,2},{4,5},{5,4},{6,7},{7,6},{8,9},{9,8},{10,11... | collective-permute-start | bytes 208904 | tf_op jit(solution)/shard_map/ppermute | solution.py:89
  3.8 1.9 %collective-permute-start.1 = (bf16[272,128]{1,0:T(8,128)(2,1)S(1)}, bf16[272,128]{1,0:T(8,128)(2,1)S(1)}, u32[]{:S(2)}, u32[]{:S(2)}) collective-permute-start(bf16[272,128]{1,0:T(8,128)(2,1)S(1)} %get-tuple-element.38), channel_id=1, source_target_pairs={{1,2},{2,1},{3,4},{4,3},{5,6},{6,5},{9,10},{10,9},{11,12},{12,11},... | collective-permute-start | bytes 208904 | tf_op jit(solution)/shard_map/ppermute | solution.py:89
  5.7 0.9 %collective-permute-done.refs_4_ = bf16[272,128]{1,0:T(8,128)(2,1)S(1)} collective-permute-done((bf16[272,128]{1,0:T(8,128)(2,1)S(1)}, bf16[272,128]{1,0:T(8,128)(2,1)S(1)}, u32[]{:S(2)}, u32[]{:S(2)}) %collective-permute-start) | collective-permute-done | bytes 69664 | tf_op jit(solution)/shard_map/ppermute | solution.py:89
  6.6 4.3 %collective-permute-done.1.refs_5_ = bf16[272,128]{1,0:T(8,128)(2,1)S(1)} collective-permute-done((bf16[272,128]{1,0:T(8,128)(2,1)S(1)}, bf16[272,128]{1,0:T(8,128)(2,1)S(1)}, u32[]{:S(2)}, u32[]{:S(2)}) %collective-permute-start.1) | collective-permute-done | bytes 69664 | tf_op jit(solution)/shard_map/ppermute | solution.py:89
  10.8 0.0 copy-done
  10.8 0.0 copy-done.1
  10.9 0.9 %first_sweep.1 = (f32[2048,128]{1,0:T(8,128)S(1)}, f32[2,128,128]{2,1,0:T(8,128)S(1)}, f32[2,8,128]{2,1,0:T(8,128)S(1)}, bf16[576,128]{1,0:T(8,128)(2,1)S(1)}, bf16[576,128]{1,0:T(8,128)(2,1)S(1)}) custom-call(f32[16,128]{1,0:T(8,128)S(1)} %get-tuple-element.31.refs_0_, f32[2048,128]{1,0:T(8,128)S(1)} %bitcast.13, f32[2048,128]{1,0:T(8,128)S(1)} %bitcast.17, ...), custom_call_target="tpu_custom_call" | custom-call | tf_op jit(solution)/shard_map/first_sweep/pallas_call | solution.py:681
  11.7 0.1 collective-permute-start.4
  11.8 0.7 %collective-permute-start.5 = (bf16[576,128]{1,0:T(8,128)(2,1)S(1)}, bf16[576,128]{1,0:T(8,128)(2,1)S(1)}, u32[]{:S(2)}, u32[]{:S(2)}) collective-permute-start(bf16[576,128]{1,0:T(8,128)(2,1)S(1)} %get-tuple-element.45), channel_id=1, source_target_pairs={{8,16},{16,8},{9,17},{17,9},{10,18},{18,10},{11,19},{19,11},{12,20... | collective-permute-start | bytes 442376 | tf_op jit(solution)/shard_map/ppermute | solution.py:89
  12.5 0.1 faces.1
  12.6 2.9 %collective-permute-start.2 = (bf16[528,128]{1,0:T(8,128)(2,1)S(1)}, bf16[528,128]{1,0:T(8,128)(2,1)S(1)}, u32[]{:S(2)}, u32[]{:S(2)}) collective-permute-start(bf16[528,128]{1,0:T(8,128)(2,1)S(1)} %get-tuple-element.42), channel_id=1, source_target_pairs={{0,8},{8,0},{16,24},{24,16},{1,9},{9,1},{17,25},{25,17},{2,10},{10... | collective-permute-start | bytes 405512 | tf_op jit(solution)/shard_map/ppermute | solution.py:89
  15.5 0.7 %collective-permute-start.3 = (bf16[528,128]{1,0:T(8,128)(2,1)S(1)}, bf16[528,128]{1,0:T(8,128)(2,1)S(1)}, u32[]{:S(2)}, u32[]{:S(2)}) collective-permute-start(bf16[528,128]{1,0:T(8,128)(2,1)S(1)} %get-tuple-element.43), channel_id=1, source_target_pairs={{8,16},{16,8},{9,17},{17,9},{10,18},{18,10},{11,19},{19,11},{12,20... | collective-permute-start | bytes 405512 | tf_op jit(solution)/shard_map/ppermute | solution.py:89
  16.2 0.0 copy-done.7
  16.2 0.0 copy-done.8
  16.2 1.0 %prepare.1 = (f32[8,2048]{1,0:T(8,128)S(1)}, f32[8,2048]{1,0:T(8,128)S(1)}, bf16[512,2048]{1,0:T(8,128)(2,1)S(1)}, s32[8,2048]{1,0:T(8,128)S(1)}) custom-call(f32[8,2048]{1,0:T(8,128)S(1)} %copy-done.7, s32[16,128]{1,0:T(8,128)S(1)} %copy-done.8), custom_call_target="tpu_custom_call" | custom-call | tf_op jit(solution)/shard_map/prepare/pallas_call | solution.py:65
  17.2 0.0 collective-permute-done.2.refs_7_
  17.2 0.0 collective-permute-done.3.refs_8_
  17.2 0.0 collective-permute-done.4.refs_9_
  17.2 0.0 collective-permute-done.5.refs_10_
  17.2 0.0 copy-start.9
  17.3 0.0 copy-start.10
  17.3 4.3 %up.1 = (f32[2048,128]{1,0:T(8,128)}, bf16[16,16,256]{2,1,0:T(8,128)(2,1)}, bf16[4,8,16,256]{3,2,1,0:T(8,128)(2,1)}) custom-call(f32[16,128]{1,0:T(8,128)S(1)} %get-tuple-element.31.refs_0_, f32[2048,128]{1,0:T(8,128)S(1)} %bitcast.15, f32[2048,128]{1,0:T(8,128)S(1)} %get-tuple-element.39.refs_2_, f32[2,128,128]{2,1,0:T(8,128)S(1)} %get-tuple-element.40.refs_3_, ...), custom_call_target="tpu_custom_call" | custom-call | tf_op jit(solution)/shard_map/up/pallas_call | solution.py:239
  21.6 0.0 copy-start.11
  21.6 8.7 %all-to-all-start = ((bf16[32,16,256]{2,1,0:T(8,128)(2,1)}), bf16[32,16,256]{2,1,0:T(8,128)(2,1)S(1)}, u32[]{:S(2)}, u32[]{:S(2)}) async-start(bf16[32,16,256]{2,1,0:T(8,128)(2,1)} %bitcast.28), calls=%async_computation | async-start | bytes 524288 | tf_op jit(solution)/shard_map/all_to_all | solution.py:746
  30.4 0.0 copy-start.4
  30.4 1.1 %copy-done.4 = f32[316,2,256]{2,1,0:T(2,128)S(1)} copy-done((f32[316,2,256]{2,1,0:T(2,128)S(1)}, f32[316,2,256]{2,1,0:T(2,128)}, u32[]{:S(2)}) %copy-start.4) | copy-done | bytes 647192
  31.4 2.5 %tables.1 = (f32[512,2,256]{2,1,0:T(2,128)S(1)}, s32[512]{0:T(512)S(1)}) custom-call(s32[8,64]{1,0:T(8,128)S(1)} %bitcast.25, s32[8,64]{1,0:T(8,128)S(1)} %bitcast.26, f32[316,2,256]{2,1,0:T(2,128)S(1)} %copy-done.4), custom_call_target="tpu_custom_call" | custom-call | tf_op jit(solution)/shard_map/tables/pallas_call | solution.py:277
  34.0 6.1 %all-to-all-done.refs_1_ = bf16[32,16,256]{2,1,0:T(8,128)(2,1)S(1)} async-done(((bf16[32,16,256]{2,1,0:T(8,128)(2,1)}), bf16[32,16,256]{2,1,0:T(8,128)(2,1)S(1)}, u32[]{:S(2)}, u32[]{:S(2)}) %all-to-all-start) | async-done | bytes 262176 | tf_op jit(solution)/shard_map/all_to_all | solution.py:746
  40.1 2.0 %far.1 = bf16[32,16,256]{2,1,0:T(8,128)(2,1)} custom-call(s32[512]{0:T(512)S(1)} %get-tuple-element.52.refs_0_, bf16[32,16,256]{2,1,0:T(8,128)(2,1)S(1)} %all-to-all-done.refs_1_, f32[512,2,256]{2,1,0:T(2,128)S(1)} %get-tuple-element.54.refs_2_), custom_call_target="tpu_custom_call" | custom-call | tf_op jit(solution)/shard_map/far/pallas_call | solution.py:329
  42.1 3.2 %all-to-all-start.1 = ((bf16[32,16,256]{2,1,0:T(8,128)(2,1)}), bf16[32,16,256]{2,1,0:T(8,128)(2,1)S(1)}, u32[]{:S(2)}, u32[]{:S(2)}) async-start(bf16[32,16,256]{2,1,0:T(8,128)(2,1)} %far.1), calls=%async_computation.1 | async-start | bytes 524288 | tf_op jit(solution)/shard_map/all_to_all | solution.py:750
  45.3 1.5 %collective-permute-start.6 = (bf16[16,16,256]{2,1,0:T(8,128)(2,1)}, bf16[16,16,256]{2,1,0:T(8,128)(2,1)S(1)}, u32[]{:S(2)}, u32[]{:S(2)}) collective-permute-start(bf16[16,16,256]{2,1,0:T(8,128)(2,1)} %get-tuple-element.55.own), channel_id=1, source_target_pairs={{0,1},{1,0},{2,3},{3,2},{4,5},{5,4},{6,7},{7,6},{8,9},{9,8},{10,11... | collective-permute-start | bytes 393224 | tf_op jit(solution)/shard_map/ppermute | solution.py:89
  46.9 2.2 %collective-permute-start.7 = (bf16[16,16,256]{2,1,0:T(8,128)(2,1)}, bf16[16,16,256]{2,1,0:T(8,128)(2,1)S(1)}, u32[]{:S(2)}, u32[]{:S(2)}) collective-permute-start(bf16[16,16,256]{2,1,0:T(8,128)(2,1)} %get-tuple-element.55.own), channel_id=1, source_target_pairs={{1,2},{2,1},{3,4},{4,3},{5,6},{6,5},{9,10},{10,9},{11,12},{12,11},... | collective-permute-start | bytes 393224 | tf_op jit(solution)/shard_map/ppermute | solution.py:89
  49.1 7.2 %collective-permute-done.6.first = bf16[16,16,256]{2,1,0:T(8,128)(2,1)S(1)} collective-permute-done((bf16[16,16,256]{2,1,0:T(8,128)(2,1)}, bf16[16,16,256]{2,1,0:T(8,128)(2,1)S(1)}, u32[]{:S(2)}, u32[]{:S(2)}) %collective-permute-start.6) | collective-permute-done | bytes 131104 | tf_op jit(solution)/shard_map/ppermute | solution.py:89
  56.3 0.0 collective-permute-done.7.second
  56.3 0.6 %copy-done.12 = bf16[16,16,256]{2,1,0:T(8,128)(2,1)} copy-done((bf16[16,16,256]{2,1,0:T(8,128)(2,1)}, bf16[16,16,256]{2,1,0:T(8,128)(2,1)S(1)}, u32[]{:S(2)}) %copy-start.12) | copy-done | bytes 131096
  57.0 0.1 copy-done.13
  57.0 1.0 %copy-done.6 = bf16[4,256,256]{2,1,0:T(8,128)(2,1)S(1)} copy-done((bf16[4,256,256]{2,1,0:T(8,128)(2,1)S(1)}, bf16[4,256,256]{2,1,0:T(8,128)(2,1)}, u32[]{:S(2)}) %copy-start.6) | copy-done | bytes 524312
  58.1 2.4 %near.1 = (f32[16,16,256]{2,1,0:T(8,128)S(1)}, f32[8,2048]{1,0:T(8,128)S(1)}, f32[8,2048]{1,0:T(8,128)S(1)}, bf16[256,512]{1,0:T(8,128)(2,1)S(1)}) custom-call(s32[4,16]{1,0:T(4,128)S(1)} %bitcast.27, bf16[16,16,256]{2,1,0:T(8,128)(2,1)} %get-tuple-element.55.own, bf16[16,16,256]{2,1,0:T(8,128)(2,1)} %copy-done.12, bf16[16,16,256]{2,1,0:T(8,128)(2,1)} %copy-done.13, ...), custom_call_target="tpu_custom_call" | custom-call | tf_op jit(solution)/shard_map/near/pallas_call | solution.py:375
  60.4 0.0 all-to-all-done.1.refs_0_
  60.4 2.2 %down.1 = f32[16,16,256]{2,1,0:T(8,128)} custom-call(bf16[32,16,256]{2,1,0:T(8,128)(2,1)S(1)} %all-to-all-done.1.refs_0_, f32[16,16,256]{2,1,0:T(8,128)S(1)} %get-tuple-element.56.refs_1_, bf16[256,512]{1,0:T(8,128)(2,1)S(1)} %get-tuple-element.57.refs_2_, bf16[512,2048]{1,0:T(8,128)(2,1)S(1)} %copy-done.2, f32[8,2048]{1,0:T(8,128)S(1)} %get-tuple-element.58.refs_4_, ...), custom_call_target="tpu_custom_call" | custom-call | tf_op jit(solution)/shard_map/down/pallas_call | solution.py:439
  (9 shorter events, 0.0 us)
Async XLA Ops:
  0.6 10.2 %copy-start = (f32[2,16,4,16,128]{4,3,2,1,0:T(8,128)S(1)}, f32[2,16,4,16,128]{4,3,2,1,0:T(8,128)}, u32[]{:S(2)}) copy-start(f32[2,16,4,16,128]{4,3,2,1,0:T(8,128)} %param.14) | copy-start | bytes 3145732
  0.6 10.2 %copy-start.1 = (f32[2,16,4,16,128]{4,3,2,1,0:T(8,128)S(1)}, f32[2,16,4,16,128]{4,3,2,1,0:T(8,128)}, u32[]{:S(2)}) copy-start(f32[2,16,4,16,128]{4,3,2,1,0:T(8,128)} %param.15) | copy-start | bytes 3145732
  0.7 10.2 %copy-start.5 = (s32[4,16,128]{2,1,0:T(8,128)S(1)}, s32[4,16,128]{2,1,0:T(8,128)}, u32[]{:S(2)}) copy-start(s32[4,16,128]{2,1,0:T(8,128)} %kinds.1) | copy-start | bytes 98308
  2.1 14.0 %copy-start.7 = (f32[8,2048]{1,0:T(8,128)S(1)}, f32[8,2048]{1,0:T(8,128)}, u32[]{:S(2)}) copy-start(f32[8,2048]{1,0:T(8,128)} %angle.3) | copy-start | bytes 196612
  2.2 14.0 %copy-start.8 = (s32[16,128]{1,0:T(8,128)S(1)}, s32[16,128]{1,0:T(8,128)}, u32[]{:S(2)}) copy-start(s32[16,128]{1,0:T(8,128)} %smap.1) | copy-start | bytes 24580
  2.2 15.1 %copy-start.2 = (bf16[512,2048]{1,0:T(8,128)(2,1)S(1)}, bf16[512,2048]{1,0:T(8,128)(2,1)}, u32[]{:S(2)}) copy-start(bf16[512,2048]{1,0:T(8,128)(2,1)} %refs_3_) | copy-start | bytes 6291460
  2.2 15.1 %copy-start.3 = (bf16[2,128,512]{2,1,0:T(8,128)(2,1)S(1)}, bf16[2,128,512]{2,1,0:T(8,128)(2,1)}, u32[]{:S(2)}) copy-start(bf16[2,128,512]{2,1,0:T(8,128)(2,1)} %param.22) | copy-start | bytes 786436
  2.2 4.4 %collective-permute-start = (bf16[272,128]{1,0:T(8,128)(2,1)S(1)}, bf16[272,128]{1,0:T(8,128)(2,1)S(1)}, u32[]{:S(2)}, u32[]{:S(2)}) collective-permute-start(bf16[272,128]{1,0:T(8,128)(2,1)S(1)} %get-tuple-element.37), channel_id=1, source_target_pairs={{0,1},{1,0},{2,3},{3,2},{4,5},{5,4},{6,7},{7,6},{8,9},{9,8},{10,11... | collective-permute-start | bytes 208904 | tf_op jit(solution)/shard_map/ppermute | solution.py:89
  3.8 7.1 %collective-permute-start.1 = (bf16[272,128]{1,0:T(8,128)(2,1)S(1)}, bf16[272,128]{1,0:T(8,128)(2,1)S(1)}, u32[]{:S(2)}, u32[]{:S(2)}) collective-permute-start(bf16[272,128]{1,0:T(8,128)(2,1)S(1)} %get-tuple-element.38), channel_id=1, source_target_pairs={{1,2},{2,1},{3,4},{4,3},{5,6},{6,5},{9,10},{10,9},{11,12},{12,11},... | collective-permute-start | bytes 208904 | tf_op jit(solution)/shard_map/ppermute | solution.py:89
  11.7 5.5 %collective-permute-start.4 = (bf16[576,128]{1,0:T(8,128)(2,1)S(1)}, bf16[576,128]{1,0:T(8,128)(2,1)S(1)}, u32[]{:S(2)}, u32[]{:S(2)}) collective-permute-start(bf16[576,128]{1,0:T(8,128)(2,1)S(1)} %get-tuple-element.44), channel_id=1, source_target_pairs={{0,8},{8,0},{16,24},{24,16},{1,9},{9,1},{17,25},{25,17},{2,10},{10... | collective-permute-start | bytes 442376 | tf_op jit(solution)/shard_map/ppermute | solution.py:89
  11.8 5.4 %collective-permute-start.5 = (bf16[576,128]{1,0:T(8,128)(2,1)S(1)}, bf16[576,128]{1,0:T(8,128)(2,1)S(1)}, u32[]{:S(2)}, u32[]{:S(2)}) collective-permute-start(bf16[576,128]{1,0:T(8,128)(2,1)S(1)} %get-tuple-element.45), channel_id=1, source_target_pairs={{8,16},{16,8},{9,17},{17,9},{10,18},{18,10},{11,19},{19,11},{12,20... | collective-permute-start | bytes 442376 | tf_op jit(solution)/shard_map/ppermute | solution.py:89
  12.6 4.6 %collective-permute-start.2 = (bf16[528,128]{1,0:T(8,128)(2,1)S(1)}, bf16[528,128]{1,0:T(8,128)(2,1)S(1)}, u32[]{:S(2)}, u32[]{:S(2)}) collective-permute-start(bf16[528,128]{1,0:T(8,128)(2,1)S(1)} %get-tuple-element.42), channel_id=1, source_target_pairs={{0,8},{8,0},{16,24},{24,16},{1,9},{9,1},{17,25},{25,17},{2,10},{10... | collective-permute-start | bytes 405512 | tf_op jit(solution)/shard_map/ppermute | solution.py:89
  15.5 1.7 %collective-permute-start.3 = (bf16[528,128]{1,0:T(8,128)(2,1)S(1)}, bf16[528,128]{1,0:T(8,128)(2,1)S(1)}, u32[]{:S(2)}, u32[]{:S(2)}) collective-permute-start(bf16[528,128]{1,0:T(8,128)(2,1)S(1)} %get-tuple-element.43), channel_id=1, source_target_pairs={{8,16},{16,8},{9,17},{17,9},{10,18},{18,10},{11,19},{19,11},{12,20... | collective-permute-start | bytes 405512 | tf_op jit(solution)/shard_map/ppermute | solution.py:89
  17.2 13.1 %copy-start.9 = (s32[64,8]{0,1:T(8,128)S(1)}, s32[64,8]{0,1:T(8,128)}, u32[]{:S(2)}) copy-start(s32[64,8]{0,1:T(8,128)} %param.25) | copy-start | bytes 6148
  17.3 13.1 %copy-start.10 = (s32[64,8]{0,1:T(8,128)S(1)}, s32[64,8]{0,1:T(8,128)}, u32[]{:S(2)}) copy-start(s32[64,8]{0,1:T(8,128)} %param.26) | copy-start | bytes 6148
  21.6 35.4 %copy-start.11 = (s32[16,4]{0,1:T(4,128)S(1)}, s32[16,4]{0,1:T(4,128)}, u32[]{:S(2)}) copy-start(s32[16,4]{0,1:T(4,128)} %param.20) | copy-start | bytes 772
  21.6 18.5 %all-to-all-start = ((bf16[32,16,256]{2,1,0:T(8,128)(2,1)}), bf16[32,16,256]{2,1,0:T(8,128)(2,1)S(1)}, u32[]{:S(2)}, u32[]{:S(2)}) async-start(bf16[32,16,256]{2,1,0:T(8,128)(2,1)} %bitcast.28), calls=%async_computation | async-start | bytes 524288 | tf_op jit(solution)/shard_map/all_to_all | solution.py:746
  30.4 1.1 %copy-start.4 = (f32[316,2,256]{2,1,0:T(2,128)S(1)}, f32[316,2,256]{2,1,0:T(2,128)}, u32[]{:S(2)}) copy-start(f32[316,2,256]{2,1,0:T(2,128)} %translate.1) | copy-start | bytes 1941508
  42.1 18.3 %all-to-all-start.1 = ((bf16[32,16,256]{2,1,0:T(8,128)(2,1)}), bf16[32,16,256]{2,1,0:T(8,128)(2,1)S(1)}, u32[]{:S(2)}, u32[]{:S(2)}) async-start(bf16[32,16,256]{2,1,0:T(8,128)(2,1)} %far.1), calls=%async_computation.1 | async-start | bytes 524288 | tf_op jit(solution)/shard_map/all_to_all | solution.py:750
  45.3 11.0 %collective-permute-start.6 = (bf16[16,16,256]{2,1,0:T(8,128)(2,1)}, bf16[16,16,256]{2,1,0:T(8,128)(2,1)S(1)}, u32[]{:S(2)}, u32[]{:S(2)}) collective-permute-start(bf16[16,16,256]{2,1,0:T(8,128)(2,1)} %get-tuple-element.55.own), channel_id=1, source_target_pairs={{0,1},{1,0},{2,3},{3,2},{4,5},{5,4},{6,7},{7,6},{8,9},{9,8},{10,11... | collective-permute-start | bytes 393224 | tf_op jit(solution)/shard_map/ppermute | solution.py:89
  46.9 9.4 %collective-permute-start.7 = (bf16[16,16,256]{2,1,0:T(8,128)(2,1)}, bf16[16,16,256]{2,1,0:T(8,128)(2,1)S(1)}, u32[]{:S(2)}, u32[]{:S(2)}) collective-permute-start(bf16[16,16,256]{2,1,0:T(8,128)(2,1)} %get-tuple-element.55.own), channel_id=1, source_target_pairs={{1,2},{2,1},{3,4},{4,3},{5,6},{6,5},{9,10},{10,9},{11,12},{12,11},... | collective-permute-start | bytes 393224 | tf_op jit(solution)/shard_map/ppermute | solution.py:89
  56.3 0.7 %copy-start.12 = (bf16[16,16,256]{2,1,0:T(8,128)(2,1)}, bf16[16,16,256]{2,1,0:T(8,128)(2,1)S(1)}, u32[]{:S(2)}) copy-start(bf16[16,16,256]{2,1,0:T(8,128)(2,1)S(1)} %collective-permute-done.6.first) | copy-start | bytes 393220
  56.3 0.7 %copy-start.13 = (bf16[16,16,256]{2,1,0:T(8,128)(2,1)}, bf16[16,16,256]{2,1,0:T(8,128)(2,1)S(1)}, u32[]{:S(2)}) copy-start(bf16[16,16,256]{2,1,0:T(8,128)(2,1)S(1)} %collective-permute-done.7.second) | copy-start | bytes 393220
  57.0 1.0 %copy-start.6 = (bf16[4,256,256]{2,1,0:T(8,128)(2,1)S(1)}, bf16[4,256,256]{2,1,0:T(8,128)(2,1)}, u32[]{:S(2)}) copy-start(bf16[4,256,256]{2,1,0:T(8,128)(2,1)} %param.21) | copy-start | bytes 1572868
